TPU v7x, 32 devices: a whole 2x2x4 slice. The times are simulated.
32 devices in a mesh: fsdp: 8 (over y, x, core), seq: 4 (over z).
Axes of the slice: x: 2, y: 2, z: 4, core: 2. Of those that a mesh axis runs over, the one named last changes fastest.
Arguments:
- tokens: float32 [16, 1568, 1024], P('fsdp', 'seq'), may hold values from -6 to 6
- visible: int32 [16, 1568], P('fsdp'), may hold values from 0 to 1, as said below
- slot_token: int32 [16, 1568], P('fsdp'), may hold values from 0 to 1567, each once within a row
- positions: float32 [1568, 384], replicated, may hold values from -6 to 6
- encoder_pre_gain: bfloat16 [1024], P('fsdp'), may hold values from 0.5 to 1.5
- encoder_pre_shift: bfloat16 [1024], P('fsdp'), may hold values from -1.75 to 1.75
- encoder_joint_weight: bfloat16 [1024, 3072], P('fsdp'), may hold values from -0.1875 to 0.1875
- encoder_query_bias: bfloat16 [1024], P('fsdp'), may hold values from -1.75 to 1.75
- encoder_value_bias: bfloat16 [1024], P('fsdp'), may hold values from -1.75 to 1.75
- encoder_out_weight: bfloat16 [1024, 1024], P('fsdp'), may hold values from -1.5 to 1.5
- encoder_out_bias: bfloat16 [1024], P('fsdp'), may hold values from -1.75 to 1.75
- encoder_mid_gain: bfloat16 [1024], P('fsdp'), may hold values from 0.5 to 1.5
- encoder_mid_shift: bfloat16 [1024], P('fsdp'), may hold values from -1.75 to 1.75
- encoder_expand_weight: bfloat16 [1024, 4096], P('fsdp'), may hold values from -0.1875 to 0.1875
- encoder_expand_bias: bfloat16 [4096], P('fsdp'), may hold values from -1.75 to 1.75
- encoder_contract_weight: bfloat16 [4096, 1024], P('fsdp'), may hold values from -0.09375 to 0.09375
- encoder_contract_bias: bfloat16 [1024], P('fsdp'), may hold values from -1.75 to 1.75
- embed_weight: bfloat16 [1024, 384], P('fsdp'), may hold values from -0.1875 to 0.1875
- embed_bias: bfloat16 [384], P('fsdp'), may hold values from -1.75 to 1.75
- mask_token: bfloat16 [384], P('fsdp'), may hold values from -6 to 6
- predictor_pre_gain: bfloat16 [384], P('fsdp'), may hold values from 0.5 to 1.5
- predictor_pre_shift: bfloat16 [384], P('fsdp'), may hold values from -1.75 to 1.75
- predictor_joint_weight: bfloat16 [384, 1152], P('fsdp'), may hold values from -0.3125 to 0.3125
- predictor_query_bias: bfloat16 [384], P('fsdp'), may hold values from -1.75 to 1.75
- predictor_value_bias: bfloat16 [384], P('fsdp'), may hold values from -1.75 to 1.75
- predictor_out_weight: bfloat16 [384, 384], P('fsdp'), may hold values from -2.5 to 2.5
- predictor_out_bias: bfloat16 [384], P('fsdp'), may hold values from -1.75 to 1.75
- predictor_mid_gain: bfloat16 [384], P('fsdp'), may hold values from 0.5 to 1.5
- predictor_mid_shift: bfloat16 [384], P('fsdp'), may hold values from -1.75 to 1.75
- predictor_expand_weight: bfloat16 [384, 1536], P('fsdp'), may hold values from -0.3125 to 0.3125
- predictor_expand_bias: bfloat16 [1536], P('fsdp'), may hold values from -1.75 to 1.75
- predictor_contract_weight: bfloat16 [1536, 384], P('fsdp'), may hold values from -0.15625 to 0.15625
- predictor_contract_bias: bfloat16 [384], P('fsdp'), may hold values from -1.75 to 1.75
- cotangent: float32 [16, 1568, 384], P('fsdp', 'seq'), may hold values from -6 to 6
Outputs:
- encoded: float32 [16, 1568, 1024], P('fsdp', 'seq')
- predicted: float32 [16, 1568, 384], P('fsdp', 'seq')
- grad_tokens: float32 [16, 1568, 1024], P('fsdp', 'seq')
- grad_encoder_pre_gain: float32 [1024], P('fsdp')
- grad_encoder_pre_shift: float32 [1024], P('fsdp')
- grad_encoder_joint_weight: float32 [1024, 3072], P('fsdp')
- grad_encoder_query_bias: float32 [1024], P('fsdp')
- grad_encoder_value_bias: float32 [1024], P('fsdp')
- grad_encoder_out_weight: float32 [1024, 1024], P('fsdp')
- grad_encoder_out_bias: float32 [1024], P('fsdp')
- grad_encoder_mid_gain: float32 [1024], P('fsdp')
- grad_encoder_mid_shift: float32 [1024], P('fsdp')
- grad_encoder_expand_weight: float32 [1024, 4096], P('fsdp')
- grad_encoder_expand_bias: float32 [4096], P('fsdp')
- grad_encoder_contract_weight: float32 [4096, 1024], P('fsdp')
- grad_encoder_contract_bias: float32 [1024], P('fsdp')
- grad_embed_weight: float32 [1024, 384], P('fsdp')
- grad_embed_bias: float32 [384], P('fsdp')
- grad_mask_token: float32 [384], P('fsdp')
- grad_predictor_pre_gain: float32 [384], P('fsdp')
- grad_predictor_pre_shift: float32 [384], P('fsdp')
- grad_predictor_joint_weight: float32 [384, 1152], P('fsdp')
- grad_predictor_query_bias: float32 [384], P('fsdp')
- grad_predictor_value_bias: float32 [384], P('fsdp')
- grad_predictor_out_weight: float32 [384, 384], P('fsdp')
- grad_predictor_out_bias: float32 [384], P('fsdp')
- grad_predictor_mid_gain: float32 [384], P('fsdp')
- grad_predictor_mid_shift: float32 [384], P('fsdp')
- grad_predictor_expand_weight: float32 [384, 1536], P('fsdp')
- grad_predictor_expand_bias: float32 [1536], P('fsdp')
- grad_predictor_contract_weight: float32 [1536, 384], P('fsdp')
- grad_predictor_contract_bias: float32 [384], P('fsdp')
Inputs may be any that keep to these rules, and one draw needn't show every extreme that they name: In every clip the visible positions form one rectangle of the 14 x 14 spatial grid, the same in all 8 frames, and cover less than half of each frame. `slot_token`: each clip's row is a permutation of the token positions.
All inputs are finite; a program needn't handle non-finite values.
Results may differ from a plain program's by a relative error of at most 0.018.
Values may be sent and summed in bfloat16 or wider, within the bound.
A program may use at most 320 MiB of HBM per device.

v0:
```python
import math

import jax
import jax.numpy as jnp
from jax import lax
from jax.sharding import PartitionSpec as P

HEADS = 16
PHEADS = 12


norm_eps = 1e-06


def norm_layer(value, gain, shift):
    center = value - jnp.mean(value, axis=-1, keepdims=True)
    spread = jnp.mean(center * center, axis=-1, keepdims=True)
    return center * lax.rsqrt(spread + norm_eps) * gain + shift


def exact_gelu(value):
    return jax.nn.gelu(value, approximate=False)


def widen(gathered):
    return [member.astype(jnp.float32) if member.ndim == 1 else member for member in gathered]


def head_layout(model_width, head_count):
    head_size = model_width // head_count
    head_group = math.gcd(head_count, max(1, 128 // head_size))
    return (head_size, head_group, head_count // head_group)


def take_lanes(array, turn_index, head_group, head_size):
    lane_count = head_group * head_size
    block_part = lax.dynamic_slice_in_dim(array, turn_index * lane_count, lane_count, 2)
    return block_part.reshape(array.shape[0], array.shape[1], head_group, head_size)


def score_block(query_block, key_block, keep, score_scale):
    scores = (
        jnp.einsum("cqhd,ckhd->chqk", query_block, key_block, preferred_element_type=jnp.float32)
        * score_scale
    )
    if keep is not None:
        scores = jnp.where(keep[:, None, None, :], scores, -1e30)
    return scores


def attend(queries, keys_all, values_all, keep, head_count):
    clip_count, query_rows, model_width = queries.shape
    head_size, head_group, turn_count = head_layout(model_width, head_count)
    lane_count = head_group * head_size
    score_scale = 1.0 / math.sqrt(head_size)

    def head_turn(turn_index, loop_state):
        mixed, log_total = loop_state
        query_block = take_lanes(queries, turn_index, head_group, head_size)
        key_block = take_lanes(keys_all, turn_index, head_group, head_size)
        value_block = take_lanes(values_all, turn_index, head_group, head_size)
        scores = score_block(query_block, key_block, keep, score_scale)
        row_max = jnp.max(scores, axis=-1, keepdims=True)
        exponent = jnp.exp(scores - row_max)
        row_total = jnp.sum(exponent, axis=-1, keepdims=True)
        chance_low = (exponent / row_total).astype(jnp.bfloat16)
        result = jnp.einsum(
            "chqk,ckhd->cqhd", chance_low, value_block, preferred_element_type=jnp.float32
        )
        result = result.reshape(clip_count, query_rows, lane_count).astype(jnp.bfloat16)
        mixed = lax.dynamic_update_slice_in_dim(mixed, result, turn_index * lane_count, 2)
        log_total = lax.dynamic_update_slice_in_dim(
            log_total, (row_max + jnp.log(row_total))[..., 0], turn_index * head_group, 1
        )
        return (mixed, log_total)

    initial = (
        jnp.zeros(queries.shape, jnp.bfloat16),
        jnp.zeros((clip_count, head_count, query_rows), jnp.float32),
    )
    return lax.fori_loop(0, turn_count, head_turn, initial)


def attend_back(queries, keys_all, values_all, keep, log_total, grad_mixed, head_count):
    clip_count, query_rows, model_width = queries.shape
    key_span = keys_all.shape[1]
    head_size, head_group, turn_count = head_layout(model_width, head_count)
    lane_count = head_group * head_size
    score_scale = 1.0 / math.sqrt(head_size)

    def head_turn(turn_index, loop_state):
        grad_queries, grad_keys, grad_values = loop_state
        query_block = take_lanes(queries, turn_index, head_group, head_size)
        key_block = take_lanes(keys_all, turn_index, head_group, head_size)
        value_block = take_lanes(values_all, turn_index, head_group, head_size)
        grad_block = take_lanes(grad_mixed, turn_index, head_group, head_size)
        scores = score_block(query_block, key_block, keep, score_scale)
        log_block = lax.dynamic_slice_in_dim(log_total, turn_index * head_group, head_group, 1)
        chance = jnp.exp(scores - log_block[..., None])
        grad_chance = jnp.einsum(
            "cqhd,ckhd->chqk", grad_block, value_block, preferred_element_type=jnp.float32
        )
        row_delta = jnp.sum(chance * grad_chance, axis=-1, keepdims=True)
        grad_scores = (chance * (grad_chance - row_delta)).astype(jnp.bfloat16)
        chance_low = chance.astype(jnp.bfloat16)
        part_queries = (
            jnp.einsum(
                "chqk,ckhd->cqhd", grad_scores, key_block, preferred_element_type=jnp.float32
            )
            * score_scale
        )
        part_keys = (
            jnp.einsum(
                "chqk,cqhd->ckhd", grad_scores, query_block, preferred_element_type=jnp.float32
            )
            * score_scale
        )
        part_values = jnp.einsum(
            "chqk,cqhd->ckhd", chance_low, grad_block, preferred_element_type=jnp.float32
        )
        grad_queries = lax.dynamic_update_slice_in_dim(
            grad_queries,
            part_queries.reshape(clip_count, query_rows, lane_count),
            turn_index * lane_count,
            2,
        )
        grad_keys = lax.dynamic_update_slice_in_dim(
            grad_keys,
            part_keys.reshape(clip_count, key_span, lane_count),
            turn_index * lane_count,
            2,
        )
        grad_values = lax.dynamic_update_slice_in_dim(
            grad_values,
            part_values.reshape(clip_count, key_span, lane_count),
            turn_index * lane_count,
            2,
        )
        return (grad_queries, grad_keys, grad_values)

    initial = (
        jnp.zeros((clip_count, query_rows, model_width), jnp.float32),
        jnp.zeros((clip_count, key_span, model_width), jnp.float32),
        jnp.zeros((clip_count, key_span, model_width), jnp.float32),
    )
    return lax.fori_loop(0, turn_count, head_turn, initial)


def block_forward(inputs, weights, keep, head_count, encoder):
    (
        pre_gain,
        pre_shift,
        joint_weight,
        query_bias,
        value_bias,
        out_weight,
        out_bias,
        mid_gain,
        mid_shift,
        expand_weight,
        expand_bias,
        contract_weight,
        contract_bias,
    ) = weights
    model_width = inputs.shape[2]
    normed = norm_layer(inputs, pre_gain, pre_shift).astype(jnp.bfloat16)
    joint = jnp.einsum("cld,de->cle", normed, joint_weight, preferred_element_type=jnp.float32)
    queries = (joint[:, :, :model_width] + query_bias).astype(jnp.bfloat16)
    own_keys = joint[:, :, model_width : 2 * model_width].astype(jnp.bfloat16)
    own_values = (joint[:, :, 2 * model_width :] + value_bias).astype(jnp.bfloat16)
    if encoder:
        keys_all, values_all = (
            lax.all_gather(own_keys, "seq", axis=1, tiled=True),
            lax.all_gather(own_values, "seq", axis=1, tiled=True),
        )
    else:
        keys_all, values_all = (
            lax.all_gather(own_keys, "seq", axis=1, tiled=True),
            lax.all_gather(own_values, "seq", axis=1, tiled=True),
        )
    mixed, log_total = attend(queries, keys_all, values_all, keep, head_count)
    middle = (
        inputs
        + jnp.einsum("cld,de->cle", mixed, out_weight, preferred_element_type=jnp.float32)
        + out_bias
    )
    normed_mid = norm_layer(middle, mid_gain, mid_shift).astype(jnp.bfloat16)
    hidden = (
        jnp.einsum("cld,df->clf", normed_mid, expand_weight, preferred_element_type=jnp.float32)
        + expand_bias
    )
    active = exact_gelu(hidden).astype(jnp.bfloat16)
    outputs = (
        middle
        + jnp.einsum("clf,fd->cld", active, contract_weight, preferred_element_type=jnp.float32)
        + contract_bias
    )
    return (
        outputs,
        (
            normed,
            queries,
            keys_all,
            values_all,
            mixed,
            log_total,
            middle,
            normed_mid,
            hidden,
            active,
        ),
    )


def block_back(grad_out, inputs, weights, saved, keep, head_count, encoder):
    (
        pre_gain,
        pre_shift,
        joint_weight,
        query_bias,
        value_bias,
        out_weight,
        out_bias,
        mid_gain,
        mid_shift,
        expand_weight,
        expand_bias,
        contract_weight,
        contract_bias,
    ) = weights
    normed, queries, keys_all, values_all, mixed, log_total, middle, normed_mid, hidden, active = (
        saved
    )
    grad_y = grad_out.astype(jnp.bfloat16)
    grad_contract = jnp.einsum("clf,cld->fd", active, grad_y, preferred_element_type=jnp.float32)
    grad_contract_bias = jnp.sum(grad_y, axis=(0, 1), dtype=jnp.float32)
    grad_active = jnp.einsum(
        "cld,fd->clf", grad_y, contract_weight, preferred_element_type=jnp.float32
    )
    _, gelu_pull = jax.vjp(exact_gelu, hidden)
    grad_hidden = gelu_pull(grad_active)[0].astype(jnp.bfloat16)
    grad_expand = jnp.einsum(
        "cld,clf->df", normed_mid, grad_hidden, preferred_element_type=jnp.float32
    )
    grad_expand_bias = jnp.sum(grad_hidden, axis=(0, 1), dtype=jnp.float32)
    grad_normed_mid = jnp.einsum(
        "clf,df->cld", grad_hidden, expand_weight, preferred_element_type=jnp.float32
    )
    _, mid_pull = jax.vjp(norm_layer, middle, mid_gain, mid_shift)
    grad_middle_norm, grad_mid_gain, grad_mid_shift = mid_pull(grad_normed_mid)
    grad_middle = grad_out + grad_middle_norm
    grad_att = grad_middle.astype(jnp.bfloat16)
    grad_out_weight = jnp.einsum("cld,cle->de", mixed, grad_att, preferred_element_type=jnp.float32)
    grad_out_bias = jnp.sum(grad_att, axis=(0, 1), dtype=jnp.float32)
    grad_mixed = jnp.einsum(
        "cle,de->cld", grad_att, out_weight, preferred_element_type=jnp.float32
    ).astype(jnp.bfloat16)
    grad_queries, grad_keys, grad_values = attend_back(
        queries, keys_all, values_all, keep, log_total, grad_mixed, head_count
    )
    if encoder:
        grad_keys, grad_values = (
            lax.psum_scatter(grad_keys, "seq", scatter_dimension=1, tiled=True),
            lax.psum_scatter(grad_values, "seq", scatter_dimension=1, tiled=True),
        )
    else:
        grad_keys, grad_values = (
            lax.psum_scatter(grad_keys, "seq", scatter_dimension=1, tiled=True),
            lax.psum_scatter(grad_values, "seq", scatter_dimension=1, tiled=True),
        )
    grad_queries = grad_queries.astype(jnp.bfloat16)
    grad_keys = grad_keys.astype(jnp.bfloat16)
    grad_values = grad_values.astype(jnp.bfloat16)
    grad_joint = jnp.concatenate([grad_queries, grad_keys, grad_values], axis=-1)
    grad_joint_weight = jnp.einsum(
        "cld,cle->de", normed, grad_joint, preferred_element_type=jnp.float32
    )
    grad_query_bias = jnp.sum(grad_queries, axis=(0, 1), dtype=jnp.float32)
    grad_value_bias = jnp.sum(grad_values, axis=(0, 1), dtype=jnp.float32)
    grad_normed = jnp.einsum(
        "cle,de->cld", grad_joint, joint_weight, preferred_element_type=jnp.float32
    )
    _, pre_pull = jax.vjp(norm_layer, inputs, pre_gain, pre_shift)
    grad_input_norm, grad_pre_gain, grad_pre_shift = pre_pull(grad_normed)
    grad_inputs = grad_middle + grad_input_norm
    return (
        grad_inputs,
        [
            grad_pre_gain,
            grad_pre_shift,
            grad_joint_weight,
            grad_query_bias,
            grad_value_bias,
            grad_out_weight,
            grad_out_bias,
            grad_mid_gain,
            grad_mid_shift,
            grad_expand,
            grad_expand_bias,
            grad_contract,
            grad_contract_bias,
        ],
    )


def body(
    tokens,
    visible,
    slot_token,
    positions,
    encoder_pre_gain,
    encoder_pre_shift,
    encoder_joint_weight,
    encoder_query_bias,
    encoder_value_bias,
    encoder_out_weight,
    encoder_out_bias,
    encoder_mid_gain,
    encoder_mid_shift,
    encoder_expand_weight,
    encoder_expand_bias,
    encoder_contract_weight,
    encoder_contract_bias,
    embed_weight,
    embed_bias,
    mask_token,
    predictor_pre_gain,
    predictor_pre_shift,
    predictor_joint_weight,
    predictor_query_bias,
    predictor_value_bias,
    predictor_out_weight,
    predictor_out_bias,
    predictor_mid_gain,
    predictor_mid_shift,
    predictor_expand_weight,
    predictor_expand_bias,
    predictor_contract_weight,
    predictor_contract_bias,
    cotangent,
):
    shard_index = lax.axis_index("seq")
    query_rows = tokens.shape[1]
    slot_visible = jnp.take_along_axis(visible, slot_token, axis=1)
    key_keep = slot_visible > 0
    own_visible = (
        lax.dynamic_slice_in_dim(slot_visible, shard_index * query_rows, query_rows, 1) > 0
    )
    own_tokens = lax.dynamic_slice_in_dim(slot_token, shard_index * query_rows, query_rows, 1)
    slot_code = jnp.take(positions, own_tokens, axis=0)
    gathered = widen(
        (
            lax.all_gather(encoder_pre_gain, "fsdp", axis=0, tiled=True),
            lax.all_gather(encoder_pre_shift, "fsdp", axis=0, tiled=True),
            lax.all_gather(encoder_joint_weight, "fsdp", axis=0, tiled=True),
            lax.all_gather(encoder_query_bias, "fsdp", axis=0, tiled=True),
            lax.all_gather(encoder_value_bias, "fsdp", axis=0, tiled=True),
            lax.all_gather(encoder_out_weight, "fsdp", axis=0, tiled=True),
            lax.all_gather(encoder_out_bias, "fsdp", axis=0, tiled=True),
            lax.all_gather(encoder_mid_gain, "fsdp", axis=0, tiled=True),
            lax.all_gather(encoder_mid_shift, "fsdp", axis=0, tiled=True),
            lax.all_gather(encoder_expand_weight, "fsdp", axis=0, tiled=True),
            lax.all_gather(encoder_expand_bias, "fsdp", axis=0, tiled=True),
            lax.all_gather(encoder_contract_weight, "fsdp", axis=0, tiled=True),
            lax.all_gather(encoder_contract_bias, "fsdp", axis=0, tiled=True),
            lax.all_gather(embed_weight, "fsdp", axis=0, tiled=True),
            lax.all_gather(embed_bias, "fsdp", axis=0, tiled=True),
            lax.all_gather(mask_token, "fsdp", axis=0, tiled=True),
            lax.all_gather(predictor_pre_gain, "fsdp", axis=0, tiled=True),
            lax.all_gather(predictor_pre_shift, "fsdp", axis=0, tiled=True),
            lax.all_gather(predictor_joint_weight, "fsdp", axis=0, tiled=True),
            lax.all_gather(predictor_query_bias, "fsdp", axis=0, tiled=True),
            lax.all_gather(predictor_value_bias, "fsdp", axis=0, tiled=True),
            lax.all_gather(predictor_out_weight, "fsdp", axis=0, tiled=True),
            lax.all_gather(predictor_out_bias, "fsdp", axis=0, tiled=True),
            lax.all_gather(predictor_mid_gain, "fsdp", axis=0, tiled=True),
            lax.all_gather(predictor_mid_shift, "fsdp", axis=0, tiled=True),
            lax.all_gather(predictor_expand_weight, "fsdp", axis=0, tiled=True),
            lax.all_gather(predictor_expand_bias, "fsdp", axis=0, tiled=True),
            lax.all_gather(predictor_contract_weight, "fsdp", axis=0, tiled=True),
            lax.all_gather(predictor_contract_bias, "fsdp", axis=0, tiled=True),
        )
    )
    encoder_weights = gathered[0:13]
    embed_full = gathered[13]
    embed_bias_full = gathered[14]
    mask_full = gathered[15]
    predictor_weights = gathered[16:29]
    encoded, encoder_saved = block_forward(tokens, encoder_weights, key_keep, HEADS, True)
    context = encoded.astype(jnp.bfloat16)
    embedded = (
        jnp.einsum("cld,dp->clp", context, embed_full, preferred_element_type=jnp.float32)
        + embed_bias_full
    )
    pred_input = jnp.where(own_visible[..., None], embedded, mask_full) + slot_code
    predicted, predictor_saved = block_forward(pred_input, predictor_weights, None, PHEADS, False)
    grad_pred_input, predictor_grads = block_back(
        cotangent, pred_input, predictor_weights, predictor_saved, None, PHEADS, False
    )
    grad_mask_token = jnp.sum(jnp.where(own_visible[..., None], 0.0, grad_pred_input), axis=(0, 1))
    grad_embedded = jnp.where(own_visible[..., None], grad_pred_input, 0.0).astype(jnp.bfloat16)
    grad_embed_weight = jnp.einsum(
        "cld,clp->dp", context, grad_embedded, preferred_element_type=jnp.float32
    )
    grad_embed_bias = jnp.sum(grad_embedded, axis=(0, 1), dtype=jnp.float32)
    grad_context = jnp.einsum(
        "clp,dp->cld", grad_embedded, embed_full, preferred_element_type=jnp.float32
    )
    weights_back = widen(
        (
            lax.all_gather(encoder_pre_gain, "fsdp", axis=0, tiled=True),
            lax.all_gather(encoder_pre_shift, "fsdp", axis=0, tiled=True),
            lax.all_gather(encoder_joint_weight, "fsdp", axis=0, tiled=True),
            lax.all_gather(encoder_query_bias, "fsdp", axis=0, tiled=True),
            lax.all_gather(encoder_value_bias, "fsdp", axis=0, tiled=True),
            lax.all_gather(encoder_out_weight, "fsdp", axis=0, tiled=True),
            lax.all_gather(encoder_out_bias, "fsdp", axis=0, tiled=True),
            lax.all_gather(encoder_mid_gain, "fsdp", axis=0, tiled=True),
            lax.all_gather(encoder_mid_shift, "fsdp", axis=0, tiled=True),
            lax.all_gather(encoder_expand_weight, "fsdp", axis=0, tiled=True),
            lax.all_gather(encoder_expand_bias, "fsdp", axis=0, tiled=True),
            lax.all_gather(encoder_contract_weight, "fsdp", axis=0, tiled=True),
            lax.all_gather(encoder_contract_bias, "fsdp", axis=0, tiled=True),
        )
    )
    _, saved_back = block_forward(tokens, weights_back, key_keep, HEADS, True)
    grad_tokens, encoder_grads = block_back(
        grad_context, tokens, weights_back, saved_back, key_keep, HEADS, True
    )
    grads = encoder_grads + [grad_embed_weight, grad_embed_bias, grad_mask_token] + predictor_grads
    summed = (
        lax.psum_scatter(grads[0], "fsdp", scatter_dimension=0, tiled=True),
        lax.psum_scatter(grads[1], "fsdp", scatter_dimension=0, tiled=True),
        lax.psum_scatter(grads[2], "fsdp", scatter_dimension=0, tiled=True),
        lax.psum_scatter(grads[3], "fsdp", scatter_dimension=0, tiled=True),
        lax.psum_scatter(grads[4], "fsdp", scatter_dimension=0, tiled=True),
        lax.psum_scatter(grads[5], "fsdp", scatter_dimension=0, tiled=True),
        lax.psum_scatter(grads[6], "fsdp", scatter_dimension=0, tiled=True),
        lax.psum_scatter(grads[7], "fsdp", scatter_dimension=0, tiled=True),
        lax.psum_scatter(grads[8], "fsdp", scatter_dimension=0, tiled=True),
        lax.psum_scatter(grads[9], "fsdp", scatter_dimension=0, tiled=True),
        lax.psum_scatter(grads[10], "fsdp", scatter_dimension=0, tiled=True),
        lax.psum_scatter(grads[11], "fsdp", scatter_dimension=0, tiled=True),
        lax.psum_scatter(grads[12], "fsdp", scatter_dimension=0, tiled=True),
        lax.psum_scatter(grads[13], "fsdp", scatter_dimension=0, tiled=True),
        lax.psum_scatter(grads[14], "fsdp", scatter_dimension=0, tiled=True),
        lax.psum_scatter(grads[15], "fsdp", scatter_dimension=0, tiled=True),
        lax.psum_scatter(grads[16], "fsdp", scatter_dimension=0, tiled=True),
        lax.psum_scatter(grads[17], "fsdp", scatter_dimension=0, tiled=True),
        lax.psum_scatter(grads[18], "fsdp", scatter_dimension=0, tiled=True),
        lax.psum_scatter(grads[19], "fsdp", scatter_dimension=0, tiled=True),
        lax.psum_scatter(grads[20], "fsdp", scatter_dimension=0, tiled=True),
        lax.psum_scatter(grads[21], "fsdp", scatter_dimension=0, tiled=True),
        lax.psum_scatter(grads[22], "fsdp", scatter_dimension=0, tiled=True),
        lax.psum_scatter(grads[23], "fsdp", scatter_dimension=0, tiled=True),
        lax.psum_scatter(grads[24], "fsdp", scatter_dimension=0, tiled=True),
        lax.psum_scatter(grads[25], "fsdp", scatter_dimension=0, tiled=True),
        lax.psum_scatter(grads[26], "fsdp", scatter_dimension=0, tiled=True),
        lax.psum_scatter(grads[27], "fsdp", scatter_dimension=0, tiled=True),
        lax.psum_scatter(grads[28], "fsdp", scatter_dimension=0, tiled=True),
    )
    totals = (
        lax.psum(summed[0].astype(jnp.bfloat16), "seq").astype(jnp.float32),
        lax.psum(summed[1].astype(jnp.bfloat16), "seq").astype(jnp.float32),
        lax.psum(summed[2].astype(jnp.bfloat16), "seq").astype(jnp.float32),
        lax.psum(summed[3].astype(jnp.bfloat16), "seq").astype(jnp.float32),
        lax.psum(summed[4].astype(jnp.bfloat16), "seq").astype(jnp.float32),
        lax.psum(summed[5].astype(jnp.bfloat16), "seq").astype(jnp.float32),
        lax.psum(summed[6].astype(jnp.bfloat16), "seq").astype(jnp.float32),
        lax.psum(summed[7].astype(jnp.bfloat16), "seq").astype(jnp.float32),
        lax.psum(summed[8].astype(jnp.bfloat16), "seq").astype(jnp.float32),
        lax.psum(summed[9].astype(jnp.bfloat16), "seq").astype(jnp.float32),
        lax.psum(summed[10].astype(jnp.bfloat16), "seq").astype(jnp.float32),
        lax.psum(summed[11].astype(jnp.bfloat16), "seq").astype(jnp.float32),
        lax.psum(summed[12].astype(jnp.bfloat16), "seq").astype(jnp.float32),
        lax.psum(summed[13].astype(jnp.bfloat16), "seq").astype(jnp.float32),
        lax.psum(summed[14].astype(jnp.bfloat16), "seq").astype(jnp.float32),
        lax.psum(summed[15].astype(jnp.bfloat16), "seq").astype(jnp.float32),
        lax.psum(summed[16].astype(jnp.bfloat16), "seq").astype(jnp.float32),
        lax.psum(summed[17].astype(jnp.bfloat16), "seq").astype(jnp.float32),
        lax.psum(summed[18].astype(jnp.bfloat16), "seq").astype(jnp.float32),
        lax.psum(summed[19].astype(jnp.bfloat16), "seq").astype(jnp.float32),
        lax.psum(summed[20].astype(jnp.bfloat16), "seq").astype(jnp.float32),
        lax.psum(summed[21].astype(jnp.bfloat16), "seq").astype(jnp.float32),
        lax.psum(summed[22].astype(jnp.bfloat16), "seq").astype(jnp.float32),
        lax.psum(summed[23].astype(jnp.bfloat16), "seq").astype(jnp.float32),
        lax.psum(summed[24].astype(jnp.bfloat16), "seq").astype(jnp.float32),
        lax.psum(summed[25].astype(jnp.bfloat16), "seq").astype(jnp.float32),
        lax.psum(summed[26].astype(jnp.bfloat16), "seq").astype(jnp.float32),
        lax.psum(summed[27].astype(jnp.bfloat16), "seq").astype(jnp.float32),
        lax.psum(summed[28].astype(jnp.bfloat16), "seq").astype(jnp.float32),
    )
    return (
        encoded,
        predicted,
        grad_tokens,
        totals[0],
        totals[1],
        totals[2],
        totals[3],
        totals[4],
        totals[5],
        totals[6],
        totals[7],
        totals[8],
        totals[9],
        totals[10],
        totals[11],
        totals[12],
        totals[13],
        totals[14],
        totals[15],
        totals[16],
        totals[17],
        totals[18],
        totals[19],
        totals[20],
        totals[21],
        totals[22],
        totals[23],
        totals[24],
        totals[25],
        totals[26],
        totals[27],
        totals[28],
    )


def solution(mesh):
    return jax.shard_map(
        body,
        mesh=mesh,
        in_specs=(
            P("fsdp", "seq", None),
            P("fsdp", None),
            P("fsdp", None),
            P(),
            P("fsdp"),
            P("fsdp"),
            P("fsdp", None),
            P("fsdp"),
            P("fsdp"),
            P("fsdp", None),
            P("fsdp"),
            P("fsdp"),
            P("fsdp"),
            P("fsdp", None),
            P("fsdp"),
            P("fsdp", None),
            P("fsdp"),
            P("fsdp", None),
            P("fsdp"),
            P("fsdp"),
            P("fsdp"),
            P("fsdp"),
            P("fsdp", None),
            P("fsdp"),
            P("fsdp"),
            P("fsdp", None),
            P("fsdp"),
            P("fsdp"),
            P("fsdp"),
            P("fsdp", None),
            P("fsdp"),
            P("fsdp", None),
            P("fsdp"),
            P("fsdp", "seq", None),
        ),
        out_specs=(
            P("fsdp", "seq", None),
            P("fsdp", "seq", None),
            P("fsdp", "seq", None),
            P("fsdp"),
            P("fsdp"),
            P("fsdp", None),
            P("fsdp"),
            P("fsdp"),
            P("fsdp", None),
            P("fsdp"),
            P("fsdp"),
            P("fsdp"),
            P("fsdp", None),
            P("fsdp"),
            P("fsdp", None),
            P("fsdp"),
            P("fsdp", None),
            P("fsdp"),
            P("fsdp"),
            P("fsdp"),
            P("fsdp"),
            P("fsdp", None),
            P("fsdp"),
            P("fsdp"),
            P("fsdp", None),
            P("fsdp"),
            P("fsdp"),
            P("fsdp"),
            P("fsdp", None),
            P("fsdp"),
            P("fsdp", None),
            P("fsdp"),
        ),
        check_vma=False,
    )
```

profile of v0, /device:TPU:0, one launch (start us, length us, event | category | flops | bytes accessed | tf_op | source)
XLA Modules:
  0.0 2922.9 jit_solution(15776845220203250091)
XLA Ops:
  77.5 25.7 gather_fusion.1
  152.8 25.7 all-reduce.32
  222.5 84.9 %all-gather.24.cloned.1.call-done = bf16[2,1568,1024]{2,1,0:T(8,128)(2,1)} async-done(((bf16[2,392,1024]{2,1,0:T(8,128)(2,1)}), bf16[2,1568,1024]{2,1,0:T(8,128)(2,1)}) %all-gather.24.cloned.1.call-update) | async-done | bytes 6422544 | tf_op jit(solution)/shard_map/all_gather | solution.py:173
  318.6 137.3 %while.80 = (s32[]{:T(128)}, bf16[2,392,1024]{1,2,0:T(8,128)(2,1)}, f32[2,16,392]{2,1,0:T(8,128)S(1)}, bf16[2,1568,1024]{1,2,0:T(8,128)(2,1)}, pred[2,1568]{1,0:...) while((s32[]{:T(128)}, bf16[2,392,1024]{1,2,0:T(8,128)(2,1)}, ...), condition=%wide.region_28.29_spmd, body=%wide.region_25.28_spmd.sunk | while | flops 659010048 | bytes 74989632 | solution.py:81
  457.4 130.1 %while.77 = (s32[]{:T(128)}, bf16[2,392,1024]{1,2,0:T(8,128)(2,1)}, bf16[2,1568,1024]{1,2,0:T(8,128)(2,1)}, pred[2,1568]{1,0:T(4,128)(4,1)S(1)}, bf16[2,392,1024...) while((s32[]{:T(128)}, bf16[2,392,1024]{1,2,0:T(8,128)(2,1)}, ...), condition=%wide.region_5.6_spmd, body=%wide.region_2.5_spmd.sunk | while | flops 644261376 | bytes 25767392 | solution.py:81
  614.9 26.5 fusion.70
  641.4 41.6 %add_add_fusion.5 = f32[2,392,1024]{2,1,0:T(8,128)S(1)} fusion(f32[2,392,1024]{2,1,0:T(8,128)} %copy-done.48, bf16[4096,1024]{1,0:T(8,128)(2,1)} %all-gather.30.cloned.1.call-done, f32[2,392,4096]{2,1,0:T(8,128)} %fusion.50, f32[4096]{0:T(1024)S(1)} %bitcast.358, u8[392,4096]{1,0:T(8,128)(4,1)} %get-tuple-element.848, ...), kind=kOutput, calls=%fused_computation.181 | convolution fusion | flops 6806274048 | bytes 30887936 | tf_op jit(solution)/shard_map/clf,fd->cld/dot_general | solution.py:195
  707.2 32.0 %all-gather.32.cloned.1.call-done = bf16[2,1568,384]{2,1,0:T(8,128)(2,1)} async-done(((bf16[2,392,384]{2,1,0:T(8,128)(2,1)}), bf16[2,1568,384]{2,1,0:T(8,128)(2,1)}) %all-gather.32.cloned.1.call-update) | async-done | bytes 2408464 | tf_op jit(solution)/shard_map/all_gather | solution.py:179
  743.6 47.3 %all-gather.34.cloned.1.call-done = bf16[2,1568,384]{2,1,0:T(8,128)(2,1)} async-done(((bf16[2,392,384]{2,1,0:T(8,128)(2,1)}), bf16[2,1568,384]{2,1,0:T(8,128)(2,1)}) %all-gather.34.cloned.1.call-update) | async-done | bytes 2408464 | tf_op jit(solution)/shard_map/all_gather | solution.py:178
  797.0 82.4 %while.78 = (s32[]{:T(128)}, bf16[2,392,384]{1,2,0:T(8,128)(2,1)}, f32[2,12,392]{2,1,0:T(8,128)}, bf16[2,1568,384]{1,2,0:T(8,128)(2,1)}, bf16[2,392,384]{1,2,0:T...) while((s32[]{:T(128)}, bf16[2,392,384]{1,2,0:T(8,128)(2,1)}, ...), condition=%wide.region_13.14_spmd, body=%wide.region_10.13_spmd.sunk | while | flops 673760192 | bytes 143869968 | solution.py:81
  919.1 207.5 %while.79 = (s32[]{:T(128)}, bf16[2,392,384]{2,1,0:T(8,128)(2,1)}, f32[2,1568,384]{2,1,0:T(8,128)}, f32[2,1568,384]{2,1,0:T(8,128)}, bf16[2,1568,384]{1,2,0:T(8,...) while((s32[]{:T(128)}, bf16[2,392,384]{2,1,0:T(8,128)(2,1)}, ...), condition=%wide.region_20.21_spmd, body=%wide.region_18.20_spmd.sunk | while | flops 1633125376 | bytes 216447088 | solution.py:146
  1127.4 31.4 %fusion.30 = f32[2,392,4096]{2,1,0:T(8,128)} fusion(f32[2,392,4096]{2,1,0:T(8,128)} %get-tuple-element.1041, f32[4096]{0:T(1024)S(1)} %bitcast.359, u8[392,4096]{1,0:T(8,128)(4,1)} %get-tuple-element.829, u8[392,4096]{1,0:T(8,128)(4,1)} %get-tuple-element.828), kind=kLoop, calls=%fused_computation.81 | loop fusion | flops 218365952 | bytes 28917760 | tf_op jit(solution)/shard_map/jvp()/erfc | solution.py:22
  1158.8 53.6 %reduce-scatter.16.cloned.1.call-done = f32[2,392,384]{2,1,0:T(8,128)} async-done(((f32[2,1568,384]{2,1,0:T(8,128)}), f32[2,392,384]{2,1,0:T(8,128)}) %reduce-scatter.16.cloned.1.call-update) | async-done | bytes 1204240 | tf_op jit(solution)/shard_map/reduce_scatter | solution.py:269
  1215.2 86.8 %reduce-scatter.14.cloned.1.call-done = f32[2,392,384]{2,1,0:T(8,128)} async-done(((f32[2,1568,384]{2,1,0:T(8,128)}), f32[2,392,384]{2,1,0:T(8,128)}) %reduce-scatter.14.cloned.1.call-update) | async-done | bytes 1204240 | tf_op jit(solution)/shard_map/reduce_scatter | solution.py:268
  1313.9 22.2 convert_reduce_fusion
  1370.7 344.1 %while.81 = (s32[]{:T(128)}, bf16[2,392,1024]{2,1,0:T(8,128)(2,1)}, f32[2,1568,1024]{2,1,0:T(8,128)}, f32[2,1568,1024]{2,1,0:T(8,128)}, bf16[2,1568,1024]{1,2,0:...) while((s32[]{:T(128)}, bf16[2,392,1024]{2,1,0:T(8,128)(2,1)}, ...), condition=%wide.region_35.36_spmd, body=%wide.region_33.35_spmd.sunk | while | flops 1596247552 | bytes 208466032 | solution.py:146
  1741.8 18.8 convolution_bitcast_fusion
  1761.4 16.1 convolution_bitcast_fusion.1
  1777.6 154.0 %reduce-scatter.18.cloned.1.call-done = f32[2,392,1024]{2,1,0:T(8,128)} async-done(((f32[2,1568,1024]{2,1,0:T(8,128)}), f32[2,392,1024]{2,1,0:T(8,128)}) %reduce-scatter.18.cloned.1.call-update) | async-done | bytes 3211280 | tf_op jit(solution)/shard_map/reduce_scatter | solution.py:263
  1934.9 216.0 %reduce-scatter.20.cloned.1.call-done = f32[2,392,1024]{2,1,0:T(8,128)} async-done(((f32[2,1568,1024]{2,1,0:T(8,128)}), f32[2,392,1024]{2,1,0:T(8,128)}) %reduce-scatter.20.cloned.1.call-update) | async-done | bytes 3211280 | tf_op jit(solution)/shard_map/reduce_scatter | solution.py:264
  2173.1 24.6 reduce-scatter.36.cloned.1.call-done
  2199.3 44.4 %reduce-scatter.38.cloned.1.call-done = f32[192,384]{1,0:T(8,128)} async-done(((f32[1536,384]{1,0:T(8,128)}), f32[192,384]{1,0:T(8,128)}) %reduce-scatter.38.cloned.1.call-update) | async-done | bytes 294928 | tf_op jit(solution)/shard_map/reduce_scatter | solution.py:459
  2245.4 40.6 %reduce-scatter.30.cloned.1.call-done = f32[128,384]{1,0:T(8,128)} async-done(((f32[1024,384]{1,0:T(8,128)}), f32[128,384]{1,0:T(8,128)}) %reduce-scatter.30.cloned.1.call-update) | async-done | bytes 196624 | tf_op jit(solution)/shard_map/reduce_scatter | solution.py:445
  2287.6 41.6 %reduce-scatter.32.cloned.1.call-done = f32[48,1152]{1,0:T(8,128)} async-done(((f32[384,1152]{1,0:T(8,128)}), f32[48,1152]{1,0:T(8,128)}) %reduce-scatter.32.cloned.1.call-update) | async-done | bytes 221200 | tf_op jit(solution)/shard_map/reduce_scatter | solution.py:450
  2330.8 53.1 %reduce-scatter.24.cloned.1.call-done = f32[128,1024]{1,0:T(8,128)} async-done(((f32[1024,1024]{1,0:T(8,128)}), f32[128,1024]{1,0:T(8,128)}) %reduce-scatter.24.cloned.1.call-update) | async-done | bytes 524304 | tf_op jit(solution)/shard_map/reduce_scatter | solution.py:437
  2385.7 118.0 %reduce-scatter.28.cloned.1.call-done = f32[512,1024]{1,0:T(8,128)} async-done(((f32[4096,1024]{1,0:T(8,128)}), f32[512,1024]{1,0:T(8,128)}) %reduce-scatter.28.cloned.1.call-update) | async-done | bytes 2097168 | tf_op jit(solution)/shard_map/reduce_scatter | solution.py:443
  2506.5 117.3 %reduce-scatter.26.cloned.1.call-done = f32[128,4096]{1,0:T(8,128)} async-done(((f32[1024,4096]{1,0:T(8,128)}), f32[128,4096]{1,0:T(8,128)}) %reduce-scatter.26.cloned.1.call-update) | async-done | bytes 2097168 | tf_op jit(solution)/shard_map/reduce_scatter | solution.py:441
  2626.4 93.7 %reduce-scatter.22.cloned.1.call-done = f32[128,3072]{1,0:T(8,128)} async-done(((f32[1024,3072]{1,0:T(8,128)}), f32[128,3072]{1,0:T(8,128)}) %reduce-scatter.22.cloned.1.call-update) | async-done | bytes 1572880 | tf_op jit(solution)/shard_map/reduce_scatter | solution.py:434
  2727.1 30.8 %reduce-scatter.34.cloned.1.call-done = f32[48,384]{1,0:T(8,128)} async-done(((f32[384,384]{1,0:T(8,128)}), f32[48,384]{1,0:T(8,128)}) %reduce-scatter.34.cloned.1.call-update) | async-done | bytes 73744 | tf_op jit(solution)/shard_map/reduce_scatter | solution.py:453
  2776.1 25.7 all-reduce.31
  2803.4 21.8 all-reduce.33
  2836.2 68.7 %all-reduce.37.cloned.1.call-done = (bf16[128,3072]{1,0:T(8,128)(2,1)}, bf16[128,1024]{1,0:T(8,128)(2,1)}, bf16[128,4096]{1,0:T(8,128)(2,1)}, bf16[512,1024]{1,0...) async-done(((bf16[128,3072]{1,0:T(8,128)(2,1)}, bf16[128,1024]{1,0:T(8,128)(2,1)}, ...) | async-done | bytes 3649552 | tf_op jit(solution)/shard_map/psum | solution.py:465
  (1035 shorter events, 1327.4 us)
Async XLA Ops:
  7.2 198.5 %copy-start = (f32[1568,384]{1,0:T(8,128)S(1)}, f32[1568,384]{1,0:T(8,128)}, u32[]{:S(2)}) copy-start(f32[1568,384]{1,0:T(8,128)} %param.47) | copy-start | bytes 7225348
  7.2 51.0 %all-gather.20.cloned.1.call-start = ((), (), s32[]{:S(2)}) async-start(), calls=%async_computation.13 | async-start | bytes 7077888 | tf_op jit(solution)/shard_map/all_gather | solution.py:355
  8.0 204.9 %all-gather.22.cloned.1.call-start = ((), (), s32[]{:S(2)}) async-start(), calls=%async_computation.14 | async-start | bytes 8028160 | tf_op jit(solution)/shard_map/all_gather | solution.py:174
  71.9 235.5 %all-gather.24.cloned.1.call-start = ((), (), s32[]{:S(2)}) async-start(), calls=%async_computation.15 | async-start | bytes 8028160 | tf_op jit(solution)/shard_map/all_gather | solution.py:173
  75.4 512.2 %all-gather.26.cloned.1.call-start = ((), (), s32[]{:S(2)}) async-start(), calls=%async_computation.16 | async-start | bytes 2359296 | tf_op jit(solution)/shard_map/all_gather | solution.py:358
  76.0 524.9 %all-gather.28.cloned.1.call-start = ((), (), s32[]{:S(2)}) async-start(), calls=%async_computation.17 | async-start | bytes 9437184 | tf_op jit(solution)/shard_map/all_gather | solution.py:362
  76.5 564.8 %all-gather.30.cloned.1.call-start = ((), (), s32[]{:S(2)}) async-start(), calls=%async_computation.18 | async-start | bytes 9437184 | tf_op jit(solution)/shard_map/all_gather | solution.py:364
  77.1 662.1 %all-gather.32.cloned.1.call-start = ((), (), s32[]{:S(2)}) async-start(), calls=%async_computation.19 | async-start | bytes 3010560 | tf_op jit(solution)/shard_map/all_gather | solution.py:179
  689.4 101.5 %all-gather.34.cloned.1.call-start = ((), (), s32[]{:S(2)}) async-start(), calls=%async_computation.20 | async-start | bytes 3010560 | tf_op jit(solution)/shard_map/all_gather | solution.py:178
  691.6 191.1 %all-gather.36.cloned.1.call-start = ((), (), s32[]{:S(2)}) async-start(), calls=%async_computation.21 | async-start | bytes 1327104 | tf_op jit(solution)/shard_map/all_gather | solution.py:378
  692.4 209.8 %all-gather.38.cloned.1.call-start = ((), (), s32[]{:S(2)}) async-start(), calls=%async_computation.22 | async-start | bytes 1327104 | tf_op jit(solution)/shard_map/all_gather | solution.py:380
  693.0 519.4 %reduce-scatter.16.cloned.1.call-start = ((), (), s32[]{:S(2)}) async-start(), calls=%async_computation.24 | async-start | bytes 6021120 | tf_op jit(solution)/shard_map/reduce_scatter | solution.py:269
  1126.7 175.3 %reduce-scatter.14.cloned.1.call-start = ((), (), s32[]{:S(2)}) async-start(), calls=%async_computation.23 | async-start | bytes 6021120 | tf_op jit(solution)/shard_map/reduce_scatter | solution.py:268
  1127.2 804.3 %reduce-scatter.18.cloned.1.call-start = ((), (), s32[]{:S(2)}) async-start(), calls=%async_computation.25 | async-start | bytes 16056320 | tf_op jit(solution)/shard_map/reduce_scatter | solution.py:263
  1127.4 176.0 %copy-start.68 = (f32[2,392]{1,0:T(2,128)S(1)}, f32[2,392]{1,0:T(2,128)}, u32[]{:S(2)}) copy-start(f32[2,392]{1,0:T(2,128)} %copy-done.67) | copy-start | bytes 9412
  1127.4 176.0 %copy-start.103 = (f32[384]{0:T(512)S(1)}, f32[384]{0:T(512)}, u32[]{:S(2)}) copy-start(f32[384]{0:T(512)} %convert_element_type.470) | copy-start | bytes 4612
  1714.8 436.1 %reduce-scatter.20.cloned.1.call-start = ((), (), s32[]{:S(2)}) async-start(), calls=%async_computation.26 | async-start | bytes 16056320 | tf_op jit(solution)/shard_map/reduce_scatter | solution.py:264
  1715.4 482.3 %reduce-scatter.36.cloned.1.call-start = ((), (), s32[]{:S(2)}) async-start(), calls=%async_computation.34 | async-start | bytes 2654208 | tf_op jit(solution)/shard_map/reduce_scatter | solution.py:457
  1720.9 522.9 %reduce-scatter.38.cloned.1.call-start = ((), (), s32[]{:S(2)}) async-start(), calls=%async_computation.35 | async-start | bytes 2654208 | tf_op jit(solution)/shard_map/reduce_scatter | solution.py:459
  1726.6 559.4 %reduce-scatter.30.cloned.1.call-start = ((), (), s32[]{:S(2)}) async-start(), calls=%async_computation.31 | async-start | bytes 1769472 | tf_op jit(solution)/shard_map/reduce_scatter | solution.py:445
  1731.1 598.2 %reduce-scatter.32.cloned.1.call-start = ((), (), s32[]{:S(2)}) async-start(), calls=%async_computation.32 | async-start | bytes 1990656 | tf_op jit(solution)/shard_map/reduce_scatter | solution.py:450
  1735.3 648.6 %reduce-scatter.24.cloned.1.call-start = ((), (), s32[]{:S(2)}) async-start(), calls=%async_computation.28 | async-start | bytes 4718592 | tf_op jit(solution)/shard_map/reduce_scatter | solution.py:437
  1741.8 762.0 %reduce-scatter.28.cloned.1.call-start = ((), (), s32[]{:S(2)}) async-start(), calls=%async_computation.30 | async-start | bytes 18874368 | tf_op jit(solution)/shard_map/reduce_scatter | solution.py:443
  1760.7 863.0 %reduce-scatter.26.cloned.1.call-start = ((), (), s32[]{:S(2)}) async-start(), calls=%async_computation.29 | async-start | bytes 18874368 | tf_op jit(solution)/shard_map/reduce_scatter | solution.py:441
  1777.5 377.0 %copy-start.74 = (f32[2,392]{1,0:T(2,128)S(1)}, f32[2,392]{1,0:T(2,128)}, u32[]{:S(2)}) copy-start(f32[2,392]{1,0:T(2,128)} %copy-done.73) | copy-start | bytes 9412
  1777.5 377.0 %copy-start.85 = (f32[8,1,128]{2,1,0:T(1,128)S(1)}, f32[8,1,128]{2,1,0:T(1,128)}, u32[]{:S(2)}) copy-start(f32[8,1,128]{2,1,0:T(1,128)} %copy-done.84) | copy-start | bytes 12292
  1777.5 377.0 %copy-start.87 = (f32[2,392]{1,0:T(2,128)S(1)}, f32[2,392]{1,0:T(2,128)}, u32[]{:S(2)}) copy-start(f32[2,392]{1,0:T(2,128)} %copy-done.86) | copy-start | bytes 9412
  1777.5 377.0 %copy-start.138 = (f32[8,1,128]{2,1,0:T(1,128)S(1)}, f32[8,1,128]{2,1,0:T(1,128)}, u32[]{:S(2)}) copy-start(f32[8,1,128]{2,1,0:T(1,128)} %copy-done.137) | copy-start | bytes 12292
  1777.5 942.5 %reduce-scatter.22.cloned.1.call-start = ((), (), s32[]{:S(2)}) async-start(), calls=%async_computation.27 | async-start | bytes 14155776 | tf_op jit(solution)/shard_map/reduce_scatter | solution.py:434
  2167.5 590.4 %reduce-scatter.34.cloned.1.call-start = ((), (), s32[]{:S(2)}) async-start(), calls=%async_computation.33 | async-start | bytes 663552 | tf_op jit(solution)/shard_map/reduce_scatter | solution.py:453
  2170.2 734.6 %all-reduce.37.cloned.1.call-start = ((), (), s32[]{:S(2)}) async-start(), calls=%async_computation.36 | async-start | bytes 7299072 | tf_op jit(solution)/shard_map/psum | solution.py:465
  2506.5 216.1 %copy-start.51 = (bf16[2,392,384]{2,1,0:T(8,128)(2,1)S(1)}, bf16[2,392,384]{2,1,0:T(8,128)(2,1)}, u32[]{:S(2)}) copy-start(bf16[2,392,384]{2,1,0:T(8,128)(2,1)} %get-tuple-element.706) | copy-start | bytes 1806340
  (222 other events, 3769.9 us)
Sparse Core Ops, SparseCore 0:
  9.9 48.2 all-gather.19
  72.0 117.4 all-gather.21
  191.7 115.6 all-gather.23
  309.2 26.0 all-gather.25
  337.0 54.3 all-gather.27
  393.2 54.3 all-gather.29
  689.5 49.6 all-gather.31
  740.8 50.0 all-gather.33
  792.8 22.8 all-gather.35
  817.5 24.0 all-gather.37
  1126.8 85.5 reduce-scatter.15
  1214.6 87.3 reduce-scatter.13
  1714.9 216.5 reduce-scatter.17
  1933.8 217.1 reduce-scatter.19
  2154.1 43.5 reduce-scatter.35
  2201.3 42.4 reduce-scatter.37
  2247.5 38.4 reduce-scatter.29
  2289.8 39.3 reduce-scatter.31
  2332.6 51.3 reduce-scatter.23
  2387.8 115.9 reduce-scatter.27
  2507.7 115.9 reduce-scatter.25
  2627.6 92.4 reduce-scatter.21
  2723.5 34.3 reduce-scatter.33
  2763.3 141.5 all-reduce.36
where the time goes:
time: 2940 us; the launch traced here: 2920 us
  waiting for transfers between devices  1320 us (45%)
  matrix products  752 us (26%)
  local copies, waits for them, and re-layouts  420 us (14%)
  other arithmetic  212 us (7%)
  blocking collectives  183 us (6%)
    reduce_scatter x2, waiting for transfers between devices, block_back(): lax.psum_scatter(grad_values, 'seq', scatter_dimension=1, tiled=True)  270 us
    reduce_scatter x2, waiting for transfers between devices, block_back(): lax.psum_scatter(grad_keys, 'seq', scatter_dimension=1, tiled=True)  241 us
    all_gather x2, waiting for transfers between devices, block_forward(): lax.all_gather(own_keys, 'seq', axis=1, tiled=True)  132 us
    dot_general x19, matrix products, head_turn(): jnp.einsum('chqk,ckhd->cqhd', chance_low, value_block, preferred_element_...  119 us
    reduce_scatter x1, waiting for transfers between devices, body(): lax.psum_scatter(grads[11], 'fsdp', scatter_dimension=0, tiled=True)  118 us
    reduce_scatter x1, waiting for transfers between devices, body(): lax.psum_scatter(grads[9], 'fsdp', scatter_dimension=0, tiled=True)  117 us
    dot_general x22, matrix products, score_block(): jnp.einsum('cqhd,ckhd->chqk', query_block, key_block, preferred_element_t...  108 us
    dynamic_slice x93, local copies, waits for them, and re-layouts, take_lanes(): lax.dynamic_slice_in_dim(array, turn_index * lane_count, lane_count, 2)  96 us
  transfers between devices with their start and end apart: 24, of which 18 were waited for; matrix products, arithmetic and copies ran while one was open for 21% of the time, Pallas kernels for 0%

commit v1 on v0

v1 whole, which is shorter than its diff:
```python
import functools
import math

import jax
import jax.numpy as jnp
from jax import lax
from jax.experimental import pallas as pl
from jax.experimental.pallas import tpu as pltpu
from jax.sharding import PartitionSpec as P

HEADS = 16
PHEADS = 12

f32 = jnp.float32
bf16 = jnp.bfloat16
norm_eps = 1e-06
LOG2E = math.log2(math.e)
NN = (((1,), (0,)), ((), ()))
NT = (((1,), (1,)), ((), ()))
TN = (((0,), (0,)), ((), ()))
VMEM_LIMIT = 60 * 2**20


def mm(left, right, dims=NN):
    return lax.dot_general(left, right, dims, preferred_element_type=f32)


def norm_parts(value):
    center = value - jnp.mean(value, axis=-1, keepdims=True)
    spread = jnp.mean(center * center, axis=-1, keepdims=True)
    scale = lax.rsqrt(spread + norm_eps)
    return center * scale, scale


def norm_layer(value, gain, shift):
    unit, _ = norm_parts(value)
    return (unit * gain + shift).astype(bf16)


def norm_back(value, gain, grad):
    unit, scale = norm_parts(value)
    grad_gain = jnp.sum(grad * unit, axis=0)
    grad_shift = jnp.sum(grad, axis=0)
    inner = grad * gain
    inner = inner - jnp.mean(inner, axis=-1, keepdims=True) - unit * jnp.mean(
        inner * unit, axis=-1, keepdims=True
    )
    return scale * inner, grad_gain, grad_shift


def gelu_parts(hidden):
    cdf = 0.5 * (1.0 + lax.erf(hidden * math.sqrt(0.5)))
    return cdf


def gelu(hidden):
    return (hidden * gelu_parts(hidden)).astype(bf16)


def gelu_slope(hidden):
    pdf = jnp.exp(-0.5 * hidden * hidden) * (1.0 / math.sqrt(2.0 * math.pi))
    return gelu_parts(hidden) + hidden * pdf


def forward_kernel(scale, head_size, q_ref, k_ref, v_ref, *rest):
    if len(rest) == 2:
        bias_ref, o_ref = rest
    else:
        bias_ref, o_ref = None, rest[0]
    head = pl.program_id(2)
    query = q_ref[0]
    lane = lax.broadcasted_iota(jnp.int32, query.shape, 1)
    mine = (lane // head_size) == head
    own_query = jnp.where(mine, query, jnp.zeros_like(query))
    scores = mm(own_query, k_ref[0], NT) * (scale * LOG2E)
    if bias_ref is not None:
        scores = scores + bias_ref[0]
    top = jnp.max(scores, axis=1, keepdims=True)
    weight = jnp.exp2(scores - top)
    total = jnp.sum(weight, axis=1, keepdims=True)
    result = (mm(weight.astype(bf16), v_ref[0]) / total).astype(bf16)

    @pl.when(head == 0)
    def _():
        o_ref[0] = result

    @pl.when(head > 0)
    def _():
        o_ref[0] = jnp.where(mine, result, o_ref[0])


def attend(queries, joined, head_size, bias):
    clips, rows, width = queries.shape
    keys = joined.shape[1]
    groups = width // 128
    in_specs = [
        pl.BlockSpec((1, rows, 128), lambda c, g, h: (c, 0, g)),
        pl.BlockSpec((1, keys, 128), lambda c, g, h: (c, 0, g)),
        pl.BlockSpec((1, keys, 128), lambda c, g, h: (c, 0, g + groups)),
    ]
    operands = [queries, joined, joined]
    if bias is not None:
        in_specs.append(pl.BlockSpec((1, 1, keys), lambda c, g, h: (c, 0, 0)))
        operands.append(bias)
    cells = clips * rows * keys * (width // head_size)
    return pl.pallas_call(
        functools.partial(forward_kernel, 1.0 / math.sqrt(head_size), head_size),
        grid=(clips, groups, 128 // head_size),
        in_specs=in_specs,
        out_specs=pl.BlockSpec((1, rows, 128), lambda c, g, h: (c, 0, g)),
        out_shape=jax.ShapeDtypeStruct((clips, rows, width), bf16),
        compiler_params=pltpu.CompilerParams(vmem_limit_bytes=VMEM_LIMIT),
        cost_estimate=pl.CostEstimate(
            flops=cells * 1024, bytes_accessed=4 * clips * keys * width, transcendentals=cells
        ),
        name="attend",
    )(*operands)


def backward_kernel(scale, head_size, q_ref, k_ref, v_ref, g_ref, *rest):
    if len(rest) == 7:
        bias_ref = rest[0]
        rest = rest[1:]
    else:
        bias_ref = None
    dq_ref, dk_ref, dv_ref, dq_sum, dk_sum, dv_sum = rest
    part = pl.program_id(2)
    head = pl.program_id(3)
    query, key, value, grad = q_ref[0], k_ref[0], v_ref[0], g_ref[0]
    lane = lax.broadcasted_iota(jnp.int32, query.shape, 1)
    mine = (lane // head_size) == head
    zero = jnp.zeros_like(query)
    own_query = jnp.where(mine, query, zero)
    own_grad = jnp.where(mine, grad, zero)
    key_lane = lax.broadcasted_iota(jnp.int32, key.shape, 1)
    own_key = jnp.where((key_lane // head_size) == head, key, jnp.zeros_like(key))
    scores = mm(own_query, key, NT) * (scale * LOG2E)
    if bias_ref is not None:
        scores = scores + bias_ref[0]
    top = jnp.max(scores, axis=1, keepdims=True)
    weight = jnp.exp2(scores - top)
    total = jnp.sum(weight, axis=1, keepdims=True)
    chance = weight * (1.0 / total)
    grad_chance = mm(own_grad, value, NT)
    delta = jnp.sum(chance * grad_chance, axis=1, keepdims=True)
    grad_scores = (chance * (grad_chance - delta)).astype(bf16)
    part_q = mm(grad_scores, own_key)
    part_v = mm(own_grad, chance.astype(bf16), TN)
    part_k = mm(own_query, grad_scores, TN)

    @pl.when(head == 0)
    def _():
        dq_sum[...] = part_q

    @pl.when(head > 0)
    def _():
        dq_sum[...] += part_q

    @pl.when((head == 0) & (part == 0))
    def _():
        dk_sum[...] = part_k
        dv_sum[...] = part_v

    @pl.when((head > 0) | (part > 0))
    def _():
        dk_sum[...] += part_k
        dv_sum[...] += part_v

    last_head = head == pl.num_programs(3) - 1

    @pl.when(last_head)
    def _():
        dq_ref[0] = (dq_sum[...] * scale).astype(bf16)

    @pl.when(last_head & (part == pl.num_programs(2) - 1))
    def _():
        dk_ref[0] = (dk_sum[...] * scale).T.astype(bf16)
        dv_ref[0] = dv_sum[...].T.astype(bf16)


def attend_back(queries, keys, values, grad_mixed, head_size, bias, parts):
    clips, length, width = queries.shape
    lanes = min(width, 128)
    groups = width // lanes
    rows = length // parts
    by_query = pl.BlockSpec((1, rows, lanes), lambda c, g, r, h: (c, r, g))
    by_key = pl.BlockSpec((1, length, lanes), lambda c, g, r, h: (c, 0, g))
    in_specs = [by_query, by_key, by_key, by_query]
    operands = [queries, keys, values, grad_mixed]
    if bias is not None:
        in_specs.append(pl.BlockSpec((1, 1, length), lambda c, g, r, h: (c, 0, 0)))
        operands.append(bias)
    cells = clips * length * length * (width // head_size)
    shape = jax.ShapeDtypeStruct((clips, length, width), bf16)
    return pl.pallas_call(
        functools.partial(backward_kernel, 1.0 / math.sqrt(head_size), head_size),
        grid=(clips, groups, parts, lanes // head_size),
        in_specs=in_specs,
        out_specs=[by_query, by_key, by_key],
        out_shape=[shape, shape, shape],
        scratch_shapes=[
            pltpu.VMEM((rows, lanes), f32),
            pltpu.VMEM((lanes, length), f32),
            pltpu.VMEM((lanes, length), f32),
        ],
        compiler_params=pltpu.CompilerParams(vmem_limit_bytes=VMEM_LIMIT),
        cost_estimate=pl.CostEstimate(
            flops=cells * 2560, bytes_accessed=14 * clips * length * width, transcendentals=cells
        ),
        name="attend_back",
    )(*operands)


def heads_from_slots(array, shards):
    if shards == 1:
        return array
    return lax.all_to_all(array, "seq", split_axis=2, concat_axis=1, tiled=True)


def slots_from_heads(array, shards):
    if shards == 1:
        return array
    return lax.all_to_all(array, "seq", split_axis=2, concat_axis=3, tiled=True)


def own_columns(joint_weight, query_bias, value_bias, shards, shard):
    width = joint_weight.shape[0]
    own = width // shards
    weight = lax.dynamic_slice_in_dim(joint_weight.reshape(width, 3, width), shard * own, own, 2)
    bias_q = lax.dynamic_slice_in_dim(query_bias, shard * own, own, 0)
    bias_v = lax.dynamic_slice_in_dim(value_bias, shard * own, own, 0)
    return weight, bias_q, bias_v


def attention_back(grad_mixed, normed_all, weights, head_size, bias, parts, shards, shard):
    joint_weight, query_bias, value_bias = weights
    clips, length, width = normed_all.shape
    own_weight, bias_q, bias_v = own_columns(joint_weight, query_bias, value_bias, shards, shard)
    own = own_weight.shape[2]
    flat = normed_all.reshape(clips * length, width)
    queries = (mm(flat, own_weight[:, 0]) + bias_q).astype(bf16).reshape(clips, length, own)
    keys = mm(flat, own_weight[:, 1]).astype(bf16).reshape(clips, length, own)
    values = (mm(flat, own_weight[:, 2]) + bias_v).astype(bf16).reshape(clips, length, own)
    own_grad = heads_from_slots(grad_mixed, shards)
    grads = attend_back(queries, keys, values, own_grad, head_size, bias, parts)
    flat_grads = [member.reshape(clips * length, own) for member in grads]
    grad_weight = [mm(flat, member, TN).astype(bf16) for member in flat_grads]
    grad_query_bias = jnp.sum(flat_grads[0].astype(f32), axis=0)
    grad_value_bias = jnp.sum(flat_grads[2].astype(f32), axis=0)
    back = slots_from_heads(jnp.stack(grads), shards)
    return back, jnp.stack(grad_weight, axis=1), grad_query_bias, grad_value_bias


def joint_back(grad_joint, joint_weight):
    _, clips, rows, width = grad_joint.shape
    total = None
    for index in range(3):
        term = mm(
            grad_joint[index].reshape(clips * rows, width),
            joint_weight[:, index * width : (index + 1) * width],
            NT,
        )
        total = term if total is None else total + term
    return total


def split_packed(packed, sizes):
    out = []
    at = 0
    for size in sizes:
        out.append(packed[:, at : at + size].reshape(-1).astype(f32))
        at += size
    return out


def gather(array):
    return lax.all_gather(array, "fsdp", axis=0, tiled=True)


def scatter(array):
    return lax.psum_scatter(array, "fsdp", scatter_dimension=0, tiled=True)


def across_slots(array):
    return lax.psum(array, "seq").astype(f32)


def body(
    fsdp_size,
    seq_size,
    tokens,
    visible,
    slot_token,
    positions,
    encoder_pre_gain,
    encoder_pre_shift,
    encoder_joint_weight,
    encoder_query_bias,
    encoder_value_bias,
    encoder_out_weight,
    encoder_out_bias,
    encoder_mid_gain,
    encoder_mid_shift,
    encoder_expand_weight,
    encoder_expand_bias,
    encoder_contract_weight,
    encoder_contract_bias,
    embed_weight,
    embed_bias,
    mask_token,
    predictor_pre_gain,
    predictor_pre_shift,
    predictor_joint_weight,
    predictor_query_bias,
    predictor_value_bias,
    predictor_out_weight,
    predictor_out_bias,
    predictor_mid_gain,
    predictor_mid_shift,
    predictor_expand_weight,
    predictor_expand_bias,
    predictor_contract_weight,
    predictor_contract_bias,
    cotangent,
):
    shard = lax.axis_index("seq")
    clips, slots, width = tokens.shape
    span = visible.shape[1]
    rows = clips * slots
    small_width = cotangent.shape[2]
    head_size = width // HEADS
    small_head = small_width // PHEADS

    vectors = (
        encoder_pre_gain,
        encoder_pre_shift,
        encoder_query_bias,
        encoder_value_bias,
        encoder_out_bias,
        encoder_mid_gain,
        encoder_mid_shift,
        encoder_expand_bias,
        encoder_contract_bias,
        embed_bias,
        mask_token,
        predictor_pre_gain,
        predictor_pre_shift,
        predictor_query_bias,
        predictor_value_bias,
        predictor_out_bias,
        predictor_mid_gain,
        predictor_mid_shift,
        predictor_expand_bias,
        predictor_contract_bias,
    )
    sizes = [member.shape[0] for member in vectors]
    packed = lax.all_gather(jnp.concatenate(vectors), "fsdp", axis=0, tiled=False)
    (
        e_pre_gain,
        e_pre_shift,
        e_query_bias,
        e_value_bias,
        e_out_bias,
        e_mid_gain,
        e_mid_shift,
        e_expand_bias,
        e_contract_bias,
        embed_bias_full,
        mask_full,
        p_pre_gain,
        p_pre_shift,
        p_query_bias,
        p_value_bias,
        p_out_bias,
        p_mid_gain,
        p_mid_shift,
        p_expand_bias,
        p_contract_bias,
    ) = split_packed(packed, sizes)

    e_joint = gather(encoder_joint_weight)
    e_out = gather(encoder_out_weight)
    e_expand = gather(encoder_expand_weight)
    e_contract = gather(encoder_contract_weight)
    embed_full = gather(embed_weight)
    p_joint = gather(predictor_joint_weight)
    p_out = gather(predictor_out_weight)
    p_expand = gather(predictor_expand_weight)
    p_contract = gather(predictor_contract_weight)

    place = lax.broadcasted_iota(jnp.int32, (1, 1, span), 2)
    slot_visible = jnp.any(
        (slot_token[:, :, None] == place) & (visible[:, None, :] > 0), axis=2
    )
    own_visible = lax.dynamic_slice_in_dim(slot_visible, shard * slots, slots, 1)
    own_flat = own_visible.reshape(rows, 1)
    own_tokens = lax.dynamic_slice_in_dim(slot_token, shard * slots, slots, 1)
    slot_code = jnp.take(positions, own_tokens.reshape(rows), axis=0)
    bias = jnp.where(slot_visible, 0.0, -1e30).astype(f32).reshape(clips, 1, span)

    inputs = tokens.reshape(rows, width)
    normed = norm_layer(inputs, e_pre_gain, e_pre_shift)
    normed_all = lax.all_gather(normed.reshape(clips, slots, width), "seq", axis=1, tiled=True)
    length = normed_all.shape[1]
    queries = (mm(normed, e_joint[:, :width]) + e_query_bias).astype(bf16)
    joined = mm(normed_all.reshape(clips * length, width), e_joint[:, width:])
    joined = (joined + jnp.concatenate([jnp.zeros_like(e_value_bias), e_value_bias])).astype(bf16)
    mixed = attend(
        queries.reshape(clips, slots, width),
        joined.reshape(clips, length, 2 * width),
        head_size,
        bias,
    ).reshape(rows, width)
    middle = inputs + mm(mixed, e_out) + e_out_bias
    normed_mid = norm_layer(middle, e_mid_gain, e_mid_shift)
    hidden = mm(normed_mid, e_expand) + e_expand_bias
    active = gelu(hidden)
    encoded = middle + mm(active, e_contract) + e_contract_bias
    context = encoded.astype(bf16)

    embedded = mm(context, embed_full) + embed_bias_full
    pred_input = jnp.where(own_flat, embedded, mask_full) + slot_code
    p_normed = norm_layer(pred_input, p_pre_gain, p_pre_shift)
    p_normed_all = lax.all_gather(
        p_normed.reshape(clips, slots, small_width), "seq", axis=1, tiled=True
    )
    p_queries = (mm(p_normed, p_joint[:, :small_width]) + p_query_bias).astype(bf16)
    p_joined = mm(p_normed_all.reshape(clips * span, small_width), p_joint[:, small_width:])
    p_joined = (p_joined + jnp.concatenate([jnp.zeros_like(p_value_bias), p_value_bias])).astype(
        bf16
    )
    p_mixed = attend(
        p_queries.reshape(clips, slots, small_width),
        p_joined.reshape(clips, span, 2 * small_width),
        small_head,
        None,
    ).reshape(rows, small_width)
    p_middle = pred_input + mm(p_mixed, p_out) + p_out_bias
    p_normed_mid = norm_layer(p_middle, p_mid_gain, p_mid_shift)
    p_hidden = mm(p_normed_mid, p_expand) + p_expand_bias
    p_active = gelu(p_hidden)
    predicted = p_middle + mm(p_active, p_contract) + p_contract_bias

    def block_back(
        grad_out,
        inputs,
        normed_all,
        mixed,
        middle,
        normed_mid,
        hidden,
        active,
        weights,
        vectors,
        head_size,
        bias,
        parts,
        clips,
    ):
        joint, out, expand, contract = weights
        pre_gain, mid_gain, query_bias, value_bias = vectors
        local_rows = inputs.shape[0] // clips
        grad_y = grad_out.astype(bf16)
        grad_contract = mm(active, grad_y, TN).astype(bf16)
        grad_contract_bias = jnp.sum(grad_y.astype(f32), axis=0)
        grad_hidden = (mm(grad_y, contract, NT) * gelu_slope(hidden)).astype(bf16)
        grad_expand = mm(normed_mid, grad_hidden, TN).astype(bf16)
        grad_expand_bias = jnp.sum(grad_hidden.astype(f32), axis=0)
        grad_norm, grad_mid_gain, grad_mid_shift = norm_back(
            middle, mid_gain, mm(grad_hidden, expand, NT)
        )
        grad_middle = grad_out + grad_norm
        grad_att = grad_middle.astype(bf16)
        grad_out_weight = mm(mixed, grad_att, TN).astype(bf16)
        grad_out_bias = jnp.sum(grad_att.astype(f32), axis=0)
        grad_mixed = mm(grad_att, out, NT).astype(bf16).reshape(clips, local_rows, -1)
        grad_joint, grad_joint_weight, grad_query_bias, grad_value_bias = attention_back(
            grad_mixed,
            normed_all,
            (joint, query_bias, value_bias),
            head_size,
            bias,
            parts,
            seq_size,
            shard,
        )
        grad_norm, grad_pre_gain, grad_pre_shift = norm_back(
            inputs, pre_gain, joint_back(grad_joint, joint)
        )
        grad_inputs = grad_middle + grad_norm
        small = dict(
            pre_gain=grad_pre_gain,
            pre_shift=grad_pre_shift,
            query_bias=grad_query_bias,
            value_bias=grad_value_bias,
            out_bias=grad_out_bias,
            mid_gain=grad_mid_gain,
            mid_shift=grad_mid_shift,
            expand_bias=grad_expand_bias,
            contract_bias=grad_contract_bias,
        )
        return (
            grad_inputs,
            (grad_joint_weight, grad_out_weight, grad_expand, grad_contract),
            small,
        )

    grad_pred_input, p_grads, p_small = block_back(
        cotangent.reshape(rows, small_width),
        pred_input,
        p_normed_all,
        p_mixed,
        p_middle,
        p_normed_mid,
        p_hidden,
        p_active,
        (p_joint, p_out, p_expand, p_contract),
        (p_pre_gain, p_mid_gain, p_query_bias, p_value_bias),
        small_head,
        None,
        seq_size,
        clips,
    )
    grad_mask_token = jnp.sum(jnp.where(own_flat, 0.0, grad_pred_input), axis=0)
    grad_embedded = jnp.where(own_flat, grad_pred_input, 0.0).astype(bf16)
    grad_embed_weight = mm(context, grad_embedded, TN).astype(bf16)
    grad_embed_bias = jnp.sum(grad_embedded.astype(f32), axis=0)

    grad_context = mm(grad_embedded, embed_full, NT)
    grad_tokens, e_grads, e_small = block_back(
        grad_context,
        inputs,
        normed_all,
        mixed,
        middle,
        normed_mid,
        hidden,
        active,
        (e_joint, e_out, e_expand, e_contract),
        (e_pre_gain, e_mid_gain, e_query_bias, e_value_bias),
        head_size,
        bias,
        seq_size,
        clips,
    )

    def joint_total(grad):
        part = scatter(grad)
        whole = lax.all_gather(part, "seq", axis=2, tiled=True)
        return whole.reshape(part.shape[0], -1).astype(f32)

    def total(grad):
        return across_slots(scatter(grad))

    def spread(vector):
        full = jnp.zeros((vector.shape[0] * seq_size,), f32)
        return lax.dynamic_update_slice_in_dim(full, vector, shard * vector.shape[0], 0)

    for small in (e_small, p_small):
        small["query_bias"] = spread(small["query_bias"])
        small["value_bias"] = spread(small["value_bias"])
    order = (
        "pre_gain",
        "pre_shift",
        "query_bias",
        "value_bias",
        "out_bias",
        "mid_gain",
        "mid_shift",
        "expand_bias",
        "contract_bias",
    )
    small_grads = [e_small[name] for name in order]
    small_grads += [grad_embed_bias, grad_mask_token]
    small_grads += [p_small[name] for name in order]
    small_packed = jnp.concatenate(
        [member.reshape(fsdp_size, -1) for member in small_grads], axis=1
    )
    small_sum = lax.psum(small_packed, ("fsdp", "seq"))
    own_small = lax.dynamic_slice_in_dim(small_sum, lax.axis_index("fsdp"), 1, 0)[0]
    small_out = []
    at = 0
    for size in sizes:
        small_out.append(own_small[at : at + size])
        at += size
    e_vec = dict(zip(order, small_out[:9]))
    embed_bias_out, mask_out = small_out[9], small_out[10]
    p_vec = dict(zip(order, small_out[11:]))

    def ordered(vec, grads):
        joint, out, expand, contract = grads
        return (
            vec["pre_gain"],
            vec["pre_shift"],
            joint_total(joint),
            vec["query_bias"],
            vec["value_bias"],
            total(out),
            vec["out_bias"],
            vec["mid_gain"],
            vec["mid_shift"],
            total(expand),
            vec["expand_bias"],
            total(contract),
            vec["contract_bias"],
        )

    return (
        encoded.reshape(tokens.shape),
        predicted.reshape(cotangent.shape),
        grad_tokens.reshape(tokens.shape),
        *ordered(e_vec, e_grads),
        total(grad_embed_weight),
        embed_bias_out,
        mask_out,
        *ordered(p_vec, p_grads),
    )


def solution(mesh):
    cut, rows, slots, vec, full = (
        P("fsdp", "seq", None),
        P("fsdp", None),
        P("fsdp", None),
        P("fsdp"),
        P(),
    )
    block = (vec, vec, rows, vec, vec, rows, vec, vec, vec, rows, vec, rows, vec)
    return jax.shard_map(
        functools.partial(body, mesh.shape["fsdp"], mesh.shape["seq"]),
        mesh=mesh,
        in_specs=(cut, slots, slots, full, *block, rows, vec, vec, *block, cut),
        out_specs=(cut, cut, cut, *block, rows, vec, vec, *block),
        check_vma=False,
    )
```

time: 2940 us -> 1330 us (0.45)
  waiting for transfers between devices: 1320 us -> 492 us
  matrix products: 752 us -> 225 us
  local copies, waits for them, and re-layouts: 420 us -> 132 us
  Pallas kernels: 0 us -> 277 us
  other arithmetic: 212 us -> 53.6 us
  blocking collectives: 183 us -> 105 us
    reduce_scatter x13 -> x8, waiting for transfers between devices: 1070 us -> 0.11 us  [scatter(): return lax.psum_scatter(array, 'fsdp', scatter_dimension=0, tiled=True)]
    dot_general x114 -> x43, matrix products: 703 us -> 225 us  [mm(): return lax.dot_general(left, right, dims, preferred_element_type=f32)]
    pallas_call x0 -> x4, Pallas kernels: none -> 277 us  [the longest x2 156 us: attend_back(): pl.pallas_call(functools.partial(backward_kernel, 1.0 / math.sqrt(head_si...]
    all_to_all x0 -> x4, waiting for transfers between devices: none -> 159 us  [the longest x2 125 us: slots_from_heads(): return lax.all_to_all(array, 'seq', split_axis=2, concat_axis=3, tiled=True)]
    dynamic_update_slice x74 -> x4, local copies, waits for them, and re-layouts: 119 us -> 0.98 us  [spread(): lax.dynamic_update_slice_in_dim(full, vector, shard * vector.shape[0], 0)]
    psum x1 -> x2, waiting for transfers between devices: 68.7 us -> 186 us  [the longest x1 110 us: across_slots(): return lax.psum(array, 'seq').astype(f32)]
    while x142 -> x0, local copies, waits for them, and re-layouts: 114 us -> none
    convert_element_type x74 -> x12, other arithmetic: 122 us -> 11.7 us  [the longest x7 8.11 us: across_slots(): return lax.psum(array, 'seq').astype(f32)]
  transfers between devices with their start and end apart: 24 -> 23, of which waited for: 18 -> 9; matrix products, arithmetic and copies ran while one was open for 21% -> 26% of each run, Pallas kernels for 0% -> 16%
where the time goes in v1:
time: 1330 us; the launch traced here: 1320 us
  waiting for transfers between devices  492 us (37%)
  Pallas kernels  277 us (21%)
  matrix products  225 us (17%)
  local copies, waits for them, and re-layouts  132 us (10%)
  blocking collectives  105 us (8%)
  other arithmetic  53.6 us (4%)
  starting transfers between devices  19.9 us (1%)
  between operations  16.9 us (1%)
    dot_general x43, matrix products, mm(): return lax.dot_general(left, right, dims, preferred_element_type=f32)  225 us
    pallas_call x2, Pallas kernels, attend_back(): pl.pallas_call(functools.partial(backward_kernel, 1.0 / math.sqrt(head_si...  156 us
    all_to_all x2, waiting for transfers between devices, slots_from_heads(): return lax.all_to_all(array, 'seq', split_axis=2, concat_axis=3, tiled=True)  125 us
    pallas_call x2, Pallas kernels, attend(): pl.pallas_call(functools.partial(forward_kernel, 1.0 / math.sqrt(head_siz...  121 us
    psum x1, waiting for transfers between devices, across_slots(): return lax.psum(array, 'seq').astype(f32)  110 us
    all_gather x1, waiting for transfers between devices, body(): lax.all_gather(normed.reshape(clips, slots, width), 'seq', axis=1, tiled=...  89.7 us
    psum x1, waiting for transfers between devices, body(): small_sum = lax.psum(small_packed, ('fsdp', 'seq'))  75.9 us
    another operation x2, local copies, waits for them, and re-layouts, attention_back(): back = slots_from_heads(jnp.stack(grads), shards)  43.2 us
  transfers between devices with their start and end apart: 23, of which 9 were waited for; matrix products, arithmetic and copies ran while one was open for 26% of the time, Pallas kernels for 16%

profile of v1, /device:TPU:0, one launch (start us, length us, event | category | flops | bytes accessed | tf_op | source)
XLA Modules:
  0.0 1321.1 jit_solution(13800016043491806611)
XLA Ops:
  11.8 13.5 %concatenate.12 = bf16[2208]{0:T(1024)(128)(2,1)S(1)} concatenate(bf16[128]{0:T(256)(128)(2,1)} %param.38, bf16[128]{0:T(256)(128)(2,1)} %param.39, bf16[128]{0:T(256)(128)(2,1)} %param.41, bf16[128]{0:T(256)(128)(2,1)} %param.42, bf16[128]{0:T(256)(128)(2,1)} %param.44, bf16[128]{0:T(256)(128)(2,1)} %param.45, bf16[128]{0:T(256)(128)(2,1)} %param.46, bf16[512]{0:T(512)(128)(2,1)} %param.48, ...), dimensions={0} | concatenate | bytes 8832 | tf_op jit(solution)/shard_map/concatenate | solution.py:357
  25.6 26.5 %all-reduce.2 = bf16[17664]{0:T(1024)(128)(2,1)S(1)} all-reduce(bf16[17664]{0:T(1024)(128)(2,1)S(1)} %dynamic-update-slice), channel_id=2, replica_groups=mesh['fsdp'=8,'seq'=4] {'fsdp'}, use_global_device_ids=true, to_apply=%add.2 | all-reduce | flops 17664 | bytes 70656
  70.7 9.6 all_gather.52
  90.2 89.7 %all-gather.12.cloned.1.call-done = bf16[2,1568,1024]{2,1,0:T(8,128)(2,1)} async-done(((bf16[2,392,1024]{2,1,0:T(8,128)(2,1)}), bf16[2,1568,1024]{2,1,0:T(8,128)(2,1)}) %all-gather.12.cloned.1.call-update) | async-done | bytes 6422544 | tf_op jit(solution)/shard_map/all_gather | solution.py:403
  179.9 20.2 %add_convert_fusion = bf16[3136,2048]{1,0:T(8,128)(2,1)} fusion(bf16[3136,1024]{1,0:T(8,128)(2,1)} %bitcast.287, f32[2048]{0:T(1024)S(1)} %concatenate.13, bf16[1024,3072]{0,1:T(8,128)(2,1)} %all-gather.10.cloned.1.call-done), kind=kOutput, calls=%fused_computation.1 | convolution fusion | flops 13166182400 | bytes 23470080 | tf_op jit(solution)/shard_map/dot_general | solution.py:25
  200.1 68.9 %attend.2 = bf16[2,392,1024]{2,1,0:T(8,128)(2,1)} custom-call(bf16[2,392,1024]{2,1,0:T(8,128)(2,1)} %bitcast.357, bf16[2,1568,2048]{2,1,0:T(8,128)(2,1)} %bitcast.348, bf16[2,1568,2048]{2,1,0:T(8,128)(2,1)} %bitcast.349, f32[2,1,1568]{2,1,0:T(1,128)} %select_n.68.rest_0_), custom_call_target="tpu_custom_call" | custom-call | flops 20141047808 | bytes 12845056 | tf_op jit(solution)/shard_map/attend/pallas_call | solution.py:106
  275.5 16.0 %multiply_convert_fusion = (bf16[784,4096]{1,0:T(8,128)(2,1)}, f32[784,4096]{1,0:T(8,128)}) fusion(f32[4096]{0:T(1024)S(1)} %bitcast.338, bf16[1024,4096]{1,0:T(8,128)(2,1)} %all-gather.16.cloned.1.call-done, f32[1024]{0:T(1024)S(1)} %get-tuple-element.337, f32[1024]{0:T(1024)S(1)} %get-tuple-element.335, f32[784]{0:T(1024)S(1)} %add_rsqrt_fusion.2, ...), kind=kOutput, calls=%fused_computation.13 | convolution fusion | flops 6600753152 | bytes 30902400 | tf_op jit(solution)/shard_map/dot_general | solution.py:25
  291.6 28.7 %all-gather.18.cloned.1.call-done = bf16[4096,1024]{1,0:T(8,128)(2,1)} async-done(((bf16[512,1024]{1,0:T(8,128)(2,1)}), bf16[4096,1024]{1,0:T(8,128)(2,1)}) %all-gather.18.cloned.1.call-update) | async-done | bytes 8388624 | tf_op jit(solution)/shard_map/all_gather | solution.py:277
  320.2 11.6 add_add_fusion.1
  336.7 10.6 all_gather.53
  347.5 9.5 all_gather.55
  361.3 25.2 %all-gather.20.cloned.1.call-done = bf16[2,1568,384]{2,1,0:T(8,128)(2,1)} async-done(((bf16[2,392,384]{2,1,0:T(8,128)(2,1)}), bf16[2,1568,384]{2,1,0:T(8,128)(2,1)}) %all-gather.20.cloned.1.call-update) | async-done | bytes 2408464 | tf_op jit(solution)/shard_map/all_gather | solution.py:424
  386.5 6.5 add_convert_fusion.1
  393.0 52.2 %attend.3 = bf16[2,392,384]{2,1,0:T(8,128)(2,1)} custom-call(bf16[2,392,384]{2,1,0:T(8,128)(2,1)} %bitcast.359, bf16[2,1568,768]{2,1,0:T(8,128)(2,1)} %bitcast.350, bf16[2,1568,768]{2,1,0:T(8,128)(2,1)} %bitcast.351), custom_call_target="tpu_custom_call" | custom-call | flops 15105785856 | bytes 4816896 | tf_op jit(solution)/shard_map/attend/pallas_call | solution.py:106
  496.9 65.7 %attend_back.2 = (bf16[2,1568,96]{2,1,0:T(8,128)(2,1)}, bf16[2,1568,96]{2,1,0:T(8,128)(2,1)}, bf16[2,1568,96]{2,1,0:T(8,128)(2,1)}) custom-call(bf16[2,1568,96]{2,1,0:T(8,128)(2,1)} %bitcast.325, bf16[2,1568,96]{2,1,0:T(8,128)(2,1)} %bitcast.326, bf16[2,1568,96]{2,1,0:T(8,128)(2,1)} %bitcast.324, bf16[2,1568,96]{2,1,0:T(8,128)(2,1)} %bitcast.327), custom_call_target="tpu_custom_call" | custom-call | flops 37764464640 | bytes 4214784 | tf_op jit(solution)/shard_map/attend_back/pallas_call | solution.py:195
  564.8 10.5 copy.199
  589.4 45.0 %all-to-all-done.1 = bf16[3,2,1568,96]{3,1,0,2:T(2,128)(2,1)} async-done(((bf16[3,2,1568,96]{3,1,0,2:T(2,128)(2,1)}), bf16[3,2,1568,96]{3,1,0,2:T(2,128)(2,1)}, u32[]{:S(2)}, u32[]{:S(2)}) %all-to-all-start.1) | async-done | bytes 1806368 | tf_op jit(solution)/shard_map/all_to_all | solution.py:223
  653.7 18.0 %convert_reduce_fusion = (f32[4096]{0:T(1024)S(1)}, bf16[784,4096]{1,0:T(8,128)(2,1)}) fusion(f32[784,4096]{1,0:T(8,128)} %get-tuple-element.346, f32[4096]{0:T(1024)S(1)} %bitcast.339, bf16[4096,1024]{1,0:T(8,128)(2,1)} %all-gather.18.cloned.1.call-done, f32[784,1024]{1,0:T(8,128)S(1)} %fusion.88), kind=kOutput, calls=%fused_computation.12 | convolution fusion | flops 6619213824 | bytes 30900224 | tf_op jit(solution)/shard_map/dot_general | solution.py:25
  671.7 12.7 multiply_reduce_fusion
  686.7 6.2 convert_reduce_fusion.3
  698.4 15.2 %convolution_convert_fusion = bf16[1024,4096]{1,0:T(8,128)(2,1)} fusion(bf16[784,4096]{1,0:T(8,128)(2,1)} %get-tuple-element.358, f32[1024]{0:T(1024)S(1)} %copy-done.65, f32[1024]{0:T(1024)S(1)} %get-tuple-element.335, f32[784,1024]{1,0:T(8,128)} %copy-done.7, f32[784]{0:T(1024)S(1)} %add_rsqrt_fusion.2, f32[784]{0:T(1024)S(1)} %broadcast_multiply_fusion.10, ...), kind=kOutput, calls=%fused_computation.16 | convolution fusion | flops 6585679872 | bytes 18040960 | tf_op jit(solution)/shard_map/dot_general | solution.py:25
  713.7 14.6 %convolution_convert_fusion.1 = bf16[4096,1024]{1,0:T(8,128)(2,1)} fusion(bf16[784,4096]{1,0:T(8,128)(2,1)} %get-tuple-element.345, f32[784,1024]{1,0:T(8,128)} %copy-done.9), kind=kOutput, calls=%fused_computation.17 | convolution fusion | flops 6581665792 | bytes 18022400 | tf_op jit(solution)/shard_map/dot_general | solution.py:25
  748.7 6.1 fusion.9
  759.0 29.7 %all-to-all-done.2 = bf16[2,392,1024]{1,0,2:T(2,128)(2,1)S(1)} async-done(((bf16[2,392,1024]{1,0,2:T(2,128)(2,1)}), bf16[2,392,1024]{1,0,2:T(2,128)(2,1)S(1)}, u32[]{:S(2)}, u32[]{:S(2)}) %all-to-all-start.2) | async-done | bytes 1605664 | tf_op jit(solution)/shard_map/all_to_all | solution.py:217
  796.2 90.3 %attend_back.3 = (bf16[2,1568,256]{2,1,0:T(8,128)(2,1)}, bf16[2,1568,256]{2,1,0:T(8,128)(2,1)}, bf16[2,1568,256]{2,1,0:T(8,128)(2,1)}) custom-call(bf16[2,1568,256]{2,1,0:T(8,128)(2,1)} %bitcast.356, bf16[2,1568,256]{2,1,0:T(8,128)(2,1)} %bitcast.354, bf16[2,1568,256]{2,1,0:T(8,128)(2,1)} %bitcast.355, bf16[2,1568,256]{2,1,0:T(8,128)(2,1)} %bitcast.317, ...), custom_call_target="tpu_custom_call" | custom-call | flops 50352619520 | bytes 11239424 | tf_op jit(solution)/shard_map/attend_back/pallas_call | solution.py:195
  889.2 32.7 %copy.207 = bf16[3,2,1568,256]{3,1,0,2:T(2,128)(2,1)} copy(bf16[3,2,1568,256]{3,2,1,0:T(8,128)(2,1)S(1)} %pad_maximum_fusion) | data formatting | bytes 9633792 | tf_op jit(solution)/shard_map/stack | solution.py:250
  953.4 79.8 %all-to-all-done.3 = bf16[3,2,1568,256]{3,1,0,2:T(2,128)(2,1)} async-done(((bf16[3,2,1568,256]{3,1,0,2:T(2,128)(2,1)}), bf16[3,2,1568,256]{3,1,0,2:T(2,128)(2,1)}, u32[]{:S(2)}, u32[]{:S(2)}) %all-to-all-start.3) | async-done | bytes 4816928 | tf_op jit(solution)/shard_map/all_to_all | solution.py:223
  1056.4 18.1 %psum.61 = bf16[48,384]{1,0:T(8,128)(2,1)S(1)} all-reduce(bf16[48,384]{1,0:T(8,128)(2,1)} %reduce-scatter.19.cloned.1.call-done), channel_id=1, replica_groups=mesh['fsdp'=8,'seq'=4] {'seq'}, use_global_device_ids=true, to_apply=%region_49.50 | all-reduce | flops 18432 | bytes 73728 | tf_op jit(solution)/shard_map/psum | solution.py:285
  1076.1 15.1 %all_gather.59 = bf16[48,3,384]{0,1,2:T(4,128)(2,1)S(1)} all-gather(bf16[48,3,96]{0,1,2:T(4,128)(2,1)S(1)} %copy.214), channel_id=1, replica_groups=mesh['fsdp'=8,'seq'=4] {'seq'}, dimensions={2}, use_global_device_ids=true | all-gather | bytes 138240 | tf_op jit(solution)/shard_map/all_gather | solution.py:549
  1092.1 16.0 %all_gather.58 = bf16[128,3,1024]{2,0,1:T(8,128)(2,1)S(1)} all-gather(bf16[128,3,256]{2,0,1:T(8,128)(2,1)} %reduce-scatter.9.cloned.1.call-done), channel_id=1, replica_groups=mesh['fsdp'=8,'seq'=4] {'seq'}, dimensions={2}, use_global_device_ids=true | all-gather | bytes 983040 | tf_op jit(solution)/shard_map/all_gather | solution.py:549
  1115.5 75.9 %all-reduce.9.cloned.1.call-done = f32[8,2208]{1,0:T(8,128)} async-done(((f32[8,2208]{1,0:T(8,128)}), f32[8,2208]{1,0:T(8,128)}) %all-reduce.9.cloned.1.call-update) | async-done | bytes 70672 | tf_op jit(solution)/shard_map/psum | solution.py:579
  1197.0 109.6 %all-reduce.13.cloned.1.call-done = (bf16[128,1024]{1,0:T(8,128)(2,1)}, bf16[128,4096]{1,0:T(8,128)(2,1)}, bf16[512,1024]{1,0:T(8,128)(2,1)}, bf16[128,384]{1,0:...) async-done(((bf16[128,1024]{1,0:T(8,128)(2,1)}, bf16[128,4096]{1,0:T(8,128)(2,1)}, bf16[512,1024]{1,0:T(8,128)(2,1)}, bf16[128,384]{1,0:T(8,128)(2,1)}, ...) | async-done | bytes 2752528 | tf_op jit(solution)/shard_map/psum | solution.py:285
  (396 shorter events, 254.1 us)
Async XLA Ops:
  7.2 60.1 %copy-start = (f32[1568,384]{1,0:T(8,128)S(1)}, f32[1568,384]{1,0:T(8,128)}, u32[]{:S(2)}) copy-start(f32[1568,384]{1,0:T(8,128)} %param.37) | copy-start | bytes 7225348
  7.2 77.4 %all-gather.10.cloned.1.call-start = ((), (), s32[]{:S(2)}) async-start(), calls=%async_computation.12 | async-start | bytes 7077888 | tf_op jit(solution)/shard_map/all_gather | solution.py:277
  9.7 170.2 %all-gather.12.cloned.1.call-start = ((), (), s32[]{:S(2)}) async-start(), calls=%async_computation.13 | async-start | bytes 8028160 | tf_op jit(solution)/shard_map/all_gather | solution.py:403
  57.0 27.6 %copy-start.44 = (f32[1024]{0:T(1024)}, f32[1024]{0:T(1024)S(1)}, u32[]{:S(2)}) copy-start(f32[1024]{0:T(1024)S(1)} %get-tuple-element.342) | copy-start | bytes 12292
  57.0 27.6 %copy-start.63 = (f32[1024]{0:T(1024)}, f32[1024]{0:T(1024)S(1)}, u32[]{:S(2)}) copy-start(f32[1024]{0:T(1024)S(1)} %get-tuple-element.340) | copy-start | bytes 12292
  57.0 218.5 %copy-start.64 = (f32[1024]{0:T(1024)}, f32[1024]{0:T(1024)S(1)}, u32[]{:S(2)}) copy-start(f32[1024]{0:T(1024)S(1)} %get-tuple-element.337) | copy-start | bytes 12292
  59.0 209.9 %all-gather.14.cloned.1.call-start = ((), (), s32[]{:S(2)}) async-start(), calls=%async_computation.14 | async-start | bytes 2359296 | tf_op jit(solution)/shard_map/all_gather | solution.py:277
  59.7 215.8 %all-gather.16.cloned.1.call-start = ((), (), s32[]{:S(2)}) async-start(), calls=%async_computation.15 | async-start | bytes 9437184 | tf_op jit(solution)/shard_map/all_gather | solution.py:277
  60.3 259.9 %all-gather.18.cloned.1.call-start = ((), (), s32[]{:S(2)}) async-start(), calls=%async_computation.16 | async-start | bytes 9437184 | tf_op jit(solution)/shard_map/all_gather | solution.py:277
  60.9 325.6 %all-gather.20.cloned.1.call-start = ((), (), s32[]{:S(2)}) async-start(), calls=%async_computation.17 | async-start | bytes 3010560 | tf_op jit(solution)/shard_map/all_gather | solution.py:424
  61.0 19.3 %copy-start.46 = (f32[784]{0:T(1024)}, f32[784]{0:T(1024)S(1)}, u32[]{:S(2)}) copy-start(f32[784]{0:T(1024)S(1)} %rsqrt.41) | copy-start | bytes 9412
  80.3 251.6 %copy-start.21 = (bf16[1024,384]{1,0:T(8,128)(2,1)}, bf16[1024,384]{1,0:T(8,128)(2,1)S(1)}, u32[]{:S(2)}) copy-start(bf16[1024,384]{1,0:T(8,128)(2,1)S(1)} %all_gather.52) | copy-start | bytes 2359300
  333.1 112.2 %copy-start.5 = (f32[784,384]{1,0:T(8,128)}, f32[784,384]{1,0:T(8,128)S(1)}, u32[]{:S(2)}) copy-start(f32[784,384]{1,0:T(8,128)S(1)} %get-tuple-element.348) | copy-start | bytes 3612676
  333.1 24.1 %copy-start.24 = (f32[2,392,384]{2,1,0:T(8,128)S(1)}, f32[2,392,384]{2,1,0:T(8,128)}, u32[]{:S(2)}) copy-start(f32[2,392,384]{2,1,0:T(8,128)} %param.67) | copy-start | bytes 3612676
  335.1 112.3 %all-gather.22.cloned.1.call-start = ((), (), s32[]{:S(2)}) async-start(), calls=%async_computation.18 | async-start | bytes 1327104 | tf_op jit(solution)/shard_map/all_gather | solution.py:277
  335.8 117.5 %all-gather.24.cloned.1.call-start = ((), (), s32[]{:S(2)}) async-start(), calls=%async_computation.19 | async-start | bytes 1327104 | tf_op jit(solution)/shard_map/all_gather | solution.py:277
  393.0 52.2 %copy-start.30 = (bf16[384,384]{1,0:T(8,128)(2,1)S(1)}, bf16[384,384]{1,0:T(8,128)(2,1)}, u32[]{:S(2)}) copy-start(bf16[384,384]{1,0:T(8,128)(2,1)} %all_gather.55) | copy-start | bytes 884740
  468.1 24.9 %all-to-all-start = ((bf16[2,392,384]{1,0,2:T(2,128)(2,1)}), bf16[2,392,384]{1,0,2:T(2,128)(2,1)}, u32[]{:S(2)}, u32[]{:S(2)}) async-start(bf16[2,392,384]{1,0,2:T(2,128)(2,1)} %copy.196), calls=%async_computation | async-start | bytes 1572864 | tf_op jit(solution)/shard_map/all_to_all | solution.py:217
  575.3 59.1 %all-to-all-start.1 = ((bf16[3,2,1568,96]{3,1,0,2:T(2,128)(2,1)}), bf16[3,2,1568,96]{3,1,0,2:T(2,128)(2,1)}, u32[]{:S(2)}, u32[]{:S(2)}) async-start(bf16[3,2,1568,96]{3,1,0,2:T(2,128)(2,1)} %copy.199), calls=%async_computation.1 | async-start | bytes 4816896 | tf_op jit(solution)/shard_map/all_to_all | solution.py:223
  580.0 470.7 %reduce-scatter.21.cloned.1.call-start = ((), (), s32[]{:S(2)}) async-start(), calls=%async_computation.27 | async-start | bytes 1327104 | tf_op jit(solution)/shard_map/reduce_scatter | solution.py:281
  584.4 466.3 %reduce-scatter.23.cloned.1.call-start = ((), (), s32[]{:S(2)}) async-start(), calls=%async_computation.28 | async-start | bytes 1327104 | tf_op jit(solution)/shard_map/reduce_scatter | solution.py:281
  589.0 461.8 %reduce-scatter.17.cloned.1.call-start = ((), (), s32[]{:S(2)}) async-start(), calls=%async_computation.25 | async-start | bytes 884736 | tf_op jit(solution)/shard_map/reduce_scatter | solution.py:281
  686.6 364.2 %reduce-scatter.11.cloned.1.call-start = ((), (), s32[]{:S(2)}) async-start(), calls=%async_computation.22 | async-start | bytes 2359296 | tf_op jit(solution)/shard_map/reduce_scatter | solution.py:281
  698.4 352.4 %reduce-scatter.13.cloned.1.call-start = ((), (), s32[]{:S(2)}) async-start(), calls=%async_computation.23 | async-start | bytes 9437184 | tf_op jit(solution)/shard_map/reduce_scatter | solution.py:281
  713.7 337.2 %reduce-scatter.15.cloned.1.call-start = ((), (), s32[]{:S(2)}) async-start(), calls=%async_computation.24 | async-start | bytes 9437184 | tf_op jit(solution)/shard_map/reduce_scatter | solution.py:281
  737.1 51.6 %all-to-all-start.2 = ((bf16[2,392,1024]{1,0,2:T(2,128)(2,1)}), bf16[2,392,1024]{1,0,2:T(2,128)(2,1)S(1)}, u32[]{:S(2)}, u32[]{:S(2)}) async-start(bf16[2,392,1024]{1,0,2:T(2,128)(2,1)} %copy.204), calls=%async_computation.2 | async-start | bytes 4194304 | tf_op jit(solution)/shard_map/all_to_all | solution.py:217
  921.9 111.3 %all-to-all-start.3 = ((bf16[3,2,1568,256]{3,1,0,2:T(2,128)(2,1)}), bf16[3,2,1568,256]{3,1,0,2:T(2,128)(2,1)}, u32[]{:S(2)}, u32[]{:S(2)}) async-start(bf16[3,2,1568,256]{3,1,0,2:T(2,128)(2,1)} %copy.207), calls=%async_computation.3 | async-start | bytes 9633792 | tf_op jit(solution)/shard_map/all_to_all | solution.py:223
  927.1 129.3 %reduce-scatter.19.cloned.1.call-start = ((), (), s32[]{:S(2)}) async-start(), calls=%async_computation.26 | async-start | bytes 331776 | tf_op jit(solution)/shard_map/reduce_scatter | solution.py:281
  930.4 144.8 %all-reduce.11.cloned.1.call-start = ((), (), s32[]{:S(2)}) async-start(), calls=%async_computation.29 | async-start | bytes 786432
  936.5 155.7 %reduce-scatter.9.cloned.1.call-start = ((), (), s32[]{:S(2)}) async-start(), calls=%async_computation.21 | async-start | bytes 1769472 | tf_op jit(solution)/shard_map/reduce_scatter | solution.py:281
  950.4 241.1 %all-reduce.9.cloned.1.call-start = ((), (), s32[]{:S(2)}) async-start(), calls=%async_computation.20 | async-start | bytes 147456 | tf_op jit(solution)/shard_map/psum | solution.py:579
  1050.4 256.2 %all-reduce.13.cloned.1.call-start = ((), (), s32[]{:S(2)}) async-start(), calls=%async_computation.30 | async-start | bytes 5505024 | tf_op jit(solution)/shard_map/psum | solution.py:285
  (72 other events, 467.5 us)
Sparse Core Ops, SparseCore 0:
  10.5 49.7 all-gather.9
  62.4 117.4 all-gather.11
  181.8 26.0 all-gather.13
  209.6 54.4 all-gather.15
  265.8 54.3 all-gather.17
  335.2 51.2 all-gather.19
  388.4 22.8 all-gather.21
  413.2 24.0 all-gather.23
  584.5 38.0 reduce-scatter.20
  626.1 36.7 reduce-scatter.22
  686.7 34.0 reduce-scatter.16
  724.6 41.2 reduce-scatter.10
  769.7 71.2 reduce-scatter.12
  844.3 71.2 reduce-scatter.14
  931.6 33.9 reduce-scatter.18
  969.4 54.0 all-reduce.10
  1027.6 37.8 reduce-scatter.8
  1072.4 119.0 all-reduce.8
  1194.6 112.0 all-reduce.12

commit v2 on v1

v2 whole, which is shorter than its diff:
```python
import functools
import math

import jax
import jax.numpy as jnp
from jax import lax
from jax.experimental import pallas as pl
from jax.experimental.pallas import tpu as pltpu
from jax.sharding import PartitionSpec as P

HEADS = 16
PHEADS = 12

f32 = jnp.float32
bf16 = jnp.bfloat16
norm_eps = 1e-06
LOG2E = math.log2(math.e)
NN = (((1,), (0,)), ((), ()))
NT = (((1,), (1,)), ((), ()))
TN = (((0,), (0,)), ((), ()))
VMEM_LIMIT = 60 * 2**20


def mm(left, right, dims=NN):
    return lax.dot_general(left, right, dims, preferred_element_type=f32)


def norm_parts(value):
    center = value - jnp.mean(value, axis=-1, keepdims=True)
    spread = jnp.mean(center * center, axis=-1, keepdims=True)
    scale = lax.rsqrt(spread + norm_eps)
    return center * scale, scale


def norm_layer(value, gain, shift):
    unit, _ = norm_parts(value)
    return (unit * gain + shift).astype(bf16)


def norm_back(value, gain, grad):
    unit, scale = norm_parts(value)
    grad_gain = jnp.sum(grad * unit, axis=0)
    grad_shift = jnp.sum(grad, axis=0)
    inner = grad * gain
    inner = inner - jnp.mean(inner, axis=-1, keepdims=True) - unit * jnp.mean(
        inner * unit, axis=-1, keepdims=True
    )
    return scale * inner, grad_gain, grad_shift


def gelu_parts(hidden):
    cdf = 0.5 * (1.0 + lax.erf(hidden * math.sqrt(0.5)))
    return cdf


def gelu(hidden):
    return (hidden * gelu_parts(hidden)).astype(bf16)


def gelu_slope(hidden):
    pdf = jnp.exp(-0.5 * hidden * hidden) * (1.0 / math.sqrt(2.0 * math.pi))
    return gelu_parts(hidden) + hidden * pdf


def forward_kernel(scale, head_size, q_ref, k_ref, v_ref, *rest):
    if len(rest) == 2:
        bias_ref, o_ref = rest
    else:
        bias_ref, o_ref = None, rest[0]
    head = pl.program_id(2)
    query = q_ref[0]
    key = k_ref[...].reshape(-1, k_ref.shape[-1])
    value = v_ref[...].reshape(-1, v_ref.shape[-1])
    lane = lax.broadcasted_iota(jnp.int32, query.shape, 1)
    mine = (lane // head_size) == head
    own_query = jnp.where(mine, query, jnp.zeros_like(query))
    scores = mm(own_query, key, NT) * (scale * LOG2E)
    if bias_ref is not None:
        scores = scores + bias_ref[0]
    top = jnp.max(scores, axis=1, keepdims=True)
    weight = jnp.exp2(scores - top)
    total = jnp.sum(weight, axis=1, keepdims=True)
    result = (mm(weight.astype(bf16), value) / total).astype(bf16)

    @pl.when(head == 0)
    def _():
        o_ref[0] = result

    @pl.when(head > 0)
    def _():
        o_ref[0] = jnp.where(mine, result, o_ref[0])


def attend(queries, joined, head_size, bias):
    clips, rows, width = queries.shape
    major, _, length, _ = joined.shape
    keys = major * length
    groups = width // 128
    in_specs = [
        pl.BlockSpec((1, rows, 128), lambda c, g, h: (c, 0, g)),
        pl.BlockSpec((major, 1, length, 128), lambda c, g, h: (0, c, 0, g)),
        pl.BlockSpec((major, 1, length, 128), lambda c, g, h: (0, c, 0, g + groups)),
    ]
    operands = [queries, joined, joined]
    if bias is not None:
        in_specs.append(pl.BlockSpec((1, 1, keys), lambda c, g, h: (c, 0, 0)))
        operands.append(bias)
    cells = clips * rows * keys * (width // head_size)
    return pl.pallas_call(
        functools.partial(forward_kernel, 1.0 / math.sqrt(head_size), head_size),
        grid=(clips, groups, 128 // head_size),
        in_specs=in_specs,
        out_specs=pl.BlockSpec((1, rows, 128), lambda c, g, h: (c, 0, g)),
        out_shape=jax.ShapeDtypeStruct((clips, rows, width), bf16),
        compiler_params=pltpu.CompilerParams(vmem_limit_bytes=VMEM_LIMIT),
        cost_estimate=pl.CostEstimate(
            flops=cells * 1024, bytes_accessed=4 * clips * keys * width, transcendentals=cells
        ),
        name="attend",
    )(*operands)


def backward_kernel(scale, head_size, shards, q_ref, k_ref, v_ref, g_ref, *rest):
    if len(rest) == 5:
        bias_ref = rest[0]
        rest = rest[1:]
    else:
        bias_ref = None
    out_ref, dq_sum, dk_sum, dv_sum = rest
    group = pl.program_id(1)
    part = pl.program_id(2)
    head = pl.program_id(3)
    lanes = q_ref.shape[-1]
    query = q_ref[...].reshape(-1, lanes)
    key = k_ref[...].reshape(-1, lanes)
    value = v_ref[...].reshape(-1, lanes)
    grad = g_ref[...].reshape(-1, lanes)
    lane = lax.broadcasted_iota(jnp.int32, query.shape, 1)
    mine = (lane // head_size) == head
    zero = jnp.zeros_like(query)
    own_query = jnp.where(mine, query, zero)
    own_grad = jnp.where(mine, grad, zero)
    key_lane = lax.broadcasted_iota(jnp.int32, key.shape, 1)
    own_key = jnp.where((key_lane // head_size) == head, key, jnp.zeros_like(key))
    scores = mm(own_query, key, NT) * (scale * LOG2E)
    if bias_ref is not None:
        scores = scores + bias_ref[0]
    top = jnp.max(scores, axis=1, keepdims=True)
    weight = jnp.exp2(scores - top)
    total = jnp.sum(weight, axis=1, keepdims=True)
    chance = weight * (1.0 / total)
    grad_chance = mm(own_grad, value, NT)
    delta = jnp.sum(chance * grad_chance, axis=1, keepdims=True)
    grad_scores = (chance * (grad_chance - delta)).astype(bf16)
    part_q = mm(grad_scores, own_key)
    part_v = mm(own_grad, chance.astype(bf16), TN)
    part_k = mm(own_query, grad_scores, TN)

    @pl.when(head == 0)
    def _():
        dq_sum[...] = part_q

    @pl.when(head > 0)
    def _():
        dq_sum[...] += part_q

    @pl.when((head == 0) & (part == 0))
    def _():
        dk_sum[...] = part_k
        dv_sum[...] = part_v

    @pl.when((head > 0) | (part > 0))
    def _():
        dk_sum[...] += part_k
        dv_sum[...] += part_v

    rows = out_ref.shape[2]
    width = out_ref.shape[3] // 3
    held = query.shape[0] // rows
    last_head = head == pl.num_programs(3) - 1

    def place(kind):
        if width == lanes:
            return slice(kind * width, (kind + 1) * width)
        return pl.ds(pl.multiple_of(kind * width + group * lanes, 128), lanes)

    @pl.when(last_head)
    def _():
        result = (dq_sum[...] * scale).astype(bf16)
        for index in range(held):
            out_ref[part * held + index, 0, :, place(0)] = result[index * rows : (index + 1) * rows]

    @pl.when(last_head & (part == pl.num_programs(2) - 1))
    def _():
        for kind, total_ref, factor in ((1, dk_sum, scale), (2, dv_sum, 1.0)):
            result = (total_ref[...] * factor).T.astype(bf16)
            for index in range(shards):
                out_ref[index, 0, :, place(kind)] = result[index * rows : (index + 1) * rows]


def attend_back(queries, keys, values, grad_mixed, head_size, bias, shards):
    major, clips, length, width = queries.shape
    lanes = min(width, 128)
    groups = width // lanes
    rows = major * length // shards
    parts = shards if major == 1 else 1
    query_rows = rows if major == 1 else length
    by_query = pl.BlockSpec((major, 1, query_rows, lanes), lambda c, g, r, h: (0, c, r, g))
    by_key = pl.BlockSpec((major, 1, length, lanes), lambda c, g, r, h: (0, c, 0, g))
    in_specs = [by_query, by_key, by_key, by_query]
    operands = [queries, keys, values, grad_mixed]
    total = major * length
    if bias is not None:
        in_specs.append(pl.BlockSpec((1, 1, total), lambda c, g, r, h: (c, 0, 0)))
        operands.append(bias)
    cells = clips * total * total * (width // head_size)
    return pl.pallas_call(
        functools.partial(backward_kernel, 1.0 / math.sqrt(head_size), head_size, shards),
        grid=(clips, groups, parts, lanes // head_size),
        in_specs=in_specs,
        out_specs=pl.BlockSpec((shards, 1, rows, 3 * width), lambda c, g, r, h: (0, c, 0, 0)),
        out_shape=jax.ShapeDtypeStruct((shards, clips, rows, 3 * width), bf16),
        scratch_shapes=[
            pltpu.VMEM((major * query_rows, lanes), f32),
            pltpu.VMEM((lanes, total), f32),
            pltpu.VMEM((lanes, total), f32),
        ],
        compiler_params=pltpu.CompilerParams(vmem_limit_bytes=VMEM_LIMIT),
        cost_estimate=pl.CostEstimate(
            flops=cells * 2560, bytes_accessed=14 * clips * total * width, transcendentals=cells
        ),
        name="attend_back",
    )(*operands)


def exchange(array):
    return lax.all_to_all(array, "seq", split_axis=0, concat_axis=0, tiled=True)


def gather(array):
    return lax.all_gather(array, "fsdp", axis=0, tiled=True)


def scatter(array):
    return lax.psum_scatter(array, "fsdp", scatter_dimension=0, tiled=True)[0]


def blocks_of(array, count, lanes):
    rows = array.shape[0] // count
    split = array.shape[1] // lanes
    array = array.reshape(count, rows, split, lanes)
    return array.transpose(0, 2, 1, 3).reshape(count, split * rows, lanes)


def from_blocks(array, lanes):
    split = lanes // array.shape[1]
    rows = array.shape[0] // split
    return array.reshape(split, rows, -1).transpose(1, 0, 2).reshape(rows, lanes)


def pack_rows(vectors):
    rows = []
    for member in vectors:
        count = -(-member.shape[0] // 128)
        padded = jnp.pad(member.astype(f32), (0, count * 128 - member.shape[0]))
        rows.append(padded.reshape(count, 128))
    total = sum(member.shape[0] for member in rows)
    if total % 8:
        rows.append(jnp.zeros((8 - total % 8, 128), f32))
    return jnp.concatenate(rows, axis=0)


def unpack_rows(packed, sizes):
    out = []
    at = 0
    for size in sizes:
        count = -(-size // 128)
        piece = packed[:, at : at + count].reshape(packed.shape[0], count * 128)[:, :size]
        out.append(piece.reshape(-1))
        at += count
    return out


def feed_back(grad_out, mixed, middle, normed_mid, hidden, active, weights, mid_gain):
    out, expand, contract = weights
    grad_y = grad_out.astype(bf16)
    grad_contract = mm(active, grad_y, TN).astype(bf16)
    grad_contract_bias = jnp.sum(grad_y.astype(f32), axis=0)
    grad_hidden = (mm(grad_y, contract, NT) * gelu_slope(hidden)).astype(bf16)
    grad_expand = mm(normed_mid, grad_hidden, TN).astype(bf16)
    grad_expand_bias = jnp.sum(grad_hidden.astype(f32), axis=0)
    grad_norm, grad_mid_gain, grad_mid_shift = norm_back(
        middle, mid_gain, mm(grad_hidden, expand, NT)
    )
    grad_middle = grad_out + grad_norm
    grad_att = grad_middle.astype(bf16)
    grad_out_weight = mm(mixed, grad_att, TN).astype(bf16)
    grad_out_bias = jnp.sum(grad_att.astype(f32), axis=0)
    grad_mixed = mm(grad_att, out, NT).astype(bf16)
    grads = (grad_out_weight, grad_expand, grad_contract)
    small = dict(
        out_bias=grad_out_bias,
        mid_gain=grad_mid_gain,
        mid_shift=grad_mid_shift,
        expand_bias=grad_expand_bias,
        contract_bias=grad_contract_bias,
    )
    return grad_middle, grad_mixed, grads, small


def own_joint(joint_weight, query_bias, value_bias, shards, shard):
    width = joint_weight.shape[0]
    own = width // shards
    weight = lax.dynamic_slice_in_dim(joint_weight.reshape(width, 3, width), shard * own, own, 2)
    bias_q = lax.dynamic_slice_in_dim(query_bias, shard * own, own, 0)
    bias_v = lax.dynamic_slice_in_dim(value_bias, shard * own, own, 0)
    return weight, (bias_q, None, bias_v)


def own_parts(normed_all, weight, biases):
    flat = normed_all.reshape(-1, normed_all.shape[3])
    out = []
    for index in range(3):
        part = mm(flat, weight[:, index])
        if biases[index] is not None:
            part = part + biases[index]
        out.append(part.astype(bf16).reshape(normed_all.shape[:3] + (weight.shape[2],)))
    return out


def by_sender(joint_weight, shards):
    width = joint_weight.shape[0]
    array = joint_weight.reshape(width, 3, shards, width // shards)
    return array.transpose(0, 2, 1, 3).reshape(width, 3 * width)


def joint_back(received, joint_by_sender):
    shards, clips, rows, width = received.shape
    flat = received.reshape(shards, clips * rows, width).transpose(1, 0, 2)
    return mm(flat.reshape(clips * rows, shards * width), joint_by_sender, NT)


def spread(vector, shards, shard):
    full = jnp.zeros((vector.shape[0] * shards,), f32)
    return lax.dynamic_update_slice_in_dim(full, vector, shard * vector.shape[0], 0)


def joint_small(columns, shards, shard):
    own = columns.shape[0] // 3
    return dict(
        query_bias=spread(columns[:own], shards, shard),
        value_bias=spread(columns[2 * own :], shards, shard),
    )


ORDER = (
    "pre_gain",
    "pre_shift",
    "query_bias",
    "value_bias",
    "out_bias",
    "mid_gain",
    "mid_shift",
    "expand_bias",
    "contract_bias",
)
BLOCK = (
    "pre_gain",
    "pre_shift",
    "joint",
    "query_bias",
    "value_bias",
    "out",
    "out_bias",
    "mid_gain",
    "mid_shift",
    "expand",
    "expand_bias",
    "contract",
    "contract_bias",
)
FRAMES = 8
GRID = 14
MOST_VISIBLE = FRAMES * max(
    high * wide
    for high in range(1, GRID + 1)
    for wide in range(1, GRID + 1)
    if 2 * high * wide < GRID * GRID
)


def body(fsdp_size, seq_size, tokens, visible, slot_token, positions, *rest):
    e_shard = dict(zip(BLOCK, rest[:13]))
    embed_weight, embed_bias, mask_token = rest[13:16]
    p_shard = dict(zip(BLOCK, rest[16:29]))
    cotangent = rest[29]
    shard = lax.axis_index("seq")
    clips, slots, width = tokens.shape
    span = visible.shape[1]

    e_out = gather(e_shard["out"])

    place = lax.broadcasted_iota(jnp.int32, (1, 1, span), 2)
    slot_visible = jnp.any(
        (slot_token[:, :, None] == place) & (visible[:, None, :] > 0), axis=2
    )
    counts = jnp.sum(slot_visible.reshape(clips, seq_size, slots).astype(jnp.int32), axis=2)
    compact = -(-MOST_VISIBLE // (16 * seq_size)) * 16
    fits = (jnp.max(counts) <= compact).astype(f32)

    vectors = [e_shard[name] for name in ORDER] + [embed_bias, mask_token]
    vectors += [p_shard[name] for name in ORDER]
    sizes = [member.shape[0] for member in vectors]
    packed = lax.all_gather(
        pack_rows(vectors + [jnp.full((1,), fits)]), "fsdp", axis=0, tiled=False
    )
    full = unpack_rows(packed, sizes + [1])
    all_fit = jnp.min(full[-1]) > 0.5

    operands = (
        tokens,
        slot_visible,
        counts,
        slot_token,
        positions,
        e_out,
        e_shard["joint"],
        e_shard["expand"],
        e_shard["contract"],
        embed_weight,
        tuple(p_shard[name] for name in ("joint", "out", "expand", "contract")),
        tuple(full[:-1]),
        cotangent,
    )
    whole = functools.partial(main, fsdp_size, seq_size, slots)
    if compact >= slots:
        return whole(*operands)
    return lax.cond(
        all_fit, functools.partial(main, fsdp_size, seq_size, compact), whole, *operands
    )


def main(
    fsdp_size,
    seq_size,
    held,
    tokens,
    slot_visible,
    counts,
    slot_token,
    positions,
    e_out,
    e_joint_shard,
    e_expand_shard,
    e_contract_shard,
    embed_shard,
    p_shards,
    vectors,
    cotangent,
):
    shard = lax.axis_index("seq")
    clips, slots, width = tokens.shape
    span = slot_visible.shape[1]
    rows = clips * slots
    small_width = cotangent.shape[2]
    head_size = width // HEADS
    small_head = small_width // PHEADS
    whole = held == slots
    e_vec = dict(zip(ORDER, vectors[:9]))
    embed_bias, mask_token = vectors[9:11]
    p_vec = dict(zip(ORDER, vectors[11:]))

    e_joint = gather(e_joint_shard)
    e_expand = gather(e_expand_shard)
    e_contract = gather(e_contract_shard)
    packed = jnp.concatenate(
        [blocks_of(member, 1, small_width)[0] for member in (*p_shards, embed_shard)], axis=0
    )
    packed = lax.all_gather(packed, "fsdp", axis=0, tiled=False)
    unpacked = []
    at = 0
    for member in (*p_shards, embed_shard):
        split = member.shape[1] // small_width
        count = member.shape[0] * split
        piece = packed[:, at : at + count].reshape(fsdp_size, split, member.shape[0], small_width)
        unpacked.append(piece.transpose(0, 2, 1, 3).reshape(-1, member.shape[1]))
        at += count
    p_joint, p_out, p_expand, p_contract, embed = unpacked

    own_visible = lax.dynamic_slice_in_dim(slot_visible, shard * slots, slots, 1)
    own_flat = own_visible.reshape(rows, 1)
    own_tokens = lax.dynamic_slice_in_dim(slot_token, shard * slots, slots, 1)
    slot_code = jnp.take(positions, own_tokens.reshape(rows), axis=0)

    if whole:
        kept = slot_visible.reshape(clips, 1, span)

        def keep(array):
            return array

        def put_back(array):
            return array

    else:
        kept = lax.broadcasted_iota(jnp.int32, (1, 1, held), 2) < counts[:, :, None]
        kept = kept.reshape(clips, 1, seq_size * held)
        ones = own_visible.astype(bf16)
        before = lax.broadcasted_iota(jnp.int32, (slots, slots), 0)
        after = lax.broadcasted_iota(jnp.int32, (slots, slots), 1)
        rank = mm(ones, (before < after).astype(bf16)).astype(jnp.int32)
        target = lax.broadcasted_iota(jnp.int32, (1, held, 1), 1)
        picks = ((rank[:, None, :] == target) & own_visible[:, None, :]).astype(bf16)

        def keep(array):
            precision = lax.Precision.HIGHEST if array.dtype == f32 else None
            picked = jnp.einsum(
                "crs,csw->crw",
                picks.astype(array.dtype),
                array.reshape(clips, slots, -1),
                precision=precision,
                preferred_element_type=f32,
            )
            return picked.astype(array.dtype).reshape(clips * held, -1)

        def put_back(array):
            placed = jnp.einsum(
                "crs,crw->csw",
                picks.astype(f32),
                array.reshape(clips, held, -1),
                precision=lax.Precision.HIGHEST,
                preferred_element_type=f32,
            )
            return placed.reshape(rows, -1)

    bias = jnp.where(kept, 0.0, -1e30).astype(f32)
    tiled = held % 16 == 0

    def by_clip(array):
        if tiled:
            return array
        shards, count, length, lanes = array.shape
        return array.transpose(1, 0, 2, 3).reshape(1, count, shards * length, lanes)

    inputs = tokens.reshape(rows, width)
    normed = norm_layer(inputs, e_vec["pre_gain"], e_vec["pre_shift"])
    normed_kept = keep(normed).reshape(1, clips, held, width)
    normed_all = exchange(jnp.broadcast_to(normed_kept, (seq_size, clips, held, width)))
    queries = (mm(normed, e_joint[:, :width]) + e_vec["query_bias"]).astype(bf16)
    joined = mm(normed_all.reshape(-1, width), e_joint[:, width:])
    joined_bias = jnp.concatenate([jnp.zeros_like(e_vec["value_bias"]), e_vec["value_bias"]])
    joined = (joined + joined_bias).astype(bf16)
    mixed = attend(
        queries.reshape(clips, slots, width),
        by_clip(joined.reshape(seq_size, clips, held, 2 * width)),
        head_size,
        bias,
    ).reshape(rows, width)
    middle = inputs + mm(mixed, e_out) + e_vec["out_bias"]
    normed_mid = norm_layer(middle, e_vec["mid_gain"], e_vec["mid_shift"])
    active = gelu(mm(normed_mid, e_expand) + e_vec["expand_bias"])
    encoded = middle + mm(active, e_contract) + e_vec["contract_bias"]
    context = encoded.astype(bf16)

    embedded = mm(context, embed) + embed_bias
    pred_input = jnp.where(own_flat, embedded, mask_token) + slot_code
    p_normed = norm_layer(pred_input, p_vec["pre_gain"], p_vec["pre_shift"])
    p_queries = (mm(p_normed, p_joint[:, :small_width]) + p_vec["query_bias"]).astype(bf16)
    p_bias = jnp.concatenate([jnp.zeros_like(p_vec["value_bias"]), p_vec["value_bias"]])
    p_normed_all = []
    p_mixed = []
    for clip in range(clips):
        own = p_normed.reshape(clips, slots, small_width)[clip]
        every = lax.all_gather(own, "seq", axis=0, tiled=True)
        p_joined = (mm(every, p_joint[:, small_width:]) + p_bias).astype(bf16)
        p_normed_all.append(every)
        p_mixed.append(
            attend(
                p_queries.reshape(clips, slots, small_width)[clip : clip + 1],
                p_joined.reshape(1, 1, span, 2 * small_width),
                small_head,
                None,
            )
        )
    p_mixed = jnp.concatenate(p_mixed, axis=0).reshape(rows, small_width)
    p_middle = pred_input + mm(p_mixed, p_out) + p_vec["out_bias"]
    p_normed_mid = norm_layer(p_middle, p_vec["mid_gain"], p_vec["mid_shift"])
    p_hidden = mm(p_normed_mid, p_expand) + p_vec["expand_bias"]
    p_active = gelu(p_hidden)
    predicted = p_middle + mm(p_active, p_contract) + p_vec["contract_bias"]

    grad_middle, grad_mixed, p_grads, p_small = feed_back(
        cotangent.reshape(rows, small_width),
        p_mixed,
        p_middle,
        p_normed_mid,
        p_hidden,
        p_active,
        (p_out, p_expand, p_contract),
        p_vec["mid_gain"],
    )
    own_weight, own_bias = own_joint(
        p_joint, p_vec["query_bias"], p_vec["value_bias"], seq_size, shard
    )
    own_width = small_width // seq_size
    grad_mixed = grad_mixed.reshape(rows, seq_size, own_width).transpose(1, 0, 2)
    grad_mixed = exchange(grad_mixed.reshape(seq_size, clips, slots, own_width))
    p_by_sender = by_sender(p_joint, seq_size)
    grad_normed = []
    p_grad_joint = 0.0
    p_columns = 0.0
    for clip in range(clips):
        every = p_normed_all[clip].reshape(1, 1, span, small_width)
        grads = attend_back(
            *own_parts(every, own_weight, own_bias),
            grad_mixed[:, clip].reshape(1, 1, span, own_width),
            small_head,
            None,
            seq_size,
        )
        flat = grads.reshape(span, 3 * own_width)
        p_grad_joint = p_grad_joint + mm(p_normed_all[clip], flat, TN)
        p_columns = p_columns + jnp.sum(flat.astype(f32), axis=0)
        grad_normed.append(joint_back(exchange(grads), p_by_sender))
    p_small.update(joint_small(p_columns, seq_size, shard))
    grad_norm, p_small["pre_gain"], p_small["pre_shift"] = norm_back(
        pred_input, p_vec["pre_gain"], jnp.concatenate(grad_normed, axis=0)
    )
    grad_pred_input = grad_middle + grad_norm
    grad_mask_token = jnp.sum(jnp.where(own_flat, 0.0, grad_pred_input), axis=0)
    grad_embedded = jnp.where(own_flat, grad_pred_input, 0.0).astype(bf16)
    grad_embed = mm(context, grad_embedded, TN).astype(bf16)
    grad_embed_bias = jnp.sum(grad_embedded.astype(f32), axis=0)

    p_grad_joint = jnp.pad(p_grad_joint.astype(bf16), ((0, 0), (0, small_width - 3 * own_width)))
    members = (p_grad_joint, *p_grads, grad_embed)
    p_part = scatter(
        jnp.concatenate([blocks_of(member, fsdp_size, small_width) for member in members], axis=1)
    )

    grad_context = mm(keep(grad_embedded), embed, NT)
    kept_mid = keep(normed_mid)
    kept_hidden = mm(kept_mid, e_expand) + e_vec["expand_bias"]
    grad_middle, grad_mixed, e_grads, e_small = feed_back(
        grad_context,
        keep(mixed),
        keep(middle),
        kept_mid,
        kept_hidden,
        gelu(kept_hidden),
        (e_out, e_expand, e_contract),
        e_vec["mid_gain"],
    )
    expand_part = scatter(e_grads[1].reshape(fsdp_size, -1, e_grads[1].shape[1]))
    contract_part = scatter(e_grads[2].reshape(fsdp_size, -1, e_grads[2].shape[1]))
    own_weight, own_bias = own_joint(
        e_joint, e_vec["query_bias"], e_vec["value_bias"], seq_size, shard
    )
    own_width = width // seq_size
    grad_mixed = grad_mixed.reshape(clips * held, seq_size, own_width).transpose(1, 0, 2)
    grad_mixed = exchange(grad_mixed.reshape(seq_size, clips, held, own_width))
    parts = own_parts(normed_all, own_weight, own_bias)
    grads = attend_back(
        *[by_clip(member) for member in (*parts, grad_mixed)], head_size, bias, seq_size
    )
    flat = grads.reshape(-1, 3 * own_width)
    e_grad_joint = mm(normed_all.reshape(-1, width), flat, TN).astype(bf16)
    e_small.update(joint_small(jnp.sum(flat.astype(f32), axis=0), seq_size, shard))
    grad_norm, e_small["pre_gain"], e_small["pre_shift"] = norm_back(
        keep(inputs),
        e_vec["pre_gain"],
        joint_back(exchange(grads), by_sender(e_joint, seq_size)),
    )
    grad_tokens = put_back(grad_middle + grad_norm)

    small = [e_small[name] for name in ORDER] + [grad_embed_bias, grad_mask_token]
    small += [p_small[name] for name in ORDER]
    small = [member.reshape(fsdp_size, -1) for member in small]
    sizes = [member.shape[1] for member in small]
    count = -(-sum(sizes) // (16 * own_width)) * 16
    small.append(jnp.zeros((fsdp_size, count * own_width - sum(sizes)), f32))
    small = jnp.concatenate(small, axis=1).astype(bf16).reshape(fsdp_size, count, own_width)
    late = scatter(
        jnp.concatenate(
            [
                blocks_of(e_grad_joint, fsdp_size, own_width),
                blocks_of(e_grads[0], fsdp_size, own_width),
                small,
            ],
            axis=1,
        )
    )
    own_rows = width // fsdp_size
    joint_rows = 3 * own_rows
    p_rows = small_width // fsdp_size
    e_columns = late[:joint_rows]
    p_columns = p_part[:p_rows, : 3 * (small_width // seq_size)]
    e_whole = lax.all_gather(e_columns, "seq", axis=0, tiled=False)
    p_whole = lax.all_gather(p_columns, "seq", axis=0, tiled=False)
    expand_sum, contract_sum, p_sum, late_sum = lax.psum(
        (expand_part, contract_part, p_part[p_rows:], late[joint_rows:]), "seq"
    )
    e_joint_out = e_whole.reshape(seq_size, 3, own_rows, own_width)
    e_joint_out = e_joint_out.transpose(2, 1, 0, 3).reshape(own_rows, 3 * width)
    p_joint_out = p_whole.reshape(seq_size, p_rows, 3, -1)
    p_joint_out = p_joint_out.transpose(1, 2, 0, 3).reshape(p_rows, 3 * small_width)
    out_sum = from_blocks(late_sum[: seq_size * own_rows], width)
    vector_sum = late_sum[seq_size * own_rows :].reshape(-1)
    small_out = []
    at = 0
    for size in sizes:
        small_out.append(vector_sum[at : at + size].astype(f32))
        at += size

    def cut(array, at, rows, lanes):
        split = lanes // small_width
        return from_blocks(array[at : at + split * rows], lanes), at + split * rows

    p_wide = p_shards[2].shape[1]
    p_out_sum, at = cut(p_sum, 0, p_rows, small_width)
    p_expand_sum, at = cut(p_sum, at, p_rows, p_wide)
    p_contract_sum, at = cut(p_sum, at, p_shards[3].shape[0], small_width)
    embed_sum, at = cut(p_sum, at, own_rows, small_width)

    def ordered(vec, joint, out, expand, contract):
        vec = dict(
            zip(ORDER, vec),
            joint=joint.astype(f32),
            out=out.astype(f32),
            expand=expand.astype(f32),
            contract=contract.astype(f32),
        )
        return tuple(vec[name] for name in BLOCK)

    return (
        encoded.reshape(tokens.shape),
        predicted.reshape(cotangent.shape),
        grad_tokens.reshape(tokens.shape),
        *ordered(small_out[:9], e_joint_out, out_sum, expand_sum, contract_sum),
        embed_sum.astype(f32),
        small_out[9],
        small_out[10],
        *ordered(small_out[11:], p_joint_out, p_out_sum, p_expand_sum, p_contract_sum),
    )


def solution(mesh):
    cut, rows, vec, full = P("fsdp", "seq", None), P("fsdp", None), P("fsdp"), P()
    block = (vec, vec, rows, vec, vec, rows, vec, vec, vec, rows, vec, rows, vec)
    return jax.shard_map(
        functools.partial(body, mesh.shape["fsdp"], mesh.shape["seq"]),
        mesh=mesh,
        in_specs=(cut, rows, rows, full, *block, rows, vec, vec, *block, cut),
        out_specs=(cut, cut, cut, *block, rows, vec, vec, *block),
        check_vma=False,
    )
```

time: 1330 us -> 1040 us (0.78)
  waiting for transfers between devices: 492 us -> 373 us
  Pallas kernels: 277 us -> 176 us
  blocking collectives: 105 us -> 55 us
  matrix products: 225 us -> 197 us
    reduce_scatter x8 -> x4, waiting for transfers between devices: 0.11 us -> 174 us  [scatter(): return lax.psum_scatter(array, 'fsdp', scatter_dimension=0, tiled=True)[0]]
    all_to_all x4 -> x6, waiting for transfers between devices: 159 us -> 41 us  [exchange(): return lax.all_to_all(array, 'seq', split_axis=0, concat_axis=0, tiled=True)]
    all_gather x2 -> x3, waiting for transfers between devices: 115 us -> 0.01 us  [the longest x2 0.01 us: main(): every = lax.all_gather(own, 'seq', axis=0, tiled=True)]
    psum x2 -> x1, waiting for transfers between devices: 186 us -> 74.6 us  [main(): lax.psum((expand_part, contract_part, p_part[p_rows:], late[joint_rows:])...]
    pallas_call x2 -> x3, Pallas kernels: 156 us -> 86.8 us  [attend_back(): pl.pallas_call(functools.partial(backward_kernel, 1.0 / math.sqrt(head_si...]
    all_gather x6 -> x4, waiting for transfers between devices: 28.7 us -> 81.1 us  [gather(): return lax.all_gather(array, 'fsdp', axis=0, tiled=True)]
    another operation x10 -> x6, local copies, waits for them, and re-layouts: 50 us -> 2.45 us  [the longest x2 43.2 us: attention_back(): back = slots_from_heads(jnp.stack(grads), shards)]
    dot_general x43 -> x42, matrix products: 225 us -> 183 us  [mm(): return lax.dot_general(left, right, dims, preferred_element_type=f32)]
  transfers between devices with their start and end apart: 23 -> 18, of which waited for: 9 -> 11; matrix products, arithmetic and copies ran while one was open for 26% -> 25% of each run, Pallas kernels for 16% -> 11%
where the time goes in v2:
time: 1040 us; the launch traced here: 1030 us
  waiting for transfers between devices  373 us (36%)
  matrix products  197 us (19%)
  Pallas kernels  176 us (17%)
  local copies, waits for them, and re-layouts  129 us (12%)
  blocking collectives  55 us (5%)
  other arithmetic  54.1 us (5%)
  starting transfers between devices  28.7 us (3%)
  between operations  16 us (2%)
    dot_general x42, matrix products, mm(): return lax.dot_general(left, right, dims, preferred_element_type=f32)  183 us
    reduce_scatter x4, waiting for transfers between devices, scatter(): return lax.psum_scatter(array, 'fsdp', scatter_dimension=0, tiled=True)[0]  174 us
    pallas_call x3, Pallas kernels, attend(): pl.pallas_call(functools.partial(forward_kernel, 1.0 / math.sqrt(head_siz...  89.3 us
    pallas_call x3, Pallas kernels, attend_back(): pl.pallas_call(functools.partial(backward_kernel, 1.0 / math.sqrt(head_si...  86.8 us
    all_gather x4, waiting for transfers between devices, gather(): return lax.all_gather(array, 'fsdp', axis=0, tiled=True)  81.1 us
    psum x1, waiting for transfers between devices, main(): lax.psum((expand_part, contract_part, p_part[p_rows:], late[joint_rows:])...  74.6 us
    all_to_all x6, waiting for transfers between devices, exchange(): return lax.all_to_all(array, 'seq', split_axis=0, concat_axis=0, tiled=True)  41 us
    all_gather x1, blocking collectives, main(): e_whole = lax.all_gather(e_columns, 'seq', axis=0, tiled=False)  29.9 us
  transfers between devices with their start and end apart: 18, of which 11 were waited for; matrix products, arithmetic and copies ran while one was open for 25% of the time, Pallas kernels for 11%

profile of v2, /device:TPU:0, one launch (start us, length us, event | category | flops | bytes accessed | tf_op | source)
XLA Modules:
  0.0 1034.7 jit_solution(4811902716009263067)
XLA Ops:
  22.3 10.7 %all-gather.4 = f32[256,128]{1,0:T(8,128)S(1)} all-gather(f32[32,128]{1,0:T(8,128)S(1)} %concatenate.53), channel_id=6, replica_groups=mesh['fsdp'=8,'seq'=4] {'fsdp'}, dimensions={0}, use_global_device_ids=true | all-gather | bytes 147456 | tf_op jit(solution)/shard_map/all_gather | solution.py:414
  35.1 5.5 all-gather.43.cloned.1.call-done
  40.6 982.8 %conditional.4 = (f32[2,392,1024]{2,1,0:T(8,128)}, f32[2,392,384]{2,1,0:T(8,128)}, f32[2,392,1024]{2,1,0:T(8,128)}, bf16[128,3072]{0,1:T(8,128)(2,1)S(1)}, bf16[...) conditional(s32[]{:T(128)} %convert_element_type.826, ...), branch_computations={%region_4.50_spmd, %region_49.99_spmd} | conditional | flops 209832574976 | bytes 1220743040
  80.2 5.8 gather_fusion.1
  108.1 29.3 %all-gather.31.cloned.1.call-done = bf16[1024,3072]{0,1:T(8,128)(2,1)} async-done(((bf16[128,3072]{0,1:T(8,128)(2,1)}), bf16[1024,3072]{0,1:T(8,128)(2,1)}) %all-gather.31.cloned.1.call-update) | async-done | bytes 6291472 | tf_op jit(solution)/shard_map/cond/branch_1_fun/all_gather | solution.py:241
  142.5 11.3 %add_convert_fusion.17 = bf16[1536,2048]{1,0:T(8,128)(2,1)} fusion(bf16[1536,1024]{1,0:T(8,128)(2,1)} %bitcast.126, f32[2048]{0:T(1024)S(1)} %concatenate.44, bf16[1024,3072]{0,1:T(8,128)(2,1)} %all-gather.31.cloned.1.call-done), kind=kOutput, calls=%fused_computation.220 | convolution fusion | flops 6448742400 | bytes 13639680 | tf_op jit(solution)/shard_map/cond/branch_1_fun/dot_general | solution.py:25
  153.7 35.2 %attend.9 = bf16[2,392,1024]{2,1,0:T(8,128)(2,1)} custom-call(bf16[2,392,1024]{2,1,0:T(8,128)(2,1)} %bitcast.952, bf16[4,2,192,2048]{3,2,1,0:T(8,128)(2,1)} %bitcast.947, bf16[4,2,192,2048]{3,2,1,0:T(8,128)(2,1)} %bitcast.948, f32[2,1,768]{2,1,0:T(1,128)} %compare_select_fusion.1.rest_0_), custom_call_target="tpu_custom_call" | custom-call | flops 9865003008 | bytes 6291456 | tf_op jit(solution)/shard_map/cond/branch_1_fun/attend/pallas_call | solution.py:109
  188.9 5.6 fusion.98
  203.6 46.4 %all-gather.35.cloned.1.call-done = bf16[4096,1024]{1,0:T(8,128)(2,1)} async-done(((bf16[512,1024]{1,0:T(8,128)(2,1)}), bf16[4096,1024]{1,0:T(8,128)(2,1)}) %all-gather.35.cloned.1.call-update) | async-done | bytes 8388624 | tf_op jit(solution)/shard_map/cond/branch_1_fun/all_gather | solution.py:241
  250.0 21.4 %add_add_fusion.1 = f32[784,1024]{1,0:T(8,128)S(1)} fusion(f32[784,1024]{1,0:T(8,128)} %fusion.98, bf16[4096,1024]{1,0:T(8,128)(2,1)} %all-gather.35.cloned.1.call-done, f32[4096]{0:T(1024)} %bitcast.927, bf16[1024,4096]{1,0:T(8,128)(2,1)} %all-gather.33.cloned.1.call-done, f32[1024]{0:T(1024)} %bitcast.936, f32[1024]{0:T(1024)S(1)} %bitcast.921, ...), kind=kOutput, calls=%fused_computation.255 | convolution fusion | flops 13178224640 | bytes 23234688 | tf_op jit(solution)/shard_map/cond/branch_1_fun/dot_general | solution.py:25
  280.4 6.2 copy.413
  302.5 9.8 convolution_add_fusion.11
  316.5 27.3 %attend.10 = bf16[1,392,384]{2,1,0:T(8,128)(2,1)} custom-call(bf16[1,392,384]{2,1,0:T(8,128)(2,1)} %get-tuple-element.1064.q_ref, bf16[1,1,1568,768]{3,2,1,0:T(8,128)(2,1)} %fusion.82.k_ref.v_ref, bf16[1,1,1568,768]{3,2,1,0:T(8,128)(2,1)} %fusion.82.k_ref.v_ref), custom_call_target="tpu_custom_call" | custom-call | flops 7552892928 | bytes 2408448 | tf_op jit(solution)/shard_map/cond/branch_1_fun/attend/pallas_call | solution.py:109
  348.1 26.9 %attend.11 = bf16[1,392,384]{2,1,0:T(8,128)(2,1)} custom-call(bf16[1,392,384]{2,1,0:T(8,128)(2,1)} %get-tuple-element.1065.q_ref, bf16[1,1,1568,768]{3,2,1,0:T(8,128)(2,1)} %fusion.83.k_ref.v_ref, bf16[1,1,1568,768]{3,2,1,0:T(8,128)(2,1)} %fusion.83.k_ref.v_ref), custom_call_target="tpu_custom_call" | custom-call | flops 7552892928 | bytes 2408448 | tf_op jit(solution)/shard_map/cond/branch_1_fun/attend/pallas_call | solution.py:109
  417.3 6.3 all-to-all-done.7
  434.3 33.5 %attend_back.9 = bf16[4,1,392,288]{3,2,1,0:T(8,128)(2,1)} custom-call(bf16[1,1,1568,96]{3,2,1,0:T(8,128)(2,1)} %fusion.93.q_ref, bf16[1,1,1568,96]{3,2,1,0:T(8,128)(2,1)} %fusion.94.k_ref, bf16[1,1,1568,96]{3,2,1,0:T(8,128)(2,1)} %fusion.92.v_ref, bf16[1,1,1568,96]{3,2,1,0:T(8,128)(2,1)} %bitcast.855), custom_call_target="tpu_custom_call" | custom-call | flops 18882232320 | bytes 2107392 | tf_op jit(solution)/shard_map/cond/branch_1_fun/attend_back/pallas_call | solution.py:217
  474.5 33.6 %attend_back.10 = bf16[4,1,392,288]{3,2,1,0:T(8,128)(2,1)} custom-call(bf16[1,1,1568,96]{3,2,1,0:T(8,128)(2,1)} %fusion.91.q_ref, bf16[1,1,1568,96]{3,2,1,0:T(8,128)(2,1)} %fusion.95.k_ref, bf16[1,1,1568,96]{3,2,1,0:T(8,128)(2,1)} %fusion.90.v_ref, bf16[1,1,1568,96]{3,2,1,0:T(8,128)(2,1)} %bitcast.853), custom_call_target="tpu_custom_call" | custom-call | flops 18882232320 | bytes 2107392 | tf_op jit(solution)/shard_map/cond/branch_1_fun/attend_back/pallas_call | solution.py:217
  536.4 7.0 all-to-all-done.9
  551.5 9.4 fusion.187
  585.4 7.4 all-to-all-done.10.g_ref
  592.9 19.8 %attend_back.11 = bf16[4,2,192,768]{3,2,1,0:T(8,128)(2,1)} custom-call(bf16[4,2,192,256]{3,2,1,0:T(8,128)(2,1)} %bitcast.959, bf16[4,2,192,256]{3,2,1,0:T(8,128)(2,1)} %bitcast.958, bf16[4,2,192,256]{3,2,1,0:T(8,128)(2,1)} %bitcast.960, bf16[4,2,192,256]{3,2,1,0:T(8,128)(2,1)} %all-to-all-done.10.g_ref, f32[2,1,768]{2,1,0:T(1,128)} %compare_select_fusion.1.rest_0_), custom_call_target="tpu_custom_call" | custom-call | flops 12079595520 | bytes 5505024 | tf_op jit(solution)/shard_map/cond/branch_1_fun/attend_back/pallas_call | solution.py:217
  635.4 5.7 bitcast_convert_fusion.2
  650.2 20.3 %all-to-all-done.11 = bf16[4,2,192,768]{3,2,1,0:T(8,128)(2,1)} async-done(((bf16[4,2,192,768]{3,2,1,0:T(8,128)(2,1)}), bf16[4,2,192,768]{3,2,1,0:T(8,128)(2,1)}, u32[]{:S(2)}, u32[]{:S(2)}) %all-to-all-start.11) | async-done | bytes 2359328 | tf_op jit(solution)/shard_map/cond/branch_1_fun/all_to_all | solution.py:237
  675.0 7.5 multiply_reduce_fusion.19
  686.1 9.2 convolution_convert_fusion.12
  696.6 8.8 convolution_convert_fusion.13
  707.5 26.2 %reduce-scatter.17.cloned.1.call-done = bf16[1,912,256]{2,1,0:T(8,128)(2,1)} async-done(((bf16[8,912,256]{2,1,0:T(8,128)(2,1)}), bf16[1,912,256]{2,1,0:T(8,128)(2,1)}) %reduce-scatter.17.cloned.1.call-update) | async-done | bytes 466960 | tf_op jit(solution)/shard_map/cond/branch_1_fun/reduce_scatter | solution.py:245
  735.3 73.4 %reduce-scatter.21.cloned.1.call-done = bf16[1,512,1024]{2,1,0:T(8,128)(2,1)} async-done(((bf16[8,512,1024]{2,1,0:T(8,128)(2,1)}), bf16[1,512,1024]{2,1,0:T(8,128)(2,1)}) %reduce-scatter.21.cloned.1.call-update) | async-done | bytes 1048592 | tf_op jit(solution)/shard_map/cond/branch_1_fun/reduce_scatter | solution.py:245
  808.7 74.8 %reduce-scatter.19.cloned.1.call-done = bf16[1,128,4096]{2,1,0:T(8,128)(2,1)} async-done(((bf16[8,128,4096]{2,1,0:T(8,128)(2,1)}), bf16[1,128,4096]{2,1,0:T(8,128)(2,1)}) %reduce-scatter.19.cloned.1.call-update) | async-done | bytes 1048592 | tf_op jit(solution)/shard_map/cond/branch_1_fun/reduce_scatter | solution.py:245
  892.8 14.4 %all-gather.3 = bf16[192,288]{1,0:T(8,128)(2,1)S(1)} all-gather(bf16[48,288]{1,0:T(8,128)(2,1)S(1)} %slice.590), channel_id=5, replica_groups=mesh['fsdp'=8,'seq'=4] {'seq'}, dimensions={0}, use_global_device_ids=true | all-gather | bytes 138240 | tf_op jit(solution)/shard_map/cond/branch_1_fun/all_gather | solution.py:698
  908.3 29.9 %all_gather.65 = bf16[4,384,256]{2,1,0:T(8,128)(2,1)S(1)} all-gather(bf16[1,384,256]{2,1,0:T(8,128)(2,1)S(1)} %slice-done.5), channel_id=1, replica_groups=mesh['fsdp'=8,'seq'=4] {'seq'}, dimensions={0}, use_global_device_ids=true | all-gather | bytes 983040 | tf_op jit(solution)/shard_map/cond/branch_1_fun/all_gather | solution.py:697
  938.6 74.6 %all-reduce.25.cloned.1.call-done = (bf16[528,256]{1,0:T(8,128)(2,1)}, bf16[128,4096]{1,0:T(8,128)(2,1)}, bf16[512,1024]{1,0:T(8,128)(2,1)}, bf16[560,384]{1,0:T(8,128)(2,1)}) async-done(((bf16[528,256]{1,0:T(8,128)(2,1)}, bf16[128,4096]{1,0:T(8,128)(2,1)}, bf16[512,1024]{1,0:T(8,128)(2,1)}, bf16[560,384]{1,0:T(8,128)(2,1)}), (bf16[528,256]{1,0:T(8,128)(2,1)}, bf16[128,4096]{1,0:T(8,128)(2,1)}, ...) | async-done | bytes 2797584 | tf_op jit(solution)/shard_map/cond/branch_1_fun/psum | solution.py:699
  (505 shorter events, 309.9 us)
Async XLA Ops:
  7.2 33.4 %all-gather.43.cloned.1.call-start = ((), (), s32[]{:S(2)}) async-start(), calls=%async_computation.42 | async-start | bytes 2359296 | tf_op jit(solution)/shard_map/all_gather | solution.py:241
  45.1 25.5 %copy-start.116 = (f32[1024]{0:T(1024)}, f32[1024]{0:T(1024)S(1)}, u32[]{:S(2)}) copy-start(f32[1024]{0:T(1024)S(1)} %get-tuple-element.399) | copy-start | bytes 12292
  45.1 44.2 %copy-start.94 = (f32[8,1,128]{2,1,0:T(1,128)}, f32[8,1,128]{2,1,0:T(1,128)S(1)}, u32[]{:S(2)}) copy-start(f32[8,1,128]{2,1,0:T(1,128)S(1)} %get-tuple-element.364) | copy-start | bytes 12292
  45.1 45.9 %all-gather.41.cloned.1.call-start = ((), (), s32[]{:S(2)}) async-start(), calls=%async_computation.40 | async-start | bytes 4866048 | tf_op jit(solution)/shard_map/cond/branch_1_fun/all_gather | solution.py:479
  50.6 86.7 %all-gather.31.cloned.1.call-start = ((), (), s32[]{:S(2)}) async-start(), calls=%async_computation.31 | async-start | bytes 7077888 | tf_op jit(solution)/shard_map/cond/branch_1_fun/all_gather | solution.py:241
  53.2 150.4 %all-gather.33.cloned.1.call-start = ((), (), s32[]{:S(2)}) async-start(), calls=%async_computation.32 | async-start | bytes 9437184 | tf_op jit(solution)/shard_map/cond/branch_1_fun/all_gather | solution.py:241
  53.8 196.2 %all-gather.35.cloned.1.call-start = ((), (), s32[]{:S(2)}) async-start(), calls=%async_computation.33 | async-start | bytes 9437184 | tf_op jit(solution)/shard_map/cond/branch_1_fun/all_gather | solution.py:241
  58.5 84.0 %all-to-all-start.6 = ((bf16[4,2,192,1024]{3,2,1,0:T(8,128)(2,1)}), bf16[4,2,192,1024]{3,2,1,0:T(8,128)(2,1)}, u32[]{:S(2)}, u32[]{:S(2)}) async-start(bf16[4,2,192,1024]{3,2,1,0:T(8,128)(2,1)} %broadcast_in_dim.111), calls=%async_computation.10 | async-start | bytes 6291456 | tf_op jit(solution)/shard_map/cond/branch_1_fun/all_to_all | solution.py:237
  63.3 249.0 %all-gather.37.cloned.1.call-start = ((), (), s32[]{:S(2)}) async-start(), calls=%async_computation.34 | async-start | bytes 1505280 | tf_op jit(solution)/shard_map/cond/branch_1_fun/all_gather | solution.py:573
  101.4 36.0 %copy-start.117 = (f32[1024]{0:T(1024)S(1)}, f32[1024]{0:T(1024)}, u32[]{:S(2)}) copy-start(f32[1024]{0:T(1024)} %copy-done.116) | copy-start | bytes 12292
  250.0 21.4 %copy-start.109 = (f32[384]{0:T(512)S(1)}, f32[384]{0:T(512)}, u32[]{:S(2)}) copy-start(f32[384]{0:T(512)} %copy-done.108) | copy-start | bytes 4612
  271.4 311.7 %copy-start.5 = (f32[784,1024]{1,0:T(8,128)}, f32[784,1024]{1,0:T(8,128)S(1)}, u32[]{:S(2)}) copy-start(f32[784,1024]{1,0:T(8,128)S(1)} %add_add_fusion.1) | copy-start | bytes 9633796
  278.3 65.5 %all-gather.39.cloned.1.call-start = ((), (), s32[]{:S(2)}) async-start(), calls=%async_computation.35 | async-start | bytes 1505280 | tf_op jit(solution)/shard_map/cond/branch_1_fun/all_gather | solution.py:573
  302.4 9.8 copy-start.143
  348.1 26.9 %copy-start.89 = (bf16[1,392,384]{2,1,0:T(8,128)(2,1)S(1)}, bf16[1,392,384]{2,1,0:T(8,128)(2,1)}, u32[]{:S(2)}) copy-start(bf16[1,392,384]{2,1,0:T(8,128)(2,1)} %attend.10) | copy-start | bytes 903172
  348.1 28.8 %copy-start.130 = (f32[384]{0:T(512)S(1)}, f32[384]{0:T(512)}, u32[]{:S(2)}) copy-start(f32[384]{0:T(512)} %add.651) | copy-start | bytes 4612
  398.0 10.3 copy-start.150
  398.0 25.5 %all-to-all-start.7 = ((bf16[4,2,392,96]{2,1,3,0:T(2,128)(2,1)}), bf16[4,2,392,96]{2,1,3,0:T(2,128)(2,1)}, u32[]{:S(2)}, u32[]{:S(2)}) async-start(bf16[4,2,392,96]{2,1,3,0:T(2,128)(2,1)} %reshape.1222), calls=%async_computation.11 | async-start | bytes 1572864 | tf_op jit(solution)/shard_map/cond/branch_1_fun/all_to_all | solution.py:237
  470.2 40.3 %all-to-all-start.8 = ((bf16[4,1,392,288]{2,3,1,0:T(8,128)(2,1)}), bf16[4,1,392,288]{2,3,1,0:T(8,128)(2,1)}, u32[]{:S(2)}, u32[]{:S(2)}) async-start(bf16[4,1,392,288]{2,3,1,0:T(8,128)(2,1)} %copy.398), calls=%async_computation.12 | async-start | bytes 2359296 | tf_op jit(solution)/shard_map/cond/branch_1_fun/all_to_all | solution.py:237
  510.5 32.9 %all-to-all-start.9 = ((bf16[4,1,392,288]{2,3,1,0:T(8,128)(2,1)}), bf16[4,1,392,288]{2,3,1,0:T(8,128)(2,1)}, u32[]{:S(2)}, u32[]{:S(2)}) async-start(bf16[4,1,392,288]{2,3,1,0:T(8,128)(2,1)} %copy.406), calls=%async_computation.13 | async-start | bytes 2359296 | tf_op jit(solution)/shard_map/cond/branch_1_fun/all_to_all | solution.py:237
  549.2 11.7 %slice-start.6 = ((s8[8388608]{0:T(1024)(128)(4,1)}), s8[4194304]{0:T(1024)(128)(4,1)S(1)}, s32[]{:S(2)}) async-start(s8[8388608]{0:T(1024)(128)(4,1)} %bitcast.945), calls=%async_computation.49 | async-start | bytes 8388608
  551.5 13.9 %copy-start.46 = (f32[384,1024]{1,0:T(8,128)}, f32[384,1024]{1,0:T(8,128)S(1)}, u32[]{:S(2)}) copy-start(f32[384,1024]{1,0:T(8,128)S(1)} %fusion.194) | copy-start | bytes 4718596
  569.0 23.9 %all-to-all-start.10 = ((bf16[4,2,192,256]{3,2,1,0:T(8,128)(2,1)}), bf16[4,2,192,256]{3,2,1,0:T(8,128)(2,1)}, u32[]{:S(2)}, u32[]{:S(2)}) async-start(bf16[4,2,192,256]{3,2,1,0:T(8,128)(2,1)} %bitcast.777), calls=%async_computation.14 | async-start | bytes 1572864 | tf_op jit(solution)/shard_map/cond/branch_1_fun/all_to_all | solution.py:237
  573.2 132.3 %reduce-scatter.23.cloned.1.call-start = ((), (), s32[]{:S(2)}) async-start(), calls=%async_computation.39 | async-start | bytes 4202496 | tf_op jit(solution)/shard_map/cond/branch_1_fun/reduce_scatter | solution.py:245
  612.6 57.9 %all-to-all-start.11 = ((bf16[4,2,192,768]{3,2,1,0:T(8,128)(2,1)}), bf16[4,2,192,768]{3,2,1,0:T(8,128)(2,1)}, u32[]{:S(2)}, u32[]{:S(2)}) async-start(bf16[4,2,192,768]{3,2,1,0:T(8,128)(2,1)} %attend_back.11), calls=%async_computation.15 | async-start | bytes 4718592 | tf_op jit(solution)/shard_map/cond/branch_1_fun/all_to_all | solution.py:237
  617.4 116.3 %reduce-scatter.17.cloned.1.call-start = ((), (), s32[]{:S(2)}) async-start(), calls=%async_computation.36 | async-start | bytes 4202496 | tf_op jit(solution)/shard_map/cond/branch_1_fun/reduce_scatter | solution.py:245
  686.1 122.6 %reduce-scatter.21.cloned.1.call-start = ((), (), s32[]{:S(2)}) async-start(), calls=%async_computation.38 | async-start | bytes 9437184 | tf_op jit(solution)/shard_map/cond/branch_1_fun/reduce_scatter | solution.py:245
  695.4 188.0 %reduce-scatter.19.cloned.1.call-start = ((), (), s32[]{:S(2)}) async-start(), calls=%async_computation.37 | async-start | bytes 9437184 | tf_op jit(solution)/shard_map/cond/branch_1_fun/reduce_scatter | solution.py:245
  705.4 178.0 %copy-start.105 = (f32[8,48]{1,0:T(8,128)S(1)}, f32[8,48]{1,0:T(8,128)}, u32[]{:S(2)}) copy-start(f32[8,48]{1,0:T(8,128)} %get-tuple-element.396) | copy-start | bytes 4612
  705.4 178.1 %copy-start.20 = (f32[784,384]{1,0:T(8,128)S(1)}, f32[784,384]{1,0:T(8,128)}, u32[]{:S(2)}) copy-start(f32[784,384]{1,0:T(8,128)} %copy-done.19) | copy-start | bytes 3612676
  705.4 307.8 %all-reduce.25.cloned.1.call-start = ((), (), s32[]{:S(2)}) async-start(), calls=%async_computation.41 | async-start | bytes 5595136 | tf_op jit(solution)/shard_map/cond/branch_1_fun/psum | solution.py:699
  888.7 19.6 %slice-start.5 = ((bf16[1,912,256]{2,1,0:T(8,128)(2,1)}), bf16[1,384,256]{2,1,0:T(8,128)(2,1)S(1)}, s32[]{:S(2)}) async-start(bf16[1,912,256]{2,1,0:T(8,128)(2,1)} %reduce-scatter.17.cloned.1.call-done), calls=%async_computation.48 | async-start | bytes 393216 | tf_op jit(solution)/shard_map/cond/branch_1_fun/slice | solution.py:695
  (96 other events, 395.0 us)
Sparse Core Ops, SparseCore 0:
  9.9 30.5 all-gather.42
  50.7 37.2 all-gather.40
  90.7 46.6 all-gather.30
  139.3 54.3 all-gather.32
  195.6 54.3 all-gather.34
  278.4 30.8 all-gather.36
  311.0 29.9 all-gather.38
  585.5 49.4 reduce-scatter.22
  686.2 47.3 reduce-scatter.16
  737.3 71.2 reduce-scatter.20
  812.1 71.2 reduce-scatter.18
  887.3 125.8 all-reduce.24

commit v3 on v2

--- a/solution.py
+++ b/solution.py
@@ -281,6 +281,126 @@
     return out
 
 
+MESH = pl.DeviceIdType.MESH
+
+
+def line_kernel(size, cuts, *refs):
+    count = len(cuts)
+    ins, outs = refs[:count], refs[count : 2 * count]
+    scratch = refs[2 * count :]
+    inner, outer, partial = (scratch[i * count : (i + 1) * count] for i in range(3))
+    to_inner, to_outer, from_inner, from_outer = scratch[3 * count :]
+    me = lax.axis_index("seq")
+    left = me < size // 2
+    toward = jnp.where(left, me + 1, me - 1)
+    away = jnp.where(left, me - 1, me + 1)
+    end = (me == 0) | (me == size - 1)
+    barrier = pltpu.get_barrier_semaphore()
+    pl.semaphore_signal(barrier, inc=1, device_id={"seq": toward}, device_id_type=MESH)
+
+    @pl.when(jnp.logical_not(end))
+    def _():
+        pl.semaphore_signal(barrier, inc=1, device_id={"seq": away}, device_id_type=MESH)
+        pl.semaphore_wait(barrier, 2)
+
+    @pl.when(end)
+    def _():
+        pl.semaphore_wait(barrier, 1)
+
+    pieces = []
+    for index, parts in enumerate(cuts):
+        rows = ins[index].shape[0] // parts
+        for part in range(parts):
+            pieces.append((part / parts, index, slice(part * rows, (part + 1) * rows)))
+    pieces.sort(key=lambda piece: piece[:2])
+    pieces = [(slot, index, cut) for slot, (_, index, cut) in enumerate(pieces)]
+
+    def inwards(slot, index, cut):
+        return pltpu.make_async_remote_copy(
+            src_ref=ins[index].at[cut],
+            dst_ref=outer[index].at[cut],
+            send_sem=to_inner.at[slot],
+            recv_sem=from_outer.at[slot],
+            device_id={"seq": toward},
+            device_id_type=MESH,
+        )
+
+    def swap(slot, index, cut):
+        return pltpu.make_async_remote_copy(
+            src_ref=partial[index].at[cut],
+            dst_ref=inner[index].at[cut],
+            send_sem=to_inner.at[slot],
+            recv_sem=from_inner.at[slot],
+            device_id={"seq": toward},
+            device_id_type=MESH,
+        )
+
+    def outwards(slot, index, cut):
+        return pltpu.make_async_remote_copy(
+            src_ref=outs[index].at[cut],
+            dst_ref=outs[index].at[cut],
+            send_sem=to_outer.at[slot],
+            recv_sem=from_inner.at[slot],
+            device_id={"seq": away},
+            device_id_type=MESH,
+        )
+
+    @pl.when(end)
+    def _():
+        for piece in pieces:
+            inwards(*piece).start()
+        for piece in pieces:
+            outwards(*piece).wait_recv()
+        for piece in pieces:
+            inwards(*piece).wait_send()
+
+    @pl.when(jnp.logical_not(end))
+    def _():
+        for piece in pieces:
+            inwards(*piece).wait_recv()
+            _, index, cut = piece
+            both = ins[index][cut].astype(f32) + outer[index][cut].astype(f32)
+            partial[index][cut] = both.astype(bf16)
+            swap(*piece).start()
+        for piece in pieces:
+            swap(*piece).wait_recv()
+            _, index, cut = piece
+            both = partial[index][cut].astype(f32) + inner[index][cut].astype(f32)
+            outs[index][cut] = both.astype(bf16)
+            outwards(*piece).start()
+        for piece in pieces:
+            swap(*piece).wait_send()
+            outwards(*piece).wait_send()
+
+
+def line_sum(arrays, size, identity):
+    cuts = []
+    for member in arrays:
+        parts = 8
+        while parts > 1 and member.shape[0] % (16 * parts):
+            parts //= 2
+        cuts.append(parts)
+    hold = [pltpu.VMEM(member.shape, bf16) for member in arrays]
+    whole = pl.BlockSpec(memory_space=pltpu.VMEM)
+    return pl.pallas_call(
+        functools.partial(line_kernel, size, tuple(cuts)),
+        out_shape=[jax.ShapeDtypeStruct(member.shape, bf16) for member in arrays],
+        in_specs=[whole] * len(arrays),
+        out_specs=[whole] * len(arrays),
+        scratch_shapes=hold * 3 + [pltpu.SemaphoreType.DMA((sum(cuts),))] * 4,
+        compiler_params=pltpu.CompilerParams(
+            collective_id=identity, has_side_effects=True, vmem_limit_bytes=VMEM_LIMIT
+        ),
+        name="line_sum",
+    )(*arrays)
+
+
+def sum_slots(arrays, size, identity):
+    if size == 4:
+        return line_sum(arrays, size, identity)
+    return lax.psum(tuple(arrays), "seq")
+
+
 def feed_back(grad_out, mixed, middle, normed_mid, hidden, active, weights, mid_gain):
     out, expand, contract = weights
     grad_y = grad_out.astype(bf16)
@@ -297,6 +417,9 @@
     grad_out_weight = mm(mixed, grad_att, TN).astype(bf16)
     grad_out_bias = jnp.sum(grad_att.astype(f32), axis=0)
     grad_mixed = mm(grad_att, out, NT).astype(bf16)
+    grad_mixed, grad_expand, grad_contract = lax.optimization_barrier(
+        (grad_mixed, grad_expand, grad_contract)
+    )
     grads = (grad_out_weight, grad_expand, grad_contract)
     small = dict(
         out_bias=grad_out_bias,
@@ -471,11 +594,14 @@
     p_vec = dict(zip(ORDER, vectors[11:]))
 
     e_joint = gather(e_joint_shard)
+    e_joint, e_expand_shard = lax.optimization_barrier((e_joint, e_expand_shard))
     e_expand = gather(e_expand_shard)
+    e_expand, e_contract_shard = lax.optimization_barrier((e_expand, e_contract_shard))
     e_contract = gather(e_contract_shard)
     packed = jnp.concatenate(
         [blocks_of(member, 1, small_width)[0] for member in (*p_shards, embed_shard)], axis=0
     )
+    e_contract, packed = lax.optimization_barrier((e_contract, packed))
     packed = lax.all_gather(packed, "fsdp", axis=0, tiled=False)
     unpacked = []
     at = 0
@@ -598,6 +724,11 @@
         (p_out, p_expand, p_contract),
         p_vec["mid_gain"],
     )
+    p_pack = jnp.concatenate(
+        [blocks_of(member, fsdp_size, small_width) for member in p_grads], axis=1
+    )
+    grad_mixed, p_pack = lax.optimization_barrier((grad_mixed, p_pack))
+    p_part = scatter(p_pack)
     own_weight, own_bias = own_joint(
         p_joint, p_vec["query_bias"], p_vec["value_bias"], seq_size, shard
     )
@@ -631,11 +762,8 @@
     grad_embed = mm(context, grad_embedded, TN).astype(bf16)
     grad_embed_bias = jnp.sum(grad_embedded.astype(f32), axis=0)
 
+    p_own_width = own_width
     p_grad_joint = jnp.pad(p_grad_joint.astype(bf16), ((0, 0), (0, small_width - 3 * own_width)))
-    members = (p_grad_joint, *p_grads, grad_embed)
-    p_part = scatter(
-        jnp.concatenate([blocks_of(member, fsdp_size, small_width) for member in members], axis=1)
-    )
 
     grad_context = mm(keep(grad_embedded), embed, NT)
     kept_mid = keep(normed_mid)
@@ -672,54 +800,56 @@
     )
     grad_tokens = put_back(grad_middle + grad_norm)
 
+    first = 0 if whole else 2
+    contract_sum, expand_sum, p_sum = sum_slots(
+        (contract_part, expand_part, p_part), seq_size, first
+    )
+
     small = [e_small[name] for name in ORDER] + [grad_embed_bias, grad_mask_token]
     small += [p_small[name] for name in ORDER]
     small = [member.reshape(fsdp_size, -1) for member in small]
     sizes = [member.shape[1] for member in small]
-    count = -(-sum(sizes) // (16 * own_width)) * 16
-    small.append(jnp.zeros((fsdp_size, count * own_width - sum(sizes)), f32))
-    small = jnp.concatenate(small, axis=1).astype(bf16).reshape(fsdp_size, count, own_width)
+    count = -(-sum(sizes) // (16 * 128)) * 16
+    small.append(jnp.zeros((fsdp_size, count * 128 - sum(sizes)), f32))
+    small = jnp.concatenate(small, axis=1).astype(bf16).reshape(fsdp_size, count, 128)
+    members = (e_grad_joint, p_grad_joint, e_grads[0], grad_embed)
     late = scatter(
         jnp.concatenate(
-            [
-                blocks_of(e_grad_joint, fsdp_size, own_width),
-                blocks_of(e_grads[0], fsdp_size, own_width),
-                small,
-            ],
-            axis=1,
+            [blocks_of(member, fsdp_size, 128) for member in members] + [small], axis=1
         )
     )
+
+    def cut(array, at, rows, lanes, block):
+        split = lanes // block
+        return from_blocks(array[at : at + split * rows], lanes), at + split * rows
+
+    def all_columns(columns, own):
+        columns = columns[:, : 3 * own].reshape(-1, 3, 1, own)
+        which = lax.broadcasted_iota(jnp.int32, (1, 1, seq_size, 1), 2)
+        placed = jnp.where(which == shard, columns, jnp.zeros_like(columns))
+        return placed.reshape(-1, 3 * own * seq_size)
+
     own_rows = width // fsdp_size
-    joint_rows = 3 * own_rows
     p_rows = small_width // fsdp_size
-    e_columns = late[:joint_rows]
-    p_columns = p_part[:p_rows, : 3 * (small_width // seq_size)]
-    e_whole = lax.all_gather(e_columns, "seq", axis=0, tiled=False)
-    p_whole = lax.all_gather(p_columns, "seq", axis=0, tiled=False)
-    expand_sum, contract_sum, p_sum, late_sum = lax.psum(
-        (expand_part, contract_part, p_part[p_rows:], late[joint_rows:]), "seq"
-    )
-    e_joint_out = e_whole.reshape(seq_size, 3, own_rows, own_width)
-    e_joint_out = e_joint_out.transpose(2, 1, 0, 3).reshape(own_rows, 3 * width)
-    p_joint_out = p_whole.reshape(seq_size, p_rows, 3, -1)
-    p_joint_out = p_joint_out.transpose(1, 2, 0, 3).reshape(p_rows, 3 * small_width)
-    out_sum = from_blocks(late_sum[: seq_size * own_rows], width)
-    vector_sum = late_sum[seq_size * own_rows :].reshape(-1)
+    e_columns, at = cut(late, 0, own_rows, 3 * own_width, 128)
+    p_columns, at = cut(late, at, p_rows, small_width, 128)
+    e_joint_out, p_joint_out, late_sum = sum_slots(
+        (all_columns(e_columns, own_width), all_columns(p_columns, p_own_width), late[at:]),
+        seq_size,
+        first + 1,
+    )
+    out_sum, at = cut(late_sum, 0, own_rows, width, 128)
+    embed_sum, at = cut(late_sum, at, own_rows, small_width, 128)
+    vector_sum = late_sum[at:].reshape(-1)
     small_out = []
     at = 0
     for size in sizes:
         small_out.append(vector_sum[at : at + size].astype(f32))
         at += size
-
-    def cut(array, at, rows, lanes):
-        split = lanes // small_width
-        return from_blocks(array[at : at + split * rows], lanes), at + split * rows
-
     p_wide = p_shards[2].shape[1]
-    p_out_sum, at = cut(p_sum, 0, p_rows, small_width)
-    p_expand_sum, at = cut(p_sum, at, p_rows, p_wide)
-    p_contract_sum, at = cut(p_sum, at, p_shards[3].shape[0], small_width)
-    embed_sum, at = cut(p_sum, at, own_rows, small_width)
+    p_out_sum, at = cut(p_sum, 0, p_rows, small_width, small_width)
+    p_expand_sum, at = cut(p_sum, at, p_rows, p_wide, small_width)
+    p_contract_sum, at = cut(p_sum, at, p_shards[3].shape[0], small_width, small_width)
 
     def ordered(vec, joint, out, expand, contract):
         vec = dict(

time: 1040 us -> 1130 us (1.087)
  Pallas kernels: 176 us -> 349 us
  blocking collectives: 55 us -> 10.7 us
  waiting for transfers between devices: 373 us -> 347 us
  matrix products: 197 us -> 181 us
    pallas_call x0 -> x2, Pallas kernels: none -> 172 us  [line_sum(): pl.pallas_call(functools.partial(line_kernel, size, tuple(cuts)), out_sha...]
    psum x1 -> x0, waiting for transfers between devices: 74.6 us -> none  [main(): lax.psum((expand_part, contract_part, p_part[p_rows:], late[joint_rows:])...]
    all_gather x2 -> x0, blocking collectives: 44.3 us -> none  [the longest x1 29.9 us: main(): e_whole = lax.all_gather(e_columns, 'seq', axis=0, tiled=False)]
    all_gather x4, waiting for transfers between devices: 81.1 us -> 108 us  [gather(): return lax.all_gather(array, 'fsdp', axis=0, tiled=True)]
    all_to_all x6, waiting for transfers between devices: 41 us -> 66.2 us  [exchange(): return lax.all_to_all(array, 'seq', split_axis=0, concat_axis=0, tiled=True)]
    dot_general x42, matrix products: 183 us -> 166 us  [mm(): return lax.dot_general(left, right, dims, preferred_element_type=f32)]
    unnamed x237 -> x308, local copies, waits for them, and re-layouts: 24.4 us -> 21.3 us
  transfers between devices with their start and end apart: 18 -> 17, of which waited for: 11 -> 14; matrix products, arithmetic and copies ran while one was open for 25% -> 22% of each run, Pallas kernels for 11% -> 14%
where the time goes in v3:
time: 1130 us; the launch traced here: 1120 us
  Pallas kernels  349 us (31%)
  waiting for transfers between devices  347 us (31%)
  matrix products  181 us (16%)
  local copies, waits for them, and re-layouts  125 us (11%)
  other arithmetic  59.4 us (5%)
  starting transfers between devices  27.4 us (2%)
  between operations  16 us (1%)
    pallas_call x2, Pallas kernels, line_sum(): pl.pallas_call(functools.partial(line_kernel, size, tuple(cuts)), out_sha...  172 us
    reduce_scatter x4, waiting for transfers between devices, scatter(): return lax.psum_scatter(array, 'fsdp', scatter_dimension=0, tiled=True)[0]  168 us
    dot_general x42, matrix products, mm(): return lax.dot_general(left, right, dims, preferred_element_type=f32)  166 us
    all_gather x4, waiting for transfers between devices, gather(): return lax.all_gather(array, 'fsdp', axis=0, tiled=True)  108 us
    pallas_call x3, Pallas kernels, attend(): pl.pallas_call(functools.partial(forward_kernel, 1.0 / math.sqrt(head_siz...  89.2 us
    pallas_call x3, Pallas kernels, attend_back(): pl.pallas_call(functools.partial(backward_kernel, 1.0 / math.sqrt(head_si...  86.9 us
    all_to_all x6, waiting for transfers between devices, exchange(): return lax.all_to_all(array, 'seq', split_axis=0, concat_axis=0, tiled=True)  66.2 us
    all_to_all x6, starting transfers between devices, exchange(): return lax.all_to_all(array, 'seq', split_axis=0, concat_axis=0, tiled=True)  26.5 us
  transfers between devices with their start and end apart: 17, of which 14 were waited for; matrix products, arithmetic and copies ran while one was open for 22% of the time, Pallas kernels for 14%

profile of v3, /device:TPU:0, one launch (start us, length us, event | category | flops | bytes accessed | tf_op | source)
XLA Modules:
  0.0 1122.4 jit_solution(9886278371657004852)
XLA Ops:
  22.3 10.7 all-gather.2
  40.6 1066.5 %conditional.4 = (f32[2,392,1024]{2,1,0:T(8,128)S(1)}, f32[2,392,384]{2,1,0:T(8,128)}, f32[2,392,1024]{2,1,0:T(8,128)}, bf16[128,3072]{1,0:T(8,128)(2,1)}, bf16[...) conditional(s32[]{:T(128)} %convert_element_type.834, ...), branch_computations={%region_4.46_spmd, %region_45.91_spmd} | conditional | flops 209827332096 | bytes 1257281408
  49.0 47.6 %all-gather.29.cloned.1.call-done = bf16[1024,3072]{0,1:T(8,128)(2,1)} async-done(((bf16[128,3072]{0,1:T(8,128)(2,1)}), bf16[1024,3072]{0,1:T(8,128)(2,1)}) %all-gather.29.cloned.1.call-update) | async-done | bytes 6291472 | tf_op jit(solution)/shard_map/cond/branch_1_fun/all_gather | solution.py:241
  96.6 56.4 %all-gather.31.cloned.1.call-done = bf16[1024,4096]{1,0:T(8,128)(2,1)} async-done(((bf16[128,4096]{1,0:T(8,128)(2,1)}), bf16[1024,4096]{1,0:T(8,128)(2,1)}) %all-gather.31.cloned.1.call-update) | async-done | bytes 8388624 | tf_op jit(solution)/shard_map/cond/branch_1_fun/all_gather | solution.py:241
  191.2 5.5 gather_fusion.1
  209.9 24.4 %all-to-all-done.6 = bf16[4,2,192,1024]{3,2,1,0:T(8,128)(2,1)} async-done(((bf16[4,2,192,1024]{3,2,1,0:T(8,128)(2,1)}), bf16[4,2,192,1024]{3,2,1,0:T(8,128)(2,1)}, u32[]{:S(2)}, u32[]{:S(2)}) %all-to-all-start.6) | async-done | bytes 3145760 | tf_op jit(solution)/shard_map/cond/branch_1_fun/all_to_all | solution.py:237
  234.3 11.4 %add_convert_fusion.17 = bf16[1536,2048]{1,0:T(8,128)(2,1)} fusion(bf16[1536,1024]{1,0:T(8,128)(2,1)} %bitcast.140, f32[2048]{0:T(1024)S(1)} %copy-done.174, bf16[1024,3072]{0,1:T(8,128)(2,1)} %all-gather.29.cloned.1.call-done), kind=kOutput, calls=%fused_computation.222 | convolution fusion | flops 6448742400 | bytes 13639680 | tf_op jit(solution)/shard_map/cond/branch_1_fun/dot_general | solution.py:25
  250.3 35.0 %attend.9 = bf16[2,392,1024]{2,1,0:T(8,128)(2,1)} custom-call(bf16[2,392,1024]{2,1,0:T(8,128)(2,1)} %bitcast.1034, bf16[4,2,192,2048]{3,2,1,0:T(8,128)(2,1)} %bitcast.1028, bf16[4,2,192,2048]{3,2,1,0:T(8,128)(2,1)} %bitcast.1029, f32[2,1,768]{2,1,0:T(1,128)} %compare_select_fusion.1.rest_0_), custom_call_target="tpu_custom_call" | custom-call | flops 9865003008 | bytes 6291456 | tf_op jit(solution)/shard_map/cond/branch_1_fun/attend/pallas_call | solution.py:109
  285.3 5.6 fusion.98
  298.0 21.4 %add_add_fusion.1 = f32[784,1024]{1,0:T(8,128)S(1)} fusion(f32[784,1024]{1,0:T(8,128)} %fusion.98, bf16[4096,1024]{1,0:T(8,128)(2,1)} %all-gather.33.cloned.1.call-done, f32[4096]{0:T(1024)S(1)} %bitcast.1004, bf16[1024,4096]{1,0:T(8,128)(2,1)} %all-gather.31.cloned.1.call-done, f32[1024]{0:T(1024)S(1)} %bitcast.1013, f32[1024]{0:T(1024)S(1)} %bitcast.997, ...), kind=kOutput, calls=%fused_computation.256 | convolution fusion | flops 13178224640 | bytes 23234688 | tf_op jit(solution)/shard_map/cond/branch_1_fun/dot_general | solution.py:25
  361.0 27.2 %attend.11 = bf16[1,392,384]{2,1,0:T(8,128)(2,1)} custom-call(bf16[1,392,384]{2,1,0:T(8,128)(2,1)} %get-tuple-element.1078.q_ref, bf16[1,1,1568,768]{3,2,1,0:T(8,128)(2,1)} %fusion.83.k_ref.v_ref, bf16[1,1,1568,768]{3,2,1,0:T(8,128)(2,1)} %fusion.83.k_ref.v_ref), custom_call_target="tpu_custom_call" | custom-call | flops 7552892928 | bytes 2408448 | tf_op jit(solution)/shard_map/cond/branch_1_fun/attend/pallas_call | solution.py:109
  392.7 27.0 %attend.10 = bf16[1,392,384]{2,1,0:T(8,128)(2,1)} custom-call(bf16[1,392,384]{2,1,0:T(8,128)(2,1)} %get-tuple-element.1077.q_ref, bf16[1,1,1568,768]{3,2,1,0:T(8,128)(2,1)} %fusion.82.k_ref.v_ref, bf16[1,1,1568,768]{3,2,1,0:T(8,128)(2,1)} %fusion.82.k_ref.v_ref), custom_call_target="tpu_custom_call" | custom-call | flops 7552892928 | bytes 2408448 | tf_op jit(solution)/shard_map/cond/branch_1_fun/attend/pallas_call | solution.py:109
  464.7 5.8 all-to-all-done.7
  475.9 33.6 %attend_back.10 = bf16[4,1,392,288]{3,2,1,0:T(8,128)(2,1)} custom-call(bf16[1,1,1568,96]{3,2,1,0:T(8,128)(2,1)} %fusion.91.q_ref, bf16[1,1,1568,96]{3,2,1,0:T(8,128)(2,1)} %fusion.95.k_ref, bf16[1,1,1568,96]{3,2,1,0:T(8,128)(2,1)} %fusion.90.v_ref, bf16[1,1,1568,96]{3,2,1,0:T(8,128)(2,1)} %bitcast.931), custom_call_target="tpu_custom_call" | custom-call | flops 18882232320 | bytes 2107392 | tf_op jit(solution)/shard_map/cond/branch_1_fun/attend_back/pallas_call | solution.py:217
  517.1 33.6 %attend_back.9 = bf16[4,1,392,288]{3,2,1,0:T(8,128)(2,1)} custom-call(bf16[1,1,1568,96]{3,2,1,0:T(8,128)(2,1)} %fusion.93.q_ref, bf16[1,1,1568,96]{3,2,1,0:T(8,128)(2,1)} %fusion.94.k_ref, bf16[1,1,1568,96]{3,2,1,0:T(8,128)(2,1)} %fusion.92.v_ref, bf16[1,1,1568,96]{3,2,1,0:T(8,128)(2,1)} %bitcast.932), custom_call_target="tpu_custom_call" | custom-call | flops 18882232320 | bytes 2107392 | tf_op jit(solution)/shard_map/cond/branch_1_fun/attend_back/pallas_call | solution.py:217
  553.1 5.5 all-to-all-start.8
  558.7 9.7 convolution_add_fusion.11
  575.3 10.9 all-to-all-done.8
  594.1 9.3 fusion.187
  603.4 6.8 convolution_convert_fusion.11
  610.3 7.0 convolution_convert_fusion.12
  632.5 6.1 copy.462
  649.2 19.8 %attend_back.11 = bf16[4,2,192,768]{3,2,1,0:T(8,128)(2,1)} custom-call(bf16[4,2,192,256]{3,2,1,0:T(8,128)(2,1)} %bitcast.1038, bf16[4,2,192,256]{3,2,1,0:T(8,128)(2,1)} %bitcast.1037, bf16[4,2,192,256]{3,2,1,0:T(8,128)(2,1)} %bitcast.1039, bf16[4,2,192,256]{3,2,1,0:T(8,128)(2,1)} %all-to-all-done.10.g_ref, f32[2,1,768]{2,1,0:T(1,128)} %compare_select_fusion.1.rest_0_), custom_call_target="tpu_custom_call" | custom-call | flops 12079595520 | bytes 5505024 | tf_op jit(solution)/shard_map/cond/branch_1_fun/attend_back/pallas_call | solution.py:217
  685.5 5.7 bitcast_convert_fusion.12
  704.6 22.4 %all-to-all-done.11 = bf16[4,2,192,768]{3,2,1,0:T(8,128)(2,1)} async-done(((bf16[4,2,192,768]{3,2,1,0:T(8,128)(2,1)}), bf16[4,2,192,768]{3,2,1,0:T(8,128)(2,1)}, u32[]{:S(2)}, u32[]{:S(2)}) %all-to-all-start.11) | async-done | bytes 2359328 | tf_op jit(solution)/shard_map/cond/branch_1_fun/all_to_all | solution.py:237
  731.5 7.5 multiply_reduce_fusion.19
  742.5 4.8 fusion.112
  751.2 42.7 %reduce-scatter.17.cloned.1.call-done = bf16[1,2352,128]{2,1,0:T(8,128)(2,1)} async-done(((bf16[8,2352,128]{2,1,0:T(8,128)(2,1)}), bf16[1,2352,128]{2,1,0:T(8,128)(2,1)}) %reduce-scatter.17.cloned.1.call-update) | async-done | bytes 602128 | tf_op jit(solution)/shard_map/cond/branch_1_fun/reduce_scatter | solution.py:245
  798.9 60.8 %line_sum.6 = (bf16[128,3072]{1,0:T(8,128)(2,1)}, bf16[48,1152]{1,0:T(8,128)(2,1)}, bf16[1440,128]{1,0:T(8,128)(2,1)}) custom-call(bf16[128,3072]{1,0:T(8,128)(2,1)} %broadcast_select_fusion.3.refs_0_, bf16[48,1152]{1,0:T(8,128)(2,1)} %broadcast_select_fusion.4.refs_1_, bf16[1440,128]{1,0:T(8,128)(2,1)} %slice_bitcast_fusion.4.refs_2_), custom_call_target="tpu_custom_call" | custom-call | tf_op jit(solution)/shard_map/cond/branch_1_fun/line_sum/pallas_call | solution.py:385
  865.7 50.5 %reduce-scatter.19.cloned.1.call-done = bf16[1,512,1024]{2,1,0:T(8,128)(2,1)} async-done(((bf16[8,512,1024]{2,1,0:T(8,128)(2,1)}), bf16[1,512,1024]{2,1,0:T(8,128)(2,1)}) %reduce-scatter.19.cloned.1.call-update) | async-done | bytes 1048592 | tf_op jit(solution)/shard_map/cond/branch_1_fun/reduce_scatter | solution.py:245
  916.2 75.1 %reduce-scatter.21.cloned.1.call-done = bf16[1,128,4096]{2,1,0:T(8,128)(2,1)} async-done(((bf16[8,128,4096]{2,1,0:T(8,128)(2,1)}), bf16[1,128,4096]{2,1,0:T(8,128)(2,1)}) %reduce-scatter.21.cloned.1.call-update) | async-done | bytes 1048592 | tf_op jit(solution)/shard_map/cond/branch_1_fun/reduce_scatter | solution.py:245
  991.3 111.6 %line_sum.7 = (bf16[512,1024]{1,0:T(8,128)(2,1)}, bf16[128,4096]{1,0:T(8,128)(2,1)}, bf16[432,384]{1,0:T(8,128)(2,1)}) custom-call(bf16[512,1024]{1,0:T(8,128)(2,1)} %bitcast.892, bf16[128,4096]{1,0:T(8,128)(2,1)} %bitcast.893, bf16[432,384]{1,0:T(8,128)(2,1)} %bitcast.938), custom_call_target="tpu_custom_call" | custom-call | tf_op jit(solution)/shard_map/cond/branch_1_fun/line_sum/pallas_call | solution.py:385
  (588 shorter events, 297.4 us)
Async XLA Ops:
  7.2 33.4 %all-gather.41.cloned.1.call-start = ((), (), s32[]{:S(2)}) async-start(), calls=%async_computation.40 | async-start | bytes 2359296 | tf_op jit(solution)/shard_map/all_gather | solution.py:241
  46.3 107.0 %copy-start.105 = (f32[8,48]{1,0:T(8,128)}, f32[8,48]{1,0:T(8,128)S(1)}, u32[]{:S(2)}) copy-start(f32[8,48]{1,0:T(8,128)S(1)} %get-tuple-element.404) | copy-start | bytes 4612
  46.3 107.0 %copy-start.110 = (f32[1024]{0:T(1024)}, f32[1024]{0:T(1024)S(1)}, u32[]{:S(2)}) copy-start(f32[1024]{0:T(1024)S(1)} %get-tuple-element.379) | copy-start | bytes 12292
  46.3 107.0 %copy-start.112 = (pred[2,1568]{1,0:T(4,128)(4,1)}, pred[2,1568]{1,0:T(4,128)(4,1)S(1)}, u32[]{:S(2)}) copy-start(pred[2,1568]{1,0:T(4,128)(4,1)S(1)} %get-tuple-element.378) | copy-start | bytes 9412
  46.4 107.0 %copy-start.131 = (f32[8,48]{1,0:T(8,128)}, f32[8,48]{1,0:T(8,128)S(1)}, u32[]{:S(2)}) copy-start(f32[8,48]{1,0:T(8,128)S(1)} %get-tuple-element.403) | copy-start | bytes 4612
  46.4 107.0 %copy-start.133 = (f32[8,48]{1,0:T(8,128)}, f32[8,48]{1,0:T(8,128)S(1)}, u32[]{:S(2)}) copy-start(f32[8,48]{1,0:T(8,128)S(1)} %get-tuple-element.402) | copy-start | bytes 4612
  46.4 107.0 %copy-start.135 = (f32[8,48]{1,0:T(8,128)}, f32[8,48]{1,0:T(8,128)S(1)}, u32[]{:S(2)}) copy-start(f32[8,48]{1,0:T(8,128)S(1)} %get-tuple-element.398) | copy-start | bytes 4612
  46.4 108.4 %copy-start.117 = (f32[8,1,128]{2,1,0:T(1,128)}, f32[8,1,128]{2,1,0:T(1,128)S(1)}, u32[]{:S(2)}) copy-start(f32[8,1,128]{2,1,0:T(1,128)S(1)} %get-tuple-element.373) | copy-start | bytes 12292
  46.4 159.7 %copy-start.96 = (f32[8,1,128]{2,1,0:T(1,128)}, f32[8,1,128]{2,1,0:T(1,128)S(1)}, u32[]{:S(2)}) copy-start(f32[8,1,128]{2,1,0:T(1,128)S(1)} %get-tuple-element.372) | copy-start | bytes 12292
  46.4 106.7 %copy-start.2 = (f32[2,392,1024]{2,1,0:T(8,128)S(1)}, f32[2,392,1024]{2,1,0:T(8,128)}, u32[]{:S(2)}) copy-start(f32[2,392,1024]{2,1,0:T(8,128)} %get-tuple-element.371) | copy-start | bytes 9633796
  46.4 50.2 %all-gather.29.cloned.1.call-start = ((), (), s32[]{:S(2)}) async-start(), calls=%async_computation.30 | async-start | bytes 7077888 | tf_op jit(solution)/shard_map/cond/branch_1_fun/all_gather | solution.py:241
  48.9 104.1 %all-gather.31.cloned.1.call-start = ((), (), s32[]{:S(2)}) async-start(), calls=%async_computation.31 | async-start | bytes 9437184 | tf_op jit(solution)/shard_map/cond/branch_1_fun/all_gather | solution.py:241
  96.6 112.8 %all-gather.33.cloned.1.call-start = ((), (), s32[]{:S(2)}) async-start(), calls=%async_computation.32 | async-start | bytes 9437184 | tf_op jit(solution)/shard_map/cond/branch_1_fun/all_gather | solution.py:241
  158.0 76.3 %all-to-all-start.6 = ((bf16[4,2,192,1024]{3,2,1,0:T(8,128)(2,1)}), bf16[4,2,192,1024]{3,2,1,0:T(8,128)(2,1)}, u32[]{:S(2)}, u32[]{:S(2)}) async-start(bf16[4,2,192,1024]{3,2,1,0:T(8,128)(2,1)} %broadcast_in_dim.252), calls=%async_computation.10 | async-start | bytes 6291456 | tf_op jit(solution)/shard_map/cond/branch_1_fun/all_to_all | solution.py:237
  162.8 156.5 %all-gather.39.cloned.1.call-start = ((), (), s32[]{:S(2)}) async-start(), calls=%async_computation.39 | async-start | bytes 4866048 | tf_op jit(solution)/shard_map/cond/branch_1_fun/all_gather | solution.py:605
  206.1 28.2 %copy-start.174 = (f32[2048]{0:T(1024)S(1)}, f32[2048]{0:T(1024)}, u32[]{:S(2)}) copy-start(f32[2048]{0:T(1024)} %concatenate.44) | copy-start | bytes 24580
  209.4 147.5 %all-gather.37.cloned.1.call-start = ((), (), s32[]{:S(2)}) async-start(), calls=%async_computation.34 | async-start | bytes 1505280 | tf_op jit(solution)/shard_map/cond/branch_1_fun/all_gather | solution.py:699
  250.3 35.0 %copy-start.102 = (f32[8,1,128]{2,1,0:T(1,128)S(1)}, f32[8,1,128]{2,1,0:T(1,128)}, u32[]{:S(2)}) copy-start(f32[8,1,128]{2,1,0:T(1,128)} %get-tuple-element.382) | copy-start | bytes 12292
  327.0 61.5 %all-gather.35.cloned.1.call-start = ((), (), s32[]{:S(2)}) async-start(), calls=%async_computation.33 | async-start | bytes 1505280 | tf_op jit(solution)/shard_map/cond/branch_1_fun/all_gather | solution.py:699
  392.7 28.0 %copy-start.16 = (f32[784,384]{1,0:T(8,128)S(1)}, f32[784,384]{1,0:T(8,128)}, u32[]{:S(2)}) copy-start(f32[784,384]{1,0:T(8,128)} %copy-done.15) | copy-start | bytes 3612676
  392.7 28.0 %copy-start.176 = (f32[384]{0:T(512)S(1)}, f32[384]{0:T(512)}, u32[]{:S(2)}) copy-start(f32[384]{0:T(512)} %add.635) | copy-start | bytes 4612
  446.9 23.6 %all-to-all-start.7 = ((bf16[4,2,392,96]{2,1,3,0:T(2,128)(2,1)}), bf16[4,2,392,96]{2,1,3,0:T(2,128)(2,1)S(1)}, u32[]{:S(2)}, u32[]{:S(2)}) async-start(bf16[4,2,392,96]{2,1,3,0:T(2,128)(2,1)} %reshape.1329), calls=%async_computation.11 | async-start | bytes 1572864 | tf_op jit(solution)/shard_map/cond/branch_1_fun/all_to_all | solution.py:237
  511.8 41.3 %all-to-all-start.9 = ((bf16[4,1,392,288]{2,3,1,0:T(8,128)(2,1)}), bf16[4,1,392,288]{2,3,1,0:T(8,128)(2,1)S(1)}, u32[]{:S(2)}, u32[]{:S(2)}) async-start(bf16[4,1,392,288]{2,3,1,0:T(8,128)(2,1)} %copy.455), calls=%async_computation.13 | async-start | bytes 2359296 | tf_op jit(solution)/shard_map/cond/branch_1_fun/all_to_all | solution.py:237
  553.1 33.0 %all-to-all-start.8 = ((bf16[4,1,392,288]{2,3,1,0:T(8,128)(2,1)}), bf16[4,1,392,288]{2,3,1,0:T(8,128)(2,1)}, u32[]{:S(2)}, u32[]{:S(2)}) async-start(bf16[4,1,392,288]{2,3,1,0:T(8,128)(2,1)} %copy.447), calls=%async_computation.12 | async-start | bytes 2359296 | tf_op jit(solution)/shard_map/cond/branch_1_fun/all_to_all | solution.py:237
  622.4 51.6 %copy-start.28 = (f32[384,1024]{1,0:T(8,128)}, f32[384,1024]{1,0:T(8,128)S(1)}, u32[]{:S(2)}) copy-start(f32[384,1024]{1,0:T(8,128)S(1)} %get-tuple-element.1019) | copy-start | bytes 4718596
  625.3 23.9 %all-to-all-start.10 = ((bf16[4,2,192,256]{3,2,1,0:T(8,128)(2,1)}), bf16[4,2,192,256]{3,2,1,0:T(8,128)(2,1)}, u32[]{:S(2)}, u32[]{:S(2)}) async-start(bf16[4,2,192,256]{3,2,1,0:T(8,128)(2,1)} %bitcast.211), calls=%async_computation.14 | async-start | bytes 1572864 | tf_op jit(solution)/shard_map/cond/branch_1_fun/all_to_all | solution.py:237
  669.0 58.0 %all-to-all-start.11 = ((bf16[4,2,192,768]{3,2,1,0:T(8,128)(2,1)}), bf16[4,2,192,768]{3,2,1,0:T(8,128)(2,1)}, u32[]{:S(2)}, u32[]{:S(2)}) async-start(bf16[4,2,192,768]{3,2,1,0:T(8,128)(2,1)} %attend_back.11), calls=%async_computation.15 | async-start | bytes 4718592 | tf_op jit(solution)/shard_map/cond/branch_1_fun/all_to_all | solution.py:237
  673.6 120.3 %reduce-scatter.17.cloned.1.call-start = ((), (), s32[]{:S(2)}) async-start(), calls=%async_computation.35 | async-start | bytes 5419008 | tf_op jit(solution)/shard_map/cond/branch_1_fun/reduce_scatter | solution.py:245
  739.9 125.8 %reduce-scatter.23.cloned.1.call-start = ((), (), s32[]{:S(2)}) async-start(), calls=%async_computation.38 | async-start | bytes 2985984 | tf_op jit(solution)/shard_map/cond/branch_1_fun/reduce_scatter | solution.py:245
  740.6 175.6 %reduce-scatter.19.cloned.1.call-start = ((), (), s32[]{:S(2)}) async-start(), calls=%async_computation.36 | async-start | bytes 9437184 | tf_op jit(solution)/shard_map/cond/branch_1_fun/reduce_scatter | solution.py:245
  741.2 250.1 %reduce-scatter.21.cloned.1.call-start = ((), (), s32[]{:S(2)}) async-start(), calls=%async_computation.37 | async-start | bytes 9437184 | tf_op jit(solution)/shard_map/cond/branch_1_fun/reduce_scatter | solution.py:245
  864.8 242.0 %copy-start.7 = (f32[784,1024]{1,0:T(8,128)S(1)}, f32[784,1024]{1,0:T(8,128)}, u32[]{:S(2)}) copy-start(f32[784,1024]{1,0:T(8,128)} %copy-done.5) | copy-start | bytes 9633796
  (131 other events, 956.8 us)
Sparse Core Ops, SparseCore 0:
  9.9 30.5 all-gather.40
  49.9 46.6 all-gather.28
  98.6 54.3 all-gather.30
  154.9 54.3 all-gather.32
  211.8 37.2 all-gather.38
  327.2 29.6 all-gather.36
  358.5 29.9 all-gather.34
  740.0 53.8 reduce-scatter.16
  797.8 43.7 reduce-scatter.22
  844.9 71.2 reduce-scatter.18
  920.1 71.2 reduce-scatter.20

commit v4 on v3

--- a/solution.py
+++ b/solution.py
@@ -356,18 +356,22 @@
 
     @pl.when(jnp.logical_not(end))
     def _():
-        for piece in pieces:
-            inwards(*piece).wait_recv()
-            _, index, cut = piece
-            both = ins[index][cut].astype(f32) + outer[index][cut].astype(f32)
-            partial[index][cut] = both.astype(bf16)
-            swap(*piece).start()
-        for piece in pieces:
-            swap(*piece).wait_recv()
-            _, index, cut = piece
-            both = partial[index][cut].astype(f32) + inner[index][cut].astype(f32)
-            outs[index][cut] = both.astype(bf16)
-            outwards(*piece).start()
+        lag = min(count, len(pieces))
+        for step in range(len(pieces) + lag):
+            if step < len(pieces):
+                piece = pieces[step]
+                inwards(*piece).wait_recv()
+                _, index, cut = piece
+                both = ins[index][cut].astype(f32) + outer[index][cut].astype(f32)
+                partial[index][cut] = both.astype(bf16)
+                swap(*piece).start()
+            if step >= lag:
+                piece = pieces[step - lag]
+                swap(*piece).wait_recv()
+                _, index, cut = piece
+                both = partial[index][cut].astype(f32) + inner[index][cut].astype(f32)
+                outs[index][cut] = both.astype(bf16)
+                outwards(*piece).start()
         for piece in pieces:
             swap(*piece).wait_send()
             outwards(*piece).wait_send()
@@ -391,6 +395,11 @@
         compiler_params=pltpu.CompilerParams(
             collective_id=identity, has_side_effects=True, vmem_limit_bytes=VMEM_LIMIT
         ),
+        cost_estimate=pl.CostEstimate(
+            flops=0,
+            bytes_accessed=40 * sum(2 * member.size for member in arrays),
+            transcendentals=0,
+        ),
         name="line_sum",
     )(*arrays)
 
@@ -407,19 +416,17 @@
     grad_contract = mm(active, grad_y, TN).astype(bf16)
     grad_contract_bias = jnp.sum(grad_y.astype(f32), axis=0)
     grad_hidden = (mm(grad_y, contract, NT) * gelu_slope(hidden)).astype(bf16)
+    grad_hidden, grad_contract = lax.optimization_barrier((grad_hidden, grad_contract))
     grad_expand = mm(normed_mid, grad_hidden, TN).astype(bf16)
     grad_expand_bias = jnp.sum(grad_hidden.astype(f32), axis=0)
-    grad_norm, grad_mid_gain, grad_mid_shift = norm_back(
-        middle, mid_gain, mm(grad_hidden, expand, NT)
-    )
+    grad_normed = mm(grad_hidden, expand, NT)
+    grad_normed, grad_expand = lax.optimization_barrier((grad_normed, grad_expand))
+    grad_norm, grad_mid_gain, grad_mid_shift = norm_back(middle, mid_gain, grad_normed)
     grad_middle = grad_out + grad_norm
     grad_att = grad_middle.astype(bf16)
     grad_out_weight = mm(mixed, grad_att, TN).astype(bf16)
     grad_out_bias = jnp.sum(grad_att.astype(f32), axis=0)
     grad_mixed = mm(grad_att, out, NT).astype(bf16)
-    grad_mixed, grad_expand, grad_contract = lax.optimization_barrier(
-        (grad_mixed, grad_expand, grad_contract)
-    )
     grads = (grad_out_weight, grad_expand, grad_contract)
     small = dict(
         out_bias=grad_out_bias,
@@ -594,24 +601,9 @@
     p_vec = dict(zip(ORDER, vectors[11:]))
 
     e_joint = gather(e_joint_shard)
-    e_joint, e_expand_shard = lax.optimization_barrier((e_joint, e_expand_shard))
-    e_expand = gather(e_expand_shard)
-    e_expand, e_contract_shard = lax.optimization_barrier((e_expand, e_contract_shard))
-    e_contract = gather(e_contract_shard)
     packed = jnp.concatenate(
         [blocks_of(member, 1, small_width)[0] for member in (*p_shards, embed_shard)], axis=0
     )
-    e_contract, packed = lax.optimization_barrier((e_contract, packed))
-    packed = lax.all_gather(packed, "fsdp", axis=0, tiled=False)
-    unpacked = []
-    at = 0
-    for member in (*p_shards, embed_shard):
-        split = member.shape[1] // small_width
-        count = member.shape[0] * split
-        piece = packed[:, at : at + count].reshape(fsdp_size, split, member.shape[0], small_width)
-        unpacked.append(piece.transpose(0, 2, 1, 3).reshape(-1, member.shape[1]))
-        at += count
-    p_joint, p_out, p_expand, p_contract, embed = unpacked
 
     own_visible = lax.dynamic_slice_in_dim(slot_visible, shard * slots, slots, 1)
     own_flat = own_visible.reshape(rows, 1)
@@ -670,21 +662,37 @@
     inputs = tokens.reshape(rows, width)
     normed = norm_layer(inputs, e_vec["pre_gain"], e_vec["pre_shift"])
     normed_kept = keep(normed).reshape(1, clips, held, width)
+    normed_kept, e_expand_shard = lax.optimization_barrier((normed_kept, e_expand_shard))
+    e_expand = gather(e_expand_shard)
     normed_all = exchange(jnp.broadcast_to(normed_kept, (seq_size, clips, held, width)))
     queries = (mm(normed, e_joint[:, :width]) + e_vec["query_bias"]).astype(bf16)
     joined = mm(normed_all.reshape(-1, width), e_joint[:, width:])
     joined_bias = jnp.concatenate([jnp.zeros_like(e_vec["value_bias"]), e_vec["value_bias"]])
     joined = (joined + joined_bias).astype(bf16)
+    joined, e_contract_shard = lax.optimization_barrier((joined, e_contract_shard))
+    e_contract = gather(e_contract_shard)
     mixed = attend(
         queries.reshape(clips, slots, width),
         by_clip(joined.reshape(seq_size, clips, held, 2 * width)),
         head_size,
         bias,
     ).reshape(rows, width)
+    mixed, packed = lax.optimization_barrier((mixed, packed))
+    packed = lax.all_gather(packed, "fsdp", axis=0, tiled=False)
     middle = inputs + mm(mixed, e_out) + e_vec["out_bias"]
     normed_mid = norm_layer(middle, e_vec["mid_gain"], e_vec["mid_shift"])
     active = gelu(mm(normed_mid, e_expand) + e_vec["expand_bias"])
     encoded = middle + mm(active, e_contract) + e_vec["contract_bias"]
+    encoded, packed = lax.optimization_barrier((encoded, packed))
+    unpacked = []
+    at = 0
+    for member in (*p_shards, embed_shard):
+        split = member.shape[1] // small_width
+        count = member.shape[0] * split
+        piece = packed[:, at : at + count].reshape(fsdp_size, split, member.shape[0], small_width)
+        unpacked.append(piece.transpose(0, 2, 1, 3).reshape(-1, member.shape[1]))
+        at += count
+    p_joint, p_out, p_expand, p_contract, embed = unpacked
     context = encoded.astype(bf16)
 
     embedded = mm(context, embed) + embed_bias
@@ -765,6 +773,7 @@
     p_own_width = own_width
     p_grad_joint = jnp.pad(p_grad_joint.astype(bf16), ((0, 0), (0, small_width - 3 * own_width)))
 
+    grad_embedded, p_part = lax.optimization_barrier((grad_embedded, p_part))
     grad_context = mm(keep(grad_embedded), embed, NT)
     kept_mid = keep(normed_mid)
     kept_hidden = mm(kept_mid, e_expand) + e_vec["expand_bias"]
@@ -793,10 +802,9 @@
     flat = grads.reshape(-1, 3 * own_width)
     e_grad_joint = mm(normed_all.reshape(-1, width), flat, TN).astype(bf16)
     e_small.update(joint_small(jnp.sum(flat.astype(f32), axis=0), seq_size, shard))
+    received, contract_part = lax.optimization_barrier((exchange(grads), contract_part))
     grad_norm, e_small["pre_gain"], e_small["pre_shift"] = norm_back(
-        keep(inputs),
-        e_vec["pre_gain"],
-        joint_back(exchange(grads), by_sender(e_joint, seq_size)),
+        keep(inputs), e_vec["pre_gain"], joint_back(received, by_sender(e_joint, seq_size))
     )
     grad_tokens = put_back(grad_middle + grad_norm)
 
@@ -819,6 +827,8 @@
         )
     )
 
+    late, contract_sum = lax.optimization_barrier((late, contract_sum))
+
     def cut(array, at, rows, lanes, block):
         split = lanes // block
         return from_blocks(array[at : at + split * rows], lanes), at + split * rows

time: 1130 us -> 868 us (0.77)
  waiting for transfers between devices: 347 us -> 129 us
  Pallas kernels: 349 us -> 291 us
    reduce_scatter x4, waiting for transfers between devices: 168 us -> 0.01 us  [scatter(): return lax.psum_scatter(array, 'fsdp', scatter_dimension=0, tiled=True)[0]]
    all_gather x4, waiting for transfers between devices: 108 us -> 1.96 us  [gather(): return lax.all_gather(array, 'fsdp', axis=0, tiled=True)]
    pallas_call x2, Pallas kernels: 172 us -> 115 us  [line_sum(): pl.pallas_call(functools.partial(line_kernel, size, tuple(cuts)), out_sha...]
    all_to_all x6, waiting for transfers between devices: 66.2 us -> 105 us  [exchange(): return lax.all_to_all(array, 'seq', split_axis=0, concat_axis=0, tiled=True)]
    all_gather x2, waiting for transfers between devices: 1.81 us -> 14.3 us  [main(): every = lax.all_gather(own, 'seq', axis=0, tiled=True)]
    unnamed x308 -> x258, local copies, waits for them, and re-layouts: 21.3 us -> 24.8 us
  transfers between devices with their start and end apart: 17 -> 17, of which waited for: 14 -> 9; matrix products, arithmetic and copies ran while one was open for 22% -> 34% of each run, Pallas kernels for 14% -> 26%
where the time goes in v4:
time: 868 us; the launch traced here: 858 us
  Pallas kernels  291 us (34%)
  matrix products  186 us (21%)
  waiting for transfers between devices  129 us (15%)
  local copies, waits for them, and re-layouts  129 us (15%)
  other arithmetic  60.9 us (7%)
  starting transfers between devices  27.2 us (3%)
  between operations  15.7 us (2%)
  blocking collectives  10.7 us (1%)
  loops' own time  9.13 us (1%)
    dot_general x42, matrix products, mm(): return lax.dot_general(left, right, dims, preferred_element_type=f32)  170 us
    pallas_call x2, Pallas kernels, line_sum(): pl.pallas_call(functools.partial(line_kernel, size, tuple(cuts)), out_sha...  115 us
    all_to_all x6, waiting for transfers between devices, exchange(): return lax.all_to_all(array, 'seq', split_axis=0, concat_axis=0, tiled=True)  105 us
    pallas_call x3, Pallas kernels, attend(): pl.pallas_call(functools.partial(forward_kernel, 1.0 / math.sqrt(head_siz...  88.9 us
    pallas_call x3, Pallas kernels, attend_back(): pl.pallas_call(functools.partial(backward_kernel, 1.0 / math.sqrt(head_si...  86.7 us
    all_to_all x6, starting transfers between devices, exchange(): return lax.all_to_all(array, 'seq', split_axis=0, concat_axis=0, tiled=True)  26.8 us
    unnamed x258, local copies, waits for them, and re-layouts  24.8 us
  transfers between devices with their start and end apart: 17, of which 9 were waited for; matrix products, arithmetic and copies ran while one was open for 34% of the time, Pallas kernels for 26%

profile of v4, /device:TPU:0, one launch (start us, length us, event | category | flops | bytes accessed | tf_op | source)
XLA Modules:
  0.0 858.1 jit_solution(16647132501477700778)
XLA Ops:
  22.9 10.7 %all-gather.2 = f32[256,128]{1,0:T(8,128)S(1)} all-gather(f32[32,128]{1,0:T(8,128)S(1)} %concatenate.53), channel_id=4, replica_groups=mesh['fsdp'=8,'seq'=4] {'fsdp'}, dimensions={0}, use_global_device_ids=true | all-gather | bytes 147456 | tf_op jit(solution)/shard_map/all_gather | solution.py:544
  40.6 803.4 %conditional.4 = (f32[2,392,1024]{2,1,0:T(8,128)}, f32[2,392,384]{2,1,0:T(8,128)}, f32[2,392,1024]{2,1,0:T(8,128)}, bf16[128,3072]{1,0:T(8,128)(2,1)S(1)}, bf16[...) conditional(s32[]{:T(128)} %convert_element_type.836, ...), branch_computations={%region_4.46_spmd, %region_45.91_spmd} | conditional | flops 209827332096 | bytes 1392628096
  59.8 4.7 all-to-all-start.6
  64.5 71.4 %all-to-all-done.6 = bf16[4,2,192,1024]{3,2,1,0:T(8,128)(2,1)} async-done(((bf16[4,2,192,1024]{3,2,1,0:T(8,128)(2,1)}), bf16[4,2,192,1024]{3,2,1,0:T(8,128)(2,1)}, u32[]{:S(2)}, u32[]{:S(2)}) %all-to-all-start.6) | async-done | bytes 3145760 | tf_op jit(solution)/shard_map/cond/branch_1_fun/all_to_all | solution.py:237
  135.9 11.4 %add_convert_fusion.17 = bf16[1536,2048]{1,0:T(8,128)(2,1)} fusion(bf16[1536,1024]{1,0:T(8,128)(2,1)} %bitcast.144, f32[2048]{0:T(1024)S(1)} %concatenate.44, bf16[1024,3072]{0,1:T(8,128)(2,1)} %all-gather.29.cloned.1.call-done), kind=kOutput, calls=%fused_computation.222 | convolution fusion | flops 6448742400 | bytes 13639680 | tf_op jit(solution)/shard_map/cond/branch_1_fun/dot_general | solution.py:25
  167.3 4.7 add_convert_fusion.22
  171.9 35.1 %attend.9 = bf16[2,392,1024]{2,1,0:T(8,128)(2,1)} custom-call(bf16[2,392,1024]{2,1,0:T(8,128)(2,1)} %bitcast.1043, bf16[4,2,192,2048]{3,2,1,0:T(8,128)(2,1)} %bitcast.1038, bf16[4,2,192,2048]{3,2,1,0:T(8,128)(2,1)} %bitcast.1039, f32[2,1,768]{2,1,0:T(1,128)} %compare_select_fusion.1.rest_0_), custom_call_target="tpu_custom_call" | custom-call | flops 9865003008 | bytes 6291456 | tf_op jit(solution)/shard_map/cond/branch_1_fun/attend/pallas_call | solution.py:109
  208.3 5.8 gather_fusion.1
  214.2 5.6 fusion.99
  223.6 21.2 %add_add_fusion.1 = f32[784,1024]{1,0:T(8,128)S(1)} fusion(f32[784,1024]{1,0:T(8,128)} %fusion.99, bf16[4096,1024]{1,0:T(8,128)(2,1)} %all-gather.33.cloned.1.call-done, f32[4096]{0:T(1024)S(1)} %bitcast.1018, bf16[1024,4096]{1,0:T(8,128)(2,1)} %all-gather.31.cloned.1.call-done, f32[1024]{0:T(1024)S(1)} %bitcast.1031, f32[1024]{0:T(1024)S(1)} %bitcast.1011, ...), kind=kOutput, calls=%fused_computation.256 | convolution fusion | flops 13178224640 | bytes 23234688 | tf_op jit(solution)/shard_map/cond/branch_1_fun/dot_general | solution.py:25
  244.8 5.8 all-gather.39.cloned.1.call-done
  274.1 13.6 %all-gather.37.cloned.1.call-done = bf16[1568,384]{1,0:T(8,128)(2,1)} async-done(((bf16[392,384]{1,0:T(8,128)(2,1)}), bf16[1568,384]{1,0:T(8,128)(2,1)}) %all-gather.37.cloned.1.call-update) | async-done | bytes 1204240 | tf_op jit(solution)/shard_map/cond/branch_1_fun/all_gather | solution.py:707
  291.8 26.8 %attend.11 = bf16[1,392,384]{2,1,0:T(8,128)(2,1)} custom-call(bf16[1,392,384]{2,1,0:T(8,128)(2,1)} %get-tuple-element.1092.q_ref, bf16[1,1,1568,768]{3,2,1,0:T(8,128)(2,1)} %fusion.84.k_ref.v_ref, bf16[1,1,1568,768]{3,2,1,0:T(8,128)(2,1)} %fusion.84.k_ref.v_ref), custom_call_target="tpu_custom_call" | custom-call | flops 7552892928 | bytes 2408448 | tf_op jit(solution)/shard_map/cond/branch_1_fun/attend/pallas_call | solution.py:109
  323.4 27.0 %attend.10 = bf16[1,392,384]{2,1,0:T(8,128)(2,1)} custom-call(bf16[1,392,384]{2,1,0:T(8,128)(2,1)} %get-tuple-element.1091.q_ref, bf16[1,1,1568,768]{3,2,1,0:T(8,128)(2,1)} %fusion.83.k_ref.v_ref, bf16[1,1,1568,768]{3,2,1,0:T(8,128)(2,1)} %fusion.83.k_ref.v_ref), custom_call_target="tpu_custom_call" | custom-call | flops 7552892928 | bytes 2408448 | tf_op jit(solution)/shard_map/cond/branch_1_fun/attend/pallas_call | solution.py:109
  396.5 4.6 all-to-all-done.7
  407.2 33.6 %attend_back.10 = bf16[4,1,392,288]{3,2,1,0:T(8,128)(2,1)} custom-call(bf16[1,1,1568,96]{3,2,1,0:T(8,128)(2,1)} %fusion.92.q_ref, bf16[1,1,1568,96]{3,2,1,0:T(8,128)(2,1)} %fusion.96.k_ref, bf16[1,1,1568,96]{3,2,1,0:T(8,128)(2,1)} %fusion.91.v_ref, bf16[1,1,1568,96]{3,2,1,0:T(8,128)(2,1)} %bitcast.943), custom_call_target="tpu_custom_call" | custom-call | flops 18882232320 | bytes 2107392 | tf_op jit(solution)/shard_map/cond/branch_1_fun/attend_back/pallas_call | solution.py:217
  449.2 33.6 %attend_back.9 = bf16[4,1,392,288]{3,2,1,0:T(8,128)(2,1)} custom-call(bf16[1,1,1568,96]{3,2,1,0:T(8,128)(2,1)} %fusion.94.q_ref, bf16[1,1,1568,96]{3,2,1,0:T(8,128)(2,1)} %fusion.95.k_ref, bf16[1,1,1568,96]{3,2,1,0:T(8,128)(2,1)} %fusion.93.v_ref, bf16[1,1,1568,96]{3,2,1,0:T(8,128)(2,1)} %bitcast.944), custom_call_target="tpu_custom_call" | custom-call | flops 18882232320 | bytes 2107392 | tf_op jit(solution)/shard_map/cond/branch_1_fun/attend_back/pallas_call | solution.py:217
  485.2 5.0 all-to-all-start.8
  493.2 8.9 %convolution_add_fusion.11 = f32[384,4096]{1,0:T(8,128)} fusion(bf16[384,1024]{1,0:T(8,128)(2,1)S(1)} %bitcast.1050, bf16[1024,4096]{1,0:T(8,128)(2,1)} %all-gather.31.cloned.1.call-done, f32[4096]{0:T(1024)S(1)} %bitcast.1019), kind=kOutput, calls=%fused_computation.237 | convolution fusion | flops 3222798336 | bytes 15482880 | tf_op jit(solution)/shard_map/cond/branch_1_fun/dot_general | solution.py:25
  509.8 8.0 all-to-all-done.8
  525.8 9.6 %convolution_convert_fusion.12 = bf16[4096,1024]{1,0:T(8,128)(2,1)} fusion(f32[384,4096]{1,0:T(8,128)} %convolution_add_fusion.11, f32[384,1024]{1,0:T(8,128)S(1)} %fusion.195), kind=kOutput, calls=%fused_computation.225 | convolution fusion | flops 3233677312 | bytes 16252928 | tf_op jit(solution)/shard_map/cond/branch_1_fun/dot_general | solution.py:25
  535.4 7.2 fusion.71
  542.7 9.1 %convolution_convert_fusion.11 = bf16[1024,4096]{1,0:T(8,128)(2,1)} fusion(bf16[384,1024]{1,0:T(8,128)(2,1)} %bitcast.1051, bf16[384,4096]{1,0:T(8,128)(2,1)S(1)} %fusion.71), kind=kOutput, calls=%fused_computation.224 | convolution fusion | flops 3225419776 | bytes 12320768 | tf_op jit(solution)/shard_map/cond/branch_1_fun/dot_general | solution.py:25
  551.8 8.0 fusion.196
  596.1 6.6 copy.462
  614.0 19.6 %attend_back.11 = bf16[4,2,192,768]{3,2,1,0:T(8,128)(2,1)} custom-call(bf16[4,2,192,256]{3,2,1,0:T(8,128)(2,1)} %bitcast.1048, bf16[4,2,192,256]{3,2,1,0:T(8,128)(2,1)} %bitcast.1047, bf16[4,2,192,256]{3,2,1,0:T(8,128)(2,1)} %bitcast.1049, bf16[4,2,192,256]{3,2,1,0:T(8,128)(2,1)} %all-to-all-done.10.g_ref, f32[2,1,768]{2,1,0:T(1,128)} %compare_select_fusion.1.rest_0_), custom_call_target="tpu_custom_call" | custom-call | flops 12079595520 | bytes 5505024 | tf_op jit(solution)/shard_map/cond/branch_1_fun/attend_back/pallas_call | solution.py:217
  633.6 4.7 all-to-all-start.11
  654.0 5.8 bitcast_convert_fusion.12
  673.3 18.5 %all-to-all-done.11 = bf16[4,2,192,768]{3,2,1,0:T(8,128)(2,1)} async-done(((bf16[4,2,192,768]{3,2,1,0:T(8,128)(2,1)}), bf16[4,2,192,768]{3,2,1,0:T(8,128)(2,1)}, u32[]{:S(2)}, u32[]{:S(2)}) %all-to-all-start.11) | async-done | bytes 2359328 | tf_op jit(solution)/shard_map/cond/branch_1_fun/all_to_all | solution.py:237
  696.2 7.5 multiply_reduce_fusion.19
  710.2 74.1 %line_sum.6 = (bf16[512,1024]{1,0:T(8,128)(2,1)}, bf16[128,4096]{1,0:T(8,128)(2,1)}, bf16[432,384]{1,0:T(8,128)(2,1)}) custom-call(bf16[512,1024]{1,0:T(8,128)(2,1)} %bitcast.897, bf16[128,4096]{1,0:T(8,128)(2,1)} %bitcast.898, bf16[432,384]{1,0:T(8,128)(2,1)} %bitcast.949), custom_call_target="tpu_custom_call" | custom-call | bytes 97157120 | tf_op jit(solution)/shard_map/cond/branch_1_fun/line_sum/pallas_call | solution.py:389
  798.1 41.1 %line_sum.7 = (bf16[128,3072]{1,0:T(8,128)(2,1)S(1)}, bf16[48,1152]{1,0:T(8,128)(2,1)S(1)}, bf16[1440,128]{1,0:T(8,128)(2,1)}) custom-call(bf16[128,3072]{1,0:T(8,128)(2,1)} %broadcast_select_fusion.3.refs_0_, bf16[48,1152]{1,0:T(8,128)(2,1)} %broadcast_select_fusion.4.refs_1_, bf16[1440,128]{1,0:T(8,128)(2,1)} %slice.429.refs_2_), custom_call_target="tpu_custom_call" | custom-call | bytes 50626560 | tf_op jit(solution)/shard_map/cond/branch_1_fun/line_sum/pallas_call | solution.py:389
  (541 shorter events, 284.2 us)
Async XLA Ops:
  7.2 33.4 %all-gather.41.cloned.1.call-start = ((), (), s32[]{:S(2)}) async-start(), calls=%async_computation.40 | async-start | bytes 2359296 | tf_op jit(solution)/shard_map/all_gather | solution.py:241
  47.9 16.6 %copy-start.117 = (f32[1024]{0:T(1024)}, f32[1024]{0:T(1024)S(1)}, u32[]{:S(2)}) copy-start(f32[1024]{0:T(1024)S(1)} %get-tuple-element.389) | copy-start | bytes 12292
  47.9 118.1 %copy-start.103 = (f32[8,1,128]{2,1,0:T(1,128)}, f32[8,1,128]{2,1,0:T(1,128)S(1)}, u32[]{:S(2)}) copy-start(f32[8,1,128]{2,1,0:T(1,128)S(1)} %get-tuple-element.382) | copy-start | bytes 12292
  47.9 215.0 %copy-start.97 = (f32[8,1,128]{2,1,0:T(1,128)}, f32[8,1,128]{2,1,0:T(1,128)S(1)}, u32[]{:S(2)}) copy-start(f32[8,1,128]{2,1,0:T(1,128)S(1)} %get-tuple-element.401) | copy-start | bytes 12292
  47.9 88.0 %all-gather.29.cloned.1.call-start = ((), (), s32[]{:S(2)}) async-start(), calls=%async_computation.30 | async-start | bytes 7077888 | tf_op jit(solution)/shard_map/cond/branch_1_fun/all_gather | solution.py:241
  50.8 172.8 %all-gather.31.cloned.1.call-start = ((), (), s32[]{:S(2)}) async-start(), calls=%async_computation.31 | async-start | bytes 9437184 | tf_op jit(solution)/shard_map/cond/branch_1_fun/all_gather | solution.py:241
  59.8 76.1 %all-to-all-start.6 = ((bf16[4,2,192,1024]{3,2,1,0:T(8,128)(2,1)}), bf16[4,2,192,1024]{3,2,1,0:T(8,128)(2,1)}, u32[]{:S(2)}, u32[]{:S(2)}) async-start(bf16[4,2,192,1024]{3,2,1,0:T(8,128)(2,1)} %broadcast_in_dim.256), calls=%async_computation.10 | async-start | bytes 6291456 | tf_op jit(solution)/shard_map/cond/branch_1_fun/all_to_all | solution.py:237
  64.5 159.1 %all-gather.33.cloned.1.call-start = ((), (), s32[]{:S(2)}) async-start(), calls=%async_computation.32 | async-start | bytes 9437184 | tf_op jit(solution)/shard_map/cond/branch_1_fun/all_gather | solution.py:241
  135.9 22.0 %copy-start.86 = (bf16[48,1536]{1,0:T(8,128)(2,1)S(1)}, bf16[48,1536]{1,0:T(8,128)(2,1)}, u32[]{:S(2)}) copy-start(bf16[48,1536]{1,0:T(8,128)(2,1)} %get-tuple-element.395) | copy-start | bytes 442372
  147.3 13.8 %copy-start.94 = (bf16[48,384]{1,0:T(8,128)(2,1)S(1)}, bf16[48,384]{1,0:T(8,128)(2,1)}, u32[]{:S(2)}) copy-start(bf16[48,384]{1,0:T(8,128)(2,1)} %get-tuple-element.394) | copy-start | bytes 110596
  147.3 15.1 %copy-start.88 = (bf16[192,384]{1,0:T(8,128)(2,1)S(1)}, bf16[192,384]{1,0:T(8,128)(2,1)}, u32[]{:S(2)}) copy-start(bf16[192,384]{1,0:T(8,128)(2,1)} %get-tuple-element.396) | copy-start | bytes 442372
  147.3 103.3 %all-gather.39.cloned.1.call-start = ((), (), s32[]{:S(2)}) async-start(), calls=%async_computation.39 | async-start | bytes 4866048 | tf_op jit(solution)/shard_map/cond/branch_1_fun/all_gather | solution.py:681
  171.9 35.2 %copy-start.115 = (pred[2,392]{1,0:T(4,128)(4,1)S(1)}, pred[2,392]{1,0:T(4,128)(4,1)}, u32[]{:S(2)}) copy-start(pred[2,392]{1,0:T(4,128)(4,1)} %copy-done.114) | copy-start | bytes 2356
  171.9 36.1 %copy-start.142 = (f32[8,48]{1,0:T(8,128)S(1)}, f32[8,48]{1,0:T(8,128)}, u32[]{:S(2)}) copy-start(f32[8,48]{1,0:T(8,128)} %get-tuple-element.410) | copy-start | bytes 4612
  171.9 36.2 %copy-start.138 = (f32[8,48]{1,0:T(8,128)S(1)}, f32[8,48]{1,0:T(8,128)}, u32[]{:S(2)}) copy-start(f32[8,48]{1,0:T(8,128)} %get-tuple-element.415) | copy-start | bytes 4612
  171.9 36.3 %copy-start.140 = (f32[8,48]{1,0:T(8,128)S(1)}, f32[8,48]{1,0:T(8,128)}, u32[]{:S(2)}) copy-start(f32[8,48]{1,0:T(8,128)} %get-tuple-element.414) | copy-start | bytes 4612
  207.1 80.6 %all-gather.37.cloned.1.call-start = ((), (), s32[]{:S(2)}) async-start(), calls=%async_computation.34 | async-start | bytes 1505280 | tf_op jit(solution)/shard_map/cond/branch_1_fun/all_gather | solution.py:707
  223.6 28.4 %copy-start.146 = (f32[384]{0:T(512)S(1)}, f32[384]{0:T(512)}, u32[]{:S(2)}) copy-start(f32[384]{0:T(512)} %get-tuple-element.411) | copy-start | bytes 4612
  256.6 62.7 %all-gather.35.cloned.1.call-start = ((), (), s32[]{:S(2)}) async-start(), calls=%async_computation.33 | async-start | bytes 1505280 | tf_op jit(solution)/shard_map/cond/branch_1_fun/all_gather | solution.py:707
  323.4 27.0 %copy-start.91 = (bf16[1,392,384]{2,1,0:T(8,128)(2,1)S(1)}, bf16[1,392,384]{2,1,0:T(8,128)(2,1)}, u32[]{:S(2)}) copy-start(bf16[1,392,384]{2,1,0:T(8,128)(2,1)} %attend.11) | copy-start | bytes 903172
  323.4 28.0 %copy-start.15 = (f32[784,384]{1,0:T(8,128)S(1)}, f32[784,384]{1,0:T(8,128)}, u32[]{:S(2)}) copy-start(f32[784,384]{1,0:T(8,128)} %copy-done.14) | copy-start | bytes 3612676
  352.1 13.0 %copy-start.18 = (f32[784,384]{1,0:T(8,128)}, f32[784,384]{1,0:T(8,128)S(1)}, u32[]{:S(2)}) copy-start(f32[784,384]{1,0:T(8,128)S(1)} %get-tuple-element.1116) | copy-start | bytes 3612676
  377.9 23.3 %all-to-all-start.7 = ((bf16[4,2,392,96]{2,1,3,0:T(2,128)(2,1)}), bf16[4,2,392,96]{2,1,3,0:T(2,128)(2,1)S(1)}, u32[]{:S(2)}, u32[]{:S(2)}) async-start(bf16[4,2,392,96]{2,1,3,0:T(2,128)(2,1)} %reshape.1321), calls=%async_computation.11 | async-start | bytes 1572864 | tf_op jit(solution)/shard_map/cond/branch_1_fun/all_to_all | solution.py:237
  381.4 143.4 %reduce-scatter.17.cloned.1.call-start = ((), (), s32[]{:S(2)}) async-start(), calls=%async_computation.35 | async-start | bytes 2985984 | tf_op jit(solution)/shard_map/cond/branch_1_fun/reduce_scatter | solution.py:245
  443.2 42.0 %all-to-all-start.9 = ((bf16[4,1,392,288]{2,3,1,0:T(8,128)(2,1)}), bf16[4,1,392,288]{2,3,1,0:T(8,128)(2,1)}, u32[]{:S(2)}, u32[]{:S(2)}) async-start(bf16[4,1,392,288]{2,3,1,0:T(8,128)(2,1)} %copy.455), calls=%async_computation.13 | async-start | bytes 2359296 | tf_op jit(solution)/shard_map/cond/branch_1_fun/all_to_all | solution.py:237
  485.2 32.6 %all-to-all-start.8 = ((bf16[4,1,392,288]{2,3,1,0:T(8,128)(2,1)}), bf16[4,1,392,288]{2,3,1,0:T(8,128)(2,1)}, u32[]{:S(2)}, u32[]{:S(2)}) async-start(bf16[4,1,392,288]{2,3,1,0:T(8,128)(2,1)} %copy.447), calls=%async_computation.12 | async-start | bytes 2359296 | tf_op jit(solution)/shard_map/cond/branch_1_fun/all_to_all | solution.py:237
  490.3 201.5 %reduce-scatter.19.cloned.1.call-start = ((), (), s32[]{:S(2)}) async-start(), calls=%async_computation.36 | async-start | bytes 9437184 | tf_op jit(solution)/shard_map/cond/branch_1_fun/reduce_scatter | solution.py:245
  542.7 167.5 %reduce-scatter.23.cloned.1.call-start = ((), (), s32[]{:S(2)}) async-start(), calls=%async_computation.38 | async-start | bytes 9437184 | tf_op jit(solution)/shard_map/cond/branch_1_fun/reduce_scatter | solution.py:245
  590.0 24.0 %all-to-all-start.10 = ((bf16[4,2,192,256]{3,2,1,0:T(8,128)(2,1)}), bf16[4,2,192,256]{3,2,1,0:T(8,128)(2,1)}, u32[]{:S(2)}, u32[]{:S(2)}) async-start(bf16[4,2,192,256]{3,2,1,0:T(8,128)(2,1)} %bitcast.216), calls=%async_computation.15 | async-start | bytes 1572864 | tf_op jit(solution)/shard_map/cond/branch_1_fun/all_to_all | solution.py:237
  633.6 58.1 %all-to-all-start.11 = ((bf16[4,2,192,768]{3,2,1,0:T(8,128)(2,1)}), bf16[4,2,192,768]{3,2,1,0:T(8,128)(2,1)}, u32[]{:S(2)}, u32[]{:S(2)}) async-start(bf16[4,2,192,768]{3,2,1,0:T(8,128)(2,1)} %attend_back.11), calls=%async_computation.16 | async-start | bytes 4718592 | tf_op jit(solution)/shard_map/cond/branch_1_fun/all_to_all | solution.py:237
  638.4 153.0 %reduce-scatter.21.cloned.1.call-start = ((), (), s32[]{:S(2)}) async-start(), calls=%async_computation.37 | async-start | bytes 5419008 | tf_op jit(solution)/shard_map/cond/branch_1_fun/reduce_scatter | solution.py:245
  710.2 77.4 %copy-start.29 = (f32[384,1024]{1,0:T(8,128)S(1)}, f32[384,1024]{1,0:T(8,128)}, u32[]{:S(2)}) copy-start(f32[384,1024]{1,0:T(8,128)} %copy-done.27) | copy-start | bytes 4718596
  (105 other events, 370.3 us)
Sparse Core Ops, SparseCore 0:
  9.9 30.5 all-gather.40
  51.4 46.6 all-gather.28
  100.1 54.3 all-gather.30
  156.5 54.4 all-gather.32
  213.4 37.2 all-gather.38
  256.7 30.8 all-gather.36
  289.3 29.9 all-gather.34
  386.1 45.1 reduce-scatter.16
  542.8 70.2 reduce-scatter.18
  616.8 71.2 reduce-scatter.22
  704.6 54.1 reduce-scatter.20

commit v5 on v4

--- a/solution.py
+++ b/solution.py
@@ -67,28 +67,24 @@
         bias_ref, o_ref = rest
     else:
         bias_ref, o_ref = None, rest[0]
-    head = pl.program_id(2)
     query = q_ref[0]
-    key = k_ref[...].reshape(-1, k_ref.shape[-1])
-    value = v_ref[...].reshape(-1, v_ref.shape[-1])
+    lanes = query.shape[1]
+    key = k_ref[...].reshape(-1, lanes)
+    value = v_ref[...].reshape(-1, lanes)
     lane = lax.broadcasted_iota(jnp.int32, query.shape, 1)
-    mine = (lane // head_size) == head
-    own_query = jnp.where(mine, query, jnp.zeros_like(query))
-    scores = mm(own_query, key, NT) * (scale * LOG2E)
-    if bias_ref is not None:
-        scores = scores + bias_ref[0]
-    top = jnp.max(scores, axis=1, keepdims=True)
-    weight = jnp.exp2(scores - top)
-    total = jnp.sum(weight, axis=1, keepdims=True)
-    result = (mm(weight.astype(bf16), value) / total).astype(bf16)
-
-    @pl.when(head == 0)
-    def _():
-        o_ref[0] = result
-
-    @pl.when(head > 0)
-    def _():
-        o_ref[0] = jnp.where(mine, result, o_ref[0])
+    result = None
+    for head in range(lanes // head_size):
+        mine = (lane // head_size) == head
+        own_query = jnp.where(mine, query, jnp.zeros_like(query))
+        scores = mm(own_query, key, NT) * (scale * LOG2E)
+        if bias_ref is not None:
+            scores = scores + bias_ref[0]
+        top = jnp.max(scores, axis=1, keepdims=True)
+        weight = jnp.exp2(scores - top)
+        total = jnp.sum(weight, axis=1, keepdims=True)
+        part = jnp.where(mine, mm(weight.astype(bf16), value) / total, 0.0)
+        result = part if result is None else result + part
+    o_ref[0] = result.astype(bf16)
 
 
 def attend(queries, joined, head_size, bias):
@@ -97,20 +93,20 @@
     keys = major * length
     groups = width // 128
     in_specs = [
-        pl.BlockSpec((1, rows, 128), lambda c, g, h: (c, 0, g)),
-        pl.BlockSpec((major, 1, length, 128), lambda c, g, h: (0, c, 0, g)),
-        pl.BlockSpec((major, 1, length, 128), lambda c, g, h: (0, c, 0, g + groups)),
+        pl.BlockSpec((1, rows, 128), lambda c, g: (c, 0, g)),
+        pl.BlockSpec((major, 1, length, 128), lambda c, g: (0, c, 0, g)),
+        pl.BlockSpec((major, 1, length, 128), lambda c, g: (0, c, 0, g + groups)),
     ]
     operands = [queries, joined, joined]
     if bias is not None:
-        in_specs.append(pl.BlockSpec((1, 1, keys), lambda c, g, h: (c, 0, 0)))
+        in_specs.append(pl.BlockSpec((1, 1, keys), lambda c, g: (c, 0, 0)))
         operands.append(bias)
     cells = clips * rows * keys * (width // head_size)
     return pl.pallas_call(
         functools.partial(forward_kernel, 1.0 / math.sqrt(head_size), head_size),
-        grid=(clips, groups, 128 // head_size),
+        grid=(clips, groups),
         in_specs=in_specs,
-        out_specs=pl.BlockSpec((1, rows, 128), lambda c, g, h: (c, 0, g)),
+        out_specs=pl.BlockSpec((1, rows, 128), lambda c, g: (c, 0, g)),
         out_shape=jax.ShapeDtypeStruct((clips, rows, width), bf16),
         compiler_params=pltpu.CompilerParams(vmem_limit_bytes=VMEM_LIMIT),
         cost_estimate=pl.CostEstimate(
@@ -121,55 +117,50 @@
 
 
 def backward_kernel(scale, head_size, shards, q_ref, k_ref, v_ref, g_ref, *rest):
-    if len(rest) == 5:
+    if len(rest) == 4:
         bias_ref = rest[0]
         rest = rest[1:]
     else:
         bias_ref = None
-    out_ref, dq_sum, dk_sum, dv_sum = rest
-    group = pl.program_id(1)
-    part = pl.program_id(2)
-    head = pl.program_id(3)
+    out_ref, dk_sum, dv_sum = rest
+    group = pl.program_id(0)
+    part = pl.program_id(1)
     lanes = q_ref.shape[-1]
     query = q_ref[...].reshape(-1, lanes)
     key = k_ref[...].reshape(-1, lanes)
     value = v_ref[...].reshape(-1, lanes)
     grad = g_ref[...].reshape(-1, lanes)
     lane = lax.broadcasted_iota(jnp.int32, query.shape, 1)
-    mine = (lane // head_size) == head
-    zero = jnp.zeros_like(query)
-    own_query = jnp.where(mine, query, zero)
-    own_grad = jnp.where(mine, grad, zero)
     key_lane = lax.broadcasted_iota(jnp.int32, key.shape, 1)
-    own_key = jnp.where((key_lane // head_size) == head, key, jnp.zeros_like(key))
-    scores = mm(own_query, key, NT) * (scale * LOG2E)
-    if bias_ref is not None:
-        scores = scores + bias_ref[0]
-    top = jnp.max(scores, axis=1, keepdims=True)
-    weight = jnp.exp2(scores - top)
-    total = jnp.sum(weight, axis=1, keepdims=True)
-    chance = weight * (1.0 / total)
-    grad_chance = mm(own_grad, value, NT)
-    delta = jnp.sum(chance * grad_chance, axis=1, keepdims=True)
-    grad_scores = (chance * (grad_chance - delta)).astype(bf16)
-    part_q = mm(grad_scores, own_key)
-    part_v = mm(own_grad, chance.astype(bf16), TN)
-    part_k = mm(own_query, grad_scores, TN)
-
-    @pl.when(head == 0)
-    def _():
-        dq_sum[...] = part_q
-
-    @pl.when(head > 0)
-    def _():
-        dq_sum[...] += part_q
-
-    @pl.when((head == 0) & (part == 0))
+    sums = None
+    for head in range(lanes // head_size):
+        mine = (lane // head_size) == head
+        own_query = jnp.where(mine, query, jnp.zeros_like(query))
+        own_grad = jnp.where(mine, grad, jnp.zeros_like(grad))
+        own_key = jnp.where((key_lane // head_size) == head, key, jnp.zeros_like(key))
+        scores = mm(own_query, key, NT) * (scale * LOG2E)
+        if bias_ref is not None:
+            scores = scores + bias_ref[0]
+        top = jnp.max(scores, axis=1, keepdims=True)
+        weight = jnp.exp2(scores - top)
+        chance = weight * (1.0 / jnp.sum(weight, axis=1, keepdims=True))
+        grad_chance = mm(own_grad, value, NT)
+        delta = jnp.sum(chance * grad_chance, axis=1, keepdims=True)
+        grad_scores = (chance * (grad_chance - delta)).astype(bf16)
+        terms = (
+            mm(grad_scores, own_key),
+            mm(own_query, grad_scores, TN),
+            mm(own_grad, chance.astype(bf16), TN),
+        )
+        sums = terms if sums is None else tuple(x + y for x, y in zip(sums, terms))
+    part_q, part_k, part_v = sums
+
+    @pl.when(part == 0)
     def _():
         dk_sum[...] = part_k
         dv_sum[...] = part_v
 
-    @pl.when((head > 0) | (part > 0))
+    @pl.when(part > 0)
     def _():
         dk_sum[...] += part_k
         dv_sum[...] += part_v
@@ -177,20 +168,17 @@
     rows = out_ref.shape[2]
     width = out_ref.shape[3] // 3
     held = query.shape[0] // rows
-    last_head = head == pl.num_programs(3) - 1
 
     def place(kind):
         if width == lanes:
             return slice(kind * width, (kind + 1) * width)
         return pl.ds(pl.multiple_of(kind * width + group * lanes, 128), lanes)
 
-    @pl.when(last_head)
-    def _():
-        result = (dq_sum[...] * scale).astype(bf16)
-        for index in range(held):
-            out_ref[part * held + index, 0, :, place(0)] = result[index * rows : (index + 1) * rows]
-
-    @pl.when(last_head & (part == pl.num_programs(2) - 1))
+    result_q = (part_q * scale).astype(bf16)
+    for index in range(held):
+        out_ref[part * held + index, 0, :, place(0)] = result_q[index * rows : (index + 1) * rows]
+
+    @pl.when(part == pl.num_programs(1) - 1)
     def _():
         for kind, total_ref, factor in ((1, dk_sum, scale), (2, dv_sum, 1.0)):
             result = (total_ref[...] * factor).T.astype(bf16)
@@ -198,36 +186,32 @@
                 out_ref[index, 0, :, place(kind)] = result[index * rows : (index + 1) * rows]
 
 
-def attend_back(queries, keys, values, grad_mixed, head_size, bias, shards):
-    major, clips, length, width = queries.shape
+def attend_back(queries, keys, values, grad_mixed, clip, head_size, bias, shards):
+    major, _, length, width = queries.shape
     lanes = min(width, 128)
     groups = width // lanes
     rows = major * length // shards
     parts = shards if major == 1 else 1
     query_rows = rows if major == 1 else length
-    by_query = pl.BlockSpec((major, 1, query_rows, lanes), lambda c, g, r, h: (0, c, r, g))
-    by_key = pl.BlockSpec((major, 1, length, lanes), lambda c, g, r, h: (0, c, 0, g))
+    by_query = pl.BlockSpec((major, 1, query_rows, lanes), lambda g, r: (0, clip, r, g))
+    by_key = pl.BlockSpec((major, 1, length, lanes), lambda g, r: (0, clip, 0, g))
     in_specs = [by_query, by_key, by_key, by_query]
     operands = [queries, keys, values, grad_mixed]
     total = major * length
     if bias is not None:
-        in_specs.append(pl.BlockSpec((1, 1, total), lambda c, g, r, h: (c, 0, 0)))
+        in_specs.append(pl.BlockSpec((1, 1, total), lambda g, r: (clip, 0, 0)))
         operands.append(bias)
-    cells = clips * total * total * (width // head_size)
+    cells = total * total * (width // head_size)
     return pl.pallas_call(
         functools.partial(backward_kernel, 1.0 / math.sqrt(head_size), head_size, shards),
-        grid=(clips, groups, parts, lanes // head_size),
+        grid=(groups, parts),
         in_specs=in_specs,
-        out_specs=pl.BlockSpec((shards, 1, rows, 3 * width), lambda c, g, r, h: (0, c, 0, 0)),
-        out_shape=jax.ShapeDtypeStruct((shards, clips, rows, 3 * width), bf16),
-        scratch_shapes=[
-            pltpu.VMEM((major * query_rows, lanes), f32),
-            pltpu.VMEM((lanes, total), f32),
-            pltpu.VMEM((lanes, total), f32),
-        ],
+        out_specs=pl.BlockSpec((shards, 1, rows, 3 * width), lambda g, r: (0, 0, 0, 0)),
+        out_shape=jax.ShapeDtypeStruct((shards, 1, rows, 3 * width), bf16),
+        scratch_shapes=[pltpu.VMEM((lanes, total), f32), pltpu.VMEM((lanes, total), f32)],
         compiler_params=pltpu.CompilerParams(vmem_limit_bytes=VMEM_LIMIT),
         cost_estimate=pl.CostEstimate(
-            flops=cells * 2560, bytes_accessed=14 * clips * total * width, transcendentals=cells
+            flops=cells * 2560, bytes_accessed=14 * total * width, transcendentals=cells
         ),
         name="attend_back",
     )(*operands)
@@ -235,6 +219,17 @@
 
 def exchange(array):
     return lax.all_to_all(array, "seq", split_axis=0, concat_axis=0, tiled=True)
+
+
+def gather_slots(array, size, shard):
+    right = [(index, index + 1) for index in range(size - 1)]
+    left = [(index + 1, index) for index in range(size - 1)]
+    from_left, from_right = [array], [array]
+    for _ in range(size - 1):
+        from_left.append(lax.ppermute(from_left[-1], "seq", right))
+        from_right.append(lax.ppermute(from_right[-1], "seq", left))
+    line = jnp.stack(from_left[:0:-1] + from_right)
+    return lax.dynamic_slice_in_dim(line, size - 1 - shard, size, 0)
 
 
 def gather(array):
@@ -415,8 +410,8 @@
     grad_y = grad_out.astype(bf16)
     grad_contract = mm(active, grad_y, TN).astype(bf16)
     grad_contract_bias = jnp.sum(grad_y.astype(f32), axis=0)
+    grad_y, grad_contract = lax.optimization_barrier((grad_y, grad_contract))
     grad_hidden = (mm(grad_y, contract, NT) * gelu_slope(hidden)).astype(bf16)
-    grad_hidden, grad_contract = lax.optimization_barrier((grad_hidden, grad_contract))
     grad_expand = mm(normed_mid, grad_hidden, TN).astype(bf16)
     grad_expand_bias = jnp.sum(grad_hidden.astype(f32), axis=0)
     grad_normed = mm(grad_hidden, expand, NT)
@@ -529,6 +524,7 @@
     span = visible.shape[1]
 
     e_out = gather(e_shard["out"])
+    e_first = jnp.concatenate([e_shard["joint"], e_shard["expand"], embed_weight], axis=1)
 
     place = lax.broadcasted_iota(jnp.int32, (1, 1, span), 2)
     slot_visible = jnp.any(
@@ -554,10 +550,8 @@
         slot_token,
         positions,
         e_out,
-        e_shard["joint"],
-        e_shard["expand"],
+        e_first,
         e_shard["contract"],
-        embed_weight,
         tuple(p_shard[name] for name in ("joint", "out", "expand", "contract")),
         tuple(full[:-1]),
         cotangent,
@@ -580,10 +574,8 @@
     slot_token,
     positions,
     e_out,
-    e_joint_shard,
-    e_expand_shard,
+    e_first_shard,
     e_contract_shard,
-    embed_shard,
     p_shards,
     vectors,
     cotangent,
@@ -600,9 +592,12 @@
     embed_bias, mask_token = vectors[9:11]
     p_vec = dict(zip(ORDER, vectors[11:]))
 
-    e_joint = gather(e_joint_shard)
+    e_first = gather(e_first_shard)
+    e_joint = e_first[:, : 3 * width]
+    e_expand = e_first[:, 3 * width : -small_width]
+    embed = e_first[:, -small_width:]
     packed = jnp.concatenate(
-        [blocks_of(member, 1, small_width)[0] for member in (*p_shards, embed_shard)], axis=0
+        [blocks_of(member, 1, small_width)[0] for member in p_shards], axis=0
     )
 
     own_visible = lax.dynamic_slice_in_dim(slot_visible, shard * slots, slots, 1)
@@ -661,10 +656,8 @@
 
     inputs = tokens.reshape(rows, width)
     normed = norm_layer(inputs, e_vec["pre_gain"], e_vec["pre_shift"])
-    normed_kept = keep(normed).reshape(1, clips, held, width)
-    normed_kept, e_expand_shard = lax.optimization_barrier((normed_kept, e_expand_shard))
-    e_expand = gather(e_expand_shard)
-    normed_all = exchange(jnp.broadcast_to(normed_kept, (seq_size, clips, held, width)))
+    normed_kept = keep(normed).reshape(clips, held, width)
+    normed_all = gather_slots(normed_kept, seq_size, shard)
     queries = (mm(normed, e_joint[:, :width]) + e_vec["query_bias"]).astype(bf16)
     joined = mm(normed_all.reshape(-1, width), e_joint[:, width:])
     joined_bias = jnp.concatenate([jnp.zeros_like(e_vec["value_bias"]), e_vec["value_bias"]])
@@ -686,19 +679,24 @@
     encoded, packed = lax.optimization_barrier((encoded, packed))
     unpacked = []
     at = 0
-    for member in (*p_shards, embed_shard):
+    for member in p_shards:
         split = member.shape[1] // small_width
         count = member.shape[0] * split
         piece = packed[:, at : at + count].reshape(fsdp_size, split, member.shape[0], small_width)
         unpacked.append(piece.transpose(0, 2, 1, 3).reshape(-1, member.shape[1]))
         at += count
-    p_joint, p_out, p_expand, p_contract, embed = unpacked
+    p_joint, p_out, p_expand, p_contract = unpacked
     context = encoded.astype(bf16)
 
     embedded = mm(context, embed) + embed_bias
     pred_input = jnp.where(own_flat, embedded, mask_token) + slot_code
     p_normed = norm_layer(pred_input, p_vec["pre_gain"], p_vec["pre_shift"])
     p_queries = (mm(p_normed, p_joint[:, :small_width]) + p_vec["query_bias"]).astype(bf16)
+    own_weight, own_bias = own_joint(
+        e_joint, e_vec["query_bias"], e_vec["value_bias"], seq_size, shard
+    )
+    own_qkv = [by_clip(member) for member in own_parts(normed_all, own_weight, own_bias)]
+    p_queries, *own_qkv = lax.optimization_barrier((p_queries, *own_qkv))
     p_bias = jnp.concatenate([jnp.zeros_like(p_vec["value_bias"]), p_vec["value_bias"]])
     p_normed_all = []
     p_mixed = []
@@ -752,6 +750,7 @@
         grads = attend_back(
             *own_parts(every, own_weight, own_bias),
             grad_mixed[:, clip].reshape(1, 1, span, own_width),
+            0,
             small_head,
             None,
             seq_size,
@@ -789,22 +788,21 @@
     )
     expand_part = scatter(e_grads[1].reshape(fsdp_size, -1, e_grads[1].shape[1]))
     contract_part = scatter(e_grads[2].reshape(fsdp_size, -1, e_grads[2].shape[1]))
-    own_weight, own_bias = own_joint(
-        e_joint, e_vec["query_bias"], e_vec["value_bias"], seq_size, shard
-    )
     own_width = width // seq_size
     grad_mixed = grad_mixed.reshape(clips * held, seq_size, own_width).transpose(1, 0, 2)
-    grad_mixed = exchange(grad_mixed.reshape(seq_size, clips, held, own_width))
-    parts = own_parts(normed_all, own_weight, own_bias)
-    grads = attend_back(
-        *[by_clip(member) for member in (*parts, grad_mixed)], head_size, bias, seq_size
-    )
-    flat = grads.reshape(-1, 3 * own_width)
+    grad_mixed = by_clip(exchange(grad_mixed.reshape(seq_size, clips, held, own_width)))
+    grads = [
+        attend_back(*own_qkv, grad_mixed, clip, head_size, bias, seq_size) for clip in range(clips)
+    ]
+    received = [exchange(member) for member in grads]
+    received[0], contract_part = lax.optimization_barrier((received[0], contract_part))
+    flat = jnp.concatenate(grads, axis=1).reshape(-1, 3 * own_width)
     e_grad_joint = mm(normed_all.reshape(-1, width), flat, TN).astype(bf16)
     e_small.update(joint_small(jnp.sum(flat.astype(f32), axis=0), seq_size, shard))
-    received, contract_part = lax.optimization_barrier((exchange(grads), contract_part))
+    e_by_sender = by_sender(e_joint, seq_size)
+    grad_normed = jnp.concatenate([joint_back(member, e_by_sender) for member in received], axis=0)
     grad_norm, e_small["pre_gain"], e_small["pre_shift"] = norm_back(
-        keep(inputs), e_vec["pre_gain"], joint_back(received, by_sender(e_joint, seq_size))
+        keep(inputs), e_vec["pre_gain"], grad_normed
     )
     grad_tokens = put_back(grad_middle + grad_norm)
 
@@ -827,7 +825,7 @@
         )
     )
 
-    late, contract_sum = lax.optimization_barrier((late, contract_sum))
+    late, expand_sum = lax.optimization_barrier((late, expand_sum))
 
     def cut(array, at, rows, lanes, block):
         split = lanes // block

time: 868 us -> 855 us (0.985)
  Pallas kernels: 291 us -> 253 us
  starting transfers between devices: 27.2 us -> 47.4 us
  local copies, waits for them, and re-layouts: 129 us -> 146 us
  waiting for transfers between devices: 129 us -> 118 us
    all_to_all x6, waiting for transfers between devices: 105 us -> 29.9 us  [exchange(): return lax.all_to_all(array, 'seq', split_axis=0, concat_axis=0, tiled=True)]
    ppermute x0 -> x6, waiting for transfers between devices: none -> 44.1 us  [the longest x3 42.7 us: gather_slots(): from_left.append(lax.ppermute(from_left[-1], 'seq', right))]
    pallas_call x3, Pallas kernels: 88.9 us -> 55.2 us  [attend(): pl.pallas_call(functools.partial(forward_kernel, 1.0 / math.sqrt(head_siz...]
    ppermute x0 -> x6, starting transfers between devices: none -> 18.1 us  [the longest x3 14.2 us: gather_slots(): from_left.append(lax.ppermute(from_left[-1], 'seq', right))]
    all_gather x4 -> x3, waiting for transfers between devices: 1.96 us -> 15.7 us  [gather(): return lax.all_gather(array, 'fsdp', axis=0, tiled=True)]
    dynamic_update_slice x4, local copies, waits for them, and re-layouts: 1.46 us -> 12.7 us  [spread(): lax.dynamic_update_slice_in_dim(full, vector, shard * vector.shape[0], 0)]
    unnamed x258 -> x267, local copies, waits for them, and re-layouts: 24.8 us -> 35.9 us
    pallas_call x3 -> x4, Pallas kernels: 86.7 us -> 82.7 us  [attend_back(): pl.pallas_call(functools.partial(backward_kernel, 1.0 / math.sqrt(head_si...]
  transfers between devices with their start and end apart: 17 -> 22, of which waited for: 9 -> 11; matrix products, arithmetic and copies ran while one was open for 34% -> 37% of each run, Pallas kernels for 26% -> 23%
where the time goes in v5:
time: 855 us; the launch traced here: 845 us
  Pallas kernels  253 us (30%)
  matrix products  183 us (21%)
  local copies, waits for them, and re-layouts  146 us (17%)
  waiting for transfers between devices  118 us (14%)
  other arithmetic  61.2 us (7%)
  starting transfers between devices  47.4 us (6%)
  between operations  16.2 us (2%)
  blocking collectives  10.7 us (1%)
  loops' own time  9.62 us (1%)
    dot_general x43, matrix products, mm(): return lax.dot_general(left, right, dims, preferred_element_type=f32)  171 us
    pallas_call x2, Pallas kernels, line_sum(): pl.pallas_call(functools.partial(line_kernel, size, tuple(cuts)), out_sha...  115 us
    pallas_call x4, Pallas kernels, attend_back(): pl.pallas_call(functools.partial(backward_kernel, 1.0 / math.sqrt(head_si...  82.7 us
    pallas_call x3, Pallas kernels, attend(): pl.pallas_call(functools.partial(forward_kernel, 1.0 / math.sqrt(head_siz...  55.2 us
    ppermute x3, waiting for transfers between devices, gather_slots(): from_left.append(lax.ppermute(from_left[-1], 'seq', right))  42.7 us
    unnamed x267, local copies, waits for them, and re-layouts  35.9 us
    all_to_all x6, waiting for transfers between devices, exchange(): return lax.all_to_all(array, 'seq', split_axis=0, concat_axis=0, tiled=True)  29.9 us
    all_to_all x6, starting transfers between devices, exchange(): return lax.all_to_all(array, 'seq', split_axis=0, concat_axis=0, tiled=True)  28 us
  transfers between devices with their start and end apart: 22, of which 11 were waited for; matrix products, arithmetic and copies ran while one was open for 37% of the time, Pallas kernels for 23%

profile of v5, /device:TPU:0, one launch (start us, length us, event | category | flops | bytes accessed | tf_op | source)
XLA Modules:
  0.0 844.6 jit_solution(10579886060238184129)
XLA Ops:
  22.9 10.7 %all-gather.2 = f32[256,128]{1,0:T(8,128)S(1)} all-gather(f32[32,128]{1,0:T(8,128)S(1)} %concatenate.72), channel_id=4, replica_groups=mesh['fsdp'=8,'seq'=4] {'fsdp'}, dimensions={0}, use_global_device_ids=true | all-gather | bytes 147456 | tf_op jit(solution)/shard_map/all_gather | solution.py:540
  50.1 779.9 %conditional.4 = (f32[2,392,1024]{2,1,0:T(8,128)}, f32[2,392,384]{2,1,0:T(8,128)}, f32[2,392,1024]{2,1,0:T(8,128)}, bf16[128,3072]{1,0:T(8,128)(2,1)S(1)}, bf16[...) conditional(s32[]{:T(128)} %convert_element_type.831, ...), branch_computations={%region_4.47_spmd, %region_46.93_spmd} | conditional | flops 209840373760 | bytes 1398152576
  67.5 15.9 %collective-permute-done.6 = bf16[2,192,1024]{2,1,0:T(8,128)(2,1)S(1)} collective-permute-done((bf16[2,192,1024]{2,1,0:T(8,128)(2,1)S(1)}, bf16[2,192,1024]{2,1,0:T(8,128)(2,1)S(1)}, u32[]{:S(2)}, u32[]{:S(2)}) %collective-permute-start.6) | collective-permute-done | bytes 786464 | tf_op jit(solution)/shard_map/cond/branch_1_fun/ppermute | solution.py:229
  90.1 14.3 %collective-permute-done.7 = bf16[2,192,1024]{2,1,0:T(8,128)(2,1)} collective-permute-done((bf16[2,192,1024]{2,1,0:T(8,128)(2,1)S(1)}, bf16[2,192,1024]{2,1,0:T(8,128)(2,1)}, u32[]{:S(2)}, u32[]{:S(2)}) %collective-permute-start.7) | collective-permute-done | bytes 786464 | tf_op jit(solution)/shard_map/cond/branch_1_fun/ppermute | solution.py:229
  104.4 5.4 collective-permute-start.8
  112.5 12.4 %collective-permute-done.8 = bf16[2,192,1024]{2,1,0:T(8,128)(2,1)} collective-permute-done((bf16[2,192,1024]{2,1,0:T(8,128)(2,1)}, bf16[2,192,1024]{2,1,0:T(8,128)(2,1)}, u32[]{:S(2)}, u32[]{:S(2)}) %collective-permute-start.8) | collective-permute-done | bytes 786464 | tf_op jit(solution)/shard_map/cond/branch_1_fun/ppermute | solution.py:229
  133.2 15.7 %all-gather.25.cloned.1.call-done = bf16[1024,7552]{0,1:T(8,128)(2,1)} async-done(((bf16[128,7552]{0,1:T(8,128)(2,1)}), bf16[1024,7552]{0,1:T(8,128)(2,1)}) %all-gather.25.cloned.1.call-update) | async-done | bytes 15466512 | tf_op jit(solution)/shard_map/cond/branch_1_fun/all_gather | solution.py:236
  148.9 11.2 %add_convert_fusion.15 = bf16[1536,2048]{1,0:T(8,128)(2,1)} fusion(bf16[1536,1024]{1,0:T(8,128)(2,1)} %bitcast.887, f32[2048]{0:T(1024)} %concatenate.59, bf16[1024,7552]{0,1:T(8,128)(2,1)} %all-gather.25.cloned.1.call-done), kind=kOutput, calls=%fused_computation.233 | convolution fusion | flops 6448742400 | bytes 13639680 | tf_op jit(solution)/shard_map/cond/branch_1_fun/dot_general | solution.py:25
  179.9 23.4 %attend.9 = bf16[2,392,1024]{2,1,0:T(8,128)(2,1)} custom-call(bf16[2,392,1024]{2,1,0:T(8,128)(2,1)} %bitcast.1082, bf16[4,2,192,2048]{3,2,1,0:T(8,128)(2,1)} %bitcast.1076, bf16[4,2,192,2048]{3,2,1,0:T(8,128)(2,1)} %bitcast.1077, f32[2,1,768]{2,1,0:T(1,128)} %compare_select_fusion.1.rest_0_), custom_call_target="tpu_custom_call" | custom-call | flops 9865003008 | bytes 6291456 | tf_op jit(solution)/shard_map/cond/branch_1_fun/attend/pallas_call | solution.py:105
  204.7 5.4 gather_fusion.1
  210.2 5.6 fusion.112
  219.3 22.4 %add_add_fusion.1 = f32[784,1024]{1,0:T(8,128)S(1)} fusion(f32[784,1024]{1,0:T(8,128)} %fusion.112, bf16[4096,1024]{1,0:T(8,128)(2,1)} %all-gather.27.cloned.1.call-done, f32[4096]{0:T(1024)S(1)} %bitcast.1060, bf16[1024,7552]{0,1:T(8,128)(2,1)} %all-gather.25.cloned.1.call-done, f32[1024]{0:T(1024)S(1)} %bitcast.1075, f32[1024]{0:T(1024)S(1)} %bitcast.1053, ...), kind=kOutput, calls=%fused_computation.272 | convolution fusion | flops 13178224640 | bytes 26445952 | tf_op jit(solution)/shard_map/cond/branch_1_fun/dot_general | solution.py:25
  241.7 9.5 %all-gather.33.cloned.1.call-done = bf16[4608,384]{1,0:T(8,128)(2,1)} async-done(((bf16[576,384]{1,0:T(8,128)(2,1)}), bf16[4608,384]{1,0:T(8,128)(2,1)}) %all-gather.33.cloned.1.call-update) | async-done | bytes 3538960 | tf_op jit(solution)/shard_map/cond/branch_1_fun/all_gather | solution.py:674
  291.4 15.9 %attend.11 = bf16[1,392,384]{2,1,0:T(8,128)(2,1)} custom-call(bf16[1,392,384]{2,1,0:T(8,128)(2,1)} %get-tuple-element.794.q_ref, bf16[1,1,1568,768]{3,2,1,0:T(8,128)(2,1)} %fusion.97.k_ref.v_ref, bf16[1,1,1568,768]{3,2,1,0:T(8,128)(2,1)} %fusion.97.k_ref.v_ref), custom_call_target="tpu_custom_call" | custom-call | flops 7552892928 | bytes 2408448 | tf_op jit(solution)/shard_map/cond/branch_1_fun/attend/pallas_call | solution.py:105
  307.3 11.4 %all-gather.29.cloned.1.call-done = bf16[1568,384]{1,0:T(8,128)(2,1)} async-done(((bf16[392,384]{1,0:T(8,128)(2,1)}), bf16[1568,384]{1,0:T(8,128)(2,1)}) %all-gather.29.cloned.1.call-update) | async-done | bytes 1204240 | tf_op jit(solution)/shard_map/cond/branch_1_fun/all_gather | solution.py:705
  322.9 15.8 %attend.10 = bf16[1,392,384]{2,1,0:T(8,128)(2,1)} custom-call(bf16[1,392,384]{2,1,0:T(8,128)(2,1)} %get-tuple-element.793.q_ref, bf16[1,1,1568,768]{3,2,1,0:T(8,128)(2,1)} %fusion.96.k_ref.v_ref, bf16[1,1,1568,768]{3,2,1,0:T(8,128)(2,1)} %fusion.96.k_ref.v_ref), custom_call_target="tpu_custom_call" | custom-call | flops 7552892928 | bytes 2408448 | tf_op jit(solution)/shard_map/cond/branch_1_fun/attend/pallas_call | solution.py:105
  391.9 31.3 %attend_back.13 = bf16[4,1,392,288]{3,2,1,0:T(8,128)(2,1)} custom-call(bf16[1,1,1568,96]{3,2,1,0:T(8,128)(2,1)} %fusion.105.q_ref, bf16[1,1,1568,96]{3,2,1,0:T(8,128)(2,1)} %fusion.109.k_ref, bf16[1,1,1568,96]{3,2,1,0:T(8,128)(2,1)} %fusion.104.v_ref, bf16[1,1,1568,96]{3,2,1,0:T(8,128)(2,1)} %bitcast.992), custom_call_target="tpu_custom_call" | custom-call | flops 18882232320 | bytes 2107392 | tf_op jit(solution)/shard_map/cond/branch_1_fun/attend_back/pallas_call | solution.py:205
  432.0 31.2 %attend_back.12 = bf16[4,1,392,288]{3,2,1,0:T(8,128)(2,1)} custom-call(bf16[1,1,1568,96]{3,2,1,0:T(8,128)(2,1)} %fusion.107.q_ref, bf16[1,1,1568,96]{3,2,1,0:T(8,128)(2,1)} %fusion.108.k_ref, bf16[1,1,1568,96]{3,2,1,0:T(8,128)(2,1)} %fusion.106.v_ref, bf16[1,1,1568,96]{3,2,1,0:T(8,128)(2,1)} %bitcast.993), custom_call_target="tpu_custom_call" | custom-call | flops 18882232320 | bytes 2107392 | tf_op jit(solution)/shard_map/cond/branch_1_fun/attend_back/pallas_call | solution.py:205
  473.0 9.8 %fusion.82 = f32[384,4096]{1,0:T(8,128)} fusion(bf16[384,1024]{1,0:T(8,128)(2,1)S(1)} %bitcast.1091, bf16[1024,7552]{0,1:T(8,128)(2,1)} %all-gather.25.cloned.1.call-done, f32[4096]{0:T(1024)S(1)} %bitcast.1061), kind=kOutput, calls=%fused_computation.253 | convolution fusion | flops 3222798336 | bytes 15482880 | tf_op jit(solution)/shard_map/cond/branch_1_fun/dot_general | solution.py:25
  489.5 8.8 %all-to-all-done.7 = bf16[4,1,392,288]{2,3,1,0:T(8,128)(2,1)} async-done(((bf16[4,1,392,288]{2,3,1,0:T(8,128)(2,1)}), bf16[4,1,392,288]{2,3,1,0:T(8,128)(2,1)}, u32[]{:S(2)}, u32[]{:S(2)}) %all-to-all-start.7) | async-done | bytes 903200 | tf_op jit(solution)/shard_map/cond/branch_1_fun/all_to_all | solution.py:221
  508.4 8.7 %convolution_convert_fusion.12 = bf16[4096,1024]{1,0:T(8,128)(2,1)} fusion(bf16[384,1024]{1,0:T(8,128)(2,1)S(1)} %get-tuple-element.422, f32[384,4096]{1,0:T(8,128)} %fusion.82), kind=kOutput, calls=%fused_computation.236 | convolution fusion | flops 3233284096 | bytes 15466496 | tf_op jit(solution)/shard_map/cond/branch_1_fun/dot_general | solution.py:25
  517.5 9.1 %fusion.214 = (bf16[4096]{0:T(1024)(128)(2,1)}, bf16[384,4096]{1,0:T(8,128)(2,1)S(1)}) fusion(f32[384,4096]{1,0:T(8,128)} %fusion.82, bf16[384,1024]{1,0:T(8,128)(2,1)S(1)} %get-tuple-element.422, bf16[4096,1024]{1,0:T(8,128)(2,1)} %all-gather.27.cloned.1.call-done), kind=kOutput, calls=%fused_computation.566 | convolution fusion | flops 3238522880 | bytes 18620416 | tf_op jit(solution)/shard_map/cond/branch_1_fun/dot_general | solution.py:25
  526.6 6.8 convolution_convert_fusion.11
  533.4 7.2 fusion.70
  550.2 6.4 copy.472
  582.4 12.3 %slice_dynamic-update-slice_fusion.6 = f32[384]{0:T(512)S(1)} fusion(f32[384]{0:T(512)S(1)} %broadcast.608.clone.1, s32[]{:T(128)S(6)} %select_n.93, f32[288]{0:T(512)S(1)} %add.684), kind=kLoop, calls=%fused_computation.498 | loop fusion | bytes 1028 | tf_op jit(solution)/shard_map/cond/branch_1_fun/dynamic_update_slice | solution.py:470
  601.3 10.2 %attend_back.15 = bf16[4,1,192,768]{3,2,1,0:T(8,128)(2,1)} custom-call(bf16[4,2,192,256]{3,2,1,0:T(8,128)(2,1)} %bitcast.1087, bf16[4,2,192,256]{3,2,1,0:T(8,128)(2,1)} %bitcast.1085, bf16[4,2,192,256]{3,2,1,0:T(8,128)(2,1)} %bitcast.1089, bf16[4,2,192,256]{3,2,1,0:T(8,128)(2,1)} %all-to-all-done.9.g_ref, f32[2,1,768]{2,1,0:T(1,128)} %compare_select_fusion.1.rest_0_), custom_call_target="tpu_custom_call" | custom-call | flops 6039797760 | bytes 2752512 | tf_op jit(solution)/shard_map/cond/branch_1_fun/attend_back/pallas_call | solution.py:205
  620.7 10.0 %attend_back.14 = bf16[4,1,192,768]{3,2,1,0:T(8,128)(2,1)} custom-call(bf16[4,2,192,256]{3,2,1,0:T(8,128)(2,1)} %bitcast.1088, bf16[4,2,192,256]{3,2,1,0:T(8,128)(2,1)} %bitcast.1086, bf16[4,2,192,256]{3,2,1,0:T(8,128)(2,1)} %bitcast.1090, bf16[4,2,192,256]{3,2,1,0:T(8,128)(2,1)} %all-to-all-done.9.g_ref, f32[2,1,768]{2,1,0:T(1,128)} %compare_select_fusion.1.rest_0_), custom_call_target="tpu_custom_call" | custom-call | flops 6039797760 | bytes 2752512 | tf_op jit(solution)/shard_map/cond/branch_1_fun/attend_back/pallas_call | solution.py:205
  630.7 6.7 bitcast_convert_fusion.12
  664.0 16.1 %all-to-all-done.10 = bf16[4,1,192,768]{3,2,1,0:T(8,128)(2,1)} async-done(((bf16[4,1,192,768]{3,2,1,0:T(8,128)(2,1)}), bf16[4,1,192,768]{3,2,1,0:T(8,128)(2,1)}, u32[]{:S(2)}, u32[]{:S(2)}) %all-to-all-start.10) | async-done | bytes 1179680 | tf_op jit(solution)/shard_map/cond/branch_1_fun/all_to_all | solution.py:221
  694.6 74.2 %line_sum.6 = (bf16[512,1024]{1,0:T(8,128)(2,1)}, bf16[128,4096]{1,0:T(8,128)(2,1)}, bf16[432,384]{1,0:T(8,128)(2,1)}) custom-call(bf16[512,1024]{1,0:T(8,128)(2,1)} %bitcast.938, bf16[128,4096]{1,0:T(8,128)(2,1)} %bitcast.939, bf16[432,384]{1,0:T(8,128)(2,1)} %bitcast.998), custom_call_target="tpu_custom_call" | custom-call | bytes 97157120 | tf_op jit(solution)/shard_map/cond/branch_1_fun/line_sum/pallas_call | solution.py:384
  784.1 41.1 %line_sum.7 = (bf16[128,3072]{1,0:T(8,128)(2,1)S(1)}, bf16[48,1152]{1,0:T(8,128)(2,1)S(1)}, bf16[1440,128]{1,0:T(8,128)(2,1)}) custom-call(bf16[128,3072]{1,0:T(8,128)(2,1)} %broadcast_select_fusion.3.refs_0_, bf16[48,1152]{1,0:T(8,128)(2,1)} %broadcast_select_fusion.4.refs_1_, bf16[1440,128]{1,0:T(8,128)(2,1)} %slice.445.refs_2_), custom_call_target="tpu_custom_call" | custom-call | bytes 50626560 | tf_op jit(solution)/shard_map/cond/branch_1_fun/line_sum/pallas_call | solution.py:384
  (564 shorter events, 333.7 us)
Async XLA Ops:
  7.2 42.8 %all-gather.35.cloned.1.call-start = ((), (), s32[]{:S(2)}) async-start(), calls=%async_computation.38 | async-start | bytes 2359296 | tf_op jit(solution)/shard_map/all_gather | solution.py:236
  57.8 116.2 %copy-start.84 = (f32[8,1,128]{2,1,0:T(1,128)}, f32[8,1,128]{2,1,0:T(1,128)S(1)}, u32[]{:S(2)}) copy-start(f32[8,1,128]{2,1,0:T(1,128)S(1)} %get-tuple-element.374) | copy-start | bytes 12292
  57.8 152.4 %copy-start.3 = (f32[2,392,1024]{2,1,0:T(8,128)}, f32[2,392,1024]{2,1,0:T(8,128)S(1)}, u32[]{:S(2)}) copy-start(f32[2,392,1024]{2,1,0:T(8,128)S(1)} %get-tuple-element.373) | copy-start | bytes 9633796
  57.8 210.9 %copy-start.95 = (f32[8,1,128]{2,1,0:T(1,128)}, f32[8,1,128]{2,1,0:T(1,128)S(1)}, u32[]{:S(2)}) copy-start(f32[8,1,128]{2,1,0:T(1,128)S(1)} %get-tuple-element.390) | copy-start | bytes 12292
  57.8 91.1 %all-gather.25.cloned.1.call-start = ((), (), s32[]{:S(2)}) async-start(), calls=%async_computation.29 | async-start | bytes 17399808 | tf_op jit(solution)/shard_map/cond/branch_1_fun/all_gather | solution.py:236
  58.6 160.7 %all-gather.27.cloned.1.call-start = ((), (), s32[]{:S(2)}) async-start(), calls=%async_computation.30 | async-start | bytes 9437184 | tf_op jit(solution)/shard_map/cond/branch_1_fun/all_gather | solution.py:236
  62.7 20.7 %collective-permute-start.6 = (bf16[2,192,1024]{2,1,0:T(8,128)(2,1)S(1)}, bf16[2,192,1024]{2,1,0:T(8,128)(2,1)S(1)}, u32[]{:S(2)}, u32[]{:S(2)}) collective-permute-start(bf16[2,192,1024]{2,1,0:T(8,128)(2,1)S(1)} %fusion.130), channel_id=1, source_target_pairs={{0,1},{1,2},{2,3},{4,5},{5,6},{6,7},{8,9},{9,10},{10,11},{12,13},{... | collective-permute-start | bytes 2359304 | tf_op jit(solution)/shard_map/cond/branch_1_fun/ppermute | solution.py:229
  66.2 22.6 %collective-permute-start.9 = (bf16[2,192,1024]{2,1,0:T(8,128)(2,1)S(1)}, bf16[2,192,1024]{2,1,0:T(8,128)(2,1)}, u32[]{:S(2)}, u32[]{:S(2)}) collective-permute-start(bf16[2,192,1024]{2,1,0:T(8,128)(2,1)S(1)} %fusion.130), channel_id=1, source_target_pairs={{1,0},{2,1},{3,2},{5,4},{6,5},{7,6},{9,8},{10,9},{11,10},{13,12},{... | collective-permute-start | bytes 2359304 | tf_op jit(solution)/shard_map/cond/branch_1_fun/ppermute | solution.py:230
  83.4 21.0 %collective-permute-start.7 = (bf16[2,192,1024]{2,1,0:T(8,128)(2,1)S(1)}, bf16[2,192,1024]{2,1,0:T(8,128)(2,1)}, u32[]{:S(2)}, u32[]{:S(2)}) collective-permute-start(bf16[2,192,1024]{2,1,0:T(8,128)(2,1)S(1)} %collective-permute-done.6), channel_id=1, source_target_pairs={{0,1},{1,2},{2,3},{4,5},{5,6},{6,7},{8,9},{9,10},{10,11},{12,13},{... | collective-permute-start | bytes 2359304 | tf_op jit(solution)/shard_map/cond/branch_1_fun/ppermute | solution.py:229
  88.8 22.4 %collective-permute-start.10 = (bf16[2,192,1024]{2,1,0:T(8,128)(2,1)}, bf16[2,192,1024]{2,1,0:T(8,128)(2,1)}, u32[]{:S(2)}, u32[]{:S(2)}) collective-permute-start(bf16[2,192,1024]{2,1,0:T(8,128)(2,1)} %collective-permute-done.9), channel_id=1, source_target_pairs={{1,0},{2,1},{3,2},{5,4},{6,5},{7,6},{9,8},{10,9},{11,10},{13,12},{... | collective-permute-start | bytes 2359304 | tf_op jit(solution)/shard_map/cond/branch_1_fun/ppermute | solution.py:230
  104.4 20.5 %collective-permute-start.8 = (bf16[2,192,1024]{2,1,0:T(8,128)(2,1)}, bf16[2,192,1024]{2,1,0:T(8,128)(2,1)}, u32[]{:S(2)}, u32[]{:S(2)}) collective-permute-start(bf16[2,192,1024]{2,1,0:T(8,128)(2,1)} %collective-permute-done.7), channel_id=1, source_target_pairs={{0,1},{1,2},{2,3},{4,5},{5,6},{6,7},{8,9},{9,10},{10,11},{12,13},{... | collective-permute-start | bytes 2359304 | tf_op jit(solution)/shard_map/cond/branch_1_fun/ppermute | solution.py:229
  111.2 20.0 %collective-permute-start.11 = (bf16[2,192,1024]{2,1,0:T(8,128)(2,1)}, bf16[2,192,1024]{2,1,0:T(8,128)(2,1)S(1)}, u32[]{:S(2)}, u32[]{:S(2)}) collective-permute-start(bf16[2,192,1024]{2,1,0:T(8,128)(2,1)} %collective-permute-done.10), channel_id=1, source_target_pairs={{1,0},{2,1},{3,2},{5,4},{6,5},{7,6},{9,8},{10,9},{11,10},{13,12},{... | collective-permute-start | bytes 2359304 | tf_op jit(solution)/shard_map/cond/branch_1_fun/ppermute | solution.py:230
  160.2 91.0 %all-gather.33.cloned.1.call-start = ((), (), s32[]{:S(2)}) async-start(), calls=%async_computation.37 | async-start | bytes 3981312 | tf_op jit(solution)/shard_map/cond/branch_1_fun/all_gather | solution.py:674
  179.9 23.6 %copy-start.116 = (pred[2,392]{1,0:T(4,128)(4,1)S(1)}, pred[2,392]{1,0:T(4,128)(4,1)}, u32[]{:S(2)}) copy-start(pred[2,392]{1,0:T(4,128)(4,1)} %copy-done.115) | copy-start | bytes 2356
  179.9 24.6 %copy-start.134 = (f32[8,48]{1,0:T(8,128)S(1)}, f32[8,48]{1,0:T(8,128)}, u32[]{:S(2)}) copy-start(f32[8,48]{1,0:T(8,128)} %get-tuple-element.397) | copy-start | bytes 4612
  179.9 24.7 %copy-start.132 = (f32[8,48]{1,0:T(8,128)S(1)}, f32[8,48]{1,0:T(8,128)}, u32[]{:S(2)}) copy-start(f32[8,48]{1,0:T(8,128)} %get-tuple-element.402) | copy-start | bytes 4612
  179.9 24.7 %copy-start.133 = (f32[8,48]{1,0:T(8,128)S(1)}, f32[8,48]{1,0:T(8,128)}, u32[]{:S(2)}) copy-start(f32[8,48]{1,0:T(8,128)} %get-tuple-element.401) | copy-start | bytes 4612
  203.3 83.9 %all-gather.31.cloned.1.call-start = ((), (), s32[]{:S(2)}) async-start(), calls=%async_computation.32 | async-start | bytes 1505280 | tf_op jit(solution)/shard_map/cond/branch_1_fun/all_gather | solution.py:705
  219.3 32.0 %copy-start.142 = (f32[384]{0:T(512)S(1)}, f32[384]{0:T(512)}, u32[]{:S(2)}) copy-start(f32[384]{0:T(512)} %get-tuple-element.398) | copy-start | bytes 4612
  256.2 62.5 %all-gather.29.cloned.1.call-start = ((), (), s32[]{:S(2)}) async-start(), calls=%async_computation.31 | async-start | bytes 1505280 | tf_op jit(solution)/shard_map/cond/branch_1_fun/all_gather | solution.py:705
  363.1 23.4 %all-to-all-start.6 = ((bf16[4,2,392,96]{2,1,3,0:T(2,128)(2,1)}), bf16[4,2,392,96]{2,1,3,0:T(2,128)(2,1)S(1)}, u32[]{:S(2)}, u32[]{:S(2)}) async-start(bf16[4,2,392,96]{2,1,3,0:T(2,128)(2,1)} %reshape.1417), calls=%async_computation.10 | async-start | bytes 1572864 | tf_op jit(solution)/shard_map/cond/branch_1_fun/all_to_all | solution.py:221
  366.8 137.8 %reduce-scatter.17.cloned.1.call-start = ((), (), s32[]{:S(2)}) async-start(), calls=%async_computation.33 | async-start | bytes 2985984 | tf_op jit(solution)/shard_map/cond/branch_1_fun/reduce_scatter | solution.py:240
  425.6 40.1 %all-to-all-start.8 = ((bf16[4,1,392,288]{2,3,1,0:T(8,128)(2,1)}), bf16[4,1,392,288]{2,3,1,0:T(8,128)(2,1)}, u32[]{:S(2)}, u32[]{:S(2)}) async-start(bf16[4,1,392,288]{2,3,1,0:T(8,128)(2,1)} %copy.468), calls=%async_computation.12 | async-start | bytes 2359296 | tf_op jit(solution)/shard_map/cond/branch_1_fun/all_to_all | solution.py:221
  465.7 32.6 %all-to-all-start.7 = ((bf16[4,1,392,288]{2,3,1,0:T(8,128)(2,1)}), bf16[4,1,392,288]{2,3,1,0:T(8,128)(2,1)}, u32[]{:S(2)}, u32[]{:S(2)}) async-start(bf16[4,1,392,288]{2,3,1,0:T(8,128)(2,1)} %copy.460), calls=%async_computation.11 | async-start | bytes 2359296 | tf_op jit(solution)/shard_map/cond/branch_1_fun/all_to_all | solution.py:221
  470.7 209.3 %reduce-scatter.19.cloned.1.call-start = ((), (), s32[]{:S(2)}) async-start(), calls=%async_computation.34 | async-start | bytes 9437184 | tf_op jit(solution)/shard_map/cond/branch_1_fun/reduce_scatter | solution.py:240
  517.2 177.5 %reduce-scatter.23.cloned.1.call-start = ((), (), s32[]{:S(2)}) async-start(), calls=%async_computation.36 | async-start | bytes 9437184 | tf_op jit(solution)/shard_map/cond/branch_1_fun/reduce_scatter | solution.py:240
  576.3 25.0 %all-to-all-start.9 = ((bf16[4,2,192,256]{3,2,1,0:T(8,128)(2,1)}), bf16[4,2,192,256]{3,2,1,0:T(8,128)(2,1)}, u32[]{:S(2)}, u32[]{:S(2)}) async-start(bf16[4,2,192,256]{3,2,1,0:T(8,128)(2,1)} %bitcast.893), calls=%async_computation.14 | async-start | bytes 1572864 | tf_op jit(solution)/shard_map/cond/branch_1_fun/all_to_all | solution.py:221
  611.5 38.0 %all-to-all-start.11 = ((bf16[4,1,192,768]{3,2,1,0:T(8,128)(2,1)}), bf16[4,1,192,768]{3,2,1,0:T(8,128)(2,1)S(1)}, u32[]{:S(2)}, u32[]{:S(2)}) async-start(bf16[4,1,192,768]{3,2,1,0:T(8,128)(2,1)} %attend_back.15), calls=%async_computation.17 | async-start | bytes 2359296 | tf_op jit(solution)/shard_map/cond/branch_1_fun/all_to_all | solution.py:221
  649.5 30.6 %all-to-all-start.10 = ((bf16[4,1,192,768]{3,2,1,0:T(8,128)(2,1)}), bf16[4,1,192,768]{3,2,1,0:T(8,128)(2,1)}, u32[]{:S(2)}, u32[]{:S(2)}) async-start(bf16[4,1,192,768]{3,2,1,0:T(8,128)(2,1)} %attend_back.14), calls=%async_computation.15 | async-start | bytes 2359296 | tf_op jit(solution)/shard_map/cond/branch_1_fun/all_to_all | solution.py:221
  654.4 123.0 %reduce-scatter.21.cloned.1.call-start = ((), (), s32[]{:S(2)}) async-start(), calls=%async_computation.35 | async-start | bytes 5419008 | tf_op jit(solution)/shard_map/cond/branch_1_fun/reduce_scatter | solution.py:240
  663.9 21.8 %copy-start.57 = (f32[192,1024]{1,0:T(8,128)}, f32[192,1024]{1,0:T(8,128)S(1)}, u32[]{:S(2)}) copy-start(f32[192,1024]{1,0:T(8,128)S(1)} %get-tuple-element.829) | copy-start | bytes 2359300
  694.6 77.5 %copy-start.58 = (f32[192,1024]{1,0:T(8,128)S(1)}, f32[192,1024]{1,0:T(8,128)}, u32[]{:S(2)}) copy-start(f32[192,1024]{1,0:T(8,128)} %copy-done.57) | copy-start | bytes 2359300
  (112 other events, 493.8 us)
Sparse Core Ops, SparseCore 0:
  9.9 30.5 all-gather.34
  61.3 87.6 all-gather.24
  160.3 54.3 all-gather.26
  217.2 33.9 all-gather.32
  256.3 30.8 all-gather.30
  288.7 29.9 all-gather.28
  371.5 45.1 reduce-scatter.16
  517.3 70.3 reduce-scatter.18
  591.5 71.2 reduce-scatter.22
  689.0 53.6 reduce-scatter.20

commit v6 on v5

--- a/solution.py
+++ b/solution.py
@@ -221,36 +221,12 @@
     return lax.all_to_all(array, "seq", split_axis=0, concat_axis=0, tiled=True)
 
 
-def gather_slots(array, size, shard):
-    right = [(index, index + 1) for index in range(size - 1)]
-    left = [(index + 1, index) for index in range(size - 1)]
-    from_left, from_right = [array], [array]
-    for _ in range(size - 1):
-        from_left.append(lax.ppermute(from_left[-1], "seq", right))
-        from_right.append(lax.ppermute(from_right[-1], "seq", left))
-    line = jnp.stack(from_left[:0:-1] + from_right)
-    return lax.dynamic_slice_in_dim(line, size - 1 - shard, size, 0)
-
-
 def gather(array):
     return lax.all_gather(array, "fsdp", axis=0, tiled=True)
 
 
 def scatter(array):
-    return lax.psum_scatter(array, "fsdp", scatter_dimension=0, tiled=True)[0]
-
-
-def blocks_of(array, count, lanes):
-    rows = array.shape[0] // count
-    split = array.shape[1] // lanes
-    array = array.reshape(count, rows, split, lanes)
-    return array.transpose(0, 2, 1, 3).reshape(count, split * rows, lanes)
-
-
-def from_blocks(array, lanes):
-    split = lanes // array.shape[1]
-    rows = array.shape[0] // split
-    return array.reshape(split, rows, -1).transpose(1, 0, 2).reshape(rows, lanes)
+    return lax.psum_scatter(array, "fsdp", scatter_dimension=0, tiled=True)
 
 
 def pack_rows(vectors):
@@ -279,12 +255,14 @@
 MESH = pl.DeviceIdType.MESH
 
 
-def line_kernel(size, cuts, *refs):
+def line_kernel(size, cuts, shares, *refs):
     count = len(cuts)
-    ins, outs = refs[:count], refs[count : 2 * count]
-    scratch = refs[2 * count :]
+    held = count + shares
+    ins, outs = refs[:count], refs[held : held + count]
+    own, every = refs[count], refs[held + count]
+    scratch = refs[2 * held :]
     inner, outer, partial = (scratch[i * count : (i + 1) * count] for i in range(3))
-    to_inner, to_outer, from_inner, from_outer = scratch[3 * count :]
+    to_inner, to_outer, from_inner, from_outer = scratch[3 * count : 3 * count + 4]
     me = lax.axis_index("seq")
     left = me < size // 2
     toward = jnp.where(left, me + 1, me - 1)
@@ -344,6 +322,68 @@
     def _():
         for piece in pieces:
             inwards(*piece).start()
+
+    if shares:
+        sent, arrived = scratch[3 * count + 4 :]
+        every[me] = own[...]
+
+        def passes(way, hop):
+            step = 1 - 2 * way
+            block = me - step * hop
+            return pltpu.make_async_remote_copy(
+                src_ref=own if hop == 0 else every.at[block],
+                dst_ref=every.at[block],
+                send_sem=sent.at[way, hop],
+                recv_sem=arrived.at[way, hop],
+                device_id={"seq": me + step},
+                device_id_type=MESH,
+            )
+
+        def sends(way, hop):
+            if way == 0:
+                return (me < size - 1) & (me - hop >= 0)
+            return (me > 0) & (me + hop <= size - 1)
+
+        def receives(way, hop):
+            return me - 1 - hop >= 0 if way == 0 else me + 1 + hop <= size - 1
+
+        def landing(way, hop):
+            block = me - 1 - hop if way == 0 else me + 1 + hop
+            return pltpu.make_async_remote_copy(
+                src_ref=every.at[block],
+                dst_ref=every.at[block],
+                send_sem=sent.at[way, hop],
+                recv_sem=arrived.at[way, hop],
+                device_id={"seq": toward},
+                device_id_type=MESH,
+            )
+
+        for hop in range(size - 1):
+            for way in (0, 1):
+                if hop > 0:
+
+                    @pl.when(receives(way, hop - 1))
+                    def _(way=way, hop=hop):
+                        landing(way, hop - 1).wait_recv()
+
+                @pl.when(sends(way, hop))
+                def _(way=way, hop=hop):
+                    passes(way, hop).start()
+
+        for way in (0, 1):
+
+            @pl.when(receives(way, size - 2))
+            def _(way=way):
+                landing(way, size - 2).wait_recv()
+
+            for hop in range(size - 1):
+
+                @pl.when(sends(way, hop))
+                def _(way=way, hop=hop):
+                    passes(way, hop).wait_send()
+
+    @pl.when(end)
+    def _():
         for piece in pieces:
             outwards(*piece).wait_recv()
         for piece in pieces:
@@ -372,7 +412,7 @@
             outwards(*piece).wait_send()
 
 
-def line_sum(arrays, size, identity):
+def line_sum(arrays, size, identity, share=None):
     cuts = []
     for member in arrays:
         parts = 8
@@ -380,32 +420,42 @@
             parts //= 2
         cuts.append(parts)
     hold = [pltpu.VMEM(member.shape, bf16) for member in arrays]
+    shapes = [jax.ShapeDtypeStruct(member.shape, bf16) for member in arrays]
+    semaphores = [pltpu.SemaphoreType.DMA((sum(cuts),))] * 4
+    operands = list(arrays)
+    if share is not None:
+        operands.append(share)
+        shapes.append(jax.ShapeDtypeStruct((size,) + share.shape, bf16))
+        semaphores += [pltpu.SemaphoreType.DMA((2, size - 1))] * 2
     whole = pl.BlockSpec(memory_space=pltpu.VMEM)
     return pl.pallas_call(
-        functools.partial(line_kernel, size, tuple(cuts)),
-        out_shape=[jax.ShapeDtypeStruct(member.shape, bf16) for member in arrays],
-        in_specs=[whole] * len(arrays),
-        out_specs=[whole] * len(arrays),
-        scratch_shapes=hold * 3 + [pltpu.SemaphoreType.DMA((sum(cuts),))] * 4,
+        functools.partial(line_kernel, size, tuple(cuts), int(share is not None)),
+        out_shape=shapes,
+        in_specs=[whole] * len(operands),
+        out_specs=[whole] * len(operands),
+        scratch_shapes=hold * 3 + semaphores,
         compiler_params=pltpu.CompilerParams(
             collective_id=identity, has_side_effects=True, vmem_limit_bytes=VMEM_LIMIT
         ),
         cost_estimate=pl.CostEstimate(
             flops=0,
-            bytes_accessed=40 * sum(2 * member.size for member in arrays),
+            bytes_accessed=40 * sum(2 * member.size for member in operands),
             transcendentals=0,
         ),
         name="line_sum",
-    )(*arrays)
-
-
-def sum_slots(arrays, size, identity):
+    )(*operands)
+
+
+def sum_slots(arrays, size, identity, share=None):
     if size == 4:
-        return line_sum(arrays, size, identity)
-    return lax.psum(tuple(arrays), "seq")
-
-
-def feed_back(grad_out, mixed, middle, normed_mid, hidden, active, weights, mid_gain):
+        return line_sum(arrays, size, identity, share)
+    sums = lax.psum(tuple(arrays), "seq")
+    if share is None:
+        return sums
+    return (*sums, lax.all_gather(share, "seq", axis=0, tiled=False))
+
+
+def feed_back(grad_out, middle, normed_mid, hidden, active, weights, mid_gain):
     out, expand, contract = weights
     grad_y = grad_out.astype(bf16)
     grad_contract = mm(active, grad_y, TN).astype(bf16)
@@ -419,10 +469,8 @@
     grad_norm, grad_mid_gain, grad_mid_shift = norm_back(middle, mid_gain, grad_normed)
     grad_middle = grad_out + grad_norm
     grad_att = grad_middle.astype(bf16)
-    grad_out_weight = mm(mixed, grad_att, TN).astype(bf16)
     grad_out_bias = jnp.sum(grad_att.astype(f32), axis=0)
     grad_mixed = mm(grad_att, out, NT).astype(bf16)
-    grads = (grad_out_weight, grad_expand, grad_contract)
     small = dict(
         out_bias=grad_out_bias,
         mid_gain=grad_mid_gain,
@@ -430,7 +478,7 @@
         expand_bias=grad_expand_bias,
         contract_bias=grad_contract_bias,
     )
-    return grad_middle, grad_mixed, grads, small
+    return grad_middle, grad_att, grad_mixed, (grad_expand, grad_contract), small
 
 
 def own_joint(joint_weight, query_bias, value_bias, shards, shard):
@@ -465,17 +513,15 @@
     return mm(flat.reshape(clips * rows, shards * width), joint_by_sender, NT)
 
 
-def spread(vector, shards, shard):
-    full = jnp.zeros((vector.shape[0] * shards,), f32)
-    return lax.dynamic_update_slice_in_dim(full, vector, shard * vector.shape[0], 0)
-
-
-def joint_small(columns, shards, shard):
+def joint_small(columns, owners, shards, shard):
     own = columns.shape[0] // 3
-    return dict(
-        query_bias=spread(columns[:own], shards, shard),
-        value_bias=spread(columns[2 * own :], shards, shard),
-    )
+    each = owners // shards
+    mine = lax.broadcasted_iota(jnp.int32, (owners, 1), 0) // each == shard
+
+    def full(vector):
+        return jnp.where(mine, jnp.tile(vector.reshape(each, -1), (shards, 1)), 0.0)
+
+    return dict(query_bias=full(columns[:own]), value_bias=full(columns[2 * own :]))
 
 
 ORDER = (
@@ -524,8 +570,6 @@
     span = visible.shape[1]
 
     e_out = gather(e_shard["out"])
-    e_first = jnp.concatenate([e_shard["joint"], e_shard["expand"], embed_weight], axis=1)
-
     place = lax.broadcasted_iota(jnp.int32, (1, 1, span), 2)
     slot_visible = jnp.any(
         (slot_token[:, :, None] == place) & (visible[:, None, :] > 0), axis=2
@@ -550,8 +594,8 @@
         slot_token,
         positions,
         e_out,
-        e_first,
-        e_shard["contract"],
+        tuple(e_shard[name] for name in ("joint", "expand", "contract")),
+        embed_weight,
         tuple(p_shard[name] for name in ("joint", "out", "expand", "contract")),
         tuple(full[:-1]),
         cotangent,
@@ -574,8 +618,8 @@
     slot_token,
     positions,
     e_out,
-    e_first_shard,
-    e_contract_shard,
+    e_shards,
+    embed_shard,
     p_shards,
     vectors,
     cotangent,
@@ -592,13 +636,9 @@
     embed_bias, mask_token = vectors[9:11]
     p_vec = dict(zip(ORDER, vectors[11:]))
 
-    e_first = gather(e_first_shard)
-    e_joint = e_first[:, : 3 * width]
-    e_expand = e_first[:, 3 * width : -small_width]
-    embed = e_first[:, -small_width:]
-    packed = jnp.concatenate(
-        [blocks_of(member, 1, small_width)[0] for member in p_shards], axis=0
-    )
+    e_joint_shard, e_expand_shard, e_contract_shard = e_shards
+    p_joint_shard, p_out_shard, p_expand_shard, p_contract_shard = p_shards
+    e_joint = gather(e_joint_shard)
 
     own_visible = lax.dynamic_slice_in_dim(slot_visible, shard * slots, slots, 1)
     own_flat = own_visible.reshape(rows, 1)
@@ -656,8 +696,15 @@
 
     inputs = tokens.reshape(rows, width)
     normed = norm_layer(inputs, e_vec["pre_gain"], e_vec["pre_shift"])
-    normed_kept = keep(normed).reshape(clips, held, width)
-    normed_all = gather_slots(normed_kept, seq_size, shard)
+    normed_kept = keep(normed).reshape(1, clips, held, width)
+    normed_kept, e_expand_shard = lax.optimization_barrier((normed_kept, e_expand_shard))
+    e_expand = gather(e_expand_shard)
+    normed_all = exchange(jnp.broadcast_to(normed_kept, (seq_size, clips, held, width)))
+    embed, p_joint, p_out = gather(embed_shard), gather(p_joint_shard), gather(p_out_shard)
+    e_by_sender = by_sender(e_joint, seq_size)
+    normed_all, embed, p_joint, p_out, e_by_sender = lax.optimization_barrier(
+        (normed_all, embed, p_joint, p_out, e_by_sender)
+    )
     queries = (mm(normed, e_joint[:, :width]) + e_vec["query_bias"]).astype(bf16)
     joined = mm(normed_all.reshape(-1, width), e_joint[:, width:])
     joined_bias = jnp.concatenate([jnp.zeros_like(e_vec["value_bias"]), e_vec["value_bias"]])
@@ -670,22 +717,10 @@
         head_size,
         bias,
     ).reshape(rows, width)
-    mixed, packed = lax.optimization_barrier((mixed, packed))
-    packed = lax.all_gather(packed, "fsdp", axis=0, tiled=False)
     middle = inputs + mm(mixed, e_out) + e_vec["out_bias"]
     normed_mid = norm_layer(middle, e_vec["mid_gain"], e_vec["mid_shift"])
     active = gelu(mm(normed_mid, e_expand) + e_vec["expand_bias"])
     encoded = middle + mm(active, e_contract) + e_vec["contract_bias"]
-    encoded, packed = lax.optimization_barrier((encoded, packed))
-    unpacked = []
-    at = 0
-    for member in p_shards:
-        split = member.shape[1] // small_width
-        count = member.shape[0] * split
-        piece = packed[:, at : at + count].reshape(fsdp_size, split, member.shape[0], small_width)
-        unpacked.append(piece.transpose(0, 2, 1, 3).reshape(-1, member.shape[1]))
-        at += count
-    p_joint, p_out, p_expand, p_contract = unpacked
     context = encoded.astype(bf16)
 
     embedded = mm(context, embed) + embed_bias
@@ -700,9 +735,16 @@
     p_bias = jnp.concatenate([jnp.zeros_like(p_vec["value_bias"]), p_vec["value_bias"]])
     p_normed_all = []
     p_mixed = []
+    everyone = [
+        lax.all_gather(p_normed.reshape(clips, slots, small_width)[clip], "seq", axis=0, tiled=True)
+        for clip in range(clips)
+    ]
+    p_expand_shard, p_contract_shard, everyone[0] = lax.optimization_barrier(
+        (p_expand_shard, p_contract_shard, everyone[0])
+    )
+    p_expand, p_contract = gather(p_expand_shard), gather(p_contract_shard)
     for clip in range(clips):
-        own = p_normed.reshape(clips, slots, small_width)[clip]
-        every = lax.all_gather(own, "seq", axis=0, tiled=True)
+        every = everyone[clip]
         p_joined = (mm(every, p_joint[:, small_width:]) + p_bias).astype(bf16)
         p_normed_all.append(every)
         p_mixed.append(
@@ -713,6 +755,12 @@
                 None,
             )
         )
+    kept_mid, kept_mixed, kept_middle, kept_inputs = (
+        keep(member) for member in (normed_mid, mixed, middle, inputs)
+    )
+    p_mixed[0], kept_mid, kept_mixed, kept_middle, kept_inputs = lax.optimization_barrier(
+        (p_mixed[0], kept_mid, kept_mixed, kept_middle, kept_inputs)
+    )
     p_mixed = jnp.concatenate(p_mixed, axis=0).reshape(rows, small_width)
     p_middle = pred_input + mm(p_mixed, p_out) + p_vec["out_bias"]
     p_normed_mid = norm_layer(p_middle, p_vec["mid_gain"], p_vec["mid_shift"])
@@ -720,9 +768,8 @@
     p_active = gelu(p_hidden)
     predicted = p_middle + mm(p_active, p_contract) + p_vec["contract_bias"]
 
-    grad_middle, grad_mixed, p_grads, p_small = feed_back(
+    grad_middle, grad_att, grad_mixed, p_grads, p_small = feed_back(
         cotangent.reshape(rows, small_width),
-        p_mixed,
         p_middle,
         p_normed_mid,
         p_hidden,
@@ -730,11 +777,11 @@
         (p_out, p_expand, p_contract),
         p_vec["mid_gain"],
     )
-    p_pack = jnp.concatenate(
-        [blocks_of(member, fsdp_size, small_width) for member in p_grads], axis=1
-    )
-    grad_mixed, p_pack = lax.optimization_barrier((grad_mixed, p_pack))
-    p_part = scatter(p_pack)
+    p_grad_out = mm(p_mixed, grad_att, TN).astype(bf16)
+    p_wide = jnp.concatenate([p_grad_out, p_grads[0]], axis=1)
+    p_tall = p_grads[1]
+    grad_mixed, p_wide, p_tall = lax.optimization_barrier((grad_mixed, p_wide, p_tall))
+    p_wide, p_tall = scatter(p_wide), scatter(p_tall)
     own_weight, own_bias = own_joint(
         p_joint, p_vec["query_bias"], p_vec["value_bias"], seq_size, shard
     )
@@ -759,105 +806,87 @@
         p_grad_joint = p_grad_joint + mm(p_normed_all[clip], flat, TN)
         p_columns = p_columns + jnp.sum(flat.astype(f32), axis=0)
         grad_normed.append(joint_back(exchange(grads), p_by_sender))
-    p_small.update(joint_small(p_columns, seq_size, shard))
+    p_small.update(joint_small(p_columns, fsdp_size, seq_size, shard))
+    p_own_width = own_width
     grad_norm, p_small["pre_gain"], p_small["pre_shift"] = norm_back(
         pred_input, p_vec["pre_gain"], jnp.concatenate(grad_normed, axis=0)
     )
     grad_pred_input = grad_middle + grad_norm
     grad_mask_token = jnp.sum(jnp.where(own_flat, 0.0, grad_pred_input), axis=0)
     grad_embedded = jnp.where(own_flat, grad_pred_input, 0.0).astype(bf16)
-    grad_embed = mm(context, grad_embedded, TN).astype(bf16)
     grad_embed_bias = jnp.sum(grad_embedded.astype(f32), axis=0)
 
-    p_own_width = own_width
-    p_grad_joint = jnp.pad(p_grad_joint.astype(bf16), ((0, 0), (0, small_width - 3 * own_width)))
-
-    grad_embedded, p_part = lax.optimization_barrier((grad_embedded, p_part))
+    grad_embedded, p_wide, p_tall = lax.optimization_barrier((grad_embedded, p_wide, p_tall))
     grad_context = mm(keep(grad_embedded), embed, NT)
-    kept_mid = keep(normed_mid)
     kept_hidden = mm(kept_mid, e_expand) + e_vec["expand_bias"]
-    grad_middle, grad_mixed, e_grads, e_small = feed_back(
+    grad_middle, grad_att, grad_mixed, e_grads, e_small = feed_back(
         grad_context,
-        keep(mixed),
-        keep(middle),
+        kept_middle,
         kept_mid,
         kept_hidden,
         gelu(kept_hidden),
         (e_out, e_expand, e_contract),
         e_vec["mid_gain"],
     )
-    expand_part = scatter(e_grads[1].reshape(fsdp_size, -1, e_grads[1].shape[1]))
-    contract_part = scatter(e_grads[2].reshape(fsdp_size, -1, e_grads[2].shape[1]))
+    expand_part, contract_part = scatter(e_grads[0]), scatter(e_grads[1])
     own_width = width // seq_size
     grad_mixed = grad_mixed.reshape(clips * held, seq_size, own_width).transpose(1, 0, 2)
     grad_mixed = by_clip(exchange(grad_mixed.reshape(seq_size, clips, held, own_width)))
     grads = [
         attend_back(*own_qkv, grad_mixed, clip, head_size, bias, seq_size) for clip in range(clips)
     ]
+    grads[-1], grad_att, late_embedded = lax.optimization_barrier(
+        (grads[-1], grad_att, grad_embedded)
+    )
     received = [exchange(member) for member in grads]
     received[0], contract_part = lax.optimization_barrier((received[0], contract_part))
     flat = jnp.concatenate(grads, axis=1).reshape(-1, 3 * own_width)
     e_grad_joint = mm(normed_all.reshape(-1, width), flat, TN).astype(bf16)
-    e_small.update(joint_small(jnp.sum(flat.astype(f32), axis=0), seq_size, shard))
-    e_by_sender = by_sender(e_joint, seq_size)
+    e_grad_out = mm(kept_mixed, grad_att, TN).astype(bf16)
+    grad_embed = mm(context, late_embedded, TN).astype(bf16)
+    e_small.update(joint_small(jnp.sum(flat.astype(f32), axis=0), fsdp_size, seq_size, shard))
     grad_normed = jnp.concatenate([joint_back(member, e_by_sender) for member in received], axis=0)
     grad_norm, e_small["pre_gain"], e_small["pre_shift"] = norm_back(
-        keep(inputs), e_vec["pre_gain"], grad_normed
-    )
-    grad_tokens = put_back(grad_middle + grad_norm)
-
-    first = 0 if whole else 2
-    contract_sum, expand_sum, p_sum = sum_slots(
-        (contract_part, expand_part, p_part), seq_size, first
-    )
-
+        kept_inputs, e_vec["pre_gain"], grad_normed
+    )
+
+    own_rows = width // fsdp_size
+    p_rows = small_width // fsdp_size
+    p_lanes = -(-3 * p_own_width // 128) * 128
+    p_grad_joint = p_grad_joint.astype(bf16).reshape(fsdp_size, p_rows, 3 * p_own_width)
+    p_grad_joint = jnp.pad(
+        p_grad_joint, ((0, 0), (0, own_rows - p_rows), (0, p_lanes - 3 * p_own_width))
+    ).reshape(width, p_lanes)
     small = [e_small[name] for name in ORDER] + [grad_embed_bias, grad_mask_token]
     small += [p_small[name] for name in ORDER]
     small = [member.reshape(fsdp_size, -1) for member in small]
     sizes = [member.shape[1] for member in small]
-    count = -(-sum(sizes) // (16 * 128)) * 16
-    small.append(jnp.zeros((fsdp_size, count * 128 - sum(sizes)), f32))
-    small = jnp.concatenate(small, axis=1).astype(bf16).reshape(fsdp_size, count, 128)
-    members = (e_grad_joint, p_grad_joint, e_grads[0], grad_embed)
-    late = scatter(
-        jnp.concatenate(
-            [blocks_of(member, fsdp_size, 128) for member in members] + [small], axis=1
-        )
-    )
-
+    small.append(jnp.zeros((fsdp_size, own_rows * 128 - sum(sizes)), f32))
+    small = jnp.concatenate(small, axis=1).astype(bf16).reshape(width, 128)
+    late = scatter(jnp.concatenate([e_grad_joint, p_grad_joint, e_grad_out, grad_embed, small], axis=1))
+    grad_tokens = put_back(grad_middle + grad_norm)
+
+    first = 0 if whole else 2
+    contract_sum, expand_sum, p_wide_sum, p_contract_sum = sum_slots(
+        (contract_part, expand_part, p_wide, p_tall), seq_size, first
+    )
     late, expand_sum = lax.optimization_barrier((late, expand_sum))
-
-    def cut(array, at, rows, lanes, block):
-        split = lanes // block
-        return from_blocks(array[at : at + split * rows], lanes), at + split * rows
-
-    def all_columns(columns, own):
-        columns = columns[:, : 3 * own].reshape(-1, 3, 1, own)
-        which = lax.broadcasted_iota(jnp.int32, (1, 1, seq_size, 1), 2)
-        placed = jnp.where(which == shard, columns, jnp.zeros_like(columns))
-        return placed.reshape(-1, 3 * own * seq_size)
-
-    own_rows = width // fsdp_size
-    p_rows = small_width // fsdp_size
-    e_columns, at = cut(late, 0, own_rows, 3 * own_width, 128)
-    p_columns, at = cut(late, at, p_rows, small_width, 128)
-    e_joint_out, p_joint_out, late_sum = sum_slots(
-        (all_columns(e_columns, own_width), all_columns(p_columns, p_own_width), late[at:]),
-        seq_size,
-        first + 1,
-    )
-    out_sum, at = cut(late_sum, 0, own_rows, width, 128)
-    embed_sum, at = cut(late_sum, at, own_rows, small_width, 128)
-    vector_sum = late_sum[at:].reshape(-1)
+    shared = 3 * own_width + p_lanes
+    late_sum, columns = sum_slots((late[:, shared:],), seq_size, first + 1, late[:, :shared])
+    e_joint_sum = columns[:, :, : 3 * own_width].reshape(seq_size, own_rows, 3, own_width)
+    e_joint_sum = e_joint_sum.transpose(1, 2, 0, 3).reshape(own_rows, 3 * width)
+    p_joint_sum = columns[:, :p_rows, 3 * own_width : 3 * (own_width + p_own_width)]
+    p_joint_sum = p_joint_sum.reshape(seq_size, p_rows, 3, p_own_width)
+    p_joint_sum = p_joint_sum.transpose(1, 2, 0, 3).reshape(p_rows, 3 * small_width)
+    out_sum = late_sum[:, :width]
+    embed_sum = late_sum[:, width : width + small_width]
+    vector_sum = late_sum[:, width + small_width :].reshape(-1)
     small_out = []
     at = 0
     for size in sizes:
         small_out.append(vector_sum[at : at + size].astype(f32))
         at += size
-    p_wide = p_shards[2].shape[1]
-    p_out_sum, at = cut(p_sum, 0, p_rows, small_width, small_width)
-    p_expand_sum, at = cut(p_sum, at, p_rows, p_wide, small_width)
-    p_contract_sum, at = cut(p_sum, at, p_shards[3].shape[0], small_width, small_width)
+    p_out_sum, p_expand_sum = p_wide_sum[:, :small_width], p_wide_sum[:, small_width:]
 
     def ordered(vec, joint, out, expand, contract):
         vec = dict(
@@ -873,11 +902,11 @@
         encoded.reshape(tokens.shape),
         predicted.reshape(cotangent.shape),
         grad_tokens.reshape(tokens.shape),
-        *ordered(small_out[:9], e_joint_out, out_sum, expand_sum, contract_sum),
+        *ordered(small_out[:9], e_joint_sum, out_sum, expand_sum, contract_sum),
         embed_sum.astype(f32),
         small_out[9],
         small_out[10],
-        *ordered(small_out[11:], p_joint_out, p_out_sum, p_expand_sum, p_contract_sum),
+        *ordered(small_out[11:], p_joint_sum, p_out_sum, p_expand_sum, p_contract_sum),
     )
 
 

time: 855 us -> 854 us (level)
  local copies, waits for them, and re-layouts: 146 us -> 79.6 us
  blocking collectives: 10.7 us -> 49.9 us
  waiting for transfers between devices: 118 us -> 139 us
  matrix products: 183 us -> 198 us
  starting transfers between devices: 47.4 us -> 33.1 us
    all_to_all x6 -> x7, waiting for transfers between devices: 29.9 us -> 82.8 us  [exchange(): return lax.all_to_all(array, 'seq', split_axis=0, concat_axis=0, tiled=True)]
    ppermute x6 -> x0, waiting for transfers between devices: 44.1 us -> none  [the longest x3 42.7 us: gather_slots(): from_left.append(lax.ppermute(from_left[-1], 'seq', right))]
    all_gather x0 -> x3, blocking collectives: none -> 39.3 us  [gather(): return lax.all_gather(array, 'fsdp', axis=0, tiled=True)]
    unnamed x267 -> x222, local copies, waits for them, and re-layouts: 35.9 us -> 12.1 us
    ppermute x6 -> x0, starting transfers between devices: 18.1 us -> none  [the longest x3 14.2 us: gather_slots(): from_left.append(lax.ppermute(from_left[-1], 'seq', right))]
    reshape x12 -> x1, local copies, waits for them, and re-layouts: 16.8 us -> 0.76 us  [main(): vector_sum = late_sum[:, width + small_width:].reshape(-1)]
    all_gather x3 -> x6, waiting for transfers between devices: 15.7 us -> 29.2 us  [gather(): return lax.all_gather(array, 'fsdp', axis=0, tiled=True)]
    dynamic_update_slice x4 -> x0, local copies, waits for them, and re-layouts: 12.7 us -> none  [spread(): lax.dynamic_update_slice_in_dim(full, vector, shard * vector.shape[0], 0)]
  transfers between devices with their start and end apart: 22 -> 20, of which waited for: 11 -> 12; matrix products, arithmetic and copies ran while one was open for 37% -> 30% of each run, Pallas kernels for 23% -> 25%
where the time goes in v6:
time: 854 us; the launch traced here: 844 us
  Pallas kernels  255 us (30%)
  matrix products  198 us (23%)
  waiting for transfers between devices  139 us (16%)
  local copies, waits for them, and re-layouts  79.6 us (9%)
  other arithmetic  65.4 us (8%)
  blocking collectives  49.9 us (6%)
  starting transfers between devices  33.1 us (4%)
  between operations  15.6 us (2%)
    dot_general x43, matrix products, mm(): return lax.dot_general(left, right, dims, preferred_element_type=f32)  181 us
    pallas_call x2, Pallas kernels, line_sum(): pl.pallas_call(functools.partial(line_kernel, size, tuple(cuts), int(shar...  118 us
    all_to_all x7, waiting for transfers between devices, exchange(): return lax.all_to_all(array, 'seq', split_axis=0, concat_axis=0, tiled=True)  82.8 us
    pallas_call x4, Pallas kernels, attend_back(): pl.pallas_call(functools.partial(backward_kernel, 1.0 / math.sqrt(head_si...  82.5 us
    pallas_call x3, Pallas kernels, attend(): pl.pallas_call(functools.partial(forward_kernel, 1.0 / math.sqrt(head_siz...  54.7 us
    all_gather x3, blocking collectives, gather(): return lax.all_gather(array, 'fsdp', axis=0, tiled=True)  39.3 us
    all_to_all x7, starting transfers between devices, exchange(): return lax.all_to_all(array, 'seq', split_axis=0, concat_axis=0, tiled=True)  31.6 us
    all_gather x6, waiting for transfers between devices, gather(): return lax.all_gather(array, 'fsdp', axis=0, tiled=True)  29.2 us
  transfers between devices with their start and end apart: 20, of which 12 were waited for; matrix products, arithmetic and copies ran while one was open for 30% of the time, Pallas kernels for 25%

profile of v6, /device:TPU:0, one launch (start us, length us, event | category | flops | bytes accessed | tf_op | source)
XLA Modules:
  0.0 844.4 jit_solution(11388978233279324561)
XLA Ops:
  22.3 10.7 %all-gather = f32[256,128]{1,0:T(8,128)S(1)} all-gather(f32[32,128]{1,0:T(8,128)S(1)} %concatenate.59), channel_id=2, replica_groups=mesh['fsdp'=8,'seq'=4] {'fsdp'}, dimensions={0}, use_global_device_ids=true | all-gather | bytes 147456 | tf_op jit(solution)/shard_map/all_gather | solution.py:584
  40.6 789.1 %conditional.4 = (f32[2,392,1024]{2,1,0:T(8,128)}, f32[2,392,384]{2,1,0:T(8,128)}, f32[2,392,1024]{2,1,0:T(8,128)}, bf16[128,4096]{1,0:T(8,128)(2,1)}, bf16[512,...) conditional(s32[]{:T(128)} %convert_element_type.821, ...), branch_computations={%region_4.52_spmd, %region_51.99_spmd} | conditional | flops 216429101056 | bytes 1308190592
  63.6 9.8 %all_gather.59 = bf16[384,384]{1,0:T(8,128)(2,1)S(1)} all-gather(bf16[48,384]{1,0:T(8,128)(2,1)S(1)} %copy-done.104), channel_id=1, replica_groups=mesh['fsdp'=8,'seq'=4] {'fsdp'}, dimensions={0}, use_global_device_ids=true | all-gather | bytes 331776 | tf_op jit(solution)/shard_map/cond/branch_1_fun/all_gather | solution.py:225
  73.4 15.5 %all_gather.57 = bf16[1024,384]{1,0:T(8,128)(2,1)} all-gather(bf16[128,384]{1,0:T(8,128)(2,1)} %get-tuple-element.410), channel_id=1, replica_groups=mesh['fsdp'=8,'seq'=4] {'fsdp'}, dimensions={0}, use_global_device_ids=true | all-gather | bytes 884736 | tf_op jit(solution)/shard_map/cond/branch_1_fun/all_gather | solution.py:225
  89.0 13.9 %all_gather.58 = bf16[384,1152]{1,0:T(8,128)(2,1)} all-gather(bf16[48,1152]{1,0:T(8,128)(2,1)} %get-tuple-element.411), channel_id=1, replica_groups=mesh['fsdp'=8,'seq'=4] {'fsdp'}, dimensions={0}, use_global_device_ids=true | all-gather | bytes 995328 | tf_op jit(solution)/shard_map/cond/branch_1_fun/all_gather | solution.py:225
  109.1 25.3 %all-to-all-done.7 = bf16[4,2,192,1024]{3,2,1,0:T(8,128)(2,1)} async-done(((bf16[4,2,192,1024]{3,2,1,0:T(8,128)(2,1)}), bf16[4,2,192,1024]{3,2,1,0:T(8,128)(2,1)}, u32[]{:S(2)}, u32[]{:S(2)}) %all-to-all-start.7) | async-done | bytes 3145760 | tf_op jit(solution)/shard_map/cond/branch_1_fun/all_to_all | solution.py:221
  134.4 11.3 %add_convert_fusion.18 = bf16[1536,2048]{1,0:T(8,128)(2,1)} fusion(bf16[1536,1024]{1,0:T(8,128)(2,1)} %bitcast.114, f32[2048]{0:T(1024)S(1)} %copy-done.151, bf16[1024,3072]{0,1:T(8,128)(2,1)} %all-gather.31.cloned.1.call-done), kind=kOutput, calls=%fused_computation.230 | convolution fusion | flops 6448742400 | bytes 13639680 | tf_op jit(solution)/shard_map/cond/branch_1_fun/dot_general | solution.py:25
  161.9 23.3 %attend.9 = bf16[2,392,1024]{2,1,0:T(8,128)(2,1)} custom-call(bf16[2,392,1024]{2,1,0:T(8,128)(2,1)} %bitcast.786, bf16[4,2,192,2048]{3,2,1,0:T(8,128)(2,1)} %bitcast.780, bf16[4,2,192,2048]{3,2,1,0:T(8,128)(2,1)} %bitcast.781, f32[2,1,768]{2,1,0:T(1,128)} %compare_select_fusion.1.rest_0_), custom_call_target="tpu_custom_call" | custom-call | flops 9865003008 | bytes 6291456 | tf_op jit(solution)/shard_map/cond/branch_1_fun/attend/pallas_call | solution.py:105
  196.1 20.3 %all-gather.35.cloned.1.call-done = bf16[4096,1024]{1,0:T(8,128)(2,1)} async-done(((bf16[512,1024]{1,0:T(8,128)(2,1)}), bf16[4096,1024]{1,0:T(8,128)(2,1)}) %all-gather.35.cloned.1.call-update) | async-done | bytes 8388624 | tf_op jit(solution)/shard_map/cond/branch_1_fun/all_gather | solution.py:225
  216.4 23.0 %add_add_fusion.2 = f32[784,1024]{1,0:T(8,128)} fusion(f32[784,1024]{1,0:T(8,128)} %fusion.108, bf16[4096,1024]{1,0:T(8,128)(2,1)} %all-gather.35.cloned.1.call-done, f32[4096]{0:T(1024)S(1)} %bitcast.754, bf16[1024,4096]{1,0:T(8,128)(2,1)} %all-gather.33.cloned.1.call-done, f32[1024]{0:T(1024)} %bitcast.777, f32[1024]{0:T(1024)S(1)} %bitcast.728, ...), kind=kOutput, calls=%fused_computation.264 | convolution fusion | flops 13178224640 | bytes 23234688 | tf_op jit(solution)/shard_map/cond/branch_1_fun/dot_general | solution.py:25
  269.3 8.3 all-gather.37.cloned.1.call-done
  300.8 8.2 all-gather.39.cloned.1.call-done
  313.2 15.7 %attend.11 = bf16[1,392,384]{2,1,0:T(8,128)(2,1)} custom-call(bf16[1,392,384]{2,1,0:T(8,128)(2,1)} %get-tuple-element.1143.q_ref, bf16[1,1,1568,768]{3,2,1,0:T(8,128)(2,1)} %fusion.93.k_ref.v_ref, bf16[1,1,1568,768]{3,2,1,0:T(8,128)(2,1)} %fusion.93.k_ref.v_ref), custom_call_target="tpu_custom_call" | custom-call | flops 7552892928 | bytes 2408448 | tf_op jit(solution)/shard_map/cond/branch_1_fun/attend/pallas_call | solution.py:105
  328.9 15.7 %attend.10 = bf16[1,392,384]{2,1,0:T(8,128)(2,1)} custom-call(bf16[1,392,384]{2,1,0:T(8,128)(2,1)} %get-tuple-element.1142.q_ref, bf16[1,1,1568,768]{3,2,1,0:T(8,128)(2,1)} %fusion.92.k_ref.v_ref, bf16[1,1,1568,768]{3,2,1,0:T(8,128)(2,1)} %fusion.92.k_ref.v_ref), custom_call_target="tpu_custom_call" | custom-call | flops 7552892928 | bytes 2408448 | tf_op jit(solution)/shard_map/cond/branch_1_fun/attend/pallas_call | solution.py:105
  396.3 6.8 all-to-all-done.8
  409.1 31.2 %attend_back.12 = bf16[4,1,392,288]{3,2,1,0:T(8,128)(2,1)} custom-call(bf16[1,1,1568,96]{3,2,1,0:T(8,128)(2,1)} %fusion.103.q_ref, bf16[1,1,1568,96]{3,2,1,0:T(8,128)(2,1)} %fusion.104.k_ref, bf16[1,1,1568,96]{3,2,1,0:T(8,128)(2,1)} %fusion.102.v_ref, bf16[1,1,1568,96]{3,2,1,0:T(8,128)(2,1)} %bitcast.700), custom_call_target="tpu_custom_call" | custom-call | flops 18882232320 | bytes 2107392 | tf_op jit(solution)/shard_map/cond/branch_1_fun/attend_back/pallas_call | solution.py:205
  449.1 31.3 %attend_back.13 = bf16[4,1,392,288]{3,2,1,0:T(8,128)(2,1)} custom-call(bf16[1,1,1568,96]{3,2,1,0:T(8,128)(2,1)} %fusion.101.q_ref, bf16[1,1,1568,96]{3,2,1,0:T(8,128)(2,1)} %fusion.105.k_ref, bf16[1,1,1568,96]{3,2,1,0:T(8,128)(2,1)} %fusion.100.v_ref, bf16[1,1,1568,96]{3,2,1,0:T(8,128)(2,1)} %bitcast.701), custom_call_target="tpu_custom_call" | custom-call | flops 18882232320 | bytes 2107392 | tf_op jit(solution)/shard_map/cond/branch_1_fun/attend_back/pallas_call | solution.py:205
  489.4 9.9 %convolution_add_fusion.11 = f32[384,4096]{1,0:T(8,128)} fusion(bf16[384,1024]{1,0:T(8,128)(2,1)} %bitcast.794, bf16[1024,4096]{1,0:T(8,128)(2,1)} %all-gather.33.cloned.1.call-done, f32[4096]{0:T(1024)S(1)} %bitcast.755), kind=kOutput, calls=%fused_computation.245 | convolution fusion | flops 3222798336 | bytes 15482880 | tf_op jit(solution)/shard_map/cond/branch_1_fun/dot_general | solution.py:25
  501.3 14.4 %all-to-all-done.10 = bf16[4,1,392,288]{2,3,1,0:T(8,128)(2,1)} async-done(((bf16[4,1,392,288]{2,3,1,0:T(8,128)(2,1)}), bf16[4,1,392,288]{2,3,1,0:T(8,128)(2,1)}, u32[]{:S(2)}, u32[]{:S(2)}) %all-to-all-start.10) | async-done | bytes 903200 | tf_op jit(solution)/shard_map/cond/branch_1_fun/all_to_all | solution.py:221
  521.7 9.2 %reduce-scatter.21.cloned.1.call-done.refs_2_ = bf16[48,1920]{1,0:T(8,128)(2,1)} async-done(((bf16[384,1920]{1,0:T(8,128)(2,1)}), bf16[48,1920]{1,0:T(8,128)(2,1)}) %reduce-scatter.21.cloned.1.call-update) | async-done | bytes 184336 | tf_op jit(solution)/shard_map/cond/branch_1_fun/reduce_scatter | solution.py:229
  533.9 8.8 %convolution_convert_fusion.12 = bf16[4096,1024]{1,0:T(8,128)(2,1)} fusion(bf16[384,1024]{1,0:T(8,128)(2,1)S(1)} %get-tuple-element.462, f32[384,4096]{1,0:T(8,128)} %convolution_add_fusion.11), kind=kOutput, calls=%fused_computation.233 | convolution fusion | flops 3233284096 | bytes 15466496 | tf_op jit(solution)/shard_map/cond/branch_1_fun/dot_general | solution.py:25
  543.8 8.5 %fusion.202 = (bf16[4096]{0:T(1024)(128)(2,1)S(1)}, bf16[384,4096]{1,0:T(8,128)(2,1)S(1)}) fusion(f32[384,4096]{1,0:T(8,128)} %convolution_add_fusion.11, bf16[384,1024]{1,0:T(8,128)(2,1)S(1)} %copy-done.79, bf16[4096,1024]{1,0:T(8,128)(2,1)} %all-gather.35.cloned.1.call-done), kind=kOutput, calls=%fused_computation.540 | convolution fusion | flops 3238522880 | bytes 18620416 | tf_op jit(solution)/shard_map/cond/branch_1_fun/dot_general | solution.py:25
  554.1 6.9 convolution_convert_fusion.11
  561.0 8.9 %fusion.212 = f32[384,1024]{1,0:T(8,128)} fusion(bf16[384,4096]{1,0:T(8,128)(2,1)} %copy-done.177, bf16[1024,4096]{1,0:T(8,128)(2,1)} %all-gather.33.cloned.1.call-done), kind=kOutput, calls=%fused_computation.550 | convolution fusion | flops 3221225472 | bytes 13107200 | tf_op jit(solution)/shard_map/cond/branch_1_fun/dot_general | solution.py:25
  591.4 12.4 %all-to-all-done.11.g_ref = bf16[4,2,192,256]{3,2,1,0:T(8,128)(2,1)} async-done(((bf16[4,2,192,256]{3,2,1,0:T(8,128)(2,1)}), bf16[4,2,192,256]{3,2,1,0:T(8,128)(2,1)}, u32[]{:S(2)}, u32[]{:S(2)}) %all-to-all-start.11) | async-done | bytes 786464 | tf_op jit(solution)/shard_map/cond/branch_1_fun/all_to_all | solution.py:221
  603.8 10.0 %attend_back.15 = bf16[4,1,192,768]{3,2,1,0:T(8,128)(2,1)} custom-call(bf16[4,2,192,256]{3,2,1,0:T(8,128)(2,1)} %bitcast.790, bf16[4,2,192,256]{3,2,1,0:T(8,128)(2,1)} %bitcast.788, bf16[4,2,192,256]{3,2,1,0:T(8,128)(2,1)} %bitcast.792, bf16[4,2,192,256]{3,2,1,0:T(8,128)(2,1)} %all-to-all-done.11.g_ref, f32[2,1,768]{2,1,0:T(1,128)} %compare_select_fusion.1.rest_0_), custom_call_target="tpu_custom_call" | custom-call | flops 6039797760 | bytes 2752512 | tf_op jit(solution)/shard_map/cond/branch_1_fun/attend_back/pallas_call | solution.py:205
  617.8 10.0 %attend_back.14 = bf16[4,1,192,768]{3,2,1,0:T(8,128)(2,1)} custom-call(bf16[4,2,192,256]{3,2,1,0:T(8,128)(2,1)} %bitcast.791, bf16[4,2,192,256]{3,2,1,0:T(8,128)(2,1)} %bitcast.789, bf16[4,2,192,256]{3,2,1,0:T(8,128)(2,1)} %bitcast.793, bf16[4,2,192,256]{3,2,1,0:T(8,128)(2,1)} %all-to-all-done.11.g_ref, f32[2,1,768]{2,1,0:T(1,128)} %compare_select_fusion.1.rest_0_), custom_call_target="tpu_custom_call" | custom-call | flops 6039797760 | bytes 2752512 | tf_op jit(solution)/shard_map/cond/branch_1_fun/attend_back/pallas_call | solution.py:205
  627.8 7.5 fusion.109
  635.3 10.0 %all-to-all-done.13 = bf16[4,1,192,768]{3,2,1,0:T(8,128)(2,1)S(1)} async-done(((bf16[4,1,192,768]{3,2,1,0:T(8,128)(2,1)}), bf16[4,1,192,768]{3,2,1,0:T(8,128)(2,1)S(1)}, u32[]{:S(2)}, u32[]{:S(2)}) %all-to-all-start.13) | async-done | bytes 1179680 | tf_op jit(solution)/shard_map/cond/branch_1_fun/all_to_all | solution.py:221
  663.7 14.0 %all-to-all-done.12 = bf16[4,1,192,768]{3,2,1,0:T(8,128)(2,1)} async-done(((bf16[4,1,192,768]{3,2,1,0:T(8,128)(2,1)}), bf16[4,1,192,768]{3,2,1,0:T(8,128)(2,1)}, u32[]{:S(2)}, u32[]{:S(2)}) %all-to-all-start.12) | async-done | bytes 1179680 | tf_op jit(solution)/shard_map/cond/branch_1_fun/all_to_all | solution.py:221
  691.3 71.7 %line_sum.6 = (bf16[512,1024]{1,0:T(8,128)(2,1)}, bf16[128,4096]{1,0:T(8,128)(2,1)}, bf16[48,1920]{1,0:T(8,128)(2,1)}, bf16[192,384]{1,0:T(8,128)(2,1)}) custom-call(bf16[512,1024]{1,0:T(8,128)(2,1)} %reduce-scatter.25.cloned.1.call-done.refs_0_, bf16[128,4096]{1,0:T(8,128)(2,1)} %reduce-scatter.29.cloned.1.call-done.refs_1_, ...), custom_call_target="tpu_custom_call" | custom-call | bytes 97157120 | tf_op jit(solution)/shard_map/cond/branch_1_fun/line_sum/pallas_call | solution.py:431
  773.1 46.0 %line_sum.7 = (bf16[128,1536]{1,0:T(8,128)(2,1)}, bf16[4,128,1152]{2,1,0:T(8,128)(2,1)}) custom-call(bf16[128,1536]{1,0:T(8,128)(2,1)} %slice.439.refs_0_, bf16[128,1152]{1,0:T(8,128)(2,1)} %slice.440.refs_1_), custom_call_target="tpu_custom_call" | custom-call | bytes 27525120 | tf_op jit(solution)/shard_map/cond/branch_1_fun/line_sum/pallas_call | solution.py:431
  (480 shorter events, 301.9 us)
Async XLA Ops:
  7.2 33.4 %all-gather.45.cloned.1.call-start = ((), (), s32[]{:S(2)}) async-start(), calls=%async_computation.48 | async-start | bytes 2359296 | tf_op jit(solution)/shard_map/all_gather | solution.py:225
  47.3 55.6 %all-gather.31.cloned.1.call-start = ((), (), s32[]{:S(2)}) async-start(), calls=%async_computation.36 | async-start | bytes 7077888 | tf_op jit(solution)/shard_map/cond/branch_1_fun/all_gather | solution.py:225
  49.6 146.4 %all-gather.33.cloned.1.call-start = ((), (), s32[]{:S(2)}) async-start(), calls=%async_computation.37 | async-start | bytes 9437184 | tf_op jit(solution)/shard_map/cond/branch_1_fun/all_gather | solution.py:225
  58.1 76.2 %all-to-all-start.7 = ((bf16[4,2,192,1024]{3,2,1,0:T(8,128)(2,1)}), bf16[4,2,192,1024]{3,2,1,0:T(8,128)(2,1)}, u32[]{:S(2)}, u32[]{:S(2)}) async-start(bf16[4,2,192,1024]{3,2,1,0:T(8,128)(2,1)} %broadcast_in_dim.212), calls=%async_computation.12 | async-start | bytes 6291456 | tf_op jit(solution)/shard_map/cond/branch_1_fun/all_to_all | solution.py:221
  63.0 153.4 %all-gather.35.cloned.1.call-start = ((), (), s32[]{:S(2)}) async-start(), calls=%async_computation.38 | async-start | bytes 9437184 | tf_op jit(solution)/shard_map/cond/branch_1_fun/all_gather | solution.py:225
  102.9 31.5 %copy-start.151 = (f32[2048]{0:T(1024)S(1)}, f32[2048]{0:T(1024)}, u32[]{:S(2)}) copy-start(f32[2048]{0:T(1024)} %concatenate.49) | copy-start | bytes 24580
  145.8 131.8 %all-gather.37.cloned.1.call-start = ((), (), s32[]{:S(2)}) async-start(), calls=%async_computation.39 | async-start | bytes 1505280 | tf_op jit(solution)/shard_map/cond/branch_1_fun/all_gather | solution.py:739
  161.9 23.3 %copy-start.159 = (f32[8,1,128]{2,1,0:T(1,128)S(1)}, f32[8,1,128]{2,1,0:T(1,128)}, u32[]{:S(2)}) copy-start(f32[8,1,128]{2,1,0:T(1,128)} %get-tuple-element.419) | copy-start | bytes 12292
  193.6 22.8 %copy-start.95 = (f32[8,1,128]{2,1,0:T(1,128)S(1)}, f32[8,1,128]{2,1,0:T(1,128)}, u32[]{:S(2)}) copy-start(f32[8,1,128]{2,1,0:T(1,128)} %copy-done.94) | copy-start | bytes 12292
  193.6 22.8 %copy-start.113 = (f32[8,1,128]{2,1,0:T(1,128)S(1)}, f32[8,1,128]{2,1,0:T(1,128)}, u32[]{:S(2)}) copy-start(f32[8,1,128]{2,1,0:T(1,128)} %copy-done.112) | copy-start | bytes 12292
  193.6 22.8 %copy-start.137 = (f32[8,4,128]{2,1,0:T(4,128)S(1)}, f32[8,4,128]{2,1,0:T(4,128)}, u32[]{:S(2)}) copy-start(f32[8,4,128]{2,1,0:T(4,128)} %copy-done.136) | copy-start | bytes 49156
  196.0 43.4 %copy-start.134 = (f32[784]{0:T(1024)}, f32[784]{0:T(1024)S(1)}, u32[]{:S(2)}) copy-start(f32[784]{0:T(1024)S(1)} %add_rsqrt_fusion.8) | copy-start | bytes 9412
  216.4 23.0 %copy-start.132 = (f32[384]{0:T(512)S(1)}, f32[384]{0:T(512)}, u32[]{:S(2)}) copy-start(f32[384]{0:T(512)} %copy-done.131) | copy-start | bytes 4612
  216.4 23.0 %copy-start.141 = (pred[784]{0:T(1024)(128)(4,1)S(1)}, pred[784]{0:T(1024)(128)(4,1)}, u32[]{:S(2)}) copy-start(pred[784]{0:T(1024)(128)(4,1)} %broadcast_in_dim.215) | copy-start | bytes 2356
  246.6 62.5 %all-gather.39.cloned.1.call-start = ((), (), s32[]{:S(2)}) async-start(), calls=%async_computation.40 | async-start | bytes 1505280 | tf_op jit(solution)/shard_map/cond/branch_1_fun/all_gather | solution.py:739
  247.1 99.6 %all-gather.41.cloned.1.call-start = ((), (), s32[]{:S(2)}) async-start(), calls=%async_computation.41 | async-start | bytes 1327104 | tf_op jit(solution)/shard_map/cond/branch_1_fun/all_gather | solution.py:225
  277.6 82.9 %all-gather.43.cloned.1.call-start = ((), (), s32[]{:S(2)}) async-start(), calls=%async_computation.42 | async-start | bytes 1327104 | tf_op jit(solution)/shard_map/cond/branch_1_fun/all_gather | solution.py:225
  346.4 19.3 %copy-start.22 = (f32[784,384]{1,0:T(8,128)}, f32[784,384]{1,0:T(8,128)S(1)}, u32[]{:S(2)}) copy-start(f32[784,384]{1,0:T(8,128)S(1)} %get-tuple-element.1173) | copy-start | bytes 3612676
  377.8 25.3 %all-to-all-start.8 = ((bf16[4,2,392,96]{2,1,3,0:T(2,128)(2,1)}), bf16[4,2,392,96]{2,1,3,0:T(2,128)(2,1)S(1)}, u32[]{:S(2)}, u32[]{:S(2)}) async-start(bf16[4,2,392,96]{2,1,3,0:T(2,128)(2,1)} %reshape.1305), calls=%async_computation.13 | async-start | bytes 1572864 | tf_op jit(solution)/shard_map/cond/branch_1_fun/all_to_all | solution.py:221
  382.5 139.2 %reduce-scatter.23.cloned.1.call-start = ((), (), s32[]{:S(2)}) async-start(), calls=%async_computation.44 | async-start | bytes 1327104 | tf_op jit(solution)/shard_map/cond/branch_1_fun/reduce_scatter | solution.py:229
  442.9 40.0 %all-to-all-start.9 = ((bf16[4,1,392,288]{2,3,1,0:T(8,128)(2,1)}), bf16[4,1,392,288]{2,3,1,0:T(8,128)(2,1)}, u32[]{:S(2)}, u32[]{:S(2)}) async-start(bf16[4,1,392,288]{2,3,1,0:T(8,128)(2,1)} %copy.351), calls=%async_computation.14 | async-start | bytes 2359296 | tf_op jit(solution)/shard_map/cond/branch_1_fun/all_to_all | solution.py:221
  482.8 32.9 %all-to-all-start.10 = ((bf16[4,1,392,288]{2,3,1,0:T(8,128)(2,1)}), bf16[4,1,392,288]{2,3,1,0:T(8,128)(2,1)}, u32[]{:S(2)}, u32[]{:S(2)}) async-start(bf16[4,1,392,288]{2,3,1,0:T(8,128)(2,1)} %copy.359), calls=%async_computation.15 | async-start | bytes 2359296 | tf_op jit(solution)/shard_map/cond/branch_1_fun/all_to_all | solution.py:221
  488.0 42.8 %reduce-scatter.21.cloned.1.call-start = ((), (), s32[]{:S(2)}) async-start(), calls=%async_computation.43 | async-start | bytes 1658880 | tf_op jit(solution)/shard_map/cond/branch_1_fun/reduce_scatter | solution.py:229
  489.1 188.6 %reduce-scatter.25.cloned.1.call-start = ((), (), s32[]{:S(2)}) async-start(), calls=%async_computation.45 | async-start | bytes 9437184 | tf_op jit(solution)/shard_map/cond/branch_1_fun/reduce_scatter | solution.py:229
  521.7 21.0 %copy-start.68 = (bf16[784,384]{1,0:T(8,128)(2,1)}, bf16[784,384]{1,0:T(8,128)(2,1)S(1)}, u32[]{:S(2)}) copy-start(bf16[784,384]{1,0:T(8,128)(2,1)S(1)} %get-tuple-element.474) | copy-start | bytes 1806340
  542.7 148.6 %reduce-scatter.29.cloned.1.call-start = ((), (), s32[]{:S(2)}) async-start(), calls=%async_computation.47 | async-start | bytes 9437184 | tf_op jit(solution)/shard_map/cond/branch_1_fun/reduce_scatter | solution.py:229
  579.0 24.8 %all-to-all-start.11 = ((bf16[4,2,192,256]{3,2,1,0:T(8,128)(2,1)}), bf16[4,2,192,256]{3,2,1,0:T(8,128)(2,1)}, u32[]{:S(2)}, u32[]{:S(2)}) async-start(bf16[4,2,192,256]{3,2,1,0:T(8,128)(2,1)} %bitcast.657), calls=%async_computation.18 | async-start | bytes 1572864 | tf_op jit(solution)/shard_map/cond/branch_1_fun/all_to_all | solution.py:221
  613.8 31.6 %all-to-all-start.13 = ((bf16[4,1,192,768]{3,2,1,0:T(8,128)(2,1)}), bf16[4,1,192,768]{3,2,1,0:T(8,128)(2,1)S(1)}, u32[]{:S(2)}, u32[]{:S(2)}) async-start(bf16[4,1,192,768]{3,2,1,0:T(8,128)(2,1)} %attend_back.15), calls=%async_computation.21 | async-start | bytes 2359296 | tf_op jit(solution)/shard_map/cond/branch_1_fun/all_to_all | solution.py:221
  645.4 32.4 %all-to-all-start.12 = ((bf16[4,1,192,768]{3,2,1,0:T(8,128)(2,1)}), bf16[4,1,192,768]{3,2,1,0:T(8,128)(2,1)}, u32[]{:S(2)}, u32[]{:S(2)}) async-start(bf16[4,1,192,768]{3,2,1,0:T(8,128)(2,1)} %attend_back.14), calls=%async_computation.19 | async-start | bytes 2359296 | tf_op jit(solution)/shard_map/cond/branch_1_fun/all_to_all | solution.py:221
  649.6 120.0 %reduce-scatter.27.cloned.1.call-start = ((), (), s32[]{:S(2)}) async-start(), calls=%async_computation.46 | async-start | bytes 6193152 | tf_op jit(solution)/shard_map/cond/branch_1_fun/reduce_scatter | solution.py:229
  663.7 19.8 %copy-start.60 = (f32[192,1024]{1,0:T(8,128)}, f32[192,1024]{1,0:T(8,128)S(1)}, u32[]{:S(2)}) copy-start(f32[192,1024]{1,0:T(8,128)S(1)} %get-tuple-element.1180) | copy-start | bytes 2359300
  691.3 73.1 %copy-start.48 = (f32[384,1024]{1,0:T(8,128)S(1)}, f32[384,1024]{1,0:T(8,128)}, u32[]{:S(2)}) copy-start(f32[384,1024]{1,0:T(8,128)} %get-tuple-element.1080) | copy-start | bytes 4718596
  (97 other events, 516.8 us)
Sparse Core Ops, SparseCore 0:
  9.9 30.5 all-gather.44
  50.7 51.9 all-gather.30
  104.8 55.1 all-gather.32
  161.9 54.3 all-gather.34
  246.7 30.8 all-gather.36
  279.1 29.9 all-gather.38
  311.1 23.1 all-gather.40
  336.4 24.0 all-gather.42
  396.4 37.2 reduce-scatter.22
  492.5 38.2 reduce-scatter.20
  542.8 71.2 reduce-scatter.24
  617.4 71.2 reduce-scatter.28
  692.6 57.8 reduce-scatter.26

commit v7 on v6

--- a/solution.py
+++ b/solution.py
@@ -358,29 +358,21 @@
                 device_id_type=MESH,
             )
 
-        for hop in range(size - 1):
+        def forward(hop):
             for way in (0, 1):
                 if hop > 0:
 
                     @pl.when(receives(way, hop - 1))
-                    def _(way=way, hop=hop):
+                    def _(way=way):
                         landing(way, hop - 1).wait_recv()
 
-                @pl.when(sends(way, hop))
-                def _(way=way, hop=hop):
-                    passes(way, hop).start()
-
-        for way in (0, 1):
-
-            @pl.when(receives(way, size - 2))
-            def _(way=way):
-                landing(way, size - 2).wait_recv()
-
-            for hop in range(size - 1):
-
-                @pl.when(sends(way, hop))
-                def _(way=way, hop=hop):
-                    passes(way, hop).wait_send()
+                if hop < size - 1:
+
+                    @pl.when(sends(way, hop))
+                    def _(way=way):
+                        passes(way, hop).start()
+
+        forward(0)
 
     @pl.when(end)
     def _():
@@ -392,7 +384,10 @@
     @pl.when(jnp.logical_not(end))
     def _():
         lag = min(count, len(pieces))
-        for step in range(len(pieces) + lag):
+        steps = len(pieces) + lag
+        for step in range(steps):
+            if shares and step in (steps // 3, 2 * steps // 3):
+                forward(1 if step == steps // 3 else 2)
             if step < len(pieces):
                 piece = pieces[step]
                 inwards(*piece).wait_recv()
@@ -410,6 +405,25 @@
         for piece in pieces:
             swap(*piece).wait_send()
             outwards(*piece).wait_send()
+
+    if shares:
+
+        @pl.when(end)
+        def _():
+            for hop in range(1, size):
+                forward(hop)
+
+        @pl.when(jnp.logical_not(end))
+        def _():
+            for hop in range(3, size):
+                forward(hop)
+
+        for way in (0, 1):
+            for hop in range(size - 1):
+
+                @pl.when(sends(way, hop))
+                def _(way=way, hop=hop):
+                    passes(way, hop).wait_send()
 
 
 def line_sum(arrays, size, identity, share=None):
@@ -726,12 +740,14 @@
     embedded = mm(context, embed) + embed_bias
     pred_input = jnp.where(own_flat, embedded, mask_token) + slot_code
     p_normed = norm_layer(pred_input, p_vec["pre_gain"], p_vec["pre_shift"])
+    p_normed, rows_all, mid_rows, mixed_rows, middle_rows = lax.optimization_barrier(
+        (p_normed, normed_all, normed_mid, mixed, middle)
+    )
     p_queries = (mm(p_normed, p_joint[:, :small_width]) + p_vec["query_bias"]).astype(bf16)
     own_weight, own_bias = own_joint(
         e_joint, e_vec["query_bias"], e_vec["value_bias"], seq_size, shard
     )
-    own_qkv = [by_clip(member) for member in own_parts(normed_all, own_weight, own_bias)]
-    p_queries, *own_qkv = lax.optimization_barrier((p_queries, *own_qkv))
+    own_qkv = [by_clip(member) for member in own_parts(rows_all, own_weight, own_bias)]
     p_bias = jnp.concatenate([jnp.zeros_like(p_vec["value_bias"]), p_vec["value_bias"]])
     p_normed_all = []
     p_mixed = []
@@ -756,10 +772,12 @@
             )
         )
     kept_mid, kept_mixed, kept_middle, kept_inputs = (
-        keep(member) for member in (normed_mid, mixed, middle, inputs)
-    )
-    p_mixed[0], kept_mid, kept_mixed, kept_middle, kept_inputs = lax.optimization_barrier(
-        (p_mixed[0], kept_mid, kept_mixed, kept_middle, kept_inputs)
+        keep(member) for member in (mid_rows, mixed_rows, middle_rows, inputs)
+    )
+    p_mixed[0], kept_mid, kept_mixed, kept_middle, kept_inputs, *own_qkv = (
+        lax.optimization_barrier(
+            (p_mixed[0], kept_mid, kept_mixed, kept_middle, kept_inputs, *own_qkv)
+        )
     )
     p_mixed = jnp.concatenate(p_mixed, axis=0).reshape(rows, small_width)
     p_middle = pred_input + mm(p_mixed, p_out) + p_vec["out_bias"]
@@ -802,6 +820,8 @@
             None,
             seq_size,
         )
+        if clip == 0:
+            grads, p_wide, p_tall = lax.optimization_barrier((grads, p_wide, p_tall))
         flat = grads.reshape(span, 3 * own_width)
         p_grad_joint = p_grad_joint + mm(p_normed_all[clip], flat, TN)
         p_columns = p_columns + jnp.sum(flat.astype(f32), axis=0)
@@ -816,7 +836,7 @@
     grad_embedded = jnp.where(own_flat, grad_pred_input, 0.0).astype(bf16)
     grad_embed_bias = jnp.sum(grad_embedded.astype(f32), axis=0)
 
-    grad_embedded, p_wide, p_tall = lax.optimization_barrier((grad_embedded, p_wide, p_tall))
+    grad_embedded, predicted = lax.optimization_barrier((grad_embedded, predicted))
     grad_context = mm(keep(grad_embedded), embed, NT)
     kept_hidden = mm(kept_mid, e_expand) + e_vec["expand_bias"]
     grad_middle, grad_att, grad_mixed, e_grads, e_small = feed_back(

time: 854 us -> 837 us (0.980)
  starting transfers between devices: 33.1 us -> 44.3 us
  waiting for transfers between devices: 139 us -> 128 us
    all_gather x2, starting transfers between devices: 0.26 us -> 11.5 us  [main(): lax.all_gather(p_normed.reshape(clips, slots, small_width)[clip], 'seq',...]
  transfers between devices with their start and end apart: 20 -> 20, of which waited for: 12 -> 11; matrix products, arithmetic and copies ran while one was open for 30% -> 30% of each run, Pallas kernels for 25% -> 26%
where the time goes in v7:
time: 837 us; the launch traced here: 827 us
  Pallas kernels  249 us (30%)
  matrix products  190 us (23%)
  waiting for transfers between devices  128 us (15%)
  local copies, waits for them, and re-layouts  77.5 us (9%)
  other arithmetic  65.1 us (8%)
  blocking collectives  49.9 us (6%)
  starting transfers between devices  44.3 us (5%)
  between operations  15.4 us (2%)
    dot_general x43, matrix products, mm(): return lax.dot_general(left, right, dims, preferred_element_type=f32)  175 us
    pallas_call x2, Pallas kernels, line_sum(): pl.pallas_call(functools.partial(line_kernel, size, tuple(cuts), int(shar...  111 us
    pallas_call x4, Pallas kernels, attend_back(): pl.pallas_call(functools.partial(backward_kernel, 1.0 / math.sqrt(head_si...  82.6 us
    all_to_all x7, waiting for transfers between devices, exchange(): return lax.all_to_all(array, 'seq', split_axis=0, concat_axis=0, tiled=True)  80.9 us
    pallas_call x3, Pallas kernels, attend(): pl.pallas_call(functools.partial(forward_kernel, 1.0 / math.sqrt(head_siz...  54.7 us
    all_gather x3, blocking collectives, gather(): return lax.all_gather(array, 'fsdp', axis=0, tiled=True)  39.3 us
    all_to_all x7, starting transfers between devices, exchange(): return lax.all_to_all(array, 'seq', split_axis=0, concat_axis=0, tiled=True)  31.2 us
    all_gather x6, waiting for transfers between devices, gather(): return lax.all_gather(array, 'fsdp', axis=0, tiled=True)  25.1 us
  transfers between devices with their start and end apart: 20, of which 11 were waited for; matrix products, arithmetic and copies ran while one was open for 30% of the time, Pallas kernels for 26%

profile of v7, /device:TPU:0, one launch (start us, length us, event | category | flops | bytes accessed | tf_op | source)
XLA Modules:
  0.0 827.1 jit_solution(912608686031395670)
XLA Ops:
  22.3 10.7 %all-gather = f32[256,128]{1,0:T(8,128)S(1)} all-gather(f32[32,128]{1,0:T(8,128)S(1)} %concatenate.59), channel_id=2, replica_groups=mesh['fsdp'=8,'seq'=4] {'fsdp'}, dimensions={0}, use_global_device_ids=true | all-gather | bytes 147456 | tf_op jit(solution)/shard_map/all_gather | solution.py:598
  40.6 771.9 %conditional.4 = (f32[2,392,1024]{2,1,0:T(8,128)}, f32[2,392,384]{2,1,0:T(8,128)}, f32[2,392,1024]{2,1,0:T(8,128)}, bf16[128,4096]{1,0:T(8,128)(2,1)}, bf16[512,...) conditional(s32[]{:T(128)} %convert_element_type.821, ...), branch_computations={%region_4.52_spmd, %region_51.99_spmd} | conditional | flops 216429101056 | bytes 1302437504
  63.5 9.8 %all_gather.59 = bf16[384,384]{1,0:T(8,128)(2,1)S(1)} all-gather(bf16[48,384]{1,0:T(8,128)(2,1)S(1)} %copy-done.101), channel_id=1, replica_groups=mesh['fsdp'=8,'seq'=4] {'fsdp'}, dimensions={0}, use_global_device_ids=true | all-gather | bytes 331776 | tf_op jit(solution)/shard_map/cond/branch_1_fun/all_gather | solution.py:225
  73.3 15.5 %all_gather.57 = bf16[1024,384]{1,0:T(8,128)(2,1)} all-gather(bf16[128,384]{1,0:T(8,128)(2,1)} %get-tuple-element.416), channel_id=1, replica_groups=mesh['fsdp'=8,'seq'=4] {'fsdp'}, dimensions={0}, use_global_device_ids=true | all-gather | bytes 884736 | tf_op jit(solution)/shard_map/cond/branch_1_fun/all_gather | solution.py:225
  88.8 13.9 %all_gather.58 = bf16[384,1152]{1,0:T(8,128)(2,1)} all-gather(bf16[48,1152]{1,0:T(8,128)(2,1)} %get-tuple-element.417), channel_id=1, replica_groups=mesh['fsdp'=8,'seq'=4] {'fsdp'}, dimensions={0}, use_global_device_ids=true | all-gather | bytes 995328 | tf_op jit(solution)/shard_map/cond/branch_1_fun/all_gather | solution.py:225
  108.9 25.3 %all-to-all-done.7 = bf16[4,2,192,1024]{3,2,1,0:T(8,128)(2,1)} async-done(((bf16[4,2,192,1024]{3,2,1,0:T(8,128)(2,1)}), bf16[4,2,192,1024]{3,2,1,0:T(8,128)(2,1)}, u32[]{:S(2)}, u32[]{:S(2)}) %all-to-all-start.7) | async-done | bytes 3145760 | tf_op jit(solution)/shard_map/cond/branch_1_fun/all_to_all | solution.py:221
  134.3 11.3 %add_convert_fusion.18 = bf16[1536,2048]{1,0:T(8,128)(2,1)} fusion(bf16[1536,1024]{1,0:T(8,128)(2,1)} %bitcast.115, f32[2048]{0:T(1024)S(1)} %copy-done.145, bf16[1024,3072]{0,1:T(8,128)(2,1)} %all-gather.31.cloned.1.call-done), kind=kOutput, calls=%fused_computation.230 | convolution fusion | flops 6448742400 | bytes 13639680 | tf_op jit(solution)/shard_map/cond/branch_1_fun/dot_general | solution.py:25
  145.6 11.4 %all-gather.37.cloned.1.call-start = ((), (), s32[]{:S(2)}) async-start(), calls=%async_computation.39 | async-start | bytes 1505280 | tf_op jit(solution)/shard_map/cond/branch_1_fun/all_gather | solution.py:755
  173.3 23.3 %attend.9 = bf16[2,392,1024]{2,1,0:T(8,128)(2,1)} custom-call(bf16[2,392,1024]{2,1,0:T(8,128)(2,1)} %bitcast.787, bf16[4,2,192,2048]{3,2,1,0:T(8,128)(2,1)} %bitcast.781, bf16[4,2,192,2048]{3,2,1,0:T(8,128)(2,1)} %bitcast.782, f32[2,1,768]{2,1,0:T(1,128)} %compare_select_fusion.1.rest_0_), custom_call_target="tpu_custom_call" | custom-call | flops 9865003008 | bytes 6291456 | tf_op jit(solution)/shard_map/cond/branch_1_fun/attend/pallas_call | solution.py:105
  209.0 7.2 all-gather.35.cloned.1.call-done
  216.2 22.9 %add_add_fusion.2 = f32[784,1024]{1,0:T(8,128)} fusion(f32[784,1024]{1,0:T(8,128)} %fusion.108, bf16[4096,1024]{1,0:T(8,128)(2,1)} %all-gather.35.cloned.1.call-done, f32[4096]{0:T(1024)S(1)} %bitcast.755, bf16[1024,4096]{1,0:T(8,128)(2,1)} %all-gather.33.cloned.1.call-done, f32[1024]{0:T(1024)} %bitcast.778, f32[1024]{0:T(1024)S(1)} %bitcast.730, ...), kind=kOutput, calls=%fused_computation.264 | convolution fusion | flops 13178224640 | bytes 23234688 | tf_op jit(solution)/shard_map/cond/branch_1_fun/dot_general | solution.py:25
  259.1 18.0 %all-gather.37.cloned.1.call-done = bf16[1568,384]{1,0:T(8,128)(2,1)} async-done(((bf16[392,384]{1,0:T(8,128)(2,1)}), bf16[1568,384]{1,0:T(8,128)(2,1)}) %all-gather.37.cloned.1.call-update) | async-done | bytes 1204240 | tf_op jit(solution)/shard_map/cond/branch_1_fun/all_gather | solution.py:755
  299.1 15.7 %attend.10 = bf16[1,392,384]{2,1,0:T(8,128)(2,1)} custom-call(bf16[1,392,384]{2,1,0:T(8,128)(2,1)} %get-tuple-element.1150.q_ref, bf16[1,1,1568,768]{3,2,1,0:T(8,128)(2,1)} %fusion.92.k_ref.v_ref, bf16[1,1,1568,768]{3,2,1,0:T(8,128)(2,1)} %fusion.92.k_ref.v_ref), custom_call_target="tpu_custom_call" | custom-call | flops 7552892928 | bytes 2408448 | tf_op jit(solution)/shard_map/cond/branch_1_fun/attend/pallas_call | solution.py:105
  318.9 15.7 %attend.11 = bf16[1,392,384]{2,1,0:T(8,128)(2,1)} custom-call(bf16[1,392,384]{2,1,0:T(8,128)(2,1)} %get-tuple-element.1151.q_ref, bf16[1,1,1568,768]{3,2,1,0:T(8,128)(2,1)} %fusion.93.k_ref.v_ref, bf16[1,1,1568,768]{3,2,1,0:T(8,128)(2,1)} %fusion.93.k_ref.v_ref), custom_call_target="tpu_custom_call" | custom-call | flops 7552892928 | bytes 2408448 | tf_op jit(solution)/shard_map/cond/branch_1_fun/attend/pallas_call | solution.py:105
  346.4 13.6 %all-gather.43.cloned.1.call-done = bf16[1536,384]{1,0:T(8,128)(2,1)} async-done(((bf16[192,384]{1,0:T(8,128)(2,1)}), bf16[1536,384]{1,0:T(8,128)(2,1)}) %all-gather.43.cloned.1.call-update) | async-done | bytes 1179664 | tf_op jit(solution)/shard_map/cond/branch_1_fun/all_gather | solution.py:225
  403.7 6.5 all-to-all-done.8
  415.9 31.3 %attend_back.13 = bf16[4,1,392,288]{3,2,1,0:T(8,128)(2,1)} custom-call(bf16[1,1,1568,96]{3,2,1,0:T(8,128)(2,1)} %fusion.101.q_ref, bf16[1,1,1568,96]{3,2,1,0:T(8,128)(2,1)} %fusion.105.k_ref, bf16[1,1,1568,96]{3,2,1,0:T(8,128)(2,1)} %fusion.100.v_ref, bf16[1,1,1568,96]{3,2,1,0:T(8,128)(2,1)} %bitcast.702), custom_call_target="tpu_custom_call" | custom-call | flops 18882232320 | bytes 2107392 | tf_op jit(solution)/shard_map/cond/branch_1_fun/attend_back/pallas_call | solution.py:205
  455.8 31.3 %attend_back.12 = bf16[4,1,392,288]{3,2,1,0:T(8,128)(2,1)} custom-call(bf16[1,1,1568,96]{3,2,1,0:T(8,128)(2,1)} %fusion.103.q_ref, bf16[1,1,1568,96]{3,2,1,0:T(8,128)(2,1)} %fusion.104.k_ref, bf16[1,1,1568,96]{3,2,1,0:T(8,128)(2,1)} %fusion.102.v_ref, bf16[1,1,1568,96]{3,2,1,0:T(8,128)(2,1)} %bitcast.700), custom_call_target="tpu_custom_call" | custom-call | flops 18882232320 | bytes 2107392 | tf_op jit(solution)/shard_map/cond/branch_1_fun/attend_back/pallas_call | solution.py:205
  495.0 8.9 %convolution_add_fusion.11 = f32[384,4096]{1,0:T(8,128)} fusion(bf16[384,1024]{1,0:T(8,128)(2,1)S(1)} %bitcast.795, bf16[1024,4096]{1,0:T(8,128)(2,1)} %all-gather.33.cloned.1.call-done, f32[4096]{0:T(1024)S(1)} %bitcast.756), kind=kOutput, calls=%fused_computation.245 | convolution fusion | flops 3222798336 | bytes 15482880 | tf_op jit(solution)/shard_map/cond/branch_1_fun/dot_general | solution.py:25
  508.3 14.1 %all-to-all-done.9 = bf16[4,1,392,288]{2,3,1,0:T(8,128)(2,1)} async-done(((bf16[4,1,392,288]{2,3,1,0:T(8,128)(2,1)}), bf16[4,1,392,288]{2,3,1,0:T(8,128)(2,1)}, u32[]{:S(2)}, u32[]{:S(2)}) %all-to-all-start.9) | async-done | bytes 903200 | tf_op jit(solution)/shard_map/cond/branch_1_fun/all_to_all | solution.py:221
  529.4 6.9 convolution_convert_fusion.12
  536.8 8.8 %fusion.202 = (bf16[4096]{0:T(1024)(128)(2,1)S(1)}, bf16[384,4096]{1,0:T(8,128)(2,1)S(1)}) fusion(f32[384,4096]{1,0:T(8,128)} %convolution_add_fusion.11, bf16[384,1024]{1,0:T(8,128)(2,1)S(1)} %get-tuple-element.474, bf16[4096,1024]{1,0:T(8,128)(2,1)} %all-gather.35.cloned.1.call-done), kind=kOutput, calls=%fused_computation.540 | convolution fusion | flops 3238522880 | bytes 18620416 | tf_op jit(solution)/shard_map/cond/branch_1_fun/dot_general | solution.py:25
  547.4 6.7 convolution_convert_fusion.11
  554.1 8.9 %fusion.212 = f32[384,1024]{1,0:T(8,128)} fusion(bf16[384,4096]{1,0:T(8,128)(2,1)} %copy-done.178, bf16[1024,4096]{1,0:T(8,128)(2,1)} %all-gather.33.cloned.1.call-done), kind=kOutput, calls=%fused_computation.550 | convolution fusion | flops 3221225472 | bytes 13107200 | tf_op jit(solution)/shard_map/cond/branch_1_fun/dot_general | solution.py:25
  585.2 11.2 %all-to-all-done.11.g_ref = bf16[4,2,192,256]{3,2,1,0:T(8,128)(2,1)} async-done(((bf16[4,2,192,256]{3,2,1,0:T(8,128)(2,1)}), bf16[4,2,192,256]{3,2,1,0:T(8,128)(2,1)}, u32[]{:S(2)}, u32[]{:S(2)}) %all-to-all-start.11) | async-done | bytes 786464 | tf_op jit(solution)/shard_map/cond/branch_1_fun/all_to_all | solution.py:221
  596.4 10.0 %attend_back.15 = bf16[4,1,192,768]{3,2,1,0:T(8,128)(2,1)} custom-call(bf16[4,2,192,256]{3,2,1,0:T(8,128)(2,1)} %bitcast.791, bf16[4,2,192,256]{3,2,1,0:T(8,128)(2,1)} %bitcast.789, bf16[4,2,192,256]{3,2,1,0:T(8,128)(2,1)} %bitcast.793, bf16[4,2,192,256]{3,2,1,0:T(8,128)(2,1)} %all-to-all-done.11.g_ref, f32[2,1,768]{2,1,0:T(1,128)} %compare_select_fusion.1.rest_0_), custom_call_target="tpu_custom_call" | custom-call | flops 6039797760 | bytes 2752512 | tf_op jit(solution)/shard_map/cond/branch_1_fun/attend_back/pallas_call | solution.py:205
  610.4 10.0 %attend_back.14 = bf16[4,1,192,768]{3,2,1,0:T(8,128)(2,1)} custom-call(bf16[4,2,192,256]{3,2,1,0:T(8,128)(2,1)} %bitcast.792, bf16[4,2,192,256]{3,2,1,0:T(8,128)(2,1)} %bitcast.790, bf16[4,2,192,256]{3,2,1,0:T(8,128)(2,1)} %bitcast.794, bf16[4,2,192,256]{3,2,1,0:T(8,128)(2,1)} %all-to-all-done.11.g_ref, f32[2,1,768]{2,1,0:T(1,128)} %compare_select_fusion.1.rest_0_), custom_call_target="tpu_custom_call" | custom-call | flops 6039797760 | bytes 2752512 | tf_op jit(solution)/shard_map/cond/branch_1_fun/attend_back/pallas_call | solution.py:205
  620.4 7.5 fusion.109
  627.9 10.0 %all-to-all-done.13 = bf16[4,1,192,768]{3,2,1,0:T(8,128)(2,1)S(1)} async-done(((bf16[4,1,192,768]{3,2,1,0:T(8,128)(2,1)}), bf16[4,1,192,768]{3,2,1,0:T(8,128)(2,1)S(1)}, u32[]{:S(2)}, u32[]{:S(2)}) %all-to-all-start.13) | async-done | bytes 1179680 | tf_op jit(solution)/shard_map/cond/branch_1_fun/all_to_all | solution.py:221
  656.4 13.9 %all-to-all-done.12 = bf16[4,1,192,768]{3,2,1,0:T(8,128)(2,1)} async-done(((bf16[4,1,192,768]{3,2,1,0:T(8,128)(2,1)}), bf16[4,1,192,768]{3,2,1,0:T(8,128)(2,1)}, u32[]{:S(2)}, u32[]{:S(2)}) %all-to-all-start.12) | async-done | bytes 1179680 | tf_op jit(solution)/shard_map/cond/branch_1_fun/all_to_all | solution.py:221
  680.5 74.4 %line_sum.6 = (bf16[512,1024]{1,0:T(8,128)(2,1)}, bf16[128,4096]{1,0:T(8,128)(2,1)}, bf16[48,1920]{1,0:T(8,128)(2,1)}, bf16[192,384]{1,0:T(8,128)(2,1)}) custom-call(bf16[512,1024]{1,0:T(8,128)(2,1)} %reduce-scatter.25.cloned.1.call-done.refs_0_, bf16[128,4096]{1,0:T(8,128)(2,1)} %reduce-scatter.29.cloned.1.call-done.refs_1_, ...), custom_call_target="tpu_custom_call" | custom-call | bytes 97157120 | tf_op jit(solution)/shard_map/cond/branch_1_fun/line_sum/pallas_call | solution.py:445
  765.1 36.9 %line_sum.7 = (bf16[128,1536]{1,0:T(8,128)(2,1)}, bf16[4,128,1152]{2,1,0:T(8,128)(2,1)}) custom-call(bf16[128,1536]{1,0:T(8,128)(2,1)} %slice.439.refs_0_, bf16[128,1152]{1,0:T(8,128)(2,1)} %slice.440.refs_1_), custom_call_target="tpu_custom_call" | custom-call | bytes 27525120 | tf_op jit(solution)/shard_map/cond/branch_1_fun/line_sum/pallas_call | solution.py:445
  (479 shorter events, 291.8 us)
Async XLA Ops:
  7.2 33.4 %all-gather.45.cloned.1.call-start = ((), (), s32[]{:S(2)}) async-start(), calls=%async_computation.48 | async-start | bytes 2359296 | tf_op jit(solution)/shard_map/all_gather | solution.py:225
  47.1 55.6 %all-gather.31.cloned.1.call-start = ((), (), s32[]{:S(2)}) async-start(), calls=%async_computation.36 | async-start | bytes 7077888 | tf_op jit(solution)/shard_map/cond/branch_1_fun/all_gather | solution.py:225
  49.5 159.5 %all-gather.33.cloned.1.call-start = ((), (), s32[]{:S(2)}) async-start(), calls=%async_computation.37 | async-start | bytes 9437184 | tf_op jit(solution)/shard_map/cond/branch_1_fun/all_gather | solution.py:225
  58.0 76.2 %all-to-all-start.7 = ((bf16[4,2,192,1024]{3,2,1,0:T(8,128)(2,1)}), bf16[4,2,192,1024]{3,2,1,0:T(8,128)(2,1)}, u32[]{:S(2)}, u32[]{:S(2)}) async-start(bf16[4,2,192,1024]{3,2,1,0:T(8,128)(2,1)} %broadcast_in_dim.212), calls=%async_computation.12 | async-start | bytes 6291456 | tf_op jit(solution)/shard_map/cond/branch_1_fun/all_to_all | solution.py:221
  62.8 153.4 %all-gather.35.cloned.1.call-start = ((), (), s32[]{:S(2)}) async-start(), calls=%async_computation.38 | async-start | bytes 9437184 | tf_op jit(solution)/shard_map/cond/branch_1_fun/all_gather | solution.py:225
  102.8 31.5 %copy-start.145 = (f32[2048]{0:T(1024)S(1)}, f32[2048]{0:T(1024)}, u32[]{:S(2)}) copy-start(f32[2048]{0:T(1024)} %concatenate.49) | copy-start | bytes 24580
  134.3 23.5 %copy-start.134 = (f32[2,392]{1,0:T(2,128)S(1)}, f32[2,392]{1,0:T(2,128)}, u32[]{:S(2)}) copy-start(f32[2,392]{1,0:T(2,128)} %copy-done.133) | copy-start | bytes 9412
  134.3 23.7 %copy-start.124 = (f32[8,48]{1,0:T(8,128)S(1)}, f32[8,48]{1,0:T(8,128)}, u32[]{:S(2)}) copy-start(f32[8,48]{1,0:T(8,128)} %copy-done.123) | copy-start | bytes 4612
  134.3 23.8 %copy-start.122 = (f32[8,48]{1,0:T(8,128)S(1)}, f32[8,48]{1,0:T(8,128)}, u32[]{:S(2)}) copy-start(f32[8,48]{1,0:T(8,128)} %copy-done.121) | copy-start | bytes 4612
  134.3 24.4 %copy-start.126 = (f32[8,48]{1,0:T(8,128)S(1)}, f32[8,48]{1,0:T(8,128)}, u32[]{:S(2)}) copy-start(f32[8,48]{1,0:T(8,128)} %copy-done.125) | copy-start | bytes 4612
  134.3 26.6 %copy-start.140 = (s32[2,4]{1,0:T(2,128)S(1)}, s32[2,4]{1,0:T(2,128)}, u32[]{:S(2)}) copy-start(s32[2,4]{1,0:T(2,128)} %get-tuple-element.423) | copy-start | bytes 100
  145.6 131.5 %all-gather.37.cloned.1.call-start = ((), (), s32[]{:S(2)}) async-start(), calls=%async_computation.39 | async-start | bytes 1505280 | tf_op jit(solution)/shard_map/cond/branch_1_fun/all_gather | solution.py:755
  173.3 23.3 %copy-start.155 = (f32[8,1,128]{2,1,0:T(1,128)S(1)}, f32[8,1,128]{2,1,0:T(1,128)}, u32[]{:S(2)}) copy-start(f32[8,1,128]{2,1,0:T(1,128)} %get-tuple-element.425) | copy-start | bytes 12292
  216.2 22.9 %copy-start.128 = (f32[384]{0:T(512)S(1)}, f32[384]{0:T(512)}, u32[]{:S(2)}) copy-start(f32[384]{0:T(512)} %copy-done.127) | copy-start | bytes 4612
  246.2 68.6 %all-gather.39.cloned.1.call-start = ((), (), s32[]{:S(2)}) async-start(), calls=%async_computation.40 | async-start | bytes 1505280 | tf_op jit(solution)/shard_map/cond/branch_1_fun/all_gather | solution.py:755
  246.7 90.0 %all-gather.41.cloned.1.call-start = ((), (), s32[]{:S(2)}) async-start(), calls=%async_computation.41 | async-start | bytes 1327104 | tf_op jit(solution)/shard_map/cond/branch_1_fun/all_gather | solution.py:225
  257.5 20.7 %copy-start.69 = (bf16[784,1024]{1,0:T(8,128)(2,1)S(1)}, bf16[784,1024]{1,0:T(8,128)(2,1)}, u32[]{:S(2)}) copy-start(bf16[784,1024]{1,0:T(8,128)(2,1)} %add_convert_fusion.21) | copy-start | bytes 4816900
  277.2 82.8 %all-gather.43.cloned.1.call-start = ((), (), s32[]{:S(2)}) async-start(), calls=%async_computation.42 | async-start | bytes 1327104 | tf_op jit(solution)/shard_map/cond/branch_1_fun/all_gather | solution.py:225
  296.1 191.0 %reduce-scatter.23.cloned.1.call-start = ((), (), s32[]{:S(2)}) async-start(), calls=%async_computation.44 | async-start | bytes 1327104 | tf_op jit(solution)/shard_map/cond/branch_1_fun/reduce_scatter | solution.py:229
  336.3 28.9 %copy-start.21 = (f32[784,384]{1,0:T(8,128)}, f32[784,384]{1,0:T(8,128)S(1)}, u32[]{:S(2)}) copy-start(f32[784,384]{1,0:T(8,128)S(1)} %get-tuple-element.1183) | copy-start | bytes 3612676
  385.0 25.1 %all-to-all-start.8 = ((bf16[4,2,392,96]{2,1,3,0:T(2,128)(2,1)}), bf16[4,2,392,96]{2,1,3,0:T(2,128)(2,1)S(1)}, u32[]{:S(2)}, u32[]{:S(2)}) async-start(bf16[4,2,392,96]{2,1,3,0:T(2,128)(2,1)} %reshape.1311), calls=%async_computation.13 | async-start | bytes 1572864 | tf_op jit(solution)/shard_map/cond/branch_1_fun/all_to_all | solution.py:221
  389.6 97.6 %reduce-scatter.21.cloned.1.call-start = ((), (), s32[]{:S(2)}) async-start(), calls=%async_computation.43 | async-start | bytes 1658880 | tf_op jit(solution)/shard_map/cond/branch_1_fun/reduce_scatter | solution.py:229
  415.9 31.3 %copy-start.58 = (bf16[4,1,392,96]{2,1,3,0:T(2,128)(2,1)S(1)}, bf16[4,1,392,96]{2,1,3,0:T(2,128)(2,1)}, u32[]{:S(2)}) copy-start(bf16[4,1,392,96]{2,1,3,0:T(2,128)(2,1)} %get-tuple-element.1148) | copy-start | bytes 903172
  451.4 38.3 %all-to-all-start.10 = ((bf16[4,1,392,288]{2,3,1,0:T(8,128)(2,1)}), bf16[4,1,392,288]{2,3,1,0:T(8,128)(2,1)}, u32[]{:S(2)}, u32[]{:S(2)}) async-start(bf16[4,1,392,288]{2,3,1,0:T(8,128)(2,1)} %copy.359), calls=%async_computation.17 | async-start | bytes 2359296 | tf_op jit(solution)/shard_map/cond/branch_1_fun/all_to_all | solution.py:221
  489.6 32.8 %all-to-all-start.9 = ((bf16[4,1,392,288]{2,3,1,0:T(8,128)(2,1)}), bf16[4,1,392,288]{2,3,1,0:T(8,128)(2,1)}, u32[]{:S(2)}, u32[]{:S(2)}) async-start(bf16[4,1,392,288]{2,3,1,0:T(8,128)(2,1)} %copy.351), calls=%async_computation.16 | async-start | bytes 2359296 | tf_op jit(solution)/shard_map/cond/branch_1_fun/all_to_all | solution.py:221
  494.7 175.6 %reduce-scatter.25.cloned.1.call-start = ((), (), s32[]{:S(2)}) async-start(), calls=%async_computation.45 | async-start | bytes 9437184 | tf_op jit(solution)/shard_map/cond/branch_1_fun/reduce_scatter | solution.py:229
  536.3 144.2 %reduce-scatter.29.cloned.1.call-start = ((), (), s32[]{:S(2)}) async-start(), calls=%async_computation.47 | async-start | bytes 9437184 | tf_op jit(solution)/shard_map/cond/branch_1_fun/reduce_scatter | solution.py:229
  572.8 23.5 %all-to-all-start.11 = ((bf16[4,2,192,256]{3,2,1,0:T(8,128)(2,1)}), bf16[4,2,192,256]{3,2,1,0:T(8,128)(2,1)}, u32[]{:S(2)}, u32[]{:S(2)}) async-start(bf16[4,2,192,256]{3,2,1,0:T(8,128)(2,1)} %bitcast.660), calls=%async_computation.18 | async-start | bytes 1572864 | tf_op jit(solution)/shard_map/cond/branch_1_fun/all_to_all | solution.py:221
  606.4 31.5 %all-to-all-start.13 = ((bf16[4,1,192,768]{3,2,1,0:T(8,128)(2,1)}), bf16[4,1,192,768]{3,2,1,0:T(8,128)(2,1)S(1)}, u32[]{:S(2)}, u32[]{:S(2)}) async-start(bf16[4,1,192,768]{3,2,1,0:T(8,128)(2,1)} %attend_back.15), calls=%async_computation.21 | async-start | bytes 2359296 | tf_op jit(solution)/shard_map/cond/branch_1_fun/all_to_all | solution.py:221
  637.9 32.4 %all-to-all-start.12 = ((bf16[4,1,192,768]{3,2,1,0:T(8,128)(2,1)}), bf16[4,1,192,768]{3,2,1,0:T(8,128)(2,1)}, u32[]{:S(2)}, u32[]{:S(2)}) async-start(bf16[4,1,192,768]{3,2,1,0:T(8,128)(2,1)} %attend_back.14), calls=%async_computation.19 | async-start | bytes 2359296 | tf_op jit(solution)/shard_map/cond/branch_1_fun/all_to_all | solution.py:221
  642.2 119.4 %reduce-scatter.27.cloned.1.call-start = ((), (), s32[]{:S(2)}) async-start(), calls=%async_computation.46 | async-start | bytes 6193152 | tf_op jit(solution)/shard_map/cond/branch_1_fun/reduce_scatter | solution.py:229
  680.5 75.8 %copy-start.46 = (f32[384,1024]{1,0:T(8,128)S(1)}, f32[384,1024]{1,0:T(8,128)}, u32[]{:S(2)}) copy-start(f32[384,1024]{1,0:T(8,128)} %get-tuple-element.1092) | copy-start | bytes 4718596
  (96 other events, 482.3 us)
Sparse Core Ops, SparseCore 0:
  9.9 30.5 all-gather.44
  50.6 51.9 all-gather.30
  104.7 55.1 all-gather.32
  161.8 54.3 all-gather.34
  246.3 30.8 all-gather.36
  278.7 29.9 all-gather.38
  310.7 23.1 all-gather.40
  335.9 24.0 all-gather.42
  374.6 36.7 reduce-scatter.22
  415.2 37.7 reduce-scatter.20
  536.4 69.3 reduce-scatter.24
  609.2 71.2 reduce-scatter.28
  684.4 57.8 reduce-scatter.26

commit v8 on v7

--- a/solution.py
+++ b/solution.py
@@ -583,7 +583,7 @@
     clips, slots, width = tokens.shape
     span = visible.shape[1]
 
-    e_out = gather(e_shard["out"])
+    e_joint = gather(e_shard["joint"])
     place = lax.broadcasted_iota(jnp.int32, (1, 1, span), 2)
     slot_visible = jnp.any(
         (slot_token[:, :, None] == place) & (visible[:, None, :] > 0), axis=2
@@ -600,6 +600,7 @@
     )
     full = unpack_rows(packed, sizes + [1])
     all_fit = jnp.min(full[-1]) > 0.5
+    normed = norm_layer(tokens.reshape(-1, width), full[0], full[1])
 
     operands = (
         tokens,
@@ -607,8 +608,9 @@
         counts,
         slot_token,
         positions,
-        e_out,
-        tuple(e_shard[name] for name in ("joint", "expand", "contract")),
+        normed,
+        e_joint,
+        tuple(e_shard[name] for name in ("out", "expand", "contract")),
         embed_weight,
         tuple(p_shard[name] for name in ("joint", "out", "expand", "contract")),
         tuple(full[:-1]),
@@ -631,7 +633,8 @@
     counts,
     slot_token,
     positions,
-    e_out,
+    normed,
+    e_joint,
     e_shards,
     embed_shard,
     p_shards,
@@ -650,9 +653,9 @@
     embed_bias, mask_token = vectors[9:11]
     p_vec = dict(zip(ORDER, vectors[11:]))
 
-    e_joint_shard, e_expand_shard, e_contract_shard = e_shards
+    e_out_shard, e_expand_shard, e_contract_shard = e_shards
     p_joint_shard, p_out_shard, p_expand_shard, p_contract_shard = p_shards
-    e_joint = gather(e_joint_shard)
+    e_out, e_expand = gather(e_out_shard), gather(e_expand_shard)
 
     own_visible = lax.dynamic_slice_in_dim(slot_visible, shard * slots, slots, 1)
     own_flat = own_visible.reshape(rows, 1)
@@ -709,10 +712,7 @@
         return array.transpose(1, 0, 2, 3).reshape(1, count, shards * length, lanes)
 
     inputs = tokens.reshape(rows, width)
-    normed = norm_layer(inputs, e_vec["pre_gain"], e_vec["pre_shift"])
     normed_kept = keep(normed).reshape(1, clips, held, width)
-    normed_kept, e_expand_shard = lax.optimization_barrier((normed_kept, e_expand_shard))
-    e_expand = gather(e_expand_shard)
     normed_all = exchange(jnp.broadcast_to(normed_kept, (seq_size, clips, held, width)))
     embed, p_joint, p_out = gather(embed_shard), gather(p_joint_shard), gather(p_out_shard)
     e_by_sender = by_sender(e_joint, seq_size)
@@ -731,6 +731,8 @@
         head_size,
         bias,
     ).reshape(rows, width)
+    mixed, p_expand_shard = lax.optimization_barrier((mixed, p_expand_shard))
+    p_expand = gather(p_expand_shard)
     middle = inputs + mm(mixed, e_out) + e_vec["out_bias"]
     normed_mid = norm_layer(middle, e_vec["mid_gain"], e_vec["mid_shift"])
     active = gelu(mm(normed_mid, e_expand) + e_vec["expand_bias"])
@@ -740,8 +742,28 @@
     embedded = mm(context, embed) + embed_bias
     pred_input = jnp.where(own_flat, embedded, mask_token) + slot_code
     p_normed = norm_layer(pred_input, p_vec["pre_gain"], p_vec["pre_shift"])
-    p_normed, rows_all, mid_rows, mixed_rows, middle_rows = lax.optimization_barrier(
-        (p_normed, normed_all, normed_mid, mixed, middle)
+    (
+        p_normed,
+        rows_all,
+        mid_rows,
+        mixed_rows,
+        middle_rows,
+        e_vec["query_bias"],
+        e_vec["value_bias"],
+        p_vec["query_bias"],
+        p_vec["value_bias"],
+    ) = lax.optimization_barrier(
+        (
+            p_normed,
+            normed_all,
+            normed_mid,
+            mixed,
+            middle,
+            e_vec["query_bias"],
+            e_vec["value_bias"],
+            p_vec["query_bias"],
+            p_vec["value_bias"],
+        )
     )
     p_queries = (mm(p_normed, p_joint[:, :small_width]) + p_vec["query_bias"]).astype(bf16)
     own_weight, own_bias = own_joint(
@@ -755,12 +777,14 @@
         lax.all_gather(p_normed.reshape(clips, slots, small_width)[clip], "seq", axis=0, tiled=True)
         for clip in range(clips)
     ]
-    p_expand_shard, p_contract_shard, everyone[0] = lax.optimization_barrier(
-        (p_expand_shard, p_contract_shard, everyone[0])
-    )
-    p_expand, p_contract = gather(p_expand_shard), gather(p_contract_shard)
+    p_contract_shard, p_expand, everyone[0] = lax.optimization_barrier(
+        (p_contract_shard, p_expand, everyone[0])
+    )
+    p_contract = gather(p_contract_shard)
     for clip in range(clips):
         every = everyone[clip]
+        if clip > 0:
+            every, p_mixed[-1] = lax.optimization_barrier((every, p_mixed[-1]))
         p_joined = (mm(every, p_joint[:, small_width:]) + p_bias).astype(bf16)
         p_normed_all.append(every)
         p_mixed.append(

time: 837 us -> 818 us (0.977)
  starting transfers between devices: 44.3 us -> 32.5 us
  other arithmetic: 65.1 us -> 54.8 us
    unnamed x220 -> x285, local copies, waits for them, and re-layouts: 10.3 us -> 23 us
    all_gather x2, starting transfers between devices: 11.5 us -> 0.7 us  [main(): lax.all_gather(p_normed.reshape(clips, slots, small_width)[clip], 'seq',...]
  transfers between devices with their start and end apart: 20 -> 20, of which waited for: 11 -> 11; matrix products, arithmetic and copies ran while one was open for 30% -> 32% of each run, Pallas kernels for 26% -> 26%
where the time goes in v8:
time: 818 us; the launch traced here: 808 us
  Pallas kernels  249 us (30%)
  matrix products  190 us (23%)
  waiting for transfers between devices  130 us (16%)
  local copies, waits for them, and re-layouts  82.1 us (10%)
  other arithmetic  54.8 us (7%)
  blocking collectives  46.3 us (6%)
  starting transfers between devices  32.5 us (4%)
  between operations  16.1 us (2%)
    dot_general x43, matrix products, mm(): return lax.dot_general(left, right, dims, preferred_element_type=f32)  176 us
    pallas_call x2, Pallas kernels, line_sum(): pl.pallas_call(functools.partial(line_kernel, size, tuple(cuts), int(shar...  111 us
    all_to_all x7, waiting for transfers between devices, exchange(): return lax.all_to_all(array, 'seq', split_axis=0, concat_axis=0, tiled=True)  85 us
    pallas_call x4, Pallas kernels, attend_back(): pl.pallas_call(functools.partial(backward_kernel, 1.0 / math.sqrt(head_si...  82.6 us
    pallas_call x3, Pallas kernels, attend(): pl.pallas_call(functools.partial(forward_kernel, 1.0 / math.sqrt(head_siz...  54.7 us
    all_gather x3, blocking collectives, gather(): return lax.all_gather(array, 'fsdp', axis=0, tiled=True)  35.3 us
    all_to_all x7, starting transfers between devices, exchange(): return lax.all_to_all(array, 'seq', split_axis=0, concat_axis=0, tiled=True)  30 us
    all_gather x6, waiting for transfers between devices, gather(): return lax.all_gather(array, 'fsdp', axis=0, tiled=True)  26.7 us
  transfers between devices with their start and end apart: 20, of which 11 were waited for; matrix products, arithmetic and copies ran while one was open for 32% of the time, Pallas kernels for 26%

profile of v8, /device:TPU:0, one launch (start us, length us, event | category | flops | bytes accessed | tf_op | source)
XLA Modules:
  0.0 808.5 jit_solution(1582355211967469762)
XLA Ops:
  19.2 11.0 %all-gather = f32[256,128]{1,0:T(8,128)S(1)} all-gather(f32[32,128]{1,0:T(8,128)S(1)} %concatenate.59), channel_id=2, replica_groups=mesh['fsdp'=8,'seq'=4] {'fsdp'}, dimensions={0}, use_global_device_ids=true | all-gather | bytes 147456 | tf_op jit(solution)/shard_map/all_gather | solution.py:598
  34.7 25.7 %all-gather.45.cloned.1.call-done = bf16[1024,3072]{0,1:T(8,128)(2,1)} async-done(((bf16[128,3072]{0,1:T(8,128)(2,1)}), bf16[1024,3072]{0,1:T(8,128)(2,1)}) %all-gather.45.cloned.1.call-update) | async-done | bytes 6291472 | tf_op jit(solution)/shard_map/all_gather | solution.py:225
  60.4 722.7 %conditional.4 = (f32[2,392,1024]{2,1,0:T(8,128)}, f32[2,392,384]{2,1,0:T(8,128)}, f32[2,392,1024]{2,1,0:T(8,128)}, bf16[128,4096]{1,0:T(8,128)(2,1)}, bf16[512,...) conditional(s32[]{:T(128)} %convert_element_type.809, ...), branch_computations={%region_6.52_spmd, %region_51.97_spmd} | conditional | flops 216417861632 | bytes 1263022720
  76.9 6.1 copy.321
  83.0 10.1 %all_gather.58 = bf16[384,384]{1,0:T(8,128)(2,1)S(1)} all-gather(bf16[48,384]{1,0:T(8,128)(2,1)S(1)} %copy-done.99), channel_id=1, replica_groups=mesh['fsdp'=8,'seq'=4] {'fsdp'}, dimensions={0}, use_global_device_ids=true | all-gather | bytes 331776 | tf_op jit(solution)/shard_map/cond/branch_1_fun/all_gather | solution.py:225
  93.2 10.8 %all_gather.56 = bf16[1024,384]{1,0:T(8,128)(2,1)} all-gather(bf16[128,384]{1,0:T(8,128)(2,1)S(1)} %copy-done.85), channel_id=1, replica_groups=mesh['fsdp'=8,'seq'=4] {'fsdp'}, dimensions={0}, use_global_device_ids=true | all-gather | bytes 884736 | tf_op jit(solution)/shard_map/cond/branch_1_fun/all_gather | solution.py:225
  103.9 14.4 %all_gather.57 = bf16[384,1152]{1,0:T(8,128)(2,1)} all-gather(bf16[48,1152]{1,0:T(8,128)(2,1)S(1)} %copy-done.80), channel_id=1, replica_groups=mesh['fsdp'=8,'seq'=4] {'fsdp'}, dimensions={0}, use_global_device_ids=true | all-gather | bytes 995328 | tf_op jit(solution)/shard_map/cond/branch_1_fun/all_gather | solution.py:225
  118.3 29.9 %all-to-all-done.7 = bf16[4,2,192,1024]{3,2,1,0:T(8,128)(2,1)} async-done(((bf16[4,2,192,1024]{3,2,1,0:T(8,128)(2,1)}), bf16[4,2,192,1024]{3,2,1,0:T(8,128)(2,1)}, u32[]{:S(2)}, u32[]{:S(2)}) %all-to-all-start.7) | async-done | bytes 3145760 | tf_op jit(solution)/shard_map/cond/branch_1_fun/all_to_all | solution.py:221
  148.2 11.4 %add_convert_fusion.13 = bf16[1536,2048]{1,0:T(8,128)(2,1)} fusion(bf16[1536,1024]{1,0:T(8,128)(2,1)} %bitcast.110, f32[2048]{0:T(1024)S(1)} %concatenate.49, bf16[1024,3072]{0,1:T(8,128)(2,1)} %get-tuple-element.411), kind=kOutput, calls=%fused_computation.220 | convolution fusion | flops 6448742400 | bytes 13639680 | tf_op jit(solution)/shard_map/cond/branch_1_fun/dot_general | solution.py:25
  174.2 23.4 %attend.9 = bf16[2,392,1024]{2,1,0:T(8,128)(2,1)} custom-call(bf16[2,392,1024]{2,1,0:T(8,128)(2,1)} %bitcast.777, bf16[4,2,192,2048]{3,2,1,0:T(8,128)(2,1)} %bitcast.771, bf16[4,2,192,2048]{3,2,1,0:T(8,128)(2,1)} %bitcast.772, f32[2,1,768]{2,1,0:T(1,128)} %compare_select_fusion.1.rest_0_), custom_call_target="tpu_custom_call" | custom-call | flops 9865003008 | bytes 6291456 | tf_op jit(solution)/shard_map/cond/branch_1_fun/attend/pallas_call | solution.py:105
  197.6 5.6 fusion.99
  212.9 22.9 %add_add_fusion.2 = f32[784,1024]{1,0:T(8,128)} fusion(f32[784,1024]{1,0:T(8,128)} %fusion.99, bf16[4096,1024]{1,0:T(8,128)(2,1)} %all-gather.35.cloned.1.call-done, f32[4096]{0:T(1024)} %bitcast.745, bf16[1024,4096]{1,0:T(8,128)(2,1)} %all-gather.33.cloned.1.call-done, f32[1024]{0:T(1024)S(1)} %bitcast.768, f32[1024]{0:T(1024)S(1)} %bitcast.722, ...), kind=kOutput, calls=%fused_computation.249 | convolution fusion | flops 13178224640 | bytes 23234688 | tf_op jit(solution)/shard_map/cond/branch_1_fun/dot_general | solution.py:25
  277.1 15.7 %attend.10 = bf16[1,392,384]{2,1,0:T(8,128)(2,1)} custom-call(bf16[1,392,384]{2,1,0:T(8,128)(2,1)} %get-tuple-element.933.q_ref, bf16[1,1,1568,768]{3,2,1,0:T(8,128)(2,1)} %fusion.83.k_ref.v_ref, bf16[1,1,1568,768]{3,2,1,0:T(8,128)(2,1)} %fusion.83.k_ref.v_ref), custom_call_target="tpu_custom_call" | custom-call | flops 7552892928 | bytes 2408448 | tf_op jit(solution)/shard_map/cond/branch_1_fun/attend/pallas_call | solution.py:105
  292.8 11.8 %all-gather.37.cloned.1.call-done = bf16[1568,384]{1,0:T(8,128)(2,1)} async-done(((bf16[392,384]{1,0:T(8,128)(2,1)}), bf16[1568,384]{1,0:T(8,128)(2,1)}) %all-gather.37.cloned.1.call-update) | async-done | bytes 1204240 | tf_op jit(solution)/shard_map/cond/branch_1_fun/all_gather | solution.py:777
  308.7 15.7 %attend.11 = bf16[1,392,384]{2,1,0:T(8,128)(2,1)} custom-call(bf16[1,392,384]{2,1,0:T(8,128)(2,1)} %get-tuple-element.934.q_ref, bf16[1,1,1568,768]{3,2,1,0:T(8,128)(2,1)} %fusion.84.k_ref.v_ref, bf16[1,1,1568,768]{3,2,1,0:T(8,128)(2,1)} %fusion.84.k_ref.v_ref), custom_call_target="tpu_custom_call" | custom-call | flops 7552892928 | bytes 2408448 | tf_op jit(solution)/shard_map/cond/branch_1_fun/attend/pallas_call | solution.py:105
  377.7 5.6 all-to-all-done.8
  389.0 31.3 %attend_back.13 = bf16[4,1,392,288]{3,2,1,0:T(8,128)(2,1)} custom-call(bf16[1,1,1568,96]{3,2,1,0:T(8,128)(2,1)} %fusion.92.q_ref, bf16[1,1,1568,96]{3,2,1,0:T(8,128)(2,1)} %fusion.96.k_ref, bf16[1,1,1568,96]{3,2,1,0:T(8,128)(2,1)} %fusion.91.v_ref, bf16[1,1,1568,96]{3,2,1,0:T(8,128)(2,1)} %bitcast.700), custom_call_target="tpu_custom_call" | custom-call | flops 18882232320 | bytes 2107392 | tf_op jit(solution)/shard_map/cond/branch_1_fun/attend_back/pallas_call | solution.py:205
  429.0 31.3 %attend_back.12 = bf16[4,1,392,288]{3,2,1,0:T(8,128)(2,1)} custom-call(bf16[1,1,1568,96]{3,2,1,0:T(8,128)(2,1)} %fusion.94.q_ref, bf16[1,1,1568,96]{3,2,1,0:T(8,128)(2,1)} %fusion.95.k_ref, bf16[1,1,1568,96]{3,2,1,0:T(8,128)(2,1)} %fusion.93.v_ref, bf16[1,1,1568,96]{3,2,1,0:T(8,128)(2,1)} %bitcast.698), custom_call_target="tpu_custom_call" | custom-call | flops 18882232320 | bytes 2107392 | tf_op jit(solution)/shard_map/cond/branch_1_fun/attend_back/pallas_call | solution.py:205
  468.1 8.8 %convolution_add_fusion.11 = f32[384,4096]{1,0:T(8,128)} fusion(bf16[384,1024]{1,0:T(8,128)(2,1)S(1)} %bitcast.787, bf16[1024,4096]{1,0:T(8,128)(2,1)} %all-gather.33.cloned.1.call-done, f32[4096]{0:T(1024)S(1)} %bitcast.746), kind=kOutput, calls=%fused_computation.235 | convolution fusion | flops 3222798336 | bytes 15482880 | tf_op jit(solution)/shard_map/cond/branch_1_fun/dot_general | solution.py:25
  481.4 14.0 %all-to-all-done.9 = bf16[4,1,392,288]{2,3,1,0:T(8,128)(2,1)} async-done(((bf16[4,1,392,288]{2,3,1,0:T(8,128)(2,1)}), bf16[4,1,392,288]{2,3,1,0:T(8,128)(2,1)}, u32[]{:S(2)}, u32[]{:S(2)}) %all-to-all-start.9) | async-done | bytes 903200 | tf_op jit(solution)/shard_map/cond/branch_1_fun/all_to_all | solution.py:221
  502.9 6.9 convolution_convert_fusion.12
  510.2 8.6 %fusion.190 = (bf16[4096]{0:T(1024)(128)(2,1)S(1)}, bf16[384,4096]{1,0:T(8,128)(2,1)S(1)}) fusion(f32[384,4096]{1,0:T(8,128)} %convolution_add_fusion.11, bf16[384,1024]{1,0:T(8,128)(2,1)S(1)} %get-tuple-element.479, bf16[4096,1024]{1,0:T(8,128)(2,1)} %all-gather.35.cloned.1.call-done), kind=kOutput, calls=%fused_computation.523 | convolution fusion | flops 3238522880 | bytes 18620416 | tf_op jit(solution)/shard_map/cond/branch_1_fun/dot_general | solution.py:25
  520.5 6.9 convolution_convert_fusion.11
  527.4 8.9 %fusion.200 = f32[384,1024]{1,0:T(8,128)} fusion(bf16[384,4096]{1,0:T(8,128)(2,1)} %copy-done.205, bf16[1024,4096]{1,0:T(8,128)(2,1)} %all-gather.33.cloned.1.call-done), kind=kOutput, calls=%fused_computation.533 | convolution fusion | flops 3221225472 | bytes 13107200 | tf_op jit(solution)/shard_map/cond/branch_1_fun/dot_general | solution.py:25
  558.1 11.6 %all-to-all-done.11.g_ref = bf16[4,2,192,256]{3,2,1,0:T(8,128)(2,1)} async-done(((bf16[4,2,192,256]{3,2,1,0:T(8,128)(2,1)}), bf16[4,2,192,256]{3,2,1,0:T(8,128)(2,1)}, u32[]{:S(2)}, u32[]{:S(2)}) %all-to-all-start.11) | async-done | bytes 786464 | tf_op jit(solution)/shard_map/cond/branch_1_fun/all_to_all | solution.py:221
  569.7 10.0 %attend_back.15 = bf16[4,1,192,768]{3,2,1,0:T(8,128)(2,1)} custom-call(bf16[4,2,192,256]{3,2,1,0:T(8,128)(2,1)} %bitcast.783, bf16[4,2,192,256]{3,2,1,0:T(8,128)(2,1)} %bitcast.781, bf16[4,2,192,256]{3,2,1,0:T(8,128)(2,1)} %bitcast.785, bf16[4,2,192,256]{3,2,1,0:T(8,128)(2,1)} %all-to-all-done.11.g_ref, f32[2,1,768]{2,1,0:T(1,128)} %compare_select_fusion.1.rest_0_), custom_call_target="tpu_custom_call" | custom-call | flops 6039797760 | bytes 2752512 | tf_op jit(solution)/shard_map/cond/branch_1_fun/attend_back/pallas_call | solution.py:205
  583.8 10.0 %attend_back.14 = bf16[4,1,192,768]{3,2,1,0:T(8,128)(2,1)} custom-call(bf16[4,2,192,256]{3,2,1,0:T(8,128)(2,1)} %bitcast.784, bf16[4,2,192,256]{3,2,1,0:T(8,128)(2,1)} %bitcast.782, bf16[4,2,192,256]{3,2,1,0:T(8,128)(2,1)} %bitcast.786, bf16[4,2,192,256]{3,2,1,0:T(8,128)(2,1)} %all-to-all-done.11.g_ref, f32[2,1,768]{2,1,0:T(1,128)} %compare_select_fusion.1.rest_0_), custom_call_target="tpu_custom_call" | custom-call | flops 6039797760 | bytes 2752512 | tf_op jit(solution)/shard_map/cond/branch_1_fun/attend_back/pallas_call | solution.py:205
  593.8 7.5 fusion.100
  601.3 10.0 %all-to-all-done.13 = bf16[4,1,192,768]{3,2,1,0:T(8,128)(2,1)S(1)} async-done(((bf16[4,1,192,768]{3,2,1,0:T(8,128)(2,1)}), bf16[4,1,192,768]{3,2,1,0:T(8,128)(2,1)S(1)}, u32[]{:S(2)}, u32[]{:S(2)}) %all-to-all-start.13) | async-done | bytes 1179680 | tf_op jit(solution)/shard_map/cond/branch_1_fun/all_to_all | solution.py:221
  629.7 13.9 %all-to-all-done.12 = bf16[4,1,192,768]{3,2,1,0:T(8,128)(2,1)} async-done(((bf16[4,1,192,768]{3,2,1,0:T(8,128)(2,1)}), bf16[4,1,192,768]{3,2,1,0:T(8,128)(2,1)}, u32[]{:S(2)}, u32[]{:S(2)}) %all-to-all-start.12) | async-done | bytes 1179680 | tf_op jit(solution)/shard_map/cond/branch_1_fun/all_to_all | solution.py:221
  654.9 74.3 %line_sum.6 = (bf16[512,1024]{1,0:T(8,128)(2,1)}, bf16[128,4096]{1,0:T(8,128)(2,1)}, bf16[48,1920]{1,0:T(8,128)(2,1)}, bf16[192,384]{1,0:T(8,128)(2,1)}) custom-call(bf16[512,1024]{1,0:T(8,128)(2,1)} %reduce-scatter.25.cloned.1.call-done.refs_0_, bf16[128,4096]{1,0:T(8,128)(2,1)} %reduce-scatter.29.cloned.1.call-done.refs_1_, ...), custom_call_target="tpu_custom_call" | custom-call | bytes 97157120 | tf_op jit(solution)/shard_map/cond/branch_1_fun/line_sum/pallas_call | solution.py:445
  739.4 36.9 %line_sum.7 = (bf16[128,1536]{1,0:T(8,128)(2,1)}, bf16[4,128,1152]{2,1,0:T(8,128)(2,1)}) custom-call(bf16[128,1536]{1,0:T(8,128)(2,1)} %slice.439.refs_0_, bf16[128,1152]{1,0:T(8,128)(2,1)} %slice.440.refs_1_), custom_call_target="tpu_custom_call" | custom-call | bytes 27525120 | tf_op jit(solution)/shard_map/cond/branch_1_fun/line_sum/pallas_call | solution.py:445
  (542 shorter events, 274.2 us)
Async XLA Ops:
  7.2 53.2 %all-gather.45.cloned.1.call-start = ((), (), s32[]{:S(2)}) async-start(), calls=%async_computation.48 | async-start | bytes 7077888 | tf_op jit(solution)/shard_map/all_gather | solution.py:225
  32.9 27.5 %copy-start.78 = (bf16[48,1152]{1,0:T(8,128)(2,1)S(1)}, bf16[48,1152]{1,0:T(8,128)(2,1)}, u32[]{:S(2)}) copy-start(bf16[48,1152]{1,0:T(8,128)(2,1)} %param.60) | copy-start | bytes 331780
  32.9 27.5 %copy-start.83 = (bf16[128,384]{1,0:T(8,128)(2,1)S(1)}, bf16[128,384]{1,0:T(8,128)(2,1)}, u32[]{:S(2)}) copy-start(bf16[128,384]{1,0:T(8,128)(2,1)} %param.55) | copy-start | bytes 294916
  32.9 27.5 %copy-start.97 = (bf16[48,384]{1,0:T(8,128)(2,1)S(1)}, bf16[48,384]{1,0:T(8,128)(2,1)}, u32[]{:S(2)}) copy-start(bf16[48,384]{1,0:T(8,128)(2,1)} %param.63) | copy-start | bytes 110596
  66.2 16.8 %copy-start.105 = (f32[1024]{0:T(1024)}, f32[1024]{0:T(1024)S(1)}, u32[]{:S(2)}) copy-start(f32[1024]{0:T(1024)S(1)} %get-tuple-element.456) | copy-start | bytes 12292
  66.2 131.4 %all-gather.31.cloned.1.call-start = ((), (), s32[]{:S(2)}) async-start(), calls=%async_computation.36 | async-start | bytes 2359296 | tf_op jit(solution)/shard_map/cond/branch_1_fun/all_gather | solution.py:225
  67.0 145.0 %all-gather.33.cloned.1.call-start = ((), (), s32[]{:S(2)}) async-start(), calls=%async_computation.37 | async-start | bytes 9437184 | tf_op jit(solution)/shard_map/cond/branch_1_fun/all_gather | solution.py:225
  72.1 76.1 %all-to-all-start.7 = ((bf16[4,2,192,1024]{3,2,1,0:T(8,128)(2,1)}), bf16[4,2,192,1024]{3,2,1,0:T(8,128)(2,1)}, u32[]{:S(2)}, u32[]{:S(2)}) async-start(bf16[4,2,192,1024]{3,2,1,0:T(8,128)(2,1)} %broadcast_in_dim.166), calls=%async_computation.12 | async-start | bytes 6291456 | tf_op jit(solution)/shard_map/cond/branch_1_fun/all_to_all | solution.py:221
  76.8 136.1 %all-gather.35.cloned.1.call-start = ((), (), s32[]{:S(2)}) async-start(), calls=%async_computation.38 | async-start | bytes 9437184 | tf_op jit(solution)/shard_map/cond/branch_1_fun/all_gather | solution.py:225
  76.9 27.1 %copy-start.80 = (bf16[48,1152]{1,0:T(8,128)(2,1)S(1)}, bf16[48,1152]{1,0:T(8,128)(2,1)}, u32[]{:S(2)}) copy-start(bf16[48,1152]{1,0:T(8,128)(2,1)} %copy-done.79) | copy-start | bytes 331780
  159.6 111.4 %all-gather.39.cloned.1.call-start = ((), (), s32[]{:S(2)}) async-start(), calls=%async_computation.40 | async-start | bytes 1327104 | tf_op jit(solution)/shard_map/cond/branch_1_fun/all_gather | solution.py:225
  174.2 23.4 %copy-start.141 = (f32[8,1,128]{2,1,0:T(1,128)S(1)}, f32[8,1,128]{2,1,0:T(1,128)}, u32[]{:S(2)}) copy-start(f32[8,1,128]{2,1,0:T(1,128)} %get-tuple-element.425) | copy-start | bytes 12292
  208.0 65.0 %all-gather.41.cloned.1.call-start = ((), (), s32[]{:S(2)}) async-start(), calls=%async_computation.41 | async-start | bytes 1505280 | tf_op jit(solution)/shard_map/cond/branch_1_fun/all_gather | solution.py:777
  212.9 22.9 %copy-start.128 = (f32[384]{0:T(512)S(1)}, f32[384]{0:T(512)}, u32[]{:S(2)}) copy-start(f32[384]{0:T(512)} %add.623) | copy-start | bytes 4612
  241.9 62.7 %all-gather.37.cloned.1.call-start = ((), (), s32[]{:S(2)}) async-start(), calls=%async_computation.39 | async-start | bytes 1505280 | tf_op jit(solution)/shard_map/cond/branch_1_fun/all_gather | solution.py:777
  253.7 81.4 %all-gather.43.cloned.1.call-start = ((), (), s32[]{:S(2)}) async-start(), calls=%async_computation.42 | async-start | bytes 1327104 | tf_op jit(solution)/shard_map/cond/branch_1_fun/all_gather | solution.py:225
  273.0 187.3 %reduce-scatter.23.cloned.1.call-start = ((), (), s32[]{:S(2)}) async-start(), calls=%async_computation.44 | async-start | bytes 1327104 | tf_op jit(solution)/shard_map/cond/branch_1_fun/reduce_scatter | solution.py:229
  308.7 16.7 %copy-start.12 = (f32[784,384]{1,0:T(8,128)S(1)}, f32[784,384]{1,0:T(8,128)}, u32[]{:S(2)}) copy-start(f32[784,384]{1,0:T(8,128)} %copy-done.11) | copy-start | bytes 3612676
  308.7 16.7 %copy-start.131 = (f32[384]{0:T(512)S(1)}, f32[384]{0:T(512)}, u32[]{:S(2)}) copy-start(f32[384]{0:T(512)} %add.642) | copy-start | bytes 4612
  360.1 23.2 %all-to-all-start.8 = ((bf16[4,2,392,96]{2,1,3,0:T(2,128)(2,1)}), bf16[4,2,392,96]{2,1,3,0:T(2,128)(2,1)S(1)}, u32[]{:S(2)}, u32[]{:S(2)}) async-start(bf16[4,2,392,96]{2,1,3,0:T(2,128)(2,1)} %reshape.1233), calls=%async_computation.13 | async-start | bytes 1572864 | tf_op jit(solution)/shard_map/cond/branch_1_fun/all_to_all | solution.py:221
  363.6 96.7 %reduce-scatter.21.cloned.1.call-start = ((), (), s32[]{:S(2)}) async-start(), calls=%async_computation.43 | async-start | bytes 1658880 | tf_op jit(solution)/shard_map/cond/branch_1_fun/reduce_scatter | solution.py:229
  389.0 31.3 %copy-start.53 = (bf16[4,1,392,96]{2,1,3,0:T(2,128)(2,1)S(1)}, bf16[4,1,392,96]{2,1,3,0:T(2,128)(2,1)}, u32[]{:S(2)}) copy-start(bf16[4,1,392,96]{2,1,3,0:T(2,128)(2,1)} %get-tuple-element.931) | copy-start | bytes 903172
  424.5 38.3 %all-to-all-start.10 = ((bf16[4,1,392,288]{2,3,1,0:T(8,128)(2,1)}), bf16[4,1,392,288]{2,3,1,0:T(8,128)(2,1)}, u32[]{:S(2)}, u32[]{:S(2)}) async-start(bf16[4,1,392,288]{2,3,1,0:T(8,128)(2,1)} %copy.340), calls=%async_computation.17 | async-start | bytes 2359296 | tf_op jit(solution)/shard_map/cond/branch_1_fun/all_to_all | solution.py:221
  462.8 32.6 %all-to-all-start.9 = ((bf16[4,1,392,288]{2,3,1,0:T(8,128)(2,1)}), bf16[4,1,392,288]{2,3,1,0:T(8,128)(2,1)}, u32[]{:S(2)}, u32[]{:S(2)}) async-start(bf16[4,1,392,288]{2,3,1,0:T(8,128)(2,1)} %copy.332), calls=%async_computation.16 | async-start | bytes 2359296 | tf_op jit(solution)/shard_map/cond/branch_1_fun/all_to_all | solution.py:221
  467.9 175.8 %reduce-scatter.25.cloned.1.call-start = ((), (), s32[]{:S(2)}) async-start(), calls=%async_computation.45 | async-start | bytes 9437184 | tf_op jit(solution)/shard_map/cond/branch_1_fun/reduce_scatter | solution.py:229
  509.8 145.1 %reduce-scatter.29.cloned.1.call-start = ((), (), s32[]{:S(2)}) async-start(), calls=%async_computation.47 | async-start | bytes 9437184 | tf_op jit(solution)/shard_map/cond/branch_1_fun/reduce_scatter | solution.py:229
  545.7 24.1 %all-to-all-start.11 = ((bf16[4,2,192,256]{3,2,1,0:T(8,128)(2,1)}), bf16[4,2,192,256]{3,2,1,0:T(8,128)(2,1)}, u32[]{:S(2)}, u32[]{:S(2)}) async-start(bf16[4,2,192,256]{3,2,1,0:T(8,128)(2,1)} %bitcast.659), calls=%async_computation.18 | async-start | bytes 1572864 | tf_op jit(solution)/shard_map/cond/branch_1_fun/all_to_all | solution.py:221
  579.7 31.5 %all-to-all-start.13 = ((bf16[4,1,192,768]{3,2,1,0:T(8,128)(2,1)}), bf16[4,1,192,768]{3,2,1,0:T(8,128)(2,1)S(1)}, u32[]{:S(2)}, u32[]{:S(2)}) async-start(bf16[4,1,192,768]{3,2,1,0:T(8,128)(2,1)} %attend_back.15), calls=%async_computation.21 | async-start | bytes 2359296 | tf_op jit(solution)/shard_map/cond/branch_1_fun/all_to_all | solution.py:221
  611.3 32.4 %all-to-all-start.12 = ((bf16[4,1,192,768]{3,2,1,0:T(8,128)(2,1)}), bf16[4,1,192,768]{3,2,1,0:T(8,128)(2,1)}, u32[]{:S(2)}, u32[]{:S(2)}) async-start(bf16[4,1,192,768]{3,2,1,0:T(8,128)(2,1)} %attend_back.14), calls=%async_computation.19 | async-start | bytes 2359296 | tf_op jit(solution)/shard_map/cond/branch_1_fun/all_to_all | solution.py:221
  615.5 120.4 %reduce-scatter.27.cloned.1.call-start = ((), (), s32[]{:S(2)}) async-start(), calls=%async_computation.46 | async-start | bytes 6193152 | tf_op jit(solution)/shard_map/cond/branch_1_fun/reduce_scatter | solution.py:229
  629.7 19.7 %copy-start.54 = (f32[192,1024]{1,0:T(8,128)}, f32[192,1024]{1,0:T(8,128)S(1)}, u32[]{:S(2)}) copy-start(f32[192,1024]{1,0:T(8,128)S(1)} %get-tuple-element.973) | copy-start | bytes 2359300
  654.9 75.8 %copy-start.41 = (f32[384,1024]{1,0:T(8,128)S(1)}, f32[384,1024]{1,0:T(8,128)}, u32[]{:S(2)}) copy-start(f32[384,1024]{1,0:T(8,128)} %get-tuple-element.875) | copy-start | bytes 4718596
  (128 other events, 536.2 us)
Sparse Core Ops, SparseCore 0:
  10.5 49.8 all-gather.44
  69.1 28.6 all-gather.30
  99.9 56.6 all-gather.32
  159.8 53.1 all-gather.34
  214.8 24.0 all-gather.38
  242.1 30.8 all-gather.40
  274.6 29.9 all-gather.36
  306.6 23.1 all-gather.42
  350.2 35.8 reduce-scatter.22
  389.9 37.7 reduce-scatter.20
  509.9 70.3 reduce-scatter.24
  583.6 71.2 reduce-scatter.28
  658.8 57.8 reduce-scatter.26

commit v9 on v8

--- a/solution.py
+++ b/solution.py
@@ -257,10 +257,10 @@
 
 def line_kernel(size, cuts, shares, *refs):
     count = len(cuts)
-    held = count + shares
-    ins, outs = refs[:count], refs[held : held + count]
-    own, every = refs[count], refs[held + count]
-    scratch = refs[2 * held :]
+    ins, outs = refs[:count], refs[count : 2 * count]
+    if shares:
+        ins, own, outs, every = (refs[0].at[:, shares:],), refs[0].at[:, :shares], refs[1:2], refs[2]
+    scratch = refs[3 if shares else 2 * count :]
     inner, outer, partial = (scratch[i * count : (i + 1) * count] for i in range(3))
     to_inner, to_outer, from_inner, from_outer = scratch[3 * count : 3 * count + 4]
     me = lax.axis_index("seq")
@@ -426,47 +426,46 @@
                     passes(way, hop).wait_send()
 
 
-def line_sum(arrays, size, identity, share=None):
+def line_sum(arrays, size, identity, shares=0):
     cuts = []
+    shapes = []
     for member in arrays:
         parts = 8
         while parts > 1 and member.shape[0] % (16 * parts):
             parts //= 2
         cuts.append(parts)
-    hold = [pltpu.VMEM(member.shape, bf16) for member in arrays]
-    shapes = [jax.ShapeDtypeStruct(member.shape, bf16) for member in arrays]
+        shapes.append((member.shape[0], member.shape[1] - shares))
+    hold = [pltpu.VMEM(shape, bf16) for shape in shapes]
     semaphores = [pltpu.SemaphoreType.DMA((sum(cuts),))] * 4
-    operands = list(arrays)
-    if share is not None:
-        operands.append(share)
-        shapes.append(jax.ShapeDtypeStruct((size,) + share.shape, bf16))
+    if shares:
+        shapes.append((size, arrays[0].shape[0], shares))
         semaphores += [pltpu.SemaphoreType.DMA((2, size - 1))] * 2
     whole = pl.BlockSpec(memory_space=pltpu.VMEM)
     return pl.pallas_call(
-        functools.partial(line_kernel, size, tuple(cuts), int(share is not None)),
-        out_shape=shapes,
-        in_specs=[whole] * len(operands),
-        out_specs=[whole] * len(operands),
+        functools.partial(line_kernel, size, tuple(cuts), shares),
+        out_shape=[jax.ShapeDtypeStruct(shape, bf16) for shape in shapes],
+        in_specs=[whole] * len(arrays),
+        out_specs=[whole] * len(shapes),
         scratch_shapes=hold * 3 + semaphores,
         compiler_params=pltpu.CompilerParams(
             collective_id=identity, has_side_effects=True, vmem_limit_bytes=VMEM_LIMIT
         ),
         cost_estimate=pl.CostEstimate(
             flops=0,
-            bytes_accessed=40 * sum(2 * member.size for member in operands),
+            bytes_accessed=40 * sum(2 * member.size for member in arrays),
             transcendentals=0,
         ),
         name="line_sum",
-    )(*operands)
-
-
-def sum_slots(arrays, size, identity, share=None):
+    )(*arrays)
+
+
+def sum_slots(arrays, size, identity, shares=0):
     if size == 4:
-        return line_sum(arrays, size, identity, share)
-    sums = lax.psum(tuple(arrays), "seq")
-    if share is None:
-        return sums
-    return (*sums, lax.all_gather(share, "seq", axis=0, tiled=False))
+        return line_sum(arrays, size, identity, shares)
+    if shares == 0:
+        return lax.psum(tuple(arrays), "seq")
+    summed = lax.psum(arrays[0][:, shares:], "seq")
+    return summed, lax.all_gather(arrays[0][:, :shares], "seq", axis=0, tiled=False)
 
 
 def feed_back(grad_out, middle, normed_mid, hidden, active, weights, mid_gain):
@@ -618,9 +617,33 @@
     )
     whole = functools.partial(main, fsdp_size, seq_size, slots)
     if compact >= slots:
-        return whole(*operands)
-    return lax.cond(
-        all_fit, functools.partial(main, fsdp_size, seq_size, compact), whole, *operands
+        results = whole(*operands)
+    else:
+        results = lax.cond(
+            all_fit, functools.partial(main, fsdp_size, seq_size, compact), whole, *operands
+        )
+    encoded, predicted, grad_tokens, e_sums, embed_sum, p_sums, vector_sum = results
+    vector_sum = vector_sum.reshape(-1).astype(f32)
+    small = []
+    at = 0
+    for size in sizes:
+        small.append(vector_sum[at : at + size])
+        at += size
+
+    def ordered(vec, sums):
+        vec = dict(zip(ORDER, vec))
+        vec.update(zip(("joint", "out", "expand", "contract"), (x.astype(f32) for x in sums)))
+        return tuple(vec[name] for name in BLOCK)
+
+    return (
+        encoded,
+        predicted,
+        grad_tokens,
+        *ordered(small[:9], e_sums),
+        embed_sum.astype(f32),
+        small[9],
+        small[10],
+        *ordered(small[11:], p_sums),
     )
 
 
@@ -916,7 +939,7 @@
     )
     late, expand_sum = lax.optimization_barrier((late, expand_sum))
     shared = 3 * own_width + p_lanes
-    late_sum, columns = sum_slots((late[:, shared:],), seq_size, first + 1, late[:, :shared])
+    late_sum, columns = sum_slots((late,), seq_size, first + 1, shared)
     e_joint_sum = columns[:, :, : 3 * own_width].reshape(seq_size, own_rows, 3, own_width)
     e_joint_sum = e_joint_sum.transpose(1, 2, 0, 3).reshape(own_rows, 3 * width)
     p_joint_sum = columns[:, :p_rows, 3 * own_width : 3 * (own_width + p_own_width)]
@@ -924,33 +947,15 @@
     p_joint_sum = p_joint_sum.transpose(1, 2, 0, 3).reshape(p_rows, 3 * small_width)
     out_sum = late_sum[:, :width]
     embed_sum = late_sum[:, width : width + small_width]
-    vector_sum = late_sum[:, width + small_width :].reshape(-1)
-    small_out = []
-    at = 0
-    for size in sizes:
-        small_out.append(vector_sum[at : at + size].astype(f32))
-        at += size
     p_out_sum, p_expand_sum = p_wide_sum[:, :small_width], p_wide_sum[:, small_width:]
-
-    def ordered(vec, joint, out, expand, contract):
-        vec = dict(
-            zip(ORDER, vec),
-            joint=joint.astype(f32),
-            out=out.astype(f32),
-            expand=expand.astype(f32),
-            contract=contract.astype(f32),
-        )
-        return tuple(vec[name] for name in BLOCK)
-
     return (
         encoded.reshape(tokens.shape),
         predicted.reshape(cotangent.shape),
         grad_tokens.reshape(tokens.shape),
-        *ordered(small_out[:9], e_joint_sum, out_sum, expand_sum, contract_sum),
-        embed_sum.astype(f32),
-        small_out[9],
-        small_out[10],
-        *ordered(small_out[11:], p_joint_sum, p_out_sum, p_expand_sum, p_contract_sum),
+        (e_joint_sum, out_sum, expand_sum, contract_sum),
+        embed_sum,
+        (p_joint_sum, p_out_sum, p_expand_sum, p_contract_sum),
+        late_sum[:, width + small_width :],
     )
 
 

time: 818 us -> 803 us (0.982)
  local copies, waits for them, and re-layouts: 82.1 us -> 67.5 us
    unnamed x285 -> x101, local copies, waits for them, and re-layouts: 23 us -> 3.39 us
    another operation x1 -> x181, local copies, waits for them, and re-layouts: 0.02 us -> 9.79 us
  transfers between devices with their start and end apart: 20 -> 20, of which waited for: 11 -> 11; matrix products, arithmetic and copies ran while one was open for 32% -> 33% of each run, Pallas kernels for 26% -> 27%
where the time goes in v9:
time: 803 us; the launch traced here: 793 us
  Pallas kernels  248 us (31%)
  matrix products  189 us (24%)
  waiting for transfers between devices  129 us (16%)
  local copies, waits for them, and re-layouts  67.5 us (8%)
  other arithmetic  55.1 us (7%)
  blocking collectives  47.7 us (6%)
  starting transfers between devices  32.6 us (4%)
  between operations  16.3 us (2%)
    dot_general x43, matrix products, mm(): return lax.dot_general(left, right, dims, preferred_element_type=f32)  174 us
    pallas_call x2, Pallas kernels, line_sum(): pl.pallas_call(functools.partial(line_kernel, size, tuple(cuts), shares),...  111 us
    all_to_all x7, waiting for transfers between devices, exchange(): return lax.all_to_all(array, 'seq', split_axis=0, concat_axis=0, tiled=True)  87 us
    pallas_call x4, Pallas kernels, attend_back(): pl.pallas_call(functools.partial(backward_kernel, 1.0 / math.sqrt(head_si...  82.7 us
    pallas_call x3, Pallas kernels, attend(): pl.pallas_call(functools.partial(forward_kernel, 1.0 / math.sqrt(head_siz...  54.8 us
    all_gather x3, blocking collectives, gather(): return lax.all_gather(array, 'fsdp', axis=0, tiled=True)  36.7 us
    all_to_all x7, starting transfers between devices, exchange(): return lax.all_to_all(array, 'seq', split_axis=0, concat_axis=0, tiled=True)  30 us
    all_gather x6, waiting for transfers between devices, gather(): return lax.all_gather(array, 'fsdp', axis=0, tiled=True)  23.2 us
  transfers between devices with their start and end apart: 20, of which 11 were waited for; matrix products, arithmetic and copies ran while one was open for 33% of the time, Pallas kernels for 27%

profile of v9, /device:TPU:0, one launch (start us, length us, event | category | flops | bytes accessed | tf_op | source)
XLA Modules:
  0.0 793.0 jit_solution(17613846682216932046)
XLA Ops:
  20.1 11.0 %all-gather = f32[256,128]{1,0:T(8,128)S(1)} all-gather(f32[32,128]{1,0:T(8,128)S(1)} %concatenate.59), channel_id=2, replica_groups=mesh['fsdp'=8,'seq'=4] {'fsdp'}, dimensions={0}, use_global_device_ids=true | all-gather | bytes 147456 | tf_op jit(solution)/shard_map/all_gather | solution.py:597
  37.4 23.0 %all-gather.45.cloned.1.call-done = bf16[1024,3072]{0,1:T(8,128)(2,1)} async-done(((bf16[128,3072]{0,1:T(8,128)(2,1)}), bf16[1024,3072]{0,1:T(8,128)(2,1)}) %all-gather.45.cloned.1.call-update) | async-done | bytes 6291472 | tf_op jit(solution)/shard_map/all_gather | solution.py:225
  60.4 718.9 %conditional.3 = (f32[2,392,1024]{2,1,0:T(8,128)}, f32[2,392,384]{2,1,0:T(8,128)}, f32[2,392,1024]{2,1,0:T(8,128)}, bf16[128,4096]{1,0:T(8,128)(2,1)}, bf16[512,...) conditional(s32[]{:T(128)} %convert_element_type.463, ...), branch_computations={%region_6.52_spmd, %region_51.97_spmd} | conditional | flops 216418254848 | bytes 1266307072
  77.7 6.1 copy.321
  84.5 10.3 %all_gather.58 = bf16[384,384]{1,0:T(8,128)(2,1)S(1)} all-gather(bf16[48,384]{1,0:T(8,128)(2,1)S(1)} %get-tuple-element.357), channel_id=1, replica_groups=mesh['fsdp'=8,'seq'=4] {'fsdp'}, dimensions={0}, use_global_device_ids=true | all-gather | bytes 331776 | tf_op jit(solution)/shard_map/cond/branch_1_fun/all_gather | solution.py:225
  94.8 10.9 %all_gather.56 = bf16[1024,384]{1,0:T(8,128)(2,1)} all-gather(bf16[128,384]{1,0:T(8,128)(2,1)S(1)} %copy-done.87), channel_id=1, replica_groups=mesh['fsdp'=8,'seq'=4] {'fsdp'}, dimensions={0}, use_global_device_ids=true | all-gather | bytes 884736 | tf_op jit(solution)/shard_map/cond/branch_1_fun/all_gather | solution.py:225
  105.7 15.5 %all_gather.57 = bf16[384,1152]{1,0:T(8,128)(2,1)} all-gather(bf16[48,1152]{1,0:T(8,128)(2,1)S(1)} %copy-done.85), channel_id=1, replica_groups=mesh['fsdp'=8,'seq'=4] {'fsdp'}, dimensions={0}, use_global_device_ids=true | all-gather | bytes 995328 | tf_op jit(solution)/shard_map/cond/branch_1_fun/all_gather | solution.py:225
  121.2 27.9 %all-to-all-done.7 = bf16[4,2,192,1024]{3,2,1,0:T(8,128)(2,1)} async-done(((bf16[4,2,192,1024]{3,2,1,0:T(8,128)(2,1)}), bf16[4,2,192,1024]{3,2,1,0:T(8,128)(2,1)}, u32[]{:S(2)}, u32[]{:S(2)}) %all-to-all-start.7) | async-done | bytes 3145760 | tf_op jit(solution)/shard_map/cond/branch_1_fun/all_to_all | solution.py:221
  149.1 11.4 %add_convert_fusion.13 = bf16[1536,2048]{1,0:T(8,128)(2,1)} fusion(bf16[1536,1024]{1,0:T(8,128)(2,1)} %bitcast.101, f32[2048]{0:T(1024)} %concatenate.49, bf16[1024,3072]{0,1:T(8,128)(2,1)} %get-tuple-element.352), kind=kOutput, calls=%fused_computation.202 | convolution fusion | flops 6448742400 | bytes 13639680 | tf_op jit(solution)/shard_map/cond/branch_1_fun/dot_general | solution.py:25
  176.2 23.4 %attend.9 = bf16[2,392,1024]{2,1,0:T(8,128)(2,1)} custom-call(bf16[2,392,1024]{2,1,0:T(8,128)(2,1)} %bitcast.740, bf16[4,2,192,2048]{3,2,1,0:T(8,128)(2,1)} %bitcast.734, bf16[4,2,192,2048]{3,2,1,0:T(8,128)(2,1)} %bitcast.735, f32[2,1,768]{2,1,0:T(1,128)} %compare_select_fusion.1.rest_0_), custom_call_target="tpu_custom_call" | custom-call | flops 9865003008 | bytes 6291456 | tf_op jit(solution)/shard_map/cond/branch_1_fun/attend/pallas_call | solution.py:105
  199.6 5.6 fusion.99
  213.9 22.9 %add_add_fusion.2 = f32[784,1024]{1,0:T(8,128)} fusion(f32[784,1024]{1,0:T(8,128)} %fusion.99, bf16[4096,1024]{1,0:T(8,128)(2,1)} %all-gather.35.cloned.1.call-done, f32[4096]{0:T(1024)} %bitcast.708, bf16[1024,4096]{1,0:T(8,128)(2,1)} %all-gather.33.cloned.1.call-done, f32[1024]{0:T(1024)} %bitcast.731, f32[1024]{0:T(1024)S(1)} %bitcast.685, ...), kind=kOutput, calls=%fused_computation.231 | convolution fusion | flops 13178224640 | bytes 23234688 | tf_op jit(solution)/shard_map/cond/branch_1_fun/dot_general | solution.py:25
  278.3 15.8 %attend.10 = bf16[1,392,384]{2,1,0:T(8,128)(2,1)} custom-call(bf16[1,392,384]{2,1,0:T(8,128)(2,1)} %get-tuple-element.894.q_ref, bf16[1,1,1568,768]{3,2,1,0:T(8,128)(2,1)} %fusion.83.k_ref.v_ref, bf16[1,1,1568,768]{3,2,1,0:T(8,128)(2,1)} %fusion.83.k_ref.v_ref), custom_call_target="tpu_custom_call" | custom-call | flops 7552892928 | bytes 2408448 | tf_op jit(solution)/shard_map/cond/branch_1_fun/attend/pallas_call | solution.py:105
  294.0 11.5 %all-gather.37.cloned.1.call-done = bf16[1568,384]{1,0:T(8,128)(2,1)} async-done(((bf16[392,384]{1,0:T(8,128)(2,1)}), bf16[1568,384]{1,0:T(8,128)(2,1)}) %all-gather.37.cloned.1.call-update) | async-done | bytes 1204240 | tf_op jit(solution)/shard_map/cond/branch_1_fun/all_gather | solution.py:800
  309.7 15.7 %attend.11 = bf16[1,392,384]{2,1,0:T(8,128)(2,1)} custom-call(bf16[1,392,384]{2,1,0:T(8,128)(2,1)} %get-tuple-element.895.q_ref, bf16[1,1,1568,768]{3,2,1,0:T(8,128)(2,1)} %fusion.84.k_ref.v_ref, bf16[1,1,1568,768]{3,2,1,0:T(8,128)(2,1)} %fusion.84.k_ref.v_ref), custom_call_target="tpu_custom_call" | custom-call | flops 7552892928 | bytes 2408448 | tf_op jit(solution)/shard_map/cond/branch_1_fun/attend/pallas_call | solution.py:105
  375.4 5.5 all-to-all-done.8
  386.6 31.3 %attend_back.13 = bf16[4,1,392,288]{3,2,1,0:T(8,128)(2,1)} custom-call(bf16[1,1,1568,96]{3,2,1,0:T(8,128)(2,1)} %fusion.92.q_ref, bf16[1,1,1568,96]{3,2,1,0:T(8,128)(2,1)} %fusion.96.k_ref, bf16[1,1,1568,96]{3,2,1,0:T(8,128)(2,1)} %fusion.91.v_ref, bf16[1,1,1568,96]{3,2,1,0:T(8,128)(2,1)} %bitcast.663), custom_call_target="tpu_custom_call" | custom-call | flops 18882232320 | bytes 2107392 | tf_op jit(solution)/shard_map/cond/branch_1_fun/attend_back/pallas_call | solution.py:205
  426.5 31.3 %attend_back.12 = bf16[4,1,392,288]{3,2,1,0:T(8,128)(2,1)} custom-call(bf16[1,1,1568,96]{3,2,1,0:T(8,128)(2,1)} %fusion.94.q_ref, bf16[1,1,1568,96]{3,2,1,0:T(8,128)(2,1)} %fusion.95.k_ref, bf16[1,1,1568,96]{3,2,1,0:T(8,128)(2,1)} %fusion.93.v_ref, bf16[1,1,1568,96]{3,2,1,0:T(8,128)(2,1)} %bitcast.661), custom_call_target="tpu_custom_call" | custom-call | flops 18882232320 | bytes 2107392 | tf_op jit(solution)/shard_map/cond/branch_1_fun/attend_back/pallas_call | solution.py:205
  465.7 8.8 %convolution_add_fusion.11 = f32[384,4096]{1,0:T(8,128)} fusion(bf16[384,1024]{1,0:T(8,128)(2,1)S(1)} %bitcast.750, bf16[1024,4096]{1,0:T(8,128)(2,1)} %all-gather.33.cloned.1.call-done, f32[4096]{0:T(1024)S(1)} %bitcast.709), kind=kOutput, calls=%fused_computation.217 | convolution fusion | flops 3222798336 | bytes 15482880 | tf_op jit(solution)/shard_map/cond/branch_1_fun/dot_general | solution.py:25
  479.0 14.0 %all-to-all-done.9 = bf16[4,1,392,288]{2,3,1,0:T(8,128)(2,1)} async-done(((bf16[4,1,392,288]{2,3,1,0:T(8,128)(2,1)}), bf16[4,1,392,288]{2,3,1,0:T(8,128)(2,1)}, u32[]{:S(2)}, u32[]{:S(2)}) %all-to-all-start.9) | async-done | bytes 903200 | tf_op jit(solution)/shard_map/cond/branch_1_fun/all_to_all | solution.py:221
  501.3 6.9 convolution_convert_fusion.12
  509.3 8.6 %fusion.194 = (bf16[4096]{0:T(1024)(128)(2,1)S(1)}, bf16[384,4096]{1,0:T(8,128)(2,1)S(1)}) fusion(f32[384,4096]{1,0:T(8,128)} %convolution_add_fusion.11, bf16[384,1024]{1,0:T(8,128)(2,1)S(1)} %copy-done.77, bf16[4096,1024]{1,0:T(8,128)(2,1)} %all-gather.35.cloned.1.call-done), kind=kOutput, calls=%fused_computation.491 | convolution fusion | flops 3238522880 | bytes 18620416 | tf_op jit(solution)/shard_map/cond/branch_1_fun/dot_general | solution.py:25
  519.6 6.7 convolution_convert_fusion.11
  526.3 8.9 %fusion.204 = f32[384,1024]{1,0:T(8,128)} fusion(bf16[384,4096]{1,0:T(8,128)(2,1)} %copy-done.216, bf16[1024,4096]{1,0:T(8,128)(2,1)} %all-gather.33.cloned.1.call-done), kind=kOutput, calls=%fused_computation.501 | convolution fusion | flops 3221225472 | bytes 13107200 | tf_op jit(solution)/shard_map/cond/branch_1_fun/dot_general | solution.py:25
  555.0 13.6 %all-to-all-done.11.g_ref = bf16[4,2,192,256]{3,2,1,0:T(8,128)(2,1)} async-done(((bf16[4,2,192,256]{3,2,1,0:T(8,128)(2,1)}), bf16[4,2,192,256]{3,2,1,0:T(8,128)(2,1)}, u32[]{:S(2)}, u32[]{:S(2)}) %all-to-all-start.11) | async-done | bytes 786464 | tf_op jit(solution)/shard_map/cond/branch_1_fun/all_to_all | solution.py:221
  568.7 10.0 %attend_back.15 = bf16[4,1,192,768]{3,2,1,0:T(8,128)(2,1)} custom-call(bf16[4,2,192,256]{3,2,1,0:T(8,128)(2,1)} %bitcast.746, bf16[4,2,192,256]{3,2,1,0:T(8,128)(2,1)} %bitcast.744, bf16[4,2,192,256]{3,2,1,0:T(8,128)(2,1)} %bitcast.748, bf16[4,2,192,256]{3,2,1,0:T(8,128)(2,1)} %all-to-all-done.11.g_ref, f32[2,1,768]{2,1,0:T(1,128)} %compare_select_fusion.1.rest_0_), custom_call_target="tpu_custom_call" | custom-call | flops 6039797760 | bytes 2752512 | tf_op jit(solution)/shard_map/cond/branch_1_fun/attend_back/pallas_call | solution.py:205
  582.7 10.1 %attend_back.14 = bf16[4,1,192,768]{3,2,1,0:T(8,128)(2,1)} custom-call(bf16[4,2,192,256]{3,2,1,0:T(8,128)(2,1)} %bitcast.747, bf16[4,2,192,256]{3,2,1,0:T(8,128)(2,1)} %bitcast.745, bf16[4,2,192,256]{3,2,1,0:T(8,128)(2,1)} %bitcast.749, bf16[4,2,192,256]{3,2,1,0:T(8,128)(2,1)} %all-to-all-done.11.g_ref, f32[2,1,768]{2,1,0:T(1,128)} %compare_select_fusion.1.rest_0_), custom_call_target="tpu_custom_call" | custom-call | flops 6039797760 | bytes 2752512 | tf_op jit(solution)/shard_map/cond/branch_1_fun/attend_back/pallas_call | solution.py:205
  592.8 6.9 fusion.100
  599.7 10.5 %all-to-all-done.13 = bf16[4,1,192,768]{3,2,1,0:T(8,128)(2,1)S(1)} async-done(((bf16[4,1,192,768]{3,2,1,0:T(8,128)(2,1)}), bf16[4,1,192,768]{3,2,1,0:T(8,128)(2,1)S(1)}, u32[]{:S(2)}, u32[]{:S(2)}) %all-to-all-start.13) | async-done | bytes 1179680 | tf_op jit(solution)/shard_map/cond/branch_1_fun/all_to_all | solution.py:221
  627.1 15.5 %all-to-all-done.12 = bf16[4,1,192,768]{3,2,1,0:T(8,128)(2,1)} async-done(((bf16[4,1,192,768]{3,2,1,0:T(8,128)(2,1)}), bf16[4,1,192,768]{3,2,1,0:T(8,128)(2,1)}, u32[]{:S(2)}, u32[]{:S(2)}) %all-to-all-start.12) | async-done | bytes 1179680 | tf_op jit(solution)/shard_map/cond/branch_1_fun/all_to_all | solution.py:221
  653.4 74.3 %line_sum.6 = (bf16[512,1024]{1,0:T(8,128)(2,1)}, bf16[128,4096]{1,0:T(8,128)(2,1)}, bf16[48,1920]{1,0:T(8,128)(2,1)}, bf16[192,384]{1,0:T(8,128)(2,1)}) custom-call(bf16[512,1024]{1,0:T(8,128)(2,1)} %reduce-scatter.25.cloned.1.call-done.refs_0_, bf16[128,4096]{1,0:T(8,128)(2,1)} %reduce-scatter.29.cloned.1.call-done.refs_1_, ...), custom_call_target="tpu_custom_call" | custom-call | bytes 97157120 | tf_op jit(solution)/shard_map/cond/branch_1_fun/line_sum/pallas_call | solution.py:444
  734.6 36.7 %line_sum.7 = (bf16[128,1536]{1,0:T(8,128)(2,1)}, bf16[4,128,1152]{2,1,0:T(8,128)(2,1)}) custom-call(bf16[128,2688]{1,0:T(8,128)(2,1)} %reduce-scatter.27.cloned.1.call-done.refs_0_), custom_call_target="tpu_custom_call" | custom-call | bytes 27525120 | tf_op jit(solution)/shard_map/cond/branch_1_fun/line_sum/pallas_call | solution.py:444
  (534 shorter events, 258.8 us)
Async XLA Ops:
  7.2 53.2 %all-gather.45.cloned.1.call-start = ((), (), s32[]{:S(2)}) async-start(), calls=%async_computation.48 | async-start | bytes 7077888 | tf_op jit(solution)/shard_map/all_gather | solution.py:225
  35.6 24.8 %copy-start.96 = (bf16[48,384]{1,0:T(8,128)(2,1)S(1)}, bf16[48,384]{1,0:T(8,128)(2,1)}, u32[]{:S(2)}) copy-start(bf16[48,384]{1,0:T(8,128)(2,1)} %param.63) | copy-start | bytes 110596
  66.0 147.9 %copy-start.93 = (f32[8,1,128]{2,1,0:T(1,128)}, f32[8,1,128]{2,1,0:T(1,128)S(1)}, u32[]{:S(2)}) copy-start(f32[8,1,128]{2,1,0:T(1,128)S(1)} %get-tuple-element.367) | copy-start | bytes 12292 | tf_op jit(solution)/shard_map/conditional.1
  66.0 133.6 %all-gather.31.cloned.1.call-start = ((), (), s32[]{:S(2)}) async-start(), calls=%async_computation.36 | async-start | bytes 2359296 | tf_op jit(solution)/shard_map/cond/branch_1_fun/all_gather | solution.py:225
  66.8 146.9 %all-gather.33.cloned.1.call-start = ((), (), s32[]{:S(2)}) async-start(), calls=%async_computation.37 | async-start | bytes 9437184 | tf_op jit(solution)/shard_map/cond/branch_1_fun/all_gather | solution.py:225
  73.0 76.1 %all-to-all-start.7 = ((bf16[4,2,192,1024]{3,2,1,0:T(8,128)(2,1)}), bf16[4,2,192,1024]{3,2,1,0:T(8,128)(2,1)}, u32[]{:S(2)}, u32[]{:S(2)}) async-start(bf16[4,2,192,1024]{3,2,1,0:T(8,128)(2,1)} %broadcast_in_dim.166), calls=%async_computation.12 | async-start | bytes 6291456 | tf_op jit(solution)/shard_map/cond/branch_1_fun/all_to_all | solution.py:221
  77.7 136.2 %all-gather.35.cloned.1.call-start = ((), (), s32[]{:S(2)}) async-start(), calls=%async_computation.38 | async-start | bytes 9437184 | tf_op jit(solution)/shard_map/cond/branch_1_fun/all_gather | solution.py:225
  77.7 28.0 %copy-start.85 = (bf16[48,1152]{1,0:T(8,128)(2,1)S(1)}, bf16[48,1152]{1,0:T(8,128)(2,1)}, u32[]{:S(2)}) copy-start(bf16[48,1152]{1,0:T(8,128)(2,1)} %get-tuple-element.356) | copy-start | bytes 331780 | tf_op jit(solution)/shard_map/conditional.1
  160.5 111.0 %all-gather.39.cloned.1.call-start = ((), (), s32[]{:S(2)}) async-start(), calls=%async_computation.40 | async-start | bytes 1327104 | tf_op jit(solution)/shard_map/cond/branch_1_fun/all_gather | solution.py:225
  176.2 23.4 %copy-start.153 = (f32[8,1,128]{2,1,0:T(1,128)S(1)}, f32[8,1,128]{2,1,0:T(1,128)}, u32[]{:S(2)}) copy-start(f32[8,1,128]{2,1,0:T(1,128)} %get-tuple-element.366) | copy-start | bytes 12292 | tf_op jit(solution)/shard_map/conditional.1
  209.8 64.1 %all-gather.41.cloned.1.call-start = ((), (), s32[]{:S(2)}) async-start(), calls=%async_computation.41 | async-start | bytes 1505280 | tf_op jit(solution)/shard_map/cond/branch_1_fun/all_gather | solution.py:800
  213.9 22.9 %copy-start.128 = (f32[384]{0:T(512)S(1)}, f32[384]{0:T(512)}, u32[]{:S(2)}) copy-start(f32[384]{0:T(512)} %get-tuple-element.376) | copy-start | bytes 4612 | tf_op jit(solution)/shard_map/conditional.1
  213.9 22.9 %copy-start.134 = (pred[784]{0:T(1024)(128)(4,1)S(1)}, pred[784]{0:T(1024)(128)(4,1)}, u32[]{:S(2)}) copy-start(pred[784]{0:T(1024)(128)(4,1)} %broadcast_in_dim.213) | copy-start | bytes 2356 | tf_op jit(solution)/shard_map/conditional.1
  213.9 22.9 %copy-start.145 = (f32[384]{0:T(512)S(1)}, f32[384]{0:T(512)}, u32[]{:S(2)}) copy-start(f32[384]{0:T(512)} %add.623) | copy-start | bytes 4612 | tf_op jit(solution)/shard_map/conditional.1
  213.9 22.9 %copy-start.151 = (pred[784]{0:T(1024)(128)(4,1)S(1)}, pred[784]{0:T(1024)(128)(4,1)}, u32[]{:S(2)}) copy-start(pred[784]{0:T(1024)(128)(4,1)} %compare_and_fusion.1) | copy-start | bytes 2356 | tf_op jit(solution)/shard_map/conditional.1
  242.9 62.7 %all-gather.37.cloned.1.call-start = ((), (), s32[]{:S(2)}) async-start(), calls=%async_computation.39 | async-start | bytes 1505280 | tf_op jit(solution)/shard_map/cond/branch_1_fun/all_gather | solution.py:800
  254.2 82.0 %all-gather.43.cloned.1.call-start = ((), (), s32[]{:S(2)}) async-start(), calls=%async_computation.42 | async-start | bytes 1327104 | tf_op jit(solution)/shard_map/cond/branch_1_fun/all_gather | solution.py:225
  273.9 183.9 %reduce-scatter.23.cloned.1.call-start = ((), (), s32[]{:S(2)}) async-start(), calls=%async_computation.44 | async-start | bytes 1327104 | tf_op jit(solution)/shard_map/cond/branch_1_fun/reduce_scatter | solution.py:229
  278.3 27.3 %copy-start.52 = (bf16[384,1152]{1,0:T(8,128)(2,1)S(1)}, bf16[384,1152]{1,0:T(8,128)(2,1)}, u32[]{:S(2)}) copy-start(bf16[384,1152]{1,0:T(8,128)(2,1)} %all_gather.57) | copy-start | bytes 2654212 | tf_op jit(solution)/shard_map/conditional.1
  357.7 23.3 %all-to-all-start.8 = ((bf16[4,2,392,96]{2,1,3,0:T(2,128)(2,1)}), bf16[4,2,392,96]{2,1,3,0:T(2,128)(2,1)S(1)}, u32[]{:S(2)}, u32[]{:S(2)}) async-start(bf16[4,2,392,96]{2,1,3,0:T(2,128)(2,1)} %reshape.1176), calls=%async_computation.13 | async-start | bytes 1572864 | tf_op jit(solution)/shard_map/cond/branch_1_fun/all_to_all | solution.py:221
  361.2 96.7 %reduce-scatter.21.cloned.1.call-start = ((), (), s32[]{:S(2)}) async-start(), calls=%async_computation.43 | async-start | bytes 1658880 | tf_op jit(solution)/shard_map/cond/branch_1_fun/reduce_scatter | solution.py:229
  386.6 31.3 %copy-start.54 = (bf16[4,1,392,96]{2,1,3,0:T(2,128)(2,1)S(1)}, bf16[4,1,392,96]{2,1,3,0:T(2,128)(2,1)}, u32[]{:S(2)}) copy-start(bf16[4,1,392,96]{2,1,3,0:T(2,128)(2,1)} %get-tuple-element.892) | copy-start | bytes 903172 | tf_op jit(solution)/shard_map/conditional.1
  422.1 38.3 %all-to-all-start.10 = ((bf16[4,1,392,288]{2,3,1,0:T(8,128)(2,1)}), bf16[4,1,392,288]{2,3,1,0:T(8,128)(2,1)}, u32[]{:S(2)}, u32[]{:S(2)}) async-start(bf16[4,1,392,288]{2,3,1,0:T(8,128)(2,1)} %copy.340), calls=%async_computation.17 | async-start | bytes 2359296 | tf_op jit(solution)/shard_map/cond/branch_1_fun/all_to_all | solution.py:221
  460.4 32.6 %all-to-all-start.9 = ((bf16[4,1,392,288]{2,3,1,0:T(8,128)(2,1)}), bf16[4,1,392,288]{2,3,1,0:T(8,128)(2,1)}, u32[]{:S(2)}, u32[]{:S(2)}) async-start(bf16[4,1,392,288]{2,3,1,0:T(8,128)(2,1)} %copy.332), calls=%async_computation.16 | async-start | bytes 2359296 | tf_op jit(solution)/shard_map/cond/branch_1_fun/all_to_all | solution.py:221
  465.4 177.1 %reduce-scatter.25.cloned.1.call-start = ((), (), s32[]{:S(2)}) async-start(), calls=%async_computation.45 | async-start | bytes 9437184 | tf_op jit(solution)/shard_map/cond/branch_1_fun/reduce_scatter | solution.py:229
  508.2 145.1 %reduce-scatter.29.cloned.1.call-start = ((), (), s32[]{:S(2)}) async-start(), calls=%async_computation.47 | async-start | bytes 9437184 | tf_op jit(solution)/shard_map/cond/branch_1_fun/reduce_scatter | solution.py:229
  544.9 23.8 %all-to-all-start.11 = ((bf16[4,2,192,256]{3,2,1,0:T(8,128)(2,1)}), bf16[4,2,192,256]{3,2,1,0:T(8,128)(2,1)}, u32[]{:S(2)}, u32[]{:S(2)}) async-start(bf16[4,2,192,256]{3,2,1,0:T(8,128)(2,1)} %bitcast.158), calls=%async_computation.18 | async-start | bytes 1572864 | tf_op jit(solution)/shard_map/cond/branch_1_fun/all_to_all | solution.py:221
  578.6 31.6 %all-to-all-start.13 = ((bf16[4,1,192,768]{3,2,1,0:T(8,128)(2,1)}), bf16[4,1,192,768]{3,2,1,0:T(8,128)(2,1)S(1)}, u32[]{:S(2)}, u32[]{:S(2)}) async-start(bf16[4,1,192,768]{3,2,1,0:T(8,128)(2,1)} %attend_back.15), calls=%async_computation.21 | async-start | bytes 2359296 | tf_op jit(solution)/shard_map/cond/branch_1_fun/all_to_all | solution.py:221
  610.2 32.4 %all-to-all-start.12 = ((bf16[4,1,192,768]{3,2,1,0:T(8,128)(2,1)}), bf16[4,1,192,768]{3,2,1,0:T(8,128)(2,1)}, u32[]{:S(2)}, u32[]{:S(2)}) async-start(bf16[4,1,192,768]{3,2,1,0:T(8,128)(2,1)} %attend_back.14), calls=%async_computation.19 | async-start | bytes 2359296 | tf_op jit(solution)/shard_map/cond/branch_1_fun/all_to_all | solution.py:221
  614.5 120.1 %reduce-scatter.27.cloned.1.call-start = ((), (), s32[]{:S(2)}) async-start(), calls=%async_computation.46 | async-start | bytes 6193152 | tf_op jit(solution)/shard_map/cond/branch_1_fun/reduce_scatter | solution.py:229
  627.1 21.4 %copy-start.55 = (f32[192,1024]{1,0:T(8,128)}, f32[192,1024]{1,0:T(8,128)S(1)}, u32[]{:S(2)}) copy-start(f32[192,1024]{1,0:T(8,128)S(1)} %get-tuple-element.934) | copy-start | bytes 2359300 | tf_op jit(solution)/shard_map/conditional.1
  653.4 75.8 %copy-start.56 = (f32[192,1024]{1,0:T(8,128)S(1)}, f32[192,1024]{1,0:T(8,128)}, u32[]{:S(2)}) copy-start(f32[192,1024]{1,0:T(8,128)} %copy-done.55) | copy-start | bytes 2359300 | tf_op jit(solution)/shard_map/conditional.1
  (126 other events, 718.1 us)
Sparse Core Ops, SparseCore 0:
  10.5 49.8 all-gather.44
  68.9 28.6 all-gather.30
  99.7 57.7 all-gather.32
  160.6 53.2 all-gather.34
  215.8 24.0 all-gather.38
  243.0 30.8 all-gather.40
  275.6 29.9 all-gather.36
  307.6 23.1 all-gather.42
  350.1 35.8 reduce-scatter.22
  389.8 37.7 reduce-scatter.20
  508.3 70.3 reduce-scatter.24
  582.1 71.2 reduce-scatter.28
  657.2 57.8 reduce-scatter.26

commit v10 on v9

--- a/solution.py
+++ b/solution.py
@@ -37,15 +37,54 @@
     return (unit * gain + shift).astype(bf16)
 
 
-def norm_back(value, gain, grad):
-    unit, scale = norm_parts(value)
-    grad_gain = jnp.sum(grad * unit, axis=0)
-    grad_shift = jnp.sum(grad, axis=0)
-    inner = grad * gain
-    inner = inner - jnp.mean(inner, axis=-1, keepdims=True) - unit * jnp.mean(
-        inner * unit, axis=-1, keepdims=True
-    )
-    return scale * inner, grad_gain, grad_shift
+def norm_back_kernel(grad_ref, value_ref, gain_ref, other_ref, total_ref, low_ref, sums_ref):
+    grad = grad_ref[...]
+    value = value_ref[...]
+    center = value - jnp.mean(value, axis=1, keepdims=True)
+    scale = lax.rsqrt(jnp.mean(center * center, axis=1, keepdims=True) + norm_eps)
+    unit = center * scale
+    inner = grad * gain_ref[...]
+    inner = inner - jnp.mean(inner, axis=1, keepdims=True) - unit * jnp.mean(
+        inner * unit, axis=1, keepdims=True
+    )
+    total = other_ref[...] + scale * inner
+    low = total.astype(bf16)
+    total_ref[...] = total
+    low_ref[...] = low
+    rows = [
+        jnp.sum(grad * unit, axis=0, keepdims=True),
+        jnp.sum(grad, axis=0, keepdims=True),
+        jnp.sum(low.astype(f32), axis=0, keepdims=True),
+    ]
+
+    @pl.when(pl.program_id(0) == 0)
+    def _():
+        sums_ref[...] = jnp.zeros_like(sums_ref)
+
+    for index, row in enumerate(rows):
+        sums_ref[index : index + 1] += row
+
+
+def norm_back(value, gain, grad, other):
+    rows, width = value.shape
+    block = max(size for size in range(8, 136, 8) if rows % size == 0)
+    by_row = pl.BlockSpec((block, width), lambda i: (i, 0))
+    total, low, sums = pl.pallas_call(
+        norm_back_kernel,
+        grid=(rows // block,),
+        in_specs=[by_row, by_row, pl.BlockSpec((1, width), lambda i: (0, 0)), by_row],
+        out_specs=[by_row, by_row, pl.BlockSpec((8, width), lambda i: (0, 0))],
+        out_shape=[
+            jax.ShapeDtypeStruct((rows, width), f32),
+            jax.ShapeDtypeStruct((rows, width), bf16),
+            jax.ShapeDtypeStruct((8, width), f32),
+        ],
+        cost_estimate=pl.CostEstimate(
+            flops=20 * rows * width, bytes_accessed=18 * rows * width, transcendentals=rows
+        ),
+        name="norm_back",
+    )(grad, value, gain.reshape(1, width), other)
+    return total, low, sums[0], sums[1], sums[2]
 
 
 def gelu_parts(hidden):
@@ -479,10 +518,9 @@
     grad_expand_bias = jnp.sum(grad_hidden.astype(f32), axis=0)
     grad_normed = mm(grad_hidden, expand, NT)
     grad_normed, grad_expand = lax.optimization_barrier((grad_normed, grad_expand))
-    grad_norm, grad_mid_gain, grad_mid_shift = norm_back(middle, mid_gain, grad_normed)
-    grad_middle = grad_out + grad_norm
-    grad_att = grad_middle.astype(bf16)
-    grad_out_bias = jnp.sum(grad_att.astype(f32), axis=0)
+    grad_middle, grad_att, grad_mid_gain, grad_mid_shift, grad_out_bias = norm_back(
+        middle, mid_gain, grad_normed, grad_out
+    )
     grad_mixed = mm(grad_att, out, NT).astype(bf16)
     small = dict(
         out_bias=grad_out_bias,
@@ -875,10 +913,9 @@
         grad_normed.append(joint_back(exchange(grads), p_by_sender))
     p_small.update(joint_small(p_columns, fsdp_size, seq_size, shard))
     p_own_width = own_width
-    grad_norm, p_small["pre_gain"], p_small["pre_shift"] = norm_back(
-        pred_input, p_vec["pre_gain"], jnp.concatenate(grad_normed, axis=0)
-    )
-    grad_pred_input = grad_middle + grad_norm
+    grad_pred_input, _, p_small["pre_gain"], p_small["pre_shift"], _ = norm_back(
+        pred_input, p_vec["pre_gain"], jnp.concatenate(grad_normed, axis=0), grad_middle
+    )
     grad_mask_token = jnp.sum(jnp.where(own_flat, 0.0, grad_pred_input), axis=0)
     grad_embedded = jnp.where(own_flat, grad_pred_input, 0.0).astype(bf16)
     grad_embed_bias = jnp.sum(grad_embedded.astype(f32), axis=0)
@@ -913,8 +950,8 @@
     grad_embed = mm(context, late_embedded, TN).astype(bf16)
     e_small.update(joint_small(jnp.sum(flat.astype(f32), axis=0), fsdp_size, seq_size, shard))
     grad_normed = jnp.concatenate([joint_back(member, e_by_sender) for member in received], axis=0)
-    grad_norm, e_small["pre_gain"], e_small["pre_shift"] = norm_back(
-        kept_inputs, e_vec["pre_gain"], grad_normed
+    grad_inputs, _, e_small["pre_gain"], e_small["pre_shift"], _ = norm_back(
+        kept_inputs, e_vec["pre_gain"], grad_normed, grad_middle
     )
 
     own_rows = width // fsdp_size
@@ -931,7 +968,7 @@
     small.append(jnp.zeros((fsdp_size, own_rows * 128 - sum(sizes)), f32))
     small = jnp.concatenate(small, axis=1).astype(bf16).reshape(width, 128)
     late = scatter(jnp.concatenate([e_grad_joint, p_grad_joint, e_grad_out, grad_embed, small], axis=1))
-    grad_tokens = put_back(grad_middle + grad_norm)
+    grad_tokens = put_back(grad_inputs)
 
     first = 0 if whole else 2
     contract_sum, expand_sum, p_wide_sum, p_contract_sum = sum_slots(

time: 803 us -> 818 us (1.019)
  Pallas kernels: 248 us -> 267 us
  matrix products: 189 us -> 202 us
    pallas_call x0 -> x4, Pallas kernels: none -> 23.4 us  [norm_back(): pl.pallas_call(norm_back_kernel, grid=(rows // block,), in_specs=[by_row,...]
    dot_general x43, matrix products: 174 us -> 183 us  [mm(): return lax.dot_general(left, right, dims, preferred_element_type=f32)]
  transfers between devices with their start and end apart: 20 -> 20, of which waited for: 11 -> 10; matrix products, arithmetic and copies ran while one was open for 33% -> 31% of each run, Pallas kernels for 27% -> 27%
where the time goes in v10:
time: 818 us; the launch traced here: 807 us
  Pallas kernels  267 us (33%)
  matrix products  202 us (25%)
  waiting for transfers between devices  128 us (16%)
  local copies, waits for them, and re-layouts  60.9 us (7%)
  other arithmetic  49.8 us (6%)
  blocking collectives  46.4 us (6%)
  starting transfers between devices  30 us (4%)
  between operations  16.2 us (2%)
    dot_general x43, matrix products, mm(): return lax.dot_general(left, right, dims, preferred_element_type=f32)  183 us
    pallas_call x2, Pallas kernels, line_sum(): pl.pallas_call(functools.partial(line_kernel, size, tuple(cuts), shares),...  106 us
    all_to_all x7, waiting for transfers between devices, exchange(): return lax.all_to_all(array, 'seq', split_axis=0, concat_axis=0, tiled=True)  87.1 us
    pallas_call x4, Pallas kernels, attend_back(): pl.pallas_call(functools.partial(backward_kernel, 1.0 / math.sqrt(head_si...  82.6 us
    pallas_call x3, Pallas kernels, attend(): pl.pallas_call(functools.partial(forward_kernel, 1.0 / math.sqrt(head_siz...  54.7 us
    all_gather x3, blocking collectives, gather(): return lax.all_gather(array, 'fsdp', axis=0, tiled=True)  35.4 us
    all_to_all x7, starting transfers between devices, exchange(): return lax.all_to_all(array, 'seq', split_axis=0, concat_axis=0, tiled=True)  28.5 us
    all_gather x6, waiting for transfers between devices, gather(): return lax.all_gather(array, 'fsdp', axis=0, tiled=True)  26.7 us
  transfers between devices with their start and end apart: 20, of which 10 were waited for; matrix products, arithmetic and copies ran while one was open for 31% of the time, Pallas kernels for 27%

profile of v10, /device:TPU:0, one launch (start us, length us, event | category | flops | bytes accessed | tf_op | source)
XLA Modules:
  0.0 806.7 jit_solution(8378971896199829748)
XLA Ops:
  20.7 11.0 %all-gather = f32[256,128]{1,0:T(8,128)S(1)} all-gather(f32[32,128]{1,0:T(8,128)S(1)} %concatenate.59), channel_id=2, replica_groups=mesh['fsdp'=8,'seq'=4] {'fsdp'}, dimensions={0}, use_global_device_ids=true | all-gather | bytes 147456 | tf_op jit(solution)/shard_map/all_gather | solution.py:635
  37.2 23.3 %all-gather.45.cloned.1.call-done = bf16[1024,3072]{0,1:T(8,128)(2,1)} async-done(((bf16[128,3072]{0,1:T(8,128)(2,1)}), bf16[1024,3072]{0,1:T(8,128)(2,1)}) %all-gather.45.cloned.1.call-update) | async-done | bytes 6291472 | tf_op jit(solution)/shard_map/all_gather | solution.py:264
  60.5 733.9 %conditional.3 = (f32[2,392,1024]{2,1,0:T(8,128)}, f32[2,392,384]{2,1,0:T(8,128)}, f32[2,392,1024]{2,1,0:T(8,128)}, bf16[128,4096]{1,0:T(8,128)(2,1)}, bf16[512,...) conditional(s32[]{:T(128)} %convert_element_type.439, ...), branch_computations={%region_6.28_spmd, %region_27.49_spmd} | conditional | flops 216414322688 | bytes 1175043584
  82.9 11.2 %all_gather.58 = bf16[384,384]{1,0:T(8,128)(2,1)} all-gather(bf16[48,384]{1,0:T(8,128)(2,1)S(1)} %get-tuple-element.367), channel_id=1, replica_groups=mesh['fsdp'=8,'seq'=4] {'fsdp'}, dimensions={0}, use_global_device_ids=true | all-gather | bytes 331776 | tf_op jit(solution)/shard_map/cond/branch_1_fun/all_gather | solution.py:264
  94.1 9.6 %all_gather.56 = bf16[1024,384]{1,0:T(8,128)(2,1)S(1)} all-gather(bf16[128,384]{1,0:T(8,128)(2,1)S(1)} %get-tuple-element.365), channel_id=1, replica_groups=mesh['fsdp'=8,'seq'=4] {'fsdp'}, dimensions={0}, use_global_device_ids=true | all-gather | bytes 884736 | tf_op jit(solution)/shard_map/cond/branch_1_fun/all_gather | solution.py:264
  103.7 14.6 %all_gather.57 = bf16[384,1152]{1,0:T(8,128)(2,1)} all-gather(bf16[48,1152]{1,0:T(8,128)(2,1)S(1)} %get-tuple-element.366), channel_id=1, replica_groups=mesh['fsdp'=8,'seq'=4] {'fsdp'}, dimensions={0}, use_global_device_ids=true | all-gather | bytes 995328 | tf_op jit(solution)/shard_map/cond/branch_1_fun/all_gather | solution.py:264
  118.3 29.9 %all-to-all-done.7 = bf16[4,2,192,1024]{3,2,1,0:T(8,128)(2,1)} async-done(((bf16[4,2,192,1024]{3,2,1,0:T(8,128)(2,1)}), bf16[4,2,192,1024]{3,2,1,0:T(8,128)(2,1)}, u32[]{:S(2)}, u32[]{:S(2)}) %all-to-all-start.7) | async-done | bytes 3145760 | tf_op jit(solution)/shard_map/cond/branch_1_fun/all_to_all | solution.py:260
  148.2 11.4 %add_convert_fusion.11 = bf16[1536,2048]{1,0:T(8,128)(2,1)} fusion(bf16[1536,1024]{1,0:T(8,128)(2,1)} %bitcast.99, f32[2048]{0:T(1024)S(1)} %concatenate.49, bf16[1024,3072]{0,1:T(8,128)(2,1)} %get-tuple-element.362), kind=kOutput, calls=%fused_computation.169 | convolution fusion | flops 6448742400 | bytes 13639680 | tf_op jit(solution)/shard_map/cond/branch_1_fun/dot_general | solution.py:25
  170.8 23.4 %attend.9 = bf16[2,392,1024]{2,1,0:T(8,128)(2,1)} custom-call(bf16[2,392,1024]{2,1,0:T(8,128)(2,1)} %bitcast.731, bf16[4,2,192,2048]{3,2,1,0:T(8,128)(2,1)} %bitcast.725, bf16[4,2,192,2048]{3,2,1,0:T(8,128)(2,1)} %bitcast.726, f32[2,1,768]{2,1,0:T(1,128)} %compare_select_fusion.1.rest_0_), custom_call_target="tpu_custom_call" | custom-call | flops 9865003008 | bytes 6291456 | tf_op jit(solution)/shard_map/cond/branch_1_fun/attend/pallas_call | solution.py:144
  194.1 6.7 fusion.96
  212.9 22.9 %add_add_fusion.2 = f32[784,1024]{1,0:T(8,128)} fusion(f32[784,1024]{1,0:T(8,128)} %fusion.96, bf16[4096,1024]{1,0:T(8,128)(2,1)} %all-gather.35.cloned.1.call-done, f32[4096]{0:T(1024)S(1)} %bitcast.696, bf16[1024,4096]{1,0:T(8,128)(2,1)} %all-gather.33.cloned.1.call-done, f32[1024]{0:T(1024)S(1)} %bitcast.721, f32[1024]{0:T(1024)S(1)} %bitcast.677, ...), kind=kOutput, calls=%fused_computation.198 | convolution fusion | flops 13178224640 | bytes 23234688 | tf_op jit(solution)/shard_map/cond/branch_1_fun/dot_general | solution.py:25
  276.6 15.7 %attend.10 = bf16[1,392,384]{2,1,0:T(8,128)(2,1)} custom-call(bf16[1,392,384]{2,1,0:T(8,128)(2,1)} %get-tuple-element.1096.q_ref, bf16[1,1,1568,768]{3,2,1,0:T(8,128)(2,1)} %fusion.80.k_ref.v_ref, bf16[1,1,1568,768]{3,2,1,0:T(8,128)(2,1)} %fusion.80.k_ref.v_ref), custom_call_target="tpu_custom_call" | custom-call | flops 7552892928 | bytes 2408448 | tf_op jit(solution)/shard_map/cond/branch_1_fun/attend/pallas_call | solution.py:144
  292.3 11.7 %all-gather.41.cloned.1.call-done = bf16[1568,384]{1,0:T(8,128)(2,1)} async-done(((bf16[392,384]{1,0:T(8,128)(2,1)}), bf16[1568,384]{1,0:T(8,128)(2,1)}) %all-gather.41.cloned.1.call-update) | async-done | bytes 1204240 | tf_op jit(solution)/shard_map/cond/branch_1_fun/all_gather | solution.py:838
  308.2 15.6 %attend.11 = bf16[1,392,384]{2,1,0:T(8,128)(2,1)} custom-call(bf16[1,392,384]{2,1,0:T(8,128)(2,1)} %get-tuple-element.1095.q_ref, bf16[1,1,1568,768]{3,2,1,0:T(8,128)(2,1)} %fusion.81.k_ref.v_ref, bf16[1,1,1568,768]{3,2,1,0:T(8,128)(2,1)} %fusion.81.k_ref.v_ref), custom_call_target="tpu_custom_call" | custom-call | flops 7552892928 | bytes 2408448 | tf_op jit(solution)/shard_map/cond/branch_1_fun/attend/pallas_call | solution.py:144
  380.9 6.4 all-to-all-done.8
  393.0 31.2 %attend_back.13 = bf16[4,1,392,288]{3,2,1,0:T(8,128)(2,1)} custom-call(bf16[1,1,1568,96]{3,2,1,0:T(8,128)(2,1)} %fusion.89.q_ref, bf16[1,1,1568,96]{3,2,1,0:T(8,128)(2,1)} %fusion.93.k_ref, bf16[1,1,1568,96]{3,2,1,0:T(8,128)(2,1)} %fusion.88.v_ref, bf16[1,1,1568,96]{3,2,1,0:T(8,128)(2,1)} %bitcast.655), custom_call_target="tpu_custom_call" | custom-call | flops 18882232320 | bytes 2107392 | tf_op jit(solution)/shard_map/cond/branch_1_fun/attend_back/pallas_call | solution.py:244
  432.1 31.2 %attend_back.12 = bf16[4,1,392,288]{3,2,1,0:T(8,128)(2,1)} custom-call(bf16[1,1,1568,96]{3,2,1,0:T(8,128)(2,1)} %fusion.91.q_ref, bf16[1,1,1568,96]{3,2,1,0:T(8,128)(2,1)} %fusion.92.k_ref, bf16[1,1,1568,96]{3,2,1,0:T(8,128)(2,1)} %fusion.90.v_ref, bf16[1,1,1568,96]{3,2,1,0:T(8,128)(2,1)} %bitcast.653), custom_call_target="tpu_custom_call" | custom-call | flops 18882232320 | bytes 2107392 | tf_op jit(solution)/shard_map/cond/branch_1_fun/attend_back/pallas_call | solution.py:244
  472.0 9.0 %convolution_add_fusion.11 = f32[384,4096]{1,0:T(8,128)} fusion(bf16[384,1024]{1,0:T(8,128)(2,1)S(1)} %bitcast.741, bf16[1024,4096]{1,0:T(8,128)(2,1)} %all-gather.33.cloned.1.call-done, f32[4096]{0:T(1024)S(1)} %bitcast.697), kind=kOutput, calls=%fused_computation.184 | convolution fusion | flops 3222798336 | bytes 15482880 | tf_op jit(solution)/shard_map/cond/branch_1_fun/dot_general | solution.py:25
  484.2 15.3 %all-to-all-done.9 = bf16[4,1,392,288]{2,3,1,0:T(8,128)(2,1)} async-done(((bf16[4,1,392,288]{2,3,1,0:T(8,128)(2,1)}), bf16[4,1,392,288]{2,3,1,0:T(8,128)(2,1)}, u32[]{:S(2)}, u32[]{:S(2)}) %all-to-all-start.9) | async-done | bytes 903200 | tf_op jit(solution)/shard_map/cond/branch_1_fun/all_to_all | solution.py:260
  502.6 6.6 norm_back.13
  513.5 8.8 %convolution_convert_fusion.12 = bf16[4096,1024]{1,0:T(8,128)(2,1)} fusion(bf16[384,1024]{1,0:T(8,128)(2,1)S(1)} %get-tuple-element.435, f32[384,4096]{1,0:T(8,128)} %convolution_add_fusion.11), kind=kOutput, calls=%fused_computation.172 | convolution fusion | flops 3233284096 | bytes 15466496 | tf_op jit(solution)/shard_map/cond/branch_1_fun/dot_general | solution.py:25
  522.3 9.4 %fusion.180 = (bf16[4096]{0:T(1024)(128)(2,1)}, bf16[384,4096]{1,0:T(8,128)(2,1)S(1)}) fusion(f32[384,4096]{1,0:T(8,128)} %convolution_add_fusion.11, bf16[384,1024]{1,0:T(8,128)(2,1)S(1)} %get-tuple-element.435, bf16[4096,1024]{1,0:T(8,128)(2,1)} %all-gather.35.cloned.1.call-done), kind=kOutput, calls=%fused_computation.417 | convolution fusion | flops 3238522880 | bytes 18620416 | tf_op jit(solution)/shard_map/cond/branch_1_fun/dot_general | solution.py:25
  533.5 6.9 convolution_convert_fusion.11
  540.4 8.9 %fusion.194.grad_ref = f32[384,1024]{1,0:T(8,128)} fusion(bf16[384,4096]{1,0:T(8,128)(2,1)} %copy-done.169, bf16[1024,4096]{1,0:T(8,128)(2,1)} %all-gather.33.cloned.1.call-done), kind=kOutput, calls=%fused_computation.431 | convolution fusion | flops 3221225472 | bytes 13107200 | tf_op jit(solution)/shard_map/cond/branch_1_fun/dot_general | solution.py:25
  571.4 11.4 %all-to-all-done.11.g_ref = bf16[4,2,192,256]{3,2,1,0:T(8,128)(2,1)S(1)} async-done(((bf16[4,2,192,256]{3,2,1,0:T(8,128)(2,1)}), bf16[4,2,192,256]{3,2,1,0:T(8,128)(2,1)S(1)}, u32[]{:S(2)}, u32[]{:S(2)}) %all-to-all-start.11) | async-done | bytes 786464 | tf_op jit(solution)/shard_map/cond/branch_1_fun/all_to_all | solution.py:260
  583.7 10.0 %attend_back.15 = bf16[4,1,192,768]{3,2,1,0:T(8,128)(2,1)} custom-call(bf16[4,2,192,256]{3,2,1,0:T(8,128)(2,1)} %bitcast.737, bf16[4,2,192,256]{3,2,1,0:T(8,128)(2,1)} %bitcast.735, bf16[4,2,192,256]{3,2,1,0:T(8,128)(2,1)} %bitcast.739, bf16[4,2,192,256]{3,2,1,0:T(8,128)(2,1)} %copy-done.69, f32[2,1,768]{2,1,0:T(1,128)} %compare_select_fusion.1.rest_0_), custom_call_target="tpu_custom_call" | custom-call | flops 6039797760 | bytes 2752512 | tf_op jit(solution)/shard_map/cond/branch_1_fun/attend_back/pallas_call | solution.py:244
  599.4 10.1 %attend_back.14 = bf16[4,1,192,768]{3,2,1,0:T(8,128)(2,1)} custom-call(bf16[4,2,192,256]{3,2,1,0:T(8,128)(2,1)} %bitcast.738, bf16[4,2,192,256]{3,2,1,0:T(8,128)(2,1)} %bitcast.736, bf16[4,2,192,256]{3,2,1,0:T(8,128)(2,1)} %bitcast.740, bf16[4,2,192,256]{3,2,1,0:T(8,128)(2,1)} %copy-done.69, f32[2,1,768]{2,1,0:T(1,128)} %compare_select_fusion.1.rest_0_), custom_call_target="tpu_custom_call" | custom-call | flops 6039797760 | bytes 2752512 | tf_op jit(solution)/shard_map/cond/branch_1_fun/attend_back/pallas_call | solution.py:244
  609.5 6.7 fusion.97
  616.3 9.3 %all-to-all-done.13 = bf16[4,1,192,768]{3,2,1,0:T(8,128)(2,1)S(1)} async-done(((bf16[4,1,192,768]{3,2,1,0:T(8,128)(2,1)}), bf16[4,1,192,768]{3,2,1,0:T(8,128)(2,1)S(1)}, u32[]{:S(2)}, u32[]{:S(2)}) %all-to-all-start.13) | async-done | bytes 1179680 | tf_op jit(solution)/shard_map/cond/branch_1_fun/all_to_all | solution.py:260
  642.3 14.8 %all-to-all-done.12 = bf16[4,1,192,768]{3,2,1,0:T(8,128)(2,1)S(1)} async-done(((bf16[4,1,192,768]{3,2,1,0:T(8,128)(2,1)}), bf16[4,1,192,768]{3,2,1,0:T(8,128)(2,1)S(1)}, u32[]{:S(2)}, u32[]{:S(2)}) %all-to-all-start.12) | async-done | bytes 1179680 | tf_op jit(solution)/shard_map/cond/branch_1_fun/all_to_all | solution.py:260
  670.1 71.4 %line_sum.6 = (bf16[512,1024]{1,0:T(8,128)(2,1)S(1)}, bf16[128,4096]{1,0:T(8,128)(2,1)}, bf16[48,1920]{1,0:T(8,128)(2,1)}, bf16[192,384]{1,0:T(8,128)(2,1)S(1)}) custom-call(bf16[512,1024]{1,0:T(8,128)(2,1)} %reduce-scatter.25.cloned.1.call-done.refs_0_, bf16[128,4096]{1,0:T(8,128)(2,1)} %reduce-scatter.29.cloned.1.call-done.refs_1_, ...), custom_call_target="tpu_custom_call" | custom-call | bytes 97157120 | tf_op jit(solution)/shard_map/cond/branch_1_fun/line_sum/pallas_call | solution.py:483
  746.9 34.9 %line_sum.7 = (bf16[128,1536]{1,0:T(8,128)(2,1)}, bf16[4,128,1152]{2,1,0:T(8,128)(2,1)}) custom-call(bf16[128,2688]{1,0:T(8,128)(2,1)} %reduce-scatter.27.cloned.1.call-done.refs_0_), custom_call_target="tpu_custom_call" | custom-call | bytes 27525120 | tf_op jit(solution)/shard_map/cond/branch_1_fun/line_sum/pallas_call | solution.py:483
  (480 shorter events, 274.2 us)
Async XLA Ops:
  7.2 53.3 %all-gather.45.cloned.1.call-start = ((), (), s32[]{:S(2)}) async-start(), calls=%async_computation.48 | async-start | bytes 7077888 | tf_op jit(solution)/shard_map/all_gather | solution.py:264
  33.3 27.1 %copy-start = (f32[1568,384]{1,0:T(8,128)S(1)}, f32[1568,384]{1,0:T(8,128)}, u32[]{:S(2)}) copy-start(f32[1568,384]{1,0:T(8,128)} %param.41) | copy-start | bytes 7225348
  33.3 27.1 %copy-start.72 = (bf16[48,1152]{1,0:T(8,128)(2,1)S(1)}, bf16[48,1152]{1,0:T(8,128)(2,1)}, u32[]{:S(2)}) copy-start(bf16[48,1152]{1,0:T(8,128)(2,1)} %param.60) | copy-start | bytes 331780
  33.3 27.1 %copy-start.73 = (bf16[128,384]{1,0:T(8,128)(2,1)S(1)}, bf16[128,384]{1,0:T(8,128)(2,1)}, u32[]{:S(2)}) copy-start(bf16[128,384]{1,0:T(8,128)(2,1)} %param.55) | copy-start | bytes 294916
  33.4 27.1 %copy-start.77 = (bf16[48,384]{1,0:T(8,128)(2,1)S(1)}, bf16[48,384]{1,0:T(8,128)(2,1)}, u32[]{:S(2)}) copy-start(bf16[48,384]{1,0:T(8,128)(2,1)} %param.63) | copy-start | bytes 110596
  33.4 27.1 %copy-start.103 = (s32[2,4]{1,0:T(2,128)S(1)}, s32[2,4]{1,0:T(2,128)}, u32[]{:S(2)}) copy-start(s32[2,4]{1,0:T(2,128)} %copy-done.102) | copy-start | bytes 100
  66.2 146.7 %copy-start.80 = (f32[8,1,128]{2,1,0:T(1,128)}, f32[8,1,128]{2,1,0:T(1,128)S(1)}, u32[]{:S(2)}) copy-start(f32[8,1,128]{2,1,0:T(1,128)S(1)} %get-tuple-element.965) | copy-start | bytes 12292 | tf_op jit(solution)/shard_map/conditional.1
  66.2 127.9 %all-gather.31.cloned.1.call-start = ((), (), s32[]{:S(2)}) async-start(), calls=%async_computation.36 | async-start | bytes 2359296 | tf_op jit(solution)/shard_map/cond/branch_1_fun/all_gather | solution.py:264
  66.9 142.5 %all-gather.33.cloned.1.call-start = ((), (), s32[]{:S(2)}) async-start(), calls=%async_computation.37 | async-start | bytes 9437184 | tf_op jit(solution)/shard_map/cond/branch_1_fun/all_gather | solution.py:264
  72.0 76.1 %all-to-all-start.7 = ((bf16[4,2,192,1024]{3,2,1,0:T(8,128)(2,1)}), bf16[4,2,192,1024]{3,2,1,0:T(8,128)(2,1)}, u32[]{:S(2)}, u32[]{:S(2)}) async-start(bf16[4,2,192,1024]{3,2,1,0:T(8,128)(2,1)} %broadcast_in_dim.178), calls=%async_computation.12 | async-start | bytes 6291456 | tf_op jit(solution)/shard_map/cond/branch_1_fun/all_to_all | solution.py:260
  76.7 136.2 %all-gather.35.cloned.1.call-start = ((), (), s32[]{:S(2)}) async-start(), calls=%async_computation.38 | async-start | bytes 9437184 | tf_op jit(solution)/shard_map/cond/branch_1_fun/all_gather | solution.py:264
  103.7 132.2 %copy-start.28 = (bf16[1024,384]{1,0:T(8,128)(2,1)}, bf16[1024,384]{1,0:T(8,128)(2,1)S(1)}, u32[]{:S(2)}) copy-start(bf16[1024,384]{1,0:T(8,128)(2,1)S(1)} %all_gather.56) | copy-start | bytes 2359300 | tf_op jit(solution)/shard_map/conditional.1
  159.6 112.1 %all-gather.37.cloned.1.call-start = ((), (), s32[]{:S(2)}) async-start(), calls=%async_computation.39 | async-start | bytes 1327104 | tf_op jit(solution)/shard_map/cond/branch_1_fun/all_gather | solution.py:264
  205.4 67.0 %all-gather.39.cloned.1.call-start = ((), (), s32[]{:S(2)}) async-start(), calls=%async_computation.40 | async-start | bytes 1505280 | tf_op jit(solution)/shard_map/cond/branch_1_fun/all_gather | solution.py:838
  212.9 23.0 %copy-start.42 = (f32[784,384]{1,0:T(8,128)S(1)}, f32[784,384]{1,0:T(8,128)}, u32[]{:S(2)}) copy-start(f32[784,384]{1,0:T(8,128)} %gather_fusion.1) | copy-start | bytes 3612676 | tf_op jit(solution)/shard_map/conditional.1
  212.9 23.0 %copy-start.92 = (f32[384]{0:T(512)S(1)}, f32[384]{0:T(512)}, u32[]{:S(2)}) copy-start(f32[384]{0:T(512)} %copy-done.91) | copy-start | bytes 4612 | tf_op jit(solution)/shard_map/conditional.1
  239.0 85.9 %copy-start.7 = (f32[784,384]{1,0:T(8,128)}, f32[784,384]{1,0:T(8,128)S(1)}, u32[]{:S(2)}) copy-start(f32[784,384]{1,0:T(8,128)S(1)} %get-tuple-element.1126.value_ref) | copy-start | bytes 3612676 | tf_op jit(solution)/shard_map/conditional.1
  241.4 62.7 %all-gather.41.cloned.1.call-start = ((), (), s32[]{:S(2)}) async-start(), calls=%async_computation.41 | async-start | bytes 1505280 | tf_op jit(solution)/shard_map/cond/branch_1_fun/all_gather | solution.py:838
  251.9 82.8 %all-gather.43.cloned.1.call-start = ((), (), s32[]{:S(2)}) async-start(), calls=%async_computation.42 | async-start | bytes 1327104 | tf_op jit(solution)/shard_map/cond/branch_1_fun/all_gather | solution.py:264
  272.4 190.9 %reduce-scatter.23.cloned.1.call-start = ((), (), s32[]{:S(2)}) async-start(), calls=%async_computation.44 | async-start | bytes 1327104 | tf_op jit(solution)/shard_map/cond/branch_1_fun/reduce_scatter | solution.py:268
  364.0 23.2 %all-to-all-start.8 = ((bf16[4,2,392,96]{2,1,3,0:T(2,128)(2,1)}), bf16[4,2,392,96]{2,1,3,0:T(2,128)(2,1)S(1)}, u32[]{:S(2)}, u32[]{:S(2)}) async-start(bf16[4,2,392,96]{2,1,3,0:T(2,128)(2,1)} %reshape.986), calls=%async_computation.13 | async-start | bytes 1572864 | tf_op jit(solution)/shard_map/cond/branch_1_fun/all_to_all | solution.py:260
  367.5 95.8 %reduce-scatter.21.cloned.1.call-start = ((), (), s32[]{:S(2)}) async-start(), calls=%async_computation.43 | async-start | bytes 1658880 | tf_op jit(solution)/shard_map/cond/branch_1_fun/reduce_scatter | solution.py:268
  428.4 37.5 %all-to-all-start.10 = ((bf16[4,1,392,288]{2,3,1,0:T(8,128)(2,1)}), bf16[4,1,392,288]{2,3,1,0:T(8,128)(2,1)S(1)}, u32[]{:S(2)}, u32[]{:S(2)}) async-start(bf16[4,1,392,288]{2,3,1,0:T(8,128)(2,1)} %copy.362), calls=%async_computation.17 | async-start | bytes 2359296 | tf_op jit(solution)/shard_map/cond/branch_1_fun/all_to_all | solution.py:260
  466.9 32.7 %all-to-all-start.9 = ((bf16[4,1,392,288]{2,3,1,0:T(8,128)(2,1)}), bf16[4,1,392,288]{2,3,1,0:T(8,128)(2,1)}, u32[]{:S(2)}, u32[]{:S(2)}) async-start(bf16[4,1,392,288]{2,3,1,0:T(8,128)(2,1)} %copy.354), calls=%async_computation.16 | async-start | bytes 2359296 | tf_op jit(solution)/shard_map/cond/branch_1_fun/all_to_all | solution.py:260
  471.9 185.2 %reduce-scatter.25.cloned.1.call-start = ((), (), s32[]{:S(2)}) async-start(), calls=%async_computation.45 | async-start | bytes 9437184 | tf_op jit(solution)/shard_map/cond/branch_1_fun/reduce_scatter | solution.py:268
  522.3 147.8 %reduce-scatter.29.cloned.1.call-start = ((), (), s32[]{:S(2)}) async-start(), calls=%async_computation.47 | async-start | bytes 9437184 | tf_op jit(solution)/shard_map/cond/branch_1_fun/reduce_scatter | solution.py:268
  550.2 47.5 %copy-start.115 = (pred[8]{0:T(512)(128)(4,1)}, pred[8]{0:T(512)(128)(4,1)S(1)}, u32[]{:S(2)}) copy-start(pred[8]{0:T(512)(128)(4,1)S(1)} %fusion.146) | copy-start | bytes 28 | tf_op jit(solution)/shard_map/conditional.1
  559.4 23.4 %all-to-all-start.11 = ((bf16[4,2,192,256]{3,2,1,0:T(8,128)(2,1)}), bf16[4,2,192,256]{3,2,1,0:T(8,128)(2,1)S(1)}, u32[]{:S(2)}, u32[]{:S(2)}) async-start(bf16[4,2,192,256]{3,2,1,0:T(8,128)(2,1)} %bitcast.158), calls=%async_computation.18 | async-start | bytes 1572864 | tf_op jit(solution)/shard_map/cond/branch_1_fun/all_to_all | solution.py:260
  593.8 31.8 %all-to-all-start.13 = ((bf16[4,1,192,768]{3,2,1,0:T(8,128)(2,1)}), bf16[4,1,192,768]{3,2,1,0:T(8,128)(2,1)S(1)}, u32[]{:S(2)}, u32[]{:S(2)}) async-start(bf16[4,1,192,768]{3,2,1,0:T(8,128)(2,1)} %attend_back.15), calls=%async_computation.21 | async-start | bytes 2359296 | tf_op jit(solution)/shard_map/cond/branch_1_fun/all_to_all | solution.py:260
  625.6 31.6 %all-to-all-start.12 = ((bf16[4,1,192,768]{3,2,1,0:T(8,128)(2,1)}), bf16[4,1,192,768]{3,2,1,0:T(8,128)(2,1)S(1)}, u32[]{:S(2)}, u32[]{:S(2)}) async-start(bf16[4,1,192,768]{3,2,1,0:T(8,128)(2,1)} %attend_back.14), calls=%async_computation.19 | async-start | bytes 2359296 | tf_op jit(solution)/shard_map/cond/branch_1_fun/all_to_all | solution.py:260
  629.2 117.7 %reduce-scatter.27.cloned.1.call-start = ((), (), s32[]{:S(2)}) async-start(), calls=%async_computation.46 | async-start | bytes 6193152 | tf_op jit(solution)/shard_map/cond/branch_1_fun/reduce_scatter | solution.py:268
  670.0 72.8 %copy-start.64 = (f32[384,1024]{1,0:T(8,128)S(1)}, f32[384,1024]{1,0:T(8,128)}, u32[]{:S(2)}) copy-start(f32[384,1024]{1,0:T(8,128)} %get-tuple-element.446) | copy-start | bytes 4718596 | tf_op jit(solution)/shard_map/conditional.1
  (103 other events, 565.4 us)
Sparse Core Ops, SparseCore 0:
  10.5 49.9 all-gather.44
  69.1 28.6 all-gather.30
  99.9 56.6 all-gather.32
  159.7 53.1 all-gather.34
  214.8 24.0 all-gather.36
  241.5 30.8 all-gather.38
  274.1 29.9 all-gather.40
  306.1 23.1 all-gather.42
  357.3 35.9 reduce-scatter.22
  397.1 37.7 reduce-scatter.20
  522.4 70.3 reduce-scatter.24
  596.1 71.2 reduce-scatter.28
  671.3 57.8 reduce-scatter.26

commit v11 on v9

--- a/solution.py
+++ b/solution.py
@@ -739,8 +739,14 @@
     normed_all = exchange(jnp.broadcast_to(normed_kept, (seq_size, clips, held, width)))
     embed, p_joint, p_out = gather(embed_shard), gather(p_joint_shard), gather(p_out_shard)
     e_by_sender = by_sender(e_joint, seq_size)
-    normed_all, embed, p_joint, p_out, e_by_sender = lax.optimization_barrier(
-        (normed_all, embed, p_joint, p_out, e_by_sender)
+    p_by_sender = by_sender(p_joint, seq_size)
+    p_own_weight = own_joint(
+        p_joint, p_vec["query_bias"], p_vec["value_bias"], seq_size, shard
+    )[0]
+    normed_all, embed, p_joint, p_out, e_by_sender, p_by_sender, p_own_weight = (
+        lax.optimization_barrier(
+            (normed_all, embed, p_joint, p_out, e_by_sender, p_by_sender, p_own_weight)
+        )
     )
     queries = (mm(normed, e_joint[:, :width]) + e_vec["query_bias"]).astype(bf16)
     joined = mm(normed_all.reshape(-1, width), e_joint[:, width:])
@@ -847,13 +853,11 @@
     p_tall = p_grads[1]
     grad_mixed, p_wide, p_tall = lax.optimization_barrier((grad_mixed, p_wide, p_tall))
     p_wide, p_tall = scatter(p_wide), scatter(p_tall)
-    own_weight, own_bias = own_joint(
-        p_joint, p_vec["query_bias"], p_vec["value_bias"], seq_size, shard
-    )
+    own_weight = p_own_weight
+    _, own_bias = own_joint(p_joint, p_vec["query_bias"], p_vec["value_bias"], seq_size, shard)
     own_width = small_width // seq_size
     grad_mixed = grad_mixed.reshape(rows, seq_size, own_width).transpose(1, 0, 2)
     grad_mixed = exchange(grad_mixed.reshape(seq_size, clips, slots, own_width))
-    p_by_sender = by_sender(p_joint, seq_size)
     grad_normed = []
     p_grad_joint = 0.0
     p_columns = 0.0

time: 803 us -> 801 us (level)
  transfers between devices with their start and end apart: 20 -> 20, of which waited for: 11 -> 10; matrix products, arithmetic and copies ran while one was open for 33% -> 33% of each run, Pallas kernels for 27% -> 27%
where the time goes in v11:
time: 801 us; the launch traced here: 791 us
  Pallas kernels  249 us (31%)
  matrix products  188 us (23%)
  waiting for transfers between devices  127 us (16%)
  local copies, waits for them, and re-layouts  69.7 us (9%)
  other arithmetic  55.1 us (7%)
  blocking collectives  46.8 us (6%)
  starting transfers between devices  31.5 us (4%)
  between operations  16.3 us (2%)
    dot_general x43, matrix products, mm(): return lax.dot_general(left, right, dims, preferred_element_type=f32)  173 us
    pallas_call x2, Pallas kernels, line_sum(): pl.pallas_call(functools.partial(line_kernel, size, tuple(cuts), shares),...  111 us
    all_to_all x7, waiting for transfers between devices, exchange(): return lax.all_to_all(array, 'seq', split_axis=0, concat_axis=0, tiled=True)  86.8 us
    pallas_call x4, Pallas kernels, attend_back(): pl.pallas_call(functools.partial(backward_kernel, 1.0 / math.sqrt(head_si...  82.6 us
    pallas_call x3, Pallas kernels, attend(): pl.pallas_call(functools.partial(forward_kernel, 1.0 / math.sqrt(head_siz...  54.8 us
    all_gather x3, blocking collectives, gather(): return lax.all_gather(array, 'fsdp', axis=0, tiled=True)  35.8 us
    all_to_all x7, starting transfers between devices, exchange(): return lax.all_to_all(array, 'seq', split_axis=0, concat_axis=0, tiled=True)  30 us
    all_gather x6, waiting for transfers between devices, gather(): return lax.all_gather(array, 'fsdp', axis=0, tiled=True)  23.4 us
  transfers between devices with their start and end apart: 20, of which 10 were waited for; matrix products, arithmetic and copies ran while one was open for 33% of the time, Pallas kernels for 27%

profile of v11, /device:TPU:0, one launch (start us, length us, event | category | flops | bytes accessed | tf_op | source)
XLA Modules:
  0.0 790.9 jit_solution(8752148232527560033)
XLA Ops:
  19.8 11.0 %all-gather = f32[256,128]{1,0:T(8,128)S(1)} all-gather(f32[32,128]{1,0:T(8,128)S(1)} %concatenate.59), channel_id=2, replica_groups=mesh['fsdp'=8,'seq'=4] {'fsdp'}, dimensions={0}, use_global_device_ids=true | all-gather | bytes 147456 | tf_op jit(solution)/shard_map/all_gather | solution.py:597
  37.0 23.4 %all-gather.45.cloned.1.call-done = bf16[1024,3072]{0,1:T(8,128)(2,1)} async-done(((bf16[128,3072]{0,1:T(8,128)(2,1)}), bf16[1024,3072]{0,1:T(8,128)(2,1)}) %all-gather.45.cloned.1.call-update) | async-done | bytes 6291472 | tf_op jit(solution)/shard_map/all_gather | solution.py:225
  60.4 716.8 %conditional.3 = (f32[2,392,1024]{2,1,0:T(8,128)}, f32[2,392,384]{2,1,0:T(8,128)}, f32[2,392,1024]{2,1,0:T(8,128)}, bf16[128,4096]{1,0:T(8,128)(2,1)}, bf16[512,...) conditional(s32[]{:T(128)} %convert_element_type.463, ...), branch_computations={%region_6.52_spmd, %region_51.97_spmd} | conditional | flops 216418254848 | bytes 1263260160
  77.5 12.2 %all_gather.57 = bf16[384,1152]{1,0:T(8,128)(2,1)} all-gather(bf16[48,1152]{1,0:T(8,128)(2,1)S(1)} %get-tuple-element.358), channel_id=1, replica_groups=mesh['fsdp'=8,'seq'=4] {'fsdp'}, dimensions={0}, use_global_device_ids=true | all-gather | bytes 995328 | tf_op jit(solution)/shard_map/cond/branch_1_fun/all_gather | solution.py:225
  94.1 6.2 copy.321
  100.9 8.4 %all_gather.58 = bf16[384,384]{1,0:T(8,128)(2,1)S(1)} all-gather(bf16[48,384]{1,0:T(8,128)(2,1)S(1)} %get-tuple-element.359), channel_id=1, replica_groups=mesh['fsdp'=8,'seq'=4] {'fsdp'}, dimensions={0}, use_global_device_ids=true | all-gather | bytes 331776 | tf_op jit(solution)/shard_map/cond/branch_1_fun/all_gather | solution.py:225
  111.0 15.2 %all_gather.56 = bf16[1024,384]{1,0:T(8,128)(2,1)} all-gather(bf16[128,384]{1,0:T(8,128)(2,1)} %get-tuple-element.357), channel_id=1, replica_groups=mesh['fsdp'=8,'seq'=4] {'fsdp'}, dimensions={0}, use_global_device_ids=true | all-gather | bytes 884736 | tf_op jit(solution)/shard_map/cond/branch_1_fun/all_gather | solution.py:225
  126.2 22.7 %all-to-all-done.7 = bf16[4,2,192,1024]{3,2,1,0:T(8,128)(2,1)} async-done(((bf16[4,2,192,1024]{3,2,1,0:T(8,128)(2,1)}), bf16[4,2,192,1024]{3,2,1,0:T(8,128)(2,1)}, u32[]{:S(2)}, u32[]{:S(2)}) %all-to-all-start.7) | async-done | bytes 3145760 | tf_op jit(solution)/shard_map/cond/branch_1_fun/all_to_all | solution.py:221
  148.9 11.5 %add_convert_fusion.13 = bf16[1536,2048]{1,0:T(8,128)(2,1)} fusion(bf16[1536,1024]{1,0:T(8,128)(2,1)} %bitcast.105, f32[2048]{0:T(1024)} %concatenate.49, bf16[1024,3072]{0,1:T(8,128)(2,1)} %get-tuple-element.354), kind=kOutput, calls=%fused_computation.206 | convolution fusion | flops 6448742400 | bytes 13639680 | tf_op jit(solution)/shard_map/cond/branch_1_fun/dot_general | solution.py:25
  176.4 23.4 %attend.9 = bf16[2,392,1024]{2,1,0:T(8,128)(2,1)} custom-call(bf16[2,392,1024]{2,1,0:T(8,128)(2,1)} %bitcast.736, bf16[4,2,192,2048]{3,2,1,0:T(8,128)(2,1)} %bitcast.730, bf16[4,2,192,2048]{3,2,1,0:T(8,128)(2,1)} %bitcast.731, f32[2,1,768]{2,1,0:T(1,128)} %compare_select_fusion.1.rest_0_), custom_call_target="tpu_custom_call" | custom-call | flops 9865003008 | bytes 6291456 | tf_op jit(solution)/shard_map/cond/branch_1_fun/attend/pallas_call | solution.py:105
  199.8 5.7 fusion.105
  214.2 22.9 %add_add_fusion.2 = f32[784,1024]{1,0:T(8,128)} fusion(f32[784,1024]{1,0:T(8,128)} %fusion.105, bf16[4096,1024]{1,0:T(8,128)(2,1)} %all-gather.35.cloned.1.call-done, f32[4096]{0:T(1024)} %bitcast.704, bf16[1024,4096]{1,0:T(8,128)(2,1)} %all-gather.33.cloned.1.call-done, f32[1024]{0:T(1024)} %bitcast.727, f32[1024]{0:T(1024)S(1)} %bitcast.681, ...), kind=kOutput, calls=%fused_computation.235 | convolution fusion | flops 13178224640 | bytes 23234688 | tf_op jit(solution)/shard_map/cond/branch_1_fun/dot_general | solution.py:25
  277.8 15.8 %attend.10 = bf16[1,392,384]{2,1,0:T(8,128)(2,1)} custom-call(bf16[1,392,384]{2,1,0:T(8,128)(2,1)} %get-tuple-element.898.q_ref, bf16[1,1,1568,768]{3,2,1,0:T(8,128)(2,1)} %fusion.89.k_ref.v_ref, bf16[1,1,1568,768]{3,2,1,0:T(8,128)(2,1)} %fusion.89.k_ref.v_ref), custom_call_target="tpu_custom_call" | custom-call | flops 7552892928 | bytes 2408448 | tf_op jit(solution)/shard_map/cond/branch_1_fun/attend/pallas_call | solution.py:105
  293.5 11.5 %all-gather.37.cloned.1.call-done = bf16[1568,384]{1,0:T(8,128)(2,1)} async-done(((bf16[392,384]{1,0:T(8,128)(2,1)}), bf16[1568,384]{1,0:T(8,128)(2,1)}) %all-gather.37.cloned.1.call-update) | async-done | bytes 1204240 | tf_op jit(solution)/shard_map/cond/branch_1_fun/all_gather | solution.py:806
  309.2 15.7 %attend.11 = bf16[1,392,384]{2,1,0:T(8,128)(2,1)} custom-call(bf16[1,392,384]{2,1,0:T(8,128)(2,1)} %get-tuple-element.899.q_ref, bf16[1,1,1568,768]{3,2,1,0:T(8,128)(2,1)} %fusion.90.k_ref.v_ref, bf16[1,1,1568,768]{3,2,1,0:T(8,128)(2,1)} %fusion.90.k_ref.v_ref), custom_call_target="tpu_custom_call" | custom-call | flops 7552892928 | bytes 2408448 | tf_op jit(solution)/shard_map/cond/branch_1_fun/attend/pallas_call | solution.py:105
  367.6 10.7 %all-to-all-done.8 = bf16[4,2,392,96]{2,1,3,0:T(2,128)(2,1)S(1)} async-done(((bf16[4,2,392,96]{2,1,3,0:T(2,128)(2,1)}), bf16[4,2,392,96]{2,1,3,0:T(2,128)(2,1)S(1)}, u32[]{:S(2)}, u32[]{:S(2)}) %all-to-all-start.8) | async-done | bytes 602144 | tf_op jit(solution)/shard_map/cond/branch_1_fun/all_to_all | solution.py:221
  384.4 31.3 %attend_back.13 = bf16[4,1,392,288]{3,2,1,0:T(8,128)(2,1)} custom-call(bf16[1,1,1568,96]{3,2,1,0:T(8,128)(2,1)} %fusion.98.q_ref, bf16[1,1,1568,96]{3,2,1,0:T(8,128)(2,1)} %fusion.102.k_ref, bf16[1,1,1568,96]{3,2,1,0:T(8,128)(2,1)} %fusion.97.v_ref, bf16[1,1,1568,96]{3,2,1,0:T(8,128)(2,1)} %bitcast.659), custom_call_target="tpu_custom_call" | custom-call | flops 18882232320 | bytes 2107392 | tf_op jit(solution)/shard_map/cond/branch_1_fun/attend_back/pallas_call | solution.py:205
  424.3 31.2 %attend_back.12 = bf16[4,1,392,288]{3,2,1,0:T(8,128)(2,1)} custom-call(bf16[1,1,1568,96]{3,2,1,0:T(8,128)(2,1)} %fusion.100.q_ref, bf16[1,1,1568,96]{3,2,1,0:T(8,128)(2,1)} %fusion.101.k_ref, bf16[1,1,1568,96]{3,2,1,0:T(8,128)(2,1)} %fusion.99.v_ref, bf16[1,1,1568,96]{3,2,1,0:T(8,128)(2,1)} %bitcast.657), custom_call_target="tpu_custom_call" | custom-call | flops 18882232320 | bytes 2107392 | tf_op jit(solution)/shard_map/cond/branch_1_fun/attend_back/pallas_call | solution.py:205
  463.1 9.0 %convolution_add_fusion.11 = f32[384,4096]{1,0:T(8,128)} fusion(bf16[384,1024]{1,0:T(8,128)(2,1)S(1)} %bitcast.746, bf16[1024,4096]{1,0:T(8,128)(2,1)} %all-gather.33.cloned.1.call-done, f32[4096]{0:T(1024)S(1)} %bitcast.705), kind=kOutput, calls=%fused_computation.221 | convolution fusion | flops 3222798336 | bytes 15482880 | tf_op jit(solution)/shard_map/cond/branch_1_fun/dot_general | solution.py:25
  476.6 14.0 %all-to-all-done.9 = bf16[4,1,392,288]{2,3,1,0:T(8,128)(2,1)} async-done(((bf16[4,1,392,288]{2,3,1,0:T(8,128)(2,1)}), bf16[4,1,392,288]{2,3,1,0:T(8,128)(2,1)}, u32[]{:S(2)}, u32[]{:S(2)}) %all-to-all-start.9) | async-done | bytes 903200 | tf_op jit(solution)/shard_map/cond/branch_1_fun/all_to_all | solution.py:221
  499.0 6.8 convolution_convert_fusion.12
  507.0 9.2 %fusion.206 = (bf16[4096]{0:T(1024)(128)(2,1)S(1)}, bf16[384,4096]{1,0:T(8,128)(2,1)S(1)}) fusion(f32[384,4096]{1,0:T(8,128)} %convolution_add_fusion.11, bf16[384,1024]{1,0:T(8,128)(2,1)S(1)} %copy-done.78, bf16[4096,1024]{1,0:T(8,128)(2,1)} %all-gather.35.cloned.1.call-done), kind=kOutput, calls=%fused_computation.499 | convolution fusion | flops 3238522880 | bytes 18620416 | tf_op jit(solution)/shard_map/cond/branch_1_fun/dot_general | solution.py:25
  517.9 6.7 convolution_convert_fusion.11
  524.6 8.9 %fusion.216 = f32[384,1024]{1,0:T(8,128)} fusion(bf16[384,4096]{1,0:T(8,128)(2,1)} %copy-done.215, bf16[1024,4096]{1,0:T(8,128)(2,1)} %all-gather.33.cloned.1.call-done), kind=kOutput, calls=%fused_computation.509 | convolution fusion | flops 3221225472 | bytes 13107200 | tf_op jit(solution)/shard_map/cond/branch_1_fun/dot_general | solution.py:25
  553.5 13.4 %all-to-all-done.11.g_ref = bf16[4,2,192,256]{3,2,1,0:T(8,128)(2,1)} async-done(((bf16[4,2,192,256]{3,2,1,0:T(8,128)(2,1)}), bf16[4,2,192,256]{3,2,1,0:T(8,128)(2,1)}, u32[]{:S(2)}, u32[]{:S(2)}) %all-to-all-start.11) | async-done | bytes 786464 | tf_op jit(solution)/shard_map/cond/branch_1_fun/all_to_all | solution.py:221
  566.9 10.0 %attend_back.15 = bf16[4,1,192,768]{3,2,1,0:T(8,128)(2,1)} custom-call(bf16[4,2,192,256]{3,2,1,0:T(8,128)(2,1)} %bitcast.742, bf16[4,2,192,256]{3,2,1,0:T(8,128)(2,1)} %bitcast.740, bf16[4,2,192,256]{3,2,1,0:T(8,128)(2,1)} %bitcast.744, bf16[4,2,192,256]{3,2,1,0:T(8,128)(2,1)} %all-to-all-done.11.g_ref, f32[2,1,768]{2,1,0:T(1,128)} %compare_select_fusion.1.rest_0_), custom_call_target="tpu_custom_call" | custom-call | flops 6039797760 | bytes 2752512 | tf_op jit(solution)/shard_map/cond/branch_1_fun/attend_back/pallas_call | solution.py:205
  580.9 10.1 %attend_back.14 = bf16[4,1,192,768]{3,2,1,0:T(8,128)(2,1)} custom-call(bf16[4,2,192,256]{3,2,1,0:T(8,128)(2,1)} %bitcast.743, bf16[4,2,192,256]{3,2,1,0:T(8,128)(2,1)} %bitcast.741, bf16[4,2,192,256]{3,2,1,0:T(8,128)(2,1)} %bitcast.745, bf16[4,2,192,256]{3,2,1,0:T(8,128)(2,1)} %all-to-all-done.11.g_ref, f32[2,1,768]{2,1,0:T(1,128)} %compare_select_fusion.1.rest_0_), custom_call_target="tpu_custom_call" | custom-call | flops 6039797760 | bytes 2752512 | tf_op jit(solution)/shard_map/cond/branch_1_fun/attend_back/pallas_call | solution.py:205
  591.0 6.9 fusion.106
  597.9 10.5 %all-to-all-done.13 = bf16[4,1,192,768]{3,2,1,0:T(8,128)(2,1)S(1)} async-done(((bf16[4,1,192,768]{3,2,1,0:T(8,128)(2,1)}), bf16[4,1,192,768]{3,2,1,0:T(8,128)(2,1)S(1)}, u32[]{:S(2)}, u32[]{:S(2)}) %all-to-all-start.13) | async-done | bytes 1179680 | tf_op jit(solution)/shard_map/cond/branch_1_fun/all_to_all | solution.py:221
  625.3 15.4 %all-to-all-done.12 = bf16[4,1,192,768]{3,2,1,0:T(8,128)(2,1)} async-done(((bf16[4,1,192,768]{3,2,1,0:T(8,128)(2,1)}), bf16[4,1,192,768]{3,2,1,0:T(8,128)(2,1)}, u32[]{:S(2)}, u32[]{:S(2)}) %all-to-all-start.12) | async-done | bytes 1179680 | tf_op jit(solution)/shard_map/cond/branch_1_fun/all_to_all | solution.py:221
  651.0 74.4 %line_sum.6 = (bf16[512,1024]{1,0:T(8,128)(2,1)}, bf16[128,4096]{1,0:T(8,128)(2,1)}, bf16[48,1920]{1,0:T(8,128)(2,1)}, bf16[192,384]{1,0:T(8,128)(2,1)}) custom-call(bf16[512,1024]{1,0:T(8,128)(2,1)} %reduce-scatter.25.cloned.1.call-done.refs_0_, bf16[128,4096]{1,0:T(8,128)(2,1)} %reduce-scatter.29.cloned.1.call-done.refs_1_, ...), custom_call_target="tpu_custom_call" | custom-call | bytes 97157120 | tf_op jit(solution)/shard_map/cond/branch_1_fun/line_sum/pallas_call | solution.py:444
  732.3 36.8 %line_sum.7 = (bf16[128,1536]{1,0:T(8,128)(2,1)}, bf16[4,128,1152]{2,1,0:T(8,128)(2,1)}) custom-call(bf16[128,2688]{1,0:T(8,128)(2,1)} %reduce-scatter.27.cloned.1.call-done.refs_0_), custom_call_target="tpu_custom_call" | custom-call | bytes 27525120 | tf_op jit(solution)/shard_map/cond/branch_1_fun/line_sum/pallas_call | solution.py:444
  (537 shorter events, 255.9 us)
Async XLA Ops:
  7.2 53.2 %all-gather.45.cloned.1.call-start = ((), (), s32[]{:S(2)}) async-start(), calls=%async_computation.48 | async-start | bytes 7077888 | tf_op jit(solution)/shard_map/all_gather | solution.py:225
  35.3 25.1 %copy-start.85 = (bf16[48,1152]{1,0:T(8,128)(2,1)S(1)}, bf16[48,1152]{1,0:T(8,128)(2,1)}, u32[]{:S(2)}) copy-start(bf16[48,1152]{1,0:T(8,128)(2,1)} %param.60) | copy-start | bytes 331780
  35.3 25.2 %copy-start.94 = (bf16[48,384]{1,0:T(8,128)(2,1)S(1)}, bf16[48,384]{1,0:T(8,128)(2,1)}, u32[]{:S(2)}) copy-start(bf16[48,384]{1,0:T(8,128)(2,1)} %param.63) | copy-start | bytes 110596
  66.3 34.1 %copy-start.103 = (f32[1024]{0:T(1024)}, f32[1024]{0:T(1024)S(1)}, u32[]{:S(2)}) copy-start(f32[1024]{0:T(1024)S(1)} %get-tuple-element.399) | copy-start | bytes 12292 | tf_op jit(solution)/shard_map/conditional.1
  66.3 147.9 %copy-start.91 = (f32[8,1,128]{2,1,0:T(1,128)}, f32[8,1,128]{2,1,0:T(1,128)S(1)}, u32[]{:S(2)}) copy-start(f32[8,1,128]{2,1,0:T(1,128)S(1)} %get-tuple-element.369) | copy-start | bytes 12292 | tf_op jit(solution)/shard_map/conditional.1
  66.3 133.5 %all-gather.31.cloned.1.call-start = ((), (), s32[]{:S(2)}) async-start(), calls=%async_computation.36 | async-start | bytes 2359296 | tf_op jit(solution)/shard_map/cond/branch_1_fun/all_gather | solution.py:225
  67.0 147.1 %all-gather.33.cloned.1.call-start = ((), (), s32[]{:S(2)}) async-start(), calls=%async_computation.37 | async-start | bytes 9437184 | tf_op jit(solution)/shard_map/cond/branch_1_fun/all_gather | solution.py:225
  72.8 76.1 %all-to-all-start.7 = ((bf16[4,2,192,1024]{3,2,1,0:T(8,128)(2,1)}), bf16[4,2,192,1024]{3,2,1,0:T(8,128)(2,1)}, u32[]{:S(2)}, u32[]{:S(2)}) async-start(bf16[4,2,192,1024]{3,2,1,0:T(8,128)(2,1)} %broadcast_in_dim.166), calls=%async_computation.12 | async-start | bytes 6291456 | tf_op jit(solution)/shard_map/cond/branch_1_fun/all_to_all | solution.py:221
  77.5 136.7 %all-gather.35.cloned.1.call-start = ((), (), s32[]{:S(2)}) async-start(), calls=%async_computation.38 | async-start | bytes 9437184 | tf_op jit(solution)/shard_map/cond/branch_1_fun/all_gather | solution.py:225
  160.4 111.5 %all-gather.39.cloned.1.call-start = ((), (), s32[]{:S(2)}) async-start(), calls=%async_computation.40 | async-start | bytes 1327104 | tf_op jit(solution)/shard_map/cond/branch_1_fun/all_gather | solution.py:225
  176.4 23.4 %copy-start.152 = (f32[8,1,128]{2,1,0:T(1,128)S(1)}, f32[8,1,128]{2,1,0:T(1,128)}, u32[]{:S(2)}) copy-start(f32[8,1,128]{2,1,0:T(1,128)} %get-tuple-element.368) | copy-start | bytes 12292 | tf_op jit(solution)/shard_map/conditional.1
  210.2 63.2 %all-gather.41.cloned.1.call-start = ((), (), s32[]{:S(2)}) async-start(), calls=%async_computation.41 | async-start | bytes 1505280 | tf_op jit(solution)/shard_map/cond/branch_1_fun/all_gather | solution.py:806
  214.1 22.9 %copy-start.126 = (f32[384]{0:T(512)S(1)}, f32[384]{0:T(512)}, u32[]{:S(2)}) copy-start(f32[384]{0:T(512)} %get-tuple-element.378) | copy-start | bytes 4612 | tf_op jit(solution)/shard_map/conditional.1
  214.2 22.9 %copy-start.132 = (pred[784]{0:T(1024)(128)(4,1)S(1)}, pred[784]{0:T(1024)(128)(4,1)}, u32[]{:S(2)}) copy-start(pred[784]{0:T(1024)(128)(4,1)} %broadcast_in_dim.213) | copy-start | bytes 2356 | tf_op jit(solution)/shard_map/conditional.1
  214.2 22.9 %copy-start.143 = (f32[384]{0:T(512)S(1)}, f32[384]{0:T(512)}, u32[]{:S(2)}) copy-start(f32[384]{0:T(512)} %add.624) | copy-start | bytes 4612 | tf_op jit(solution)/shard_map/conditional.1
  214.2 22.9 %copy-start.150 = (pred[784]{0:T(1024)(128)(4,1)S(1)}, pred[784]{0:T(1024)(128)(4,1)}, u32[]{:S(2)}) copy-start(pred[784]{0:T(1024)(128)(4,1)} %compare_and_fusion.1) | copy-start | bytes 2356 | tf_op jit(solution)/shard_map/conditional.1
  243.3 61.8 %all-gather.37.cloned.1.call-start = ((), (), s32[]{:S(2)}) async-start(), calls=%async_computation.39 | async-start | bytes 1505280 | tf_op jit(solution)/shard_map/cond/branch_1_fun/all_gather | solution.py:806
  254.5 81.0 %all-gather.43.cloned.1.call-start = ((), (), s32[]{:S(2)}) async-start(), calls=%async_computation.42 | async-start | bytes 1327104 | tf_op jit(solution)/shard_map/cond/branch_1_fun/all_gather | solution.py:225
  273.4 182.1 %reduce-scatter.23.cloned.1.call-start = ((), (), s32[]{:S(2)}) async-start(), calls=%async_computation.44 | async-start | bytes 1327104 | tf_op jit(solution)/shard_map/cond/branch_1_fun/reduce_scatter | solution.py:229
  277.7 27.3 %copy-start.51 = (bf16[384,1152]{1,0:T(8,128)(2,1)S(1)}, bf16[384,1152]{1,0:T(8,128)(2,1)}, u32[]{:S(2)}) copy-start(bf16[384,1152]{1,0:T(8,128)(2,1)} %all_gather.57) | copy-start | bytes 2654212 | tf_op jit(solution)/shard_map/conditional.1
  355.1 23.2 %all-to-all-start.8 = ((bf16[4,2,392,96]{2,1,3,0:T(2,128)(2,1)}), bf16[4,2,392,96]{2,1,3,0:T(2,128)(2,1)S(1)}, u32[]{:S(2)}, u32[]{:S(2)}) async-start(bf16[4,2,392,96]{2,1,3,0:T(2,128)(2,1)} %reshape.1178), calls=%async_computation.13 | async-start | bytes 1572864 | tf_op jit(solution)/shard_map/cond/branch_1_fun/all_to_all | solution.py:221
  358.6 96.9 %reduce-scatter.21.cloned.1.call-start = ((), (), s32[]{:S(2)}) async-start(), calls=%async_computation.43 | async-start | bytes 1658880 | tf_op jit(solution)/shard_map/cond/branch_1_fun/reduce_scatter | solution.py:229
  384.4 31.3 %copy-start.53 = (bf16[4,1,392,96]{2,1,3,0:T(2,128)(2,1)S(1)}, bf16[4,1,392,96]{2,1,3,0:T(2,128)(2,1)}, u32[]{:S(2)}) copy-start(bf16[4,1,392,96]{2,1,3,0:T(2,128)(2,1)} %get-tuple-element.896) | copy-start | bytes 903172 | tf_op jit(solution)/shard_map/conditional.1
  419.8 38.2 %all-to-all-start.10 = ((bf16[4,1,392,288]{2,3,1,0:T(8,128)(2,1)}), bf16[4,1,392,288]{2,3,1,0:T(8,128)(2,1)}, u32[]{:S(2)}, u32[]{:S(2)}) async-start(bf16[4,1,392,288]{2,3,1,0:T(8,128)(2,1)} %copy.340), calls=%async_computation.17 | async-start | bytes 2359296 | tf_op jit(solution)/shard_map/cond/branch_1_fun/all_to_all | solution.py:221
  458.0 32.6 %all-to-all-start.9 = ((bf16[4,1,392,288]{2,3,1,0:T(8,128)(2,1)}), bf16[4,1,392,288]{2,3,1,0:T(8,128)(2,1)}, u32[]{:S(2)}, u32[]{:S(2)}) async-start(bf16[4,1,392,288]{2,3,1,0:T(8,128)(2,1)} %copy.334), calls=%async_computation.16 | async-start | bytes 2359296 | tf_op jit(solution)/shard_map/cond/branch_1_fun/all_to_all | solution.py:221
  463.1 177.7 %reduce-scatter.25.cloned.1.call-start = ((), (), s32[]{:S(2)}) async-start(), calls=%async_computation.45 | async-start | bytes 9437184 | tf_op jit(solution)/shard_map/cond/branch_1_fun/reduce_scatter | solution.py:229
  505.9 145.1 %reduce-scatter.29.cloned.1.call-start = ((), (), s32[]{:S(2)}) async-start(), calls=%async_computation.47 | async-start | bytes 9437184 | tf_op jit(solution)/shard_map/cond/branch_1_fun/reduce_scatter | solution.py:229
  543.3 23.6 %all-to-all-start.11 = ((bf16[4,2,192,256]{3,2,1,0:T(8,128)(2,1)}), bf16[4,2,192,256]{3,2,1,0:T(8,128)(2,1)}, u32[]{:S(2)}, u32[]{:S(2)}) async-start(bf16[4,2,192,256]{3,2,1,0:T(8,128)(2,1)} %bitcast.158), calls=%async_computation.18 | async-start | bytes 1572864 | tf_op jit(solution)/shard_map/cond/branch_1_fun/all_to_all | solution.py:221
  576.9 31.5 %all-to-all-start.13 = ((bf16[4,1,192,768]{3,2,1,0:T(8,128)(2,1)}), bf16[4,1,192,768]{3,2,1,0:T(8,128)(2,1)S(1)}, u32[]{:S(2)}, u32[]{:S(2)}) async-start(bf16[4,1,192,768]{3,2,1,0:T(8,128)(2,1)} %attend_back.15), calls=%async_computation.21 | async-start | bytes 2359296 | tf_op jit(solution)/shard_map/cond/branch_1_fun/all_to_all | solution.py:221
  608.4 32.4 %all-to-all-start.12 = ((bf16[4,1,192,768]{3,2,1,0:T(8,128)(2,1)}), bf16[4,1,192,768]{3,2,1,0:T(8,128)(2,1)}, u32[]{:S(2)}, u32[]{:S(2)}) async-start(bf16[4,1,192,768]{3,2,1,0:T(8,128)(2,1)} %attend_back.14), calls=%async_computation.19 | async-start | bytes 2359296 | tf_op jit(solution)/shard_map/cond/branch_1_fun/all_to_all | solution.py:221
  612.7 119.6 %reduce-scatter.27.cloned.1.call-start = ((), (), s32[]{:S(2)}) async-start(), calls=%async_computation.46 | async-start | bytes 6193152 | tf_op jit(solution)/shard_map/cond/branch_1_fun/reduce_scatter | solution.py:229
  651.0 75.8 %copy-start.55 = (f32[192,1024]{1,0:T(8,128)S(1)}, f32[192,1024]{1,0:T(8,128)}, u32[]{:S(2)}) copy-start(f32[192,1024]{1,0:T(8,128)} %copy-done.54) | copy-start | bytes 2359300 | tf_op jit(solution)/shard_map/conditional.1
  (127 other events, 703.7 us)
Sparse Core Ops, SparseCore 0:
  10.5 49.8 all-gather.44
  69.2 28.1 all-gather.30
  99.4 57.4 all-gather.32
  160.5 52.7 all-gather.34
  215.2 24.0 all-gather.38
  243.4 29.9 all-gather.40
  275.1 29.9 all-gather.36
  307.1 23.1 all-gather.42
  349.4 35.8 reduce-scatter.22
  389.2 37.7 reduce-scatter.20
  506.0 70.3 reduce-scatter.24
  579.7 71.2 reduce-scatter.28
  654.9 57.8 reduce-scatter.26
